TPU v7x, 32 devices: a whole 2x2x4 slice. The times are simulated.
32 devices in a mesh: dp: 8 (over z, x), code: 4 (over y, core).
Axes of the slice: x: 2, y: 2, z: 4, core: 2. Of those that a mesh axis runs over, the one named last changes fastest.
Arguments:
- tokens: int32 [2, 8, 4, 256], P(None, 'dp'), may hold values from 0 to 1023
- masked: int32 [2, 8, 4, 256], P(None, 'dp'), may hold values from 0 to 1, as said below
- small_grid: int32 [2, 8], P(None, 'dp'), may hold values from 0 to 1, as said below
- domains: int32 [2, 8, 4], P(None, 'dp'), may hold values from 0 to 3, as said below
- attend_in: float32 [2, 1024, 3072], P(None, ('dp', 'code')), may hold values from -0.1875 to 0.1875
- attend_out: float32 [2, 1024, 1024], P(None, ('dp', 'code')), may hold values from -0.75 to 0.75
- expand: float32 [1024, 4096], P(('dp', 'code')), may hold values from -0.1875 to 0.1875
- contract: float32 [4096, 1024], P(('dp', 'code')), may hold values from -0.09375 to 0.09375
- gains: float32 [5, 1024], P(None, ('dp', 'code')), may hold values from 0.1 to 1.9
- tables: float32 [2, 1024, 1024], P(None, 'code'), may hold values from -0.1875 to 0.1875
- mean_in: float32 [2, 1024, 3072], P(None, ('dp', 'code')), may hold values from -7.1525574e-07 to 7.1525574e-07
- mean_out: float32 [2, 1024, 1024], P(None, ('dp', 'code')), may hold values from -7.1525574e-07 to 7.1525574e-07
- mean_expand: float32 [1024, 4096], P(('dp', 'code')), may hold values from -7.1525574e-07 to 7.1525574e-07
- mean_contract: float32 [4096, 1024], P(('dp', 'code')), may hold values from -7.1525574e-07 to 7.1525574e-07
- mean_gains: float32 [5, 1024], P(None, ('dp', 'code')), may hold values from -7.6293945e-06 to 7.6293945e-06
- mean_tables: float32 [2, 1024, 1024], P(None, 'code'), may hold values from -7.1525574e-07 to 7.1525574e-07
- square_in: float32 [2, 1024, 3072], P(None, ('dp', 'code')), may hold values from 6.965231e-14 to 2.7874166e-13
- square_out: float32 [2, 1024, 1024], P(None, ('dp', 'code')), may hold values from 6.965231e-14 to 2.7874166e-13
- square_expand: float32 [1024, 4096], P(('dp', 'code')), may hold values from 6.965231e-14 to 2.7874166e-13
- square_contract: float32 [4096, 1024], P(('dp', 'code')), may hold values from 6.965231e-14 to 2.7874166e-13
- square_gains: float32 [5, 1024], P(None, ('dp', 'code')), may hold values from 6.9652313e-12 to 2.7874167e-11
- square_tables: float32 [2, 1024, 1024], P(None, 'code'), may hold values from 6.965231e-14 to 2.7874166e-13
Outputs:
- total_loss: float32 [], replicated
- gradient_norm: float32 [], replicated
- updated_in: float32 [2, 1024, 3072], P(None, ('dp', 'code'))
- updated_out: float32 [2, 1024, 1024], P(None, ('dp', 'code'))
- updated_expand: float32 [1024, 4096], P(('dp', 'code'))
- updated_contract: float32 [4096, 1024], P(('dp', 'code'))
- updated_gains: float32 [5, 1024], P(None, ('dp', 'code'))
- updated_tables: float32 [2, 1024, 1024], P(None, 'code')
- averaged_in: float32 [2, 1024, 3072], P(None, ('dp', 'code'))
- averaged_out: float32 [2, 1024, 1024], P(None, ('dp', 'code'))
- averaged_expand: float32 [1024, 4096], P(('dp', 'code'))
- averaged_contract: float32 [4096, 1024], P(('dp', 'code'))
- averaged_gains: float32 [5, 1024], P(None, ('dp', 'code'))
- averaged_tables: float32 [2, 1024, 1024], P(None, 'code')
- squared_in: float32 [2, 1024, 3072], P(None, ('dp', 'code'))
- squared_out: float32 [2, 1024, 1024], P(None, ('dp', 'code'))
- squared_expand: float32 [1024, 4096], P(('dp', 'code'))
- squared_contract: float32 [4096, 1024], P(('dp', 'code'))
- squared_gains: float32 [5, 1024], P(None, ('dp', 'code'))
- squared_tables: float32 [2, 1024, 1024], P(None, 'code')
Inputs may be any that keep to these rules, and one draw needn't show every extreme that they name: In micro-batch 1 no token whose clip has domain 3 is masked. `small_grid`: group 0 holds four small clips in micro-batch 0 and one large clip in micro-batch 1. `domains`: clip 0 of group 0 in micro-batch 1 has domain 3.
All inputs are finite; a program needn't handle non-finite values.
Results may differ from a plain program's by a relative error of at most 0.0065.
The roundings to bfloat16 on the way count: a program that leaves them out, or rounds other values in their place, can miss the bound.
Values may be sent and summed in bfloat16 or wider, within the bound.
No kernel may reach another device: no remote copies, remote signals or barrier semaphores. Data moves between devices by JAX's collectives and lax.ppermute only.
A program may use at most 320 MiB of HBM per device.

v0:
```python
import jax
import jax.numpy as jnp
from jax import lax
from jax.sharding import PartitionSpec as P

D = 1024
HEADS = 16
HEAD = 64
FRAMES = 4
SLOTS = 256
SMALL_TOKENS = 64
CLIPS = 4
DOMAINS = 4
MICRO = 2
STEP = 10


EPS = 1e-05
NEG = -1e30
BETA_ONE = 0.9
BETA_TWO = 0.95
ADAM_EPS = 1e-08
DECAY = 0.1
RATE = 0.02
RATE_SMALL = 0.2
CLIP = 0.005
HIGH = lax.Precision.HIGHEST


def merged(array, axis, combine):
    everything = jax.tree.map(lambda part: lax.all_gather(part, axis), array)
    initial = jax.tree.map(lambda part: part[0], everything)

    def turn(k, so_far):
        return combine(so_far, jax.tree.map(lambda part: part[k], everything))

    return lax.fori_loop(1, lax.axis_size(axis), turn, initial)


def as_sent(array):

    def short(part):
        return part.astype(jnp.bfloat16) if part.dtype == jnp.float32 else part

    return jax.tree.map(short, array)


def norm_forward(values, gain):
    return values * lax.rsqrt(jnp.mean(values * values, axis=-1, keepdims=True) + EPS) * gain


def norm_backward(values, gain, upstream):
    factor = lax.rsqrt(jnp.mean(values * values, axis=-1, keepdims=True) + EPS)
    scaled = upstream * gain
    inward = factor * scaled - values * factor**3 * jnp.mean(
        scaled * values, axis=-1, keepdims=True
    )
    gain_grad = jnp.sum((upstream * values * factor).reshape(-1, values.shape[-1]), axis=0)
    return (inward, gain_grad)


def project(left, right):
    return jnp.einsum("abd,dn->abn", left, right, preferred_element_type=jnp.float32)


def split_heads(packed):
    parts = packed.reshape(packed.shape[0], packed.shape[1], 3, HEADS, HEAD)
    return (parts[:, :, 0], parts[:, :, 1], parts[:, :, 2])


def masked_scores(query, key, allowed, row, col):
    scores = jnp.einsum(
        row + "he," + col + "he->bhqk", query, key, preferred_element_type=jnp.float32
    ) * HEAD ** (-0.5)
    return jnp.where(allowed, scores, NEG)


def attend_forward(normed, w_in, w_out, allowed, row, col):
    first, second = (normed.shape[0], normed.shape[1])
    packed = project(normed, w_in).astype(jnp.bfloat16)
    query, key, value = split_heads(packed)
    scores = masked_scores(query, key, allowed, row, col)
    top = jnp.max(scores, axis=-1, keepdims=True)
    expd = jnp.exp(scores - top)
    summed = jnp.sum(expd, axis=-1, keepdims=True)
    probs = (expd / summed).astype(jnp.bfloat16)
    mixed = jnp.einsum(
        "bhqk," + col + "he->" + row + "he", probs, value, preferred_element_type=jnp.float32
    )
    mixed = mixed.reshape(first, second, D).astype(jnp.bfloat16)
    return (project(mixed, w_out), (packed, mixed, top + jnp.log(summed)))


def attend_backward(normed, w_in, w_out, allowed, row, col, kept, upstream):
    packed, mixed, log_total = kept
    first, second = (normed.shape[0], normed.shape[1])
    up_low = upstream.astype(jnp.bfloat16)
    grad_out = jnp.einsum("abd,abn->dn", mixed, up_low, preferred_element_type=jnp.float32)
    grad_mixed = jnp.einsum("abn,dn->abd", up_low, w_out, preferred_element_type=jnp.float32)
    grad_mixed = grad_mixed.astype(jnp.bfloat16).reshape(first, second, HEADS, HEAD)
    query, key, value = split_heads(packed)
    probs = jnp.exp(masked_scores(query, key, allowed, row, col) - log_total)
    grad_value = jnp.einsum(
        "bhqk," + row + "he->" + col + "he",
        probs.astype(jnp.bfloat16),
        grad_mixed,
        preferred_element_type=jnp.float32,
    )
    grad_probs = jnp.einsum(
        row + "he," + col + "he->bhqk", grad_mixed, value, preferred_element_type=jnp.float32
    )
    grad_scores = (
        probs * (grad_probs - jnp.sum(probs * grad_probs, axis=-1, keepdims=True)) * HEAD ** (-0.5)
    )
    grad_scores = grad_scores.astype(jnp.bfloat16)
    grad_query = jnp.einsum(
        "bhqk," + col + "he->" + row + "he", grad_scores, key, preferred_element_type=jnp.float32
    )
    grad_key = jnp.einsum(
        "bhqk," + row + "he->" + col + "he", grad_scores, query, preferred_element_type=jnp.float32
    )
    grad_packed = jnp.concatenate(
        [piece.reshape(first, second, D) for piece in (grad_query, grad_key, grad_value)], axis=-1
    )
    grad_packed = grad_packed.astype(jnp.bfloat16)
    grad_in = jnp.einsum("abd,abn->dn", normed, grad_packed, preferred_element_type=jnp.float32)
    grad_normed = jnp.einsum("abn,dn->abd", grad_packed, w_in, preferred_element_type=jnp.float32)
    return (grad_normed, grad_in, grad_out)


def combine_rows(left, right):
    top = jnp.maximum(left[0], right[0])
    return (
        top,
        left[1] * jnp.exp(left[0] - top) + right[1] * jnp.exp(right[0] - top),
        left[2] + right[2],
    )


def reduce_all(layer_grads, table_grad):
    shards = (
        lax.psum_scatter(layer_grads[0], ("dp", "code"), scatter_dimension=1, tiled=True),
        lax.psum_scatter(layer_grads[1], ("dp", "code"), scatter_dimension=1, tiled=True),
        lax.psum_scatter(layer_grads[2], ("dp", "code"), scatter_dimension=0, tiled=True),
        lax.psum_scatter(layer_grads[3], ("dp", "code"), scatter_dimension=0, tiled=True),
        lax.psum_scatter(layer_grads[4], ("dp", "code"), scatter_dimension=1, tiled=True),
    )
    table_sum = lax.psum(table_grad, "dp")
    return (tuple(shards), table_sum)


def adamw(weight, grad, first, second, rate, decay):
    first_new = BETA_ONE * first + (1.0 - BETA_ONE) * grad
    second_new = BETA_TWO * second + (1.0 - BETA_TWO) * grad * grad
    unbiased_first = first_new / (1.0 - BETA_ONE**STEP)
    unbiased_second = second_new / (1.0 - BETA_TWO**STEP)
    updated = weight - rate * (
        unbiased_first / (jnp.sqrt(unbiased_second) + ADAM_EPS) + decay * weight
    )
    return (updated, first_new, second_new)


def on_device(
    tokens,
    masked,
    small_grid,
    domains,
    attend_in,
    attend_out,
    expand,
    contract,
    gains,
    tables,
    mean_in,
    mean_out,
    mean_expand,
    mean_contract,
    mean_gains,
    mean_tables,
    square_in,
    square_out,
    square_expand,
    square_contract,
    square_gains,
    square_tables,
):
    w_in, w_out, w_up, w_down, gain_low = (
        lax.all_gather(attend_in.astype(jnp.bfloat16), ("dp", "code"), axis=1, tiled=True),
        lax.all_gather(attend_out.astype(jnp.bfloat16), ("dp", "code"), axis=1, tiled=True),
        lax.all_gather(expand.astype(jnp.bfloat16), ("dp", "code"), axis=0, tiled=True),
        lax.all_gather(contract.astype(jnp.bfloat16), ("dp", "code"), axis=0, tiled=True),
        lax.all_gather(gains.astype(jnp.bfloat16), ("dp", "code"), axis=1, tiled=True),
    )
    gain_all = gain_low.astype(jnp.float32)
    table_low = tables.astype(jnp.bfloat16)
    code_index = lax.axis_index("code")
    rows_local = tables.shape[1]
    frames_local = FRAMES // lax.axis_size("code")
    slot_ids = jnp.arange(SLOTS)
    frame_ids = jnp.arange(FRAMES)
    causal = frame_ids[None, :] <= frame_ids[:, None]
    clip_of = jnp.where(small_grid > 0, slot_ids[None, :] // SMALL_TOKENS, 0)
    dom_slot = jnp.sum(
        (clip_of[:, :, None] == jnp.arange(CLIPS)[None, None, :]) * domains[:, 0][:, None, :],
        axis=-1,
    )
    domain_hot = (dom_slot[:, :, None] == jnp.arange(DOMAINS)[None, None, :]).astype(jnp.float32)
    mask_f = masked[:, 0].astype(jnp.float32)
    local_counts = jnp.einsum("mfs,msd->md", mask_f, domain_hot, precision=HIGH)
    counts = lax.psum(local_counts, "dp")
    scale = 1.0 / (MICRO * DOMAINS * jnp.maximum(counts, 1.0))
    token_weight = mask_f * jnp.einsum("msd,md->ms", domain_hot, scale, precision=HIGH)[:, None, :]
    code_ids = jnp.arange(rows_local)
    layer_sum = None
    table_total = None
    loss_part = jnp.zeros((), jnp.float32)
    for micro in range(MICRO):
        codes = tokens[micro, 0]
        hidden_mask = mask_f[micro]
        weight_all = token_weight[micro]
        own_mask = lax.dynamic_slice_in_dim(hidden_mask, code_index * frames_local, frames_local, 0)
        local_id = codes - code_index * rows_local
        present = (local_id >= 0) & (local_id < rows_local) & (hidden_mask == 0)
        picked = jnp.take(table_low[0], jnp.clip(local_id, 0, rows_local - 1), axis=0).astype(
            jnp.float32
        )
        picked = picked * present[:, :, None]
        looked = lax.psum_scatter(
            picked.astype(jnp.bfloat16), "code", scatter_dimension=0, tiled=True
        ).astype(jnp.float32)
        start = jnp.where(own_mask[:, :, None] > 0, gain_all[4], looked)
        segment = jnp.where(small_grid[micro, 0] > 0, slot_ids // SMALL_TOKENS, 0)
        within = segment[:, None] == segment[None, :]
        normed_space = norm_forward(start, gain_all[0]).astype(jnp.bfloat16)
        branch_space, kept_space = attend_forward(
            normed_space, w_in[0], w_out[0], within, "bq", "bk"
        )
        after_space = lax.all_to_all(
            start + branch_space, "code", split_axis=1, concat_axis=0, tiled=True
        )
        normed_time = norm_forward(after_space, gain_all[1]).astype(jnp.bfloat16)
        branch_time, kept_time = attend_forward(normed_time, w_in[1], w_out[1], causal, "qb", "kb")
        after_time = after_space + branch_time
        normed_ffn = norm_forward(after_time, gain_all[2]).astype(jnp.bfloat16)
        pre = project(normed_ffn, w_up)
        activ = jax.nn.gelu(pre, approximate=True).astype(jnp.bfloat16)
        after_ffn = after_time + project(activ, w_down)
        final = norm_forward(after_ffn, gain_all[3]).astype(jnp.bfloat16)
        whole = lax.all_gather(final, "code", axis=1, tiled=True)
        flat_hidden = whole.reshape(-1, D)
        head_low = table_low[1]
        logits = lax.dot_general(
            flat_hidden, head_low, (((1,), (1,)), ((), ())), preferred_element_type=jnp.float32
        )
        hits = local_id.reshape(-1)[:, None] == code_ids[None, :]
        local_top = jnp.max(logits, axis=1)
        local_target = jnp.sum(jnp.where(hits, logits, 0.0), axis=1)
        top, row_total, target = merged(
            (local_top, jnp.sum(jnp.exp(logits - local_top[:, None]), axis=1), local_target),
            "code",
            combine_rows,
        )
        log_total = top + jnp.log(row_total)
        weight_flat = weight_all.reshape(-1)
        loss_part = loss_part + jnp.where(
            code_index == 0, jnp.sum(weight_flat * (log_total - target)), 0.0
        )
        grad_logits = (weight_flat[:, None] * (jnp.exp(logits - log_total[:, None]) - hits)).astype(
            jnp.bfloat16
        )
        head_grad = lax.dot_general(
            grad_logits, flat_hidden, (((0,), (0,)), ((), ())), preferred_element_type=jnp.float32
        )
        back_hidden = jnp.dot(grad_logits, head_low, preferred_element_type=jnp.float32)
        grad_final = lax.psum_scatter(
            back_hidden.reshape(FRAMES, SLOTS, D).astype(jnp.bfloat16),
            "code",
            scatter_dimension=1,
            tiled=True,
        ).astype(jnp.float32)
        grad_ffn, gain_three = norm_backward(after_ffn, gain_all[3], grad_final)
        up_low = grad_ffn.astype(jnp.bfloat16)
        grad_down = jnp.einsum("abn,abd->nd", activ, up_low, preferred_element_type=jnp.float32)
        grad_activ = jnp.einsum("abd,nd->abn", up_low, w_down, preferred_element_type=jnp.float32)
        grad_pre = jax.vjp(lambda inner: jax.nn.gelu(inner, approximate=True), pre)[1](grad_activ)[
            0
        ].astype(jnp.bfloat16)
        grad_up = jnp.einsum(
            "abd,abn->dn", normed_ffn, grad_pre, preferred_element_type=jnp.float32
        )
        inward, gain_two = norm_backward(
            after_time,
            gain_all[2],
            jnp.einsum("abn,dn->abd", grad_pre, w_up, preferred_element_type=jnp.float32),
        )
        grad_time = grad_ffn + inward
        grad_normed, grad_in_time, grad_out_time = attend_backward(
            normed_time, w_in[1], w_out[1], causal, "qb", "kb", kept_time, grad_time
        )
        inward, gain_one = norm_backward(after_space, gain_all[1], grad_normed)
        grad_space = lax.all_to_all(
            (grad_time + inward).astype(jnp.bfloat16),
            "code",
            split_axis=0,
            concat_axis=1,
            tiled=True,
        ).astype(jnp.float32)
        grad_normed, grad_in_space, grad_out_space = attend_backward(
            normed_space, w_in[0], w_out[0], within, "bq", "bk", kept_space, grad_space
        )
        inward, gain_zero = norm_backward(start, gain_all[0], grad_normed)
        grad_start = grad_space + inward
        mask_grad = jnp.sum((grad_start * own_mask[:, :, None]).reshape(-1, D), axis=0)
        every_grad = lax.all_gather(as_sent(grad_start), "code", axis=0, tiled=True).astype(
            grad_start.dtype
        )
        chosen = (
            (local_id.reshape(-1)[:, None] == code_ids[None, :])
            & (hidden_mask.reshape(-1) == 0)[:, None]
        ).astype(jnp.float32)
        embed_grad = lax.dot_general(
            chosen, every_grad.reshape(-1, D), (((0,), (0,)), ((), ())), precision=HIGH
        )
        layer_grads = (
            jnp.stack([grad_in_space, grad_in_time]),
            jnp.stack([grad_out_space, grad_out_time]),
            grad_up,
            grad_down,
            jnp.stack([gain_zero, gain_one, gain_two, gain_three, mask_grad]),
        )
        table_grad = jnp.stack([embed_grad, head_grad])
        if layer_sum is None:
            layer_sum, table_total = (layer_grads, table_grad)
        else:
            layer_sum = tuple((a + b for a, b in zip(layer_sum, layer_grads)))
            table_total = table_total + table_grad
    layer_sum, table_total = reduce_all(layer_sum, table_total)
    owned = sum((jnp.sum(g * g) for g in layer_sum))
    owned = owned + jnp.where(lax.axis_index("dp") == 0, jnp.sum(table_total * table_total), 0.0)
    square_sum, loss = lax.psum((owned, loss_part), ("dp", "code"))
    norm = jnp.sqrt(square_sum)
    factor = jnp.minimum(1.0, CLIP / (norm + 1e-06))
    params = (attend_in, attend_out, expand, contract, gains, tables)
    grads = tuple(layer_sum) + (table_total,)
    firsts = (mean_in, mean_out, mean_expand, mean_contract, mean_gains, mean_tables)
    seconds = (square_in, square_out, square_expand, square_contract, square_gains, square_tables)
    rates = (RATE, RATE, RATE, RATE, RATE_SMALL, RATE)
    decays = (DECAY, DECAY, DECAY, DECAY, 0.0, DECAY)
    results = [
        adamw(p, factor * g, f, s, r, k)
        for p, g, f, s, r, k in zip(params, grads, firsts, seconds, rates, decays)
    ]
    return (
        loss,
        norm,
        results[0][0],
        results[1][0],
        results[2][0],
        results[3][0],
        results[4][0],
        results[5][0],
        results[0][1],
        results[1][1],
        results[2][1],
        results[3][1],
        results[4][1],
        results[5][1],
        results[0][2],
        results[1][2],
        results[2][2],
        results[3][2],
        results[4][2],
        results[5][2],
    )


def solution(mesh):
    placed = (
        P(None, "dp", None, None),
        P(None, "dp", None, None),
        P(None, "dp"),
        P(None, "dp", None),
        P(None, ("dp", "code"), None),
        P(None, ("dp", "code"), None),
        P(("dp", "code"), None),
        P(("dp", "code"), None),
        P(None, ("dp", "code")),
        P(None, "code", None),
        P(None, ("dp", "code"), None),
        P(None, ("dp", "code"), None),
        P(("dp", "code"), None),
        P(("dp", "code"), None),
        P(None, ("dp", "code")),
        P(None, "code", None),
        P(None, ("dp", "code"), None),
        P(None, ("dp", "code"), None),
        P(("dp", "code"), None),
        P(("dp", "code"), None),
        P(None, ("dp", "code")),
        P(None, "code", None),
    )
    return jax.shard_map(
        on_device,
        mesh=mesh,
        in_specs=placed,
        out_specs=(
            P(),
            P(),
            P(None, ("dp", "code"), None),
            P(None, ("dp", "code"), None),
            P(("dp", "code"), None),
            P(("dp", "code"), None),
            P(None, ("dp", "code")),
            P(None, "code", None),
            P(None, ("dp", "code"), None),
            P(None, ("dp", "code"), None),
            P(("dp", "code"), None),
            P(("dp", "code"), None),
            P(None, ("dp", "code")),
            P(None, "code", None),
            P(None, ("dp", "code"), None),
            P(None, ("dp", "code"), None),
            P(("dp", "code"), None),
            P(("dp", "code"), None),
            P(None, ("dp", "code")),
            P(None, "code", None),
        ),
        check_vma=False,
    )
```

profile of v0, /device:TPU:0, one launch (start us, length us, event | category | flops | bytes accessed | tf_op | source)
XLA Modules:
  0.0 1766.3 jit_solution(12722642824506199047)
XLA Ops:
  12.3 4.1 gather_fusion
  18.3 4.1 gather_fusion.1
  28.6 43.8 %all-gather.6 = bf16[32,32,5]{1,2,0:T(8,128)(2,1)S(1)} all-gather(bf16[1,32,5]{1,2,0:T(8,128)(2,1)S(1)} %convert_bitcast_fusion.2), channel_id=1, replica_groups=mesh['dp'=8,'code'=4] {'dp','code'}, dimensions={0}, use_global_device_ids=true | all-gather | bytes 10560 | tf_op jit(solution)/shard_map/all_gather | solution.py:192
  75.4 12.3 reduce-scatter.14.cloned.1.call-done
  90.5 44.4 %all-gather.16.cloned.1.call-done = bf16[2,1024,3072]{2,1,0:T(8,128)(2,1)} async-done(((bf16[2,32,3072]{2,1,0:T(8,128)(2,1)}), bf16[2,1024,3072]{2,1,0:T(8,128)(2,1)}) %all-gather.16.cloned.1.call-update) | async-done | bytes 12582928 | tf_op jit(solution)/shard_map/all_gather | solution.py:188
  134.9 6.0 fusion.44
  146.4 52.1 %all-gather.18.cloned.1.call-done = bf16[2,1024,1024]{2,1,0:T(8,128)(2,1)} async-done(((bf16[2,32,1024]{2,1,0:T(8,128)(2,1)}), bf16[2,1024,1024]{2,1,0:T(8,128)(2,1)}) %all-gather.18.cloned.1.call-update) | async-done | bytes 4194320 | tf_op jit(solution)/shard_map/all_gather | solution.py:189
  202.9 3.7 all-to-all-start
  206.6 6.0 fusion.45
  222.8 3.5 all-to-all-start.1
  228.0 16.6 all-to-all-done.1
  248.0 5.7 fusion.42
  253.7 3.8 reshape.928
  263.4 5.7 fusion.43
  269.1 3.7 reshape.935
  288.7 7.9 fusion.14
  296.6 63.3 %all-gather.22.cloned.1.call-done = bf16[4096,1024]{1,0:T(8,128)(2,1)} async-done(((bf16[128,1024]{1,0:T(8,128)(2,1)}), bf16[4096,1024]{1,0:T(8,128)(2,1)}) %all-gather.22.cloned.1.call-update) | async-done | bytes 8388624 | tf_op jit(solution)/shard_map/all_gather | solution.py:191
  360.0 7.5 multiply_reduce_fusion.13
  369.6 19.9 %psum.28 = f32[2,4]{1,0:T(2,128)S(1)} all-reduce(f32[2,4]{1,0:T(2,128)S(1)} %bitcast.619), channel_id=1, replica_groups=mesh['dp'=8,'code'=4] {'dp'}, use_global_device_ids=true, to_apply=%region_2.3 | all-reduce | flops 8 | bytes 64 | tf_op jit(solution)/shard_map/psum | solution.py:210
  395.1 5.2 all-gather.4
  400.9 5.2 all-gather.5
  406.7 5.6 all-gather.3
  422.6 29.6 %reduce-scatter.18.cloned.1.call-done = bf16[4,64,1024]{2,1,0:T(8,128)(2,1)} async-done(((bf16[4,256,1024]{2,1,0:T(8,128)(2,1)}), bf16[4,64,1024]{2,1,0:T(8,128)(2,1)}) %reduce-scatter.18.cloned.1.call-update) | async-done | bytes 524304 | tf_op jit(solution)/shard_map/reduce_scatter | solution.py:275
  455.7 11.4 fusion.31
  491.6 5.9 fusion.16
  502.7 22.0 %all-gather.24.cloned.1.call-done = bf16[4,256,1024]{2,1,0:T(8,128)(2,1)} async-done(((bf16[4,64,1024]{2,1,0:T(8,128)(2,1)}), bf16[4,256,1024]{2,1,0:T(8,128)(2,1)}) %all-gather.24.cloned.1.call-update) | async-done | bytes 2097168 | tf_op jit(solution)/shard_map/all_gather | solution.py:249
  527.9 5.6 all-gather.1
  535.5 5.6 all-gather.2
  543.2 5.6 all-gather
  550.8 5.0 while.38
  564.5 28.1 %reduce-scatter.16.cloned.1.call-done = bf16[4,64,1024]{2,1,0:T(8,128)(2,1)} async-done(((bf16[4,256,1024]{2,1,0:T(8,128)(2,1)}), bf16[4,64,1024]{2,1,0:T(8,128)(2,1)}) %reduce-scatter.16.cloned.1.call-update) | async-done | bytes 524304 | tf_op jit(solution)/shard_map/reduce_scatter | solution.py:275
  596.1 11.4 fusion.24
  630.3 3.5 fusion.94
  633.8 3.6 fusion.93
  644.8 7.1 multiply_reduce_fusion.5
  662.5 7.7 multiply_reduce_fusion.8
  671.3 3.6 all-to-all-start.2
  675.0 8.7 all-to-all-done.2
  683.7 3.5 all-to-all-start.3
  694.8 8.4 fusion.129
  703.2 8.4 fusion.132
  711.6 3.9 fusion.111
  722.8 8.4 fusion.123
  731.2 8.4 fusion.126
  742.9 5.1 fusion.35
  748.1 5.3 fusion.147
  765.1 15.1 all-gather.28.cloned.1.call-done
  780.2 3.7 convolution_bitcast_fusion.11
  783.9 20.8 %all-gather.30.cloned.1.call-done = bf16[4,256,1024]{2,1,0:T(8,128)(2,1)} async-done(((bf16[1,256,1024]{2,1,0:T(8,128)(2,1)}), bf16[4,256,1024]{2,1,0:T(8,128)(2,1)}) %all-gather.30.cloned.1.call-update) | async-done | bytes 2097168 | tf_op jit(solution)/shard_map/all_gather | solution.py:314
  814.4 4.3 maximum_add_fusion.1
  819.8 11.0 fusion.230
  830.7 11.2 bitcast_add_fusion
  842.6 4.4 fusion.199
  847.0 10.0 bitcast_add_fusion.1
  857.6 8.3 convolution_bitcast_fusion.2
  866.0 6.5 convolution_bitcast_fusion.3
  876.8 18.9 %maximum_add_fusion = f32[2,1024,3072]{2,1,0:T(8,128)} fusion(f32[1,1024,3072]{2,1,0:T(8,128)} %convolution_bitcast_fusion.3, f32[1,1024,3072]{2,1,0:T(8,128)S(1)} %convolution_bitcast_fusion.1, f32[1,1024,3072]{2,1,0:T(8,128)} %convolution_bitcast_fusion.2, f32[1,1024,3072]{2,1,0:T(8,128)S(1)} %convolution_bitcast_fusion), kind=kLoop, calls=%fused_computation.12 | loop fusion | flops 18874368 | bytes 75497472 | tf_op jit(solution)/shard_map/add | solution.py:335
  897.2 30.0 %reduce-scatter.28.cloned.1.call-done = f32[32,5]{1,0:T(8,128)} async-done(((f32[1024,5]{1,0:T(8,128)}), f32[32,5]{1,0:T(8,128)}) %reduce-scatter.28.cloned.1.call-update) | async-done | bytes 656
  932.0 146.6 %reduce-scatter.22.cloned.1.call-done = f32[2,32,1024]{2,1,0:T(8,128)} async-done(((f32[2,1024,1024]{2,1,0:T(8,128)}), f32[2,32,1024]{2,1,0:T(8,128)}) %reduce-scatter.22.cloned.1.call-update) | async-done | bytes 262160 | tf_op jit(solution)/shard_map/reduce_scatter | solution.py:143
  1080.3 179.5 %reduce-scatter.26.cloned.1.call-done = f32[128,1024]{1,0:T(8,128)} async-done(((f32[4096,1024]{1,0:T(8,128)}), f32[128,1024]{1,0:T(8,128)}) %reduce-scatter.26.cloned.1.call-update) | async-done | bytes 524304 | tf_op jit(solution)/shard_map/reduce_scatter | solution.py:145
  1261.6 185.0 %reduce-scatter.24.cloned.1.call-done = f32[32,4096]{1,0:T(8,128)} async-done(((f32[1024,4096]{1,0:T(8,128)}), f32[32,4096]{1,0:T(8,128)}) %reduce-scatter.24.cloned.1.call-update) | async-done | bytes 524304 | tf_op jit(solution)/shard_map/reduce_scatter | solution.py:144
  1448.3 248.9 %reduce-scatter.20.cloned.1.call-done = f32[2,32,3072]{2,1,0:T(8,128)} async-done(((f32[2,1024,3072]{2,1,0:T(8,128)}), f32[2,32,3072]{2,1,0:T(8,128)}) %reduce-scatter.20.cloned.1.call-update) | async-done | bytes 786448 | tf_op jit(solution)/shard_map/reduce_scatter | solution.py:142
  1702.4 40.5 %all-reduce = (f32[]{:T(128)}, f32[]{:T(128)}) all-reduce(f32[]{:T(128)S(6)} %add.508, f32[]{:T(128)S(6)} %add.529), channel_id=1, replica_groups=mesh['dp'=8,'code'=4] {'dp','code'}, use_global_device_ids=true, to_apply=%region_33.35 | all-reduce | flops 2 | bytes 16 | tf_op jit(solution)/shard_map/psum | solution.py:340
  1744.3 7.1 multiply_subtract_fusion
  (656 shorter events, 247.6 us)
Async XLA Ops:
  8.0 67.4 %reduce-scatter.12.cloned.1.call-start = ((), (), s32[]{:S(2)}) async-start(), calls=%async_computation.13 | async-start | bytes 2621440 | tf_op jit(solution)/shard_map/reduce_scatter | solution.py:228
  18.3 69.4 %reduce-scatter.14.cloned.1.call-start = ((), (), s32[]{:S(2)}) async-start(), calls=%async_computation.19 | async-start | bytes 2621440 | tf_op jit(solution)/shard_map/reduce_scatter | solution.py:228
  24.3 48.2 %copy-start.176 = (s32[2,1]{0,1:T(1,128)S(1)}, s32[2,1]{0,1:T(1,128)}, u32[]{:S(2)}) copy-start(s32[2,1]{0,1:T(1,128)} %param.30) | copy-start | bytes 28
  24.4 110.6 %all-gather.16.cloned.1.call-start = ((), (), s32[]{:S(2)}) async-start(), calls=%async_computation.14 | async-start | bytes 12976128 | tf_op jit(solution)/shard_map/all_gather | solution.py:188
  25.2 173.2 %all-gather.18.cloned.1.call-start = ((), (), s32[]{:S(2)}) async-start(), calls=%async_computation.15 | async-start | bytes 4325376 | tf_op jit(solution)/shard_map/all_gather | solution.py:189
  26.9 261.8 %all-gather.20.cloned.1.call-start = ((), (), s32[]{:S(2)}) async-start(), calls=%async_computation.16 | async-start | bytes 8650752 | tf_op jit(solution)/shard_map/all_gather | solution.py:190
  27.7 332.2 %all-gather.22.cloned.1.call-start = ((), (), s32[]{:S(2)}) async-start(), calls=%async_computation.17 | async-start | bytes 8650752 | tf_op jit(solution)/shard_map/all_gather | solution.py:191
  74.5 142.8 %copy-start.125 = (pred[256]{0:T(512)(128)(4,1)}, pred[256]{0:T(512)(128)(4,1)S(1)}, u32[]{:S(2)}) copy-start(pred[256]{0:T(512)(128)(4,1)S(1)} %broadcast_compare_fusion.4) | copy-start | bytes 772
  75.1 123.3 %copy-start.123 = (pred[256]{0:T(512)(128)(4,1)}, pred[256]{0:T(512)(128)(4,1)S(1)}, u32[]{:S(2)}) copy-start(pred[256]{0:T(512)(128)(4,1)S(1)} %broadcast_compare_fusion.5) | copy-start | bytes 772
  75.1 131.5 %copy-start.78 = (f32[1,1024]{1,0:T(1,128)}, f32[1,1024]{1,0:T(1,128)S(1)}, u32[]{:S(2)}) copy-start(f32[1,1024]{1,0:T(1,128)S(1)} %get-tuple-element.496) | copy-start | bytes 12292
  75.1 142.1 %copy-start.62 = (f32[1,1024]{1,0:T(1,128)}, f32[1,1024]{1,0:T(1,128)S(1)}, u32[]{:S(2)}) copy-start(f32[1,1024]{1,0:T(1,128)S(1)} %get-tuple-element.497) | copy-start | bytes 12292
  75.1 170.9 %copy-start.131 = (f32[1,1024]{1,0:T(1,128)}, f32[1,1024]{1,0:T(1,128)S(1)}, u32[]{:S(2)}) copy-start(f32[1,1024]{1,0:T(1,128)S(1)} %get-tuple-element.495) | copy-start | bytes 12292
  90.0 51.0 %copy-start.134 = (f32[256]{0:T(256)}, f32[256]{0:T(256)S(1)}, u32[]{:S(2)}) copy-start(f32[256]{0:T(256)S(1)} %get-tuple-element.526) | copy-start | bytes 3076
  90.5 116.1 %copy-start.136 = (f32[256]{0:T(256)}, f32[256]{0:T(256)S(1)}, u32[]{:S(2)}) copy-start(f32[256]{0:T(256)S(1)} %get-tuple-element.524) | copy-start | bytes 3076
  145.5 53.0 %copy-start.5 = (bf16[1,256,1024]{2,1,0:T(8,128)(2,1)S(1)}, bf16[1,256,1024]{2,1,0:T(8,128)(2,1)}, u32[]{:S(2)}) copy-start(bf16[1,256,1024]{2,1,0:T(8,128)(2,1)} %reduce-scatter.12.cloned.1.call-done) | copy-start | bytes 1572868
  146.4 56.5 %copy-start.41 = (bf16[16,64,256]{2,1,0:T(8,128)(2,1)}, bf16[16,64,256]{2,1,0:T(8,128)(2,1)S(1)}, u32[]{:S(2)}) copy-start(bf16[16,64,256]{2,1,0:T(8,128)(2,1)S(1)} %fusion.122) | copy-start | bytes 1572868
  202.9 19.9 %all-to-all-start = ((f32[1,256,1024]{2,0,1:T(1,128)}), f32[1,256,1024]{2,0,1:T(1,128)S(1)}, u32[]{:S(2)}, u32[]{:S(2)}) async-start(f32[1,256,1024]{2,0,1:T(1,128)} %copy.227), calls=%async_computation.1 | async-start | bytes 2097152 | tf_op jit(solution)/shard_map/all_to_all | solution.py:238
  222.8 21.7 %all-to-all-start.1 = ((f32[1,256,1024]{2,0,1:T(1,128)}), f32[1,256,1024]{2,0,1:T(1,128)S(1)}, u32[]{:S(2)}, u32[]{:S(2)}) async-start(f32[1,256,1024]{2,0,1:T(1,128)} %copy.237), calls=%async_computation.3 | async-start | bytes 2097152 | tf_op jit(solution)/shard_map/all_to_all | solution.py:238
  226.3 164.7 %all-gather.26.cloned.1.call-start = ((), (), s32[]{:S(2)}) async-start(), calls=%async_computation.20 | async-start | bytes 2621440 | tf_op jit(solution)/shard_map/all_gather | solution.py:249
  226.4 52.5 %copy-start.139 = (pred[4,4]{1,0:T(4,128)(4,1)}, pred[4,4]{1,0:T(4,128)(4,1)S(1)}, u32[]{:S(2)}) copy-start(pred[4,4]{1,0:T(4,128)(4,1)S(1)} %iota_compare_fusion.6) | copy-start | bytes 52
  228.0 25.7 %copy-start.153 = (f32[256]{0:T(256)}, f32[256]{0:T(256)S(1)}, u32[]{:S(2)}) copy-start(f32[256]{0:T(256)S(1)} %add_rsqrt_fusion.6) | copy-start | bytes 3076
  288.0 182.2 %copy-start.3 = (f32[4,64,1024]{2,1,0:T(8,128)}, f32[4,64,1024]{2,1,0:T(8,128)S(1)}, u32[]{:S(2)}) copy-start(f32[4,64,1024]{2,1,0:T(8,128)S(1)} %get-tuple-element.535) | copy-start | bytes 3145732
  288.7 181.6 %copy-start.107 = (f32[4,64]{1,0:T(4,128)}, f32[4,64]{1,0:T(4,128)S(1)}, u32[]{:S(2)}) copy-start(f32[4,64]{1,0:T(4,128)S(1)} %get-tuple-element.520) | copy-start | bytes 3076
  296.6 72.5 %copy-start.177 = (s32[2,1]{0,1:T(1,128)S(1)}, s32[2,1]{0,1:T(1,128)}, u32[]{:S(2)}) copy-start(s32[2,1]{0,1:T(1,128)} %param.30) | copy-start | bytes 28
  296.6 72.6 %copy-start.178 = (s32[2,1,4]{2,1,0:T(1,128)S(1)}, s32[2,1,4]{2,1,0:T(1,128)}, u32[]{:S(2)}) copy-start(s32[2,1,4]{2,1,0:T(1,128)} %param.31) | copy-start | bytes 100
  296.6 94.4 %copy-start.11 = (bf16[2,256,1024]{2,1,0:T(8,128)(2,1)S(1)}, bf16[2,256,1024]{2,1,0:T(8,128)(2,1)}, u32[]{:S(2)}) copy-start(bf16[2,256,1024]{2,1,0:T(8,128)(2,1)} %copy-done.10) | copy-start | bytes 3145732
  368.0 25.4 %copy-start.119 = (f32[4,64]{1,0:T(4,128)}, f32[4,64]{1,0:T(4,128)S(1)}, u32[]{:S(2)}) copy-start(f32[4,64]{1,0:T(4,128)S(1)} %get-tuple-element.522) | copy-start | bytes 3076
  369.0 83.2 %reduce-scatter.18.cloned.1.call-start = ((), (), s32[]{:S(2)}) async-start(), calls=%async_computation.22 | async-start | bytes 2621440 | tf_op jit(solution)/shard_map/reduce_scatter | solution.py:275
  390.1 26.8 %copy-start.127 = (s32[1,2,4,128]{3,1,2,0:T(2,128)}, s32[1,2,4,128]{3,1,2,0:T(2,128)S(1)}, u32[]{:S(2)}) copy-start(s32[1,2,4,128]{3,1,2,0:T(2,128)S(1)} %copy.300) | copy-start | bytes 12292
  394.4 57.8 %copy-start.120 = (f32[4,64]{1,0:T(4,128)S(1)}, f32[4,64]{1,0:T(4,128)}, u32[]{:S(2)}) copy-start(f32[4,64]{1,0:T(4,128)} %copy-done.119) | copy-start | bytes 3076
  416.8 37.4 %copy-start.142 = (f32[4,64]{1,0:T(4,128)S(1)}, f32[4,64]{1,0:T(4,128)}, u32[]{:S(2)}) copy-start(f32[4,64]{1,0:T(4,128)} %get-tuple-element.521) | copy-start | bytes 3076
  421.6 103.2 %all-gather.24.cloned.1.call-start = ((), (), s32[]{:S(2)}) async-start(), calls=%async_computation.18 | async-start | bytes 2621440 | tf_op jit(solution)/shard_map/all_gather | solution.py:249
  454.2 12.9 slice-start
  501.1 26.1 %copy-start.121 = (f32[4,64]{1,0:T(4,128)}, f32[4,64]{1,0:T(4,128)S(1)}, u32[]{:S(2)}) copy-start(f32[4,64]{1,0:T(4,128)S(1)} %get-tuple-element.518) | copy-start | bytes 3076
  502.0 90.6 %reduce-scatter.16.cloned.1.call-start = ((), (), s32[]{:S(2)}) async-start(), calls=%async_computation.21 | async-start | bytes 2621440 | tf_op jit(solution)/shard_map/reduce_scatter | solution.py:275
  502.1 39.1 %copy-start.129 = (s32[1,2,4,128]{3,1,2,0:T(2,128)}, s32[1,2,4,128]{3,1,2,0:T(2,128)S(1)}, u32[]{:S(2)}) copy-start(s32[1,2,4,128]{3,1,2,0:T(2,128)S(1)} %copy.297) | copy-start | bytes 12292
  527.2 29.9 %copy-start.34 = (f32[1024,256]{1,0:T(8,128)}, f32[1024,256]{1,0:T(8,128)S(1)}, u32[]{:S(2)}) copy-start(f32[1024,256]{1,0:T(8,128)S(1)} %get-tuple-element.546) | copy-start | bytes 3145732
  557.1 37.7 %copy-start.122 = (f32[4,64]{1,0:T(4,128)S(1)}, f32[4,64]{1,0:T(4,128)}, u32[]{:S(2)}) copy-start(f32[4,64]{1,0:T(4,128)} %copy-done.121) | copy-start | bytes 3076
  557.1 37.7 %copy-start.143 = (f32[4,64]{1,0:T(4,128)S(1)}, f32[4,64]{1,0:T(4,128)}, u32[]{:S(2)}) copy-start(f32[4,64]{1,0:T(4,128)} %get-tuple-element.517) | copy-start | bytes 3076
  559.2 36.9 %copy-start.18 = (bf16[1024,256]{1,0:T(8,128)(2,1)}, bf16[1024,256]{1,0:T(8,128)(2,1)S(1)}, u32[]{:S(2)}) copy-start(bf16[1024,256]{1,0:T(8,128)(2,1)S(1)} %multiply_convert_fusion.9) | copy-start | bytes 1572868
  562.0 45.6 %copy-start.158 = (f32[4,64]{1,0:T(4,128)}, f32[4,64]{1,0:T(4,128)S(1)}, u32[]{:S(2)}) copy-start(f32[4,64]{1,0:T(4,128)S(1)} %rsqrt.113) | copy-start | bytes 3076
  562.7 32.1 %copy-start.144 = (f32[4,64]{1,0:T(4,128)}, f32[4,64]{1,0:T(4,128)S(1)}, u32[]{:S(2)}) copy-start(f32[4,64]{1,0:T(4,128)S(1)} %rsqrt.112) | copy-start | bytes 3076
  592.6 14.9 slice-start.2
  596.1 11.5 slice-start.3
  596.1 11.5 copy-start.30
  671.3 20.8 %copy-start.13 = (bf16[256,3072]{0,1:T(8,128)(2,1)S(1)}, bf16[256,3072]{0,1:T(8,128)(2,1)}, u32[]{:S(2)}) copy-start(bf16[256,3072]{0,1:T(8,128)(2,1)} %copy-done.12) | copy-start | bytes 4718596
  671.3 12.4 all-to-all-start.2
  683.7 31.8 %all-to-all-start.3 = ((bf16[4,64,1024]{2,1,0:T(8,128)(2,1)}), bf16[4,64,1024]{2,1,0:T(8,128)(2,1)S(1)}, u32[]{:S(2)}, u32[]{:S(2)}) async-start(bf16[4,64,1024]{2,1,0:T(8,128)(2,1)} %get-tuple-element.514), calls=%async_computation.7 | async-start | bytes 1048576 | tf_op jit(solution)/shard_map/all_to_all | solution.py:301
  687.2 93.0 %all-gather.28.cloned.1.call-start = ((), (), s32[]{:S(2)}) async-start(), calls=%async_computation.27 | async-start | bytes 2621440 | tf_op jit(solution)/shard_map/all_gather | solution.py:314
  756.0 48.6 %all-gather.30.cloned.1.call-start = ((), (), s32[]{:S(2)}) async-start(), calls=%async_computation.28 | async-start | bytes 2621440 | tf_op jit(solution)/shard_map/all_gather | solution.py:314
  756.8 170.5 %reduce-scatter.28.cloned.1.call-start = ((), (), s32[]{:S(2)}) async-start(), calls=%async_computation.30 | async-start | bytes 540672
  760.5 19.7 %copy-start.130 = (s32[1,2,4,128]{3,1,2,0:T(2,128)S(1)}, s32[1,2,4,128]{3,1,2,0:T(2,128)}, u32[]{:S(2)}) copy-start(s32[1,2,4,128]{3,1,2,0:T(2,128)} %copy-done.129) | copy-start | bytes 12292
  762.2 42.5 %copy-start.128 = (s32[1,2,4,128]{3,1,2,0:T(2,128)S(1)}, s32[1,2,4,128]{3,1,2,0:T(2,128)}, u32[]{:S(2)}) copy-start(s32[1,2,4,128]{3,1,2,0:T(2,128)} %copy-done.127) | copy-start | bytes 12292
  763.9 43.7 %copy-start.36 = (f32[1,256,1024]{2,1,0:T(8,128)S(1)}, f32[1,256,1024]{2,1,0:T(8,128)}, u32[]{:S(2)}) copy-start(f32[1,256,1024]{2,1,0:T(8,128)} %convolution_bitcast_fusion.8) | copy-start | bytes 3145732
  765.0 163.6 %all-reduce.3.cloned.1.call-start = ((), (), s32[]{:S(2)}) async-start(), calls=%async_computation.29 | async-start | bytes 4194304 | tf_op jit(solution)/shard_map/psum | solution.py:148
  809.3 269.3 %reduce-scatter.22.cloned.1.call-start = ((), (), s32[]{:S(2)}) async-start(), calls=%async_computation.24 | async-start | bytes 8650752 | tf_op jit(solution)/shard_map/reduce_scatter | solution.py:143
  818.8 12.0 copy-start.49
  818.8 441.0 %reduce-scatter.26.cloned.1.call-start = ((), (), s32[]{:S(2)}) async-start(), calls=%async_computation.26 | async-start | bytes 17301504 | tf_op jit(solution)/shard_map/reduce_scatter | solution.py:145
  842.0 604.5 %reduce-scatter.24.cloned.1.call-start = ((), (), s32[]{:S(2)}) async-start(), calls=%async_computation.25 | async-start | bytes 17301504 | tf_op jit(solution)/shard_map/reduce_scatter | solution.py:144
  857.0 840.2 %reduce-scatter.20.cloned.1.call-start = ((), (), s32[]{:S(2)}) async-start(), calls=%async_computation.23 | async-start | bytes 25952256 | tf_op jit(solution)/shard_map/reduce_scatter | solution.py:142
  895.7 847.9 %copy-start.150 = (f32[5,32]{1,0:T(8,128)S(1)}, f32[5,32]{1,0:T(8,128)}, u32[]{:S(2)}) copy-start(f32[5,32]{1,0:T(8,128)} %param.36) | copy-start | bytes 1924
  895.7 847.9 %copy-start.167 = (f32[5,32]{1,0:T(8,128)S(1)}, f32[5,32]{1,0:T(8,128)}, u32[]{:S(2)}) copy-start(f32[5,32]{1,0:T(8,128)} %param.42) | copy-start | bytes 1924
  895.8 847.9 %copy-start.168 = (f32[5,32]{1,0:T(8,128)S(1)}, f32[5,32]{1,0:T(8,128)}, u32[]{:S(2)}) copy-start(f32[5,32]{1,0:T(8,128)} %param.48) | copy-start | bytes 1924
  895.8 848.5 %copy-start.9 = (f32[2,256,1024]{2,1,0:T(8,128)S(1)}, f32[2,256,1024]{2,1,0:T(8,128)}, u32[]{:S(2)}) copy-start(f32[2,256,1024]{2,1,0:T(8,128)} %param.37) | copy-start | bytes 6291460
  (144 other events, 671.1 us)
Sparse Core Ops, SparseCore 0:
  18.4 34.4 reduce-scatter.11
  56.0 31.6 reduce-scatter.13
  369.1 21.1 all-gather.25
  421.7 30.4 reduce-scatter.17
  502.1 22.5 all-gather.23
  561.4 31.1 reduce-scatter.15
  756.2 24.0 all-gather.27
  781.8 22.8 all-gather.29
  809.4 102.7 all-reduce.2
Sparse Core Ops, SparseCore 1:
  28.4 106.5 all-gather.15
  138.3 60.1 all-gather.17
  201.8 79.1 all-gather.19
  284.4 75.5 all-gather.21
  765.1 162.1 reduce-scatter.27
  929.6 149.0 reduce-scatter.21
  1080.8 178.9 reduce-scatter.25
  1261.9 184.5 reduce-scatter.23
  1452.8 244.3 reduce-scatter.19
where the time goes:
time: 1780 us; the launch traced here: 1770 us
  waiting for transfers between devices  1110 us (62%)
  matrix products  278 us (16%)
  blocking collectives  137 us (8%)
  local copies, waits for them, and re-layouts  102 us (6%)
  other arithmetic  100 us (6%)
  between operations  27.5 us (2%)
    reduce_scatter x1, waiting for transfers between devices, reduce_all(): lax.psum_scatter(layer_grads[0], ('dp', 'code'), scatter_dimension=1, til...  249 us
    reduce_scatter x1, waiting for transfers between devices, reduce_all(): lax.psum_scatter(layer_grads[2], ('dp', 'code'), scatter_dimension=0, til...  185 us
    reduce_scatter x1, waiting for transfers between devices, reduce_all(): lax.psum_scatter(layer_grads[3], ('dp', 'code'), scatter_dimension=0, til...  180 us
    reduce_scatter x1, waiting for transfers between devices, reduce_all(): lax.psum_scatter(layer_grads[1], ('dp', 'code'), scatter_dimension=1, til...  147 us
    all_gather x1, waiting for transfers between devices, on_device(): lax.all_gather(contract.astype(jnp.bfloat16), ('dp', 'code'), axis=0, til...  63.3 us
    reduce_scatter x2, waiting for transfers between devices, on_device(): lax.psum_scatter(back_hidden.reshape(FRAMES, SLOTS, D).astype(jnp.bfloat1...  57.8 us
    dot_general x12, matrix products, project(): jnp.einsum('abd,dn->abn', left, right, preferred_element_type=jnp.float32)  56 us
    all_gather x1, waiting for transfers between devices, on_device(): lax.all_gather(attend_out.astype(jnp.bfloat16), ('dp', 'code'), axis=1, t...  52.1 us
  transfers between devices with their start and end apart: 22, of which 17 were waited for; matrix products, arithmetic and copies ran while one was open for 13% of the time, Pallas kernels for 0%

commit v1 on v0

v1 whole, which is shorter than its diff:
```python
import jax
import jax.numpy as jnp
from jax import lax
from jax.sharding import Mesh, PartitionSpec as P

D = 1024
HEADS = 16
HEAD = 64
FRAMES = 4
SLOTS = 256
SMALL_TOKENS = 64
CLIPS = 4
DOMAINS = 4
MICRO = 2
STEP = 10


EPS = 1e-05
NEG = -1e30
BETA_ONE = 0.9
BETA_TWO = 0.95
ADAM_EPS = 1e-08
DECAY = 0.1
RATE = 0.02
RATE_SMALL = 0.2
CLIP = 0.005
HIGH = lax.Precision.HIGHEST
LOW = jnp.bfloat16
WIDE = jnp.float32
ALL = ("z", "r", "m", "h")


def shifted(part, axis, shift):
    n = lax.axis_size(axis)
    return lax.ppermute(part, axis, [((i + shift) % n, i) for i in range(n)])


def gather_axis(part, axis, dim):
    n = lax.axis_size(axis)
    mine = lax.axis_index(axis)
    whole = jnp.broadcast_to(
        jnp.expand_dims(part, dim), part.shape[:dim] + (n,) + part.shape[dim:]
    )
    for shift in range(1, n):
        other = shifted(part, axis, shift)
        whole = lax.dynamic_update_index_in_dim(whole, other, (mine + shift) % n, dim)
    return whole


def scatter_axis(parts, axis, dim, sent=LOW):
    n = lax.axis_size(axis)
    mine = lax.axis_index(axis)
    total = lax.dynamic_index_in_dim(parts, mine, dim, keepdims=False).astype(WIDE)
    for shift in range(1, n):
        piece = lax.dynamic_index_in_dim(parts, (mine + shift) % n, dim, keepdims=False)
        total = total + shifted(piece.astype(sent), axis, n - shift).astype(WIDE)
    return total


def gather_rows(shard):
    low = shard.astype(LOW)
    half = low.shape[1] // 2
    first = gather_axis(low[:, :half], "z", 0)
    first = gather_axis(first, "r", 1)
    first = gather_axis(first, "m", 2)
    second = gather_axis(low[:, half:], "z", 0)
    second = gather_axis(second, "m", 1)
    second = gather_axis(second, "r", 1)
    first = gather_axis(first, "h", 3)
    second = gather_axis(second, "h", 3)
    return jnp.concatenate([first, second], axis=-1).reshape(-1, low.shape[1])


def gather_table(shard):
    low = shard.astype(LOW)
    return gather_axis(gather_axis(low, "m", 0), "h", 1).reshape(-1, low.shape[1])


def split_pair(lhs, lead, tail):
    pair = lax.axis_size("h")
    mine = lax.axis_index("h")
    seen = lhs.reshape(lhs.shape[0], lead, pair, tail)
    return [
        lax.dynamic_index_in_dim(seen, (mine + shift) % pair, 2, keepdims=False).reshape(
            lhs.shape[0], lead * tail
        )
        for shift in range(1, pair)
    ] + [lax.dynamic_index_in_dim(seen, mine, 2, keepdims=False).reshape(lhs.shape[0], lead * tail)]


def pair_product(others, own, rhs):
    pair = lax.axis_size("h")
    arrived = []
    for shift, lhs in zip(range(1, pair), others):
        term = lax.dot_general(lhs, rhs, (((0,), (0,)), ((), ())), preferred_element_type=WIDE)
        arrived.append(shifted(term.astype(LOW), "h", pair - shift))
    total = lax.dot_general(own, rhs, (((0,), (0,)), ((), ())), preferred_element_type=WIDE)
    total = total.astype(LOW).astype(WIDE)
    for term in arrived:
        total = total + term.astype(WIDE)
    return total


def scatter_product(lhs, rhs):
    zs, rs, ms, hs = (lax.axis_size(axis) for axis in ALL)
    tail = lhs.shape[1] // (zs * rs * ms * hs)
    *others, own = split_pair(lhs, zs * rs * ms, tail)
    total = pair_product(others, own, rhs).reshape(zs, rs, ms, tail, rhs.shape[1])
    half = rhs.shape[1] // 2
    first = scatter_axis(total[..., :half], "r", 1)
    first = scatter_axis(first, "m", 1)
    first = scatter_axis(first, "z", 0)
    second = scatter_axis(total[..., half:], "m", 2)
    second = scatter_axis(second, "r", 1)
    second = scatter_axis(second, "z", 0)
    return jnp.concatenate([first, second], axis=-1)


def scatter_table(others, own, rhs):
    zs, rs, ms, hs = (lax.axis_size(axis) for axis in ALL)
    total = pair_product(others, own, rhs)
    total = total.reshape(ms, rs, zs, -1, rhs.shape[1])
    total = scatter_axis(total, "m", 0)
    total = scatter_axis(total, "r", 0)
    return scatter_axis(total, "z", 0)


def norm_forward(values, gain):
    return values * lax.rsqrt(jnp.mean(values * values, axis=-1, keepdims=True) + EPS) * gain


def norm_backward(values, gain, upstream):
    factor = lax.rsqrt(jnp.mean(values * values, axis=-1, keepdims=True) + EPS)
    scaled = upstream * gain
    inward = factor * scaled - values * factor**3 * jnp.mean(
        scaled * values, axis=-1, keepdims=True
    )
    gain_grad = jnp.sum((upstream * values * factor).reshape(-1, values.shape[-1]), axis=0)
    return (inward, gain_grad)


def project(left, right):
    return jnp.dot(left, right, preferred_element_type=WIDE)


def project_back(left, right):
    return lax.dot_general(left, right, (((1,), (1,)), ((), ())), preferred_element_type=WIDE)


def split_heads(packed, first, second):
    parts = packed.reshape(first, second, 3, HEADS, HEAD)
    return (parts[:, :, 0], parts[:, :, 1], parts[:, :, 2])


def masked_scores(query, key, allowed, row, col):
    scores = jnp.einsum(
        row + "he," + col + "he->bhqk", query, key, preferred_element_type=WIDE
    ) * HEAD ** (-0.5)
    return jnp.where(allowed, scores, NEG)


def attend_forward(normed, shape, w_in, w_out, allowed, row, col):
    packed = project(normed, w_in).astype(LOW)
    query, key, value = split_heads(packed, *shape)
    scores = masked_scores(query, key, allowed, row, col)
    top = jnp.max(scores, axis=-1, keepdims=True)
    expd = jnp.exp(scores - top)
    summed = jnp.sum(expd, axis=-1, keepdims=True)
    probs = (expd / summed).astype(LOW)
    mixed = jnp.einsum(
        "bhqk," + col + "he->" + row + "he", probs, value, preferred_element_type=WIDE
    )
    mixed = mixed.reshape(-1, D).astype(LOW)
    return (project(mixed, w_out), (packed, mixed, top + jnp.log(summed)))


def attend_backward(normed, shape, w_in, w_out, allowed, row, col, kept, upstream):
    packed, mixed, log_total = kept
    up_low = upstream.astype(LOW)
    grad_out = scatter_product(mixed, up_low)
    grad_mixed = project_back(up_low, w_out)
    grad_mixed = grad_mixed.astype(LOW).reshape(shape + (HEADS, HEAD))
    query, key, value = split_heads(packed, *shape)
    probs = jnp.exp(masked_scores(query, key, allowed, row, col) - log_total)
    grad_value = jnp.einsum(
        "bhqk," + row + "he->" + col + "he",
        probs.astype(LOW),
        grad_mixed,
        preferred_element_type=WIDE,
    )
    grad_probs = jnp.einsum(
        row + "he," + col + "he->bhqk", grad_mixed, value, preferred_element_type=WIDE
    )
    grad_scores = (
        probs * (grad_probs - jnp.sum(probs * grad_probs, axis=-1, keepdims=True)) * HEAD ** (-0.5)
    )
    grad_scores = grad_scores.astype(LOW)
    grad_query = jnp.einsum(
        "bhqk," + col + "he->" + row + "he", grad_scores, key, preferred_element_type=WIDE
    )
    grad_key = jnp.einsum(
        "bhqk," + row + "he->" + col + "he", grad_scores, query, preferred_element_type=WIDE
    )
    grad_packed = jnp.concatenate(
        [piece.reshape(-1, D) for piece in (grad_query, grad_key, grad_value)], axis=-1
    ).astype(LOW)
    grad_normed = project_back(grad_packed, w_in)
    grad_in = scatter_product(normed, grad_packed)
    return (grad_normed, grad_in, grad_out)


def adamw(weight, grad, first, second, rate, decay):
    first_new = BETA_ONE * first + (1.0 - BETA_ONE) * grad
    second_new = BETA_TWO * second + (1.0 - BETA_TWO) * grad * grad
    unbiased_first = first_new / (1.0 - BETA_ONE**STEP)
    unbiased_second = second_new / (1.0 - BETA_TWO**STEP)
    updated = weight - rate * (
        unbiased_first / (jnp.sqrt(unbiased_second) + ADAM_EPS) + decay * weight
    )
    return (updated, first_new, second_new)


def swap_frames(values):
    hs = lax.axis_size("h")
    frames = values.shape[0]
    seen = values.reshape(frames, hs, SLOTS // hs, D)
    mine = lax.axis_index("h")
    whole = jnp.broadcast_to(
        lax.dynamic_index_in_dim(seen, mine, 1, keepdims=False)[None],
        (hs, frames, SLOTS // hs, D),
    )
    for shift in range(1, hs):
        piece = lax.dynamic_index_in_dim(seen, (mine + shift) % hs, 1, keepdims=False)
        other = shifted(piece, "h", hs - shift)
        whole = lax.dynamic_update_index_in_dim(whole, other, (mine + hs - shift) % hs, 0)
    return whole.reshape(hs * frames, SLOTS // hs, D)


def swap_slots(values):
    hs = lax.axis_size("h")
    frames = values.shape[0] // hs
    seen = values.reshape(hs, frames, SLOTS // hs, D)
    mine = lax.axis_index("h")
    own = lax.dynamic_index_in_dim(seen, mine, 0, keepdims=False)
    whole = jnp.broadcast_to(own[:, None], (frames, hs, SLOTS // hs, D))
    for shift in range(1, hs):
        piece = lax.dynamic_index_in_dim(seen, (mine + shift) % hs, 0, keepdims=False)
        other = shifted(piece, "h", hs - shift)
        whole = lax.dynamic_update_index_in_dim(whole, other, (mine + hs - shift) % hs, 1)
    return whole.reshape(frames, SLOTS, D)


def on_device(
    tokens,
    masked,
    small_grid,
    domains,
    attend_in,
    attend_out,
    expand,
    contract,
    gains,
    tables,
    mean_in,
    mean_out,
    mean_expand,
    mean_contract,
    mean_gains,
    mean_tables,
    square_in,
    square_out,
    square_expand,
    square_contract,
    square_gains,
    square_tables,
):
    zs, rs, ms, hs = (lax.axis_size(axis) for axis in ALL)
    micro = lax.axis_index("m")
    half = lax.axis_index("h")

    def of_micro(array):
        return lax.dynamic_index_in_dim(array[:, 0], micro, 0, keepdims=False)

    codes = of_micro(tokens)
    hidden_mask = of_micro(masked).astype(WIDE)
    small = of_micro(small_grid)
    doms = of_micro(domains)

    table_in = gather_table(tables[0])
    gain_low = gains.astype(LOW)
    gain_all = gather_axis(
        gather_axis(gather_axis(gather_axis(gain_low, "z", 0), "r", 1), "m", 2), "h", 3
    )
    gain_all = jnp.moveaxis(gain_all, 4, 0).reshape(gains.shape[0], D).astype(WIDE)
    w_in = [gather_rows(attend_in[0]), None]
    w_out = [gather_rows(attend_out[0]), None]
    w_in[1] = gather_rows(attend_in[1])
    w_out[1] = gather_rows(attend_out[1])
    w_up = gather_rows(expand)
    w_down = gather_rows(contract)
    table_out = gather_table(tables[1])

    slot_ids = jnp.arange(SLOTS)
    frame_ids = jnp.arange(FRAMES)
    causal = frame_ids[None, :] <= frame_ids[:, None]
    segment = jnp.where(small > 0, slot_ids // SMALL_TOKENS, 0)
    within = segment[:, None] == segment[None, :]
    dom_slot = jnp.sum((segment[:, None] == jnp.arange(CLIPS)[None, :]) * doms[None, :], axis=-1)
    domain_hot = (dom_slot[:, None] == jnp.arange(DOMAINS)[None, :]).astype(WIDE)
    counts = jnp.sum(jnp.sum(hidden_mask, axis=0)[:, None] * domain_hot, axis=0)[None, :]
    counts = jnp.sum(gather_axis(counts, "z", 0), axis=0)
    counts = jnp.sum(gather_axis(counts, "r", 0), axis=0)[0]
    scale = 1.0 / (MICRO * DOMAINS * jnp.maximum(counts, 1.0))
    slot_scale = jnp.sum(domain_hot * scale[None, :], axis=1)

    frames = FRAMES // hs
    slots = SLOTS // hs
    space = (frames, SLOTS)
    time = (FRAMES, slots)
    code_ids = jnp.arange(table_in.shape[0])

    space_codes = lax.dynamic_slice_in_dim(codes, half * frames, frames, 0).reshape(-1)
    space_mask = lax.dynamic_slice_in_dim(hidden_mask, half * frames, frames, 0).reshape(-1)
    time_codes = lax.dynamic_slice_in_dim(codes, half * slots, slots, 1).reshape(-1)
    time_weight = (
        lax.dynamic_slice_in_dim(hidden_mask, half * slots, slots, 1)
        * lax.dynamic_slice_in_dim(slot_scale, half * slots, slots, 0)[None, :]
    ).reshape(-1)

    picked = project((space_codes[:, None] == code_ids[None, :]).astype(LOW), table_in)
    start = jnp.where(space_mask[:, None] > 0, gain_all[4], picked)
    normed_space = norm_forward(start, gain_all[0]).astype(LOW)
    branch_space, kept_space = attend_forward(
        normed_space, space, w_in[0], w_out[0], within, "bq", "bk"
    )
    after_space = swap_frames((start + branch_space).reshape(space + (D,))).reshape(-1, D)
    normed_time = norm_forward(after_space, gain_all[1]).astype(LOW)
    branch_time, kept_time = attend_forward(
        normed_time, time, w_in[1], w_out[1], causal, "qb", "kb"
    )
    after_time = after_space + branch_time
    normed_ffn = norm_forward(after_time, gain_all[2]).astype(LOW)
    pre = project(normed_ffn, w_up)
    activ = jax.nn.gelu(pre, approximate=True).astype(LOW)
    after_ffn = after_time + project(activ, w_down)
    final = norm_forward(after_ffn, gain_all[3]).astype(LOW)
    logits = project_back(final, table_out)
    hits = time_codes[:, None] == code_ids[None, :]
    top = jnp.max(logits, axis=1, keepdims=True)
    log_total = top + jnp.log(jnp.sum(jnp.exp(logits - top), axis=1, keepdims=True))
    target = jnp.sum(jnp.where(hits, logits, 0.0), axis=1)
    loss_part = jnp.sum(time_weight * (log_total[:, 0] - target))
    grad_logits = (time_weight[:, None] * (jnp.exp(logits - log_total) - hits)).astype(LOW)

    *others, own = split_pair(grad_logits, ms, tables.shape[1])
    head_grad = scatter_table(others, own, final)
    grad_final = project(grad_logits, table_out)
    grad_ffn, gain_three = norm_backward(after_ffn, gain_all[3], grad_final)
    up_low = grad_ffn.astype(LOW)
    grad_down = scatter_product(activ, up_low)
    grad_activ = project_back(up_low, w_down)
    grad_pre = jax.vjp(lambda inner: jax.nn.gelu(inner, approximate=True), pre)[1](grad_activ)[
        0
    ].astype(LOW)
    grad_up = scatter_product(normed_ffn, grad_pre)
    inward, gain_two = norm_backward(after_time, gain_all[2], project_back(grad_pre, w_up))
    grad_time = grad_ffn + inward
    grad_normed, grad_in_time, grad_out_time = attend_backward(
        normed_time, time, w_in[1], w_out[1], causal, "qb", "kb", kept_time, grad_time
    )
    inward, gain_one = norm_backward(after_space, gain_all[1], grad_normed)
    grad_space = swap_slots((grad_time + inward).reshape(time + (D,))).reshape(-1, D)
    grad_normed, grad_in_space, grad_out_space = attend_backward(
        normed_space, space, w_in[0], w_out[0], within, "bq", "bk", kept_space, grad_space
    )
    inward, gain_zero = norm_backward(start, gain_all[0], grad_normed)
    grad_start = grad_space + inward
    mask_grad = jnp.sum(grad_start * space_mask[:, None], axis=0)
    seen_codes = jnp.where(space_mask > 0, -1, space_codes)
    rows = tables.shape[1]
    chosen = []
    for shift in list(range(1, hs)) + [0]:
        ids = (jnp.arange(ms)[:, None] * hs + (half + shift) % hs) * rows + jnp.arange(rows)[None, :]
        chosen.append((seen_codes[:, None] == ids.reshape(1, -1)).astype(LOW))
    embed_grad = scatter_table(chosen[:-1], chosen[-1], grad_start.astype(LOW))

    gain_grads = jnp.stack([gain_zero, gain_one, gain_two, gain_three, mask_grad])
    gain_grads = jnp.moveaxis(gain_grads.reshape(-1, zs, rs, ms, hs, gains.shape[1]), 0, 4)
    gain_grads = scatter_axis(gain_grads, "h", 3, WIDE)
    gain_grads = scatter_axis(gain_grads, "r", 1, WIDE)
    gain_grads = scatter_axis(gain_grads, "m", 1, WIDE)
    gain_grads = scatter_axis(gain_grads, "z", 0, WIDE)

    layer_grads = (
        jnp.stack([grad_in_space, grad_in_time]),
        jnp.stack([grad_out_space, grad_out_time]),
        grad_up,
        grad_down,
        gain_grads,
    )
    owned = sum((jnp.sum(g * g) for g in layer_grads + (embed_grad, head_grad)))
    sums = lax.all_gather(jnp.stack([owned, loss_part]).reshape(1, 2), ALL, axis=0, tiled=True)
    square_sum, loss = jnp.sum(sums, axis=0)
    norm = jnp.sqrt(square_sum)
    factor = jnp.minimum(1.0, CLIP / (norm + 1e-06))

    def spread(grad):
        grad = gather_axis(gather_axis(grad.astype(LOW), "z", 0), "r", 0)
        return grad.reshape(rows, D).astype(WIDE)

    table_grad = jnp.stack([spread(embed_grad), spread(head_grad)])
    params = (attend_in, attend_out, expand, contract, gains, tables)
    grads = layer_grads + (table_grad,)
    firsts = (mean_in, mean_out, mean_expand, mean_contract, mean_gains, mean_tables)
    seconds = (square_in, square_out, square_expand, square_contract, square_gains, square_tables)
    rates = (RATE, RATE, RATE, RATE, RATE_SMALL, RATE)
    decays = (DECAY, DECAY, DECAY, DECAY, 0.0, DECAY)
    results = [
        adamw(p, factor * g, f, s, r, k)
        for p, g, f, s, r, k in zip(params, grads, firsts, seconds, rates, decays)
    ]
    return (loss, norm) + tuple(result[k] for k in range(3) for result in results)


def solution(mesh):
    dp, code = mesh.shape["dp"], mesh.shape["code"]
    deep = next(n for n in (4, 2, 1) if dp % n == 0)
    fine = Mesh(mesh.devices.reshape(deep, dp // deep, MICRO, code // MICRO), ALL)
    group = ("z", "r")
    weights = (
        P(None, ALL, None),
        P(None, ALL, None),
        P(ALL, None),
        P(ALL, None),
        P(None, ALL),
        P(None, ("m", "h"), None),
    )
    return jax.shard_map(
        on_device,
        mesh=fine,
        in_specs=(
            P(None, group, None, None),
            P(None, group, None, None),
            P(None, group),
            P(None, group, None),
        )
        + weights * 3,
        out_specs=(P(), P()) + weights * 3,
        check_vma=False,
    )
```

time: 1780 us -> 1190 us (0.67)
  waiting for transfers between devices: 1110 us -> 319 us
  starting transfers between devices: 16.2 us -> 218 us
  local copies, waits for them, and re-layouts: 102 us -> 297 us
  blocking collectives: 137 us -> 37.9 us
  matrix products: 278 us -> 213 us
    reduce_scatter x8 -> x0, waiting for transfers between devices: 830 us -> none  [the longest x1 249 us: reduce_all(): lax.psum_scatter(layer_grads[0], ('dp', 'code'), scatter_dimension=1, til...]
    ppermute x0 -> x180, waiting for transfers between devices: none -> 319 us  [shifted(): return lax.ppermute(part, axis, [((i + shift) % n, i) for i in range(n)])]
    all_gather x8 -> x0, waiting for transfers between devices: 218 us -> none  [the longest x1 63.3 us: on_device(): lax.all_gather(contract.astype(jnp.bfloat16), ('dp', 'code'), axis=0, til...]
    ppermute x0 -> x180, starting transfers between devices: none -> 218 us  [shifted(): return lax.ppermute(part, axis, [((i + shift) % n, i) for i in range(n)])]
    all_gather x7 -> x0, blocking collectives: 76.7 us -> none  [the longest x1 43.8 us: on_device(): lax.all_gather(gains.astype(jnp.bfloat16), ('dp', 'code'), axis=1, tiled=...]
    dot_general x50 -> x33, matrix products: 209 us -> 140 us  [the longest x8 42.1 us: project(): return jnp.dot(left, right, preferred_element_type=WIDE)]
    psum x2 -> x0, blocking collectives: 60.4 us -> none  [the longest x1 40.5 us: on_device(): square_sum, loss = lax.psum((owned, loss_part), ('dp', 'code'))]
    unnamed x385 -> x281, local copies, waits for them, and re-layouts: 20.2 us -> 65.2 us
  transfers between devices with their start and end apart: 22 -> 180, of which waited for: 17 -> 75; matrix products, arithmetic and copies ran while one was open for 13% -> 32% of each run, Pallas kernels for 0% -> 0%
where the time goes in v1:
time: 1190 us; the launch traced here: 1180 us
  waiting for transfers between devices  319 us (27%)
  local copies, waits for them, and re-layouts  297 us (25%)
  starting transfers between devices  218 us (18%)
  matrix products  213 us (18%)
  other arithmetic  83.9 us (7%)
  blocking collectives  37.9 us (3%)
    ppermute x180, waiting for transfers between devices, shifted(): return lax.ppermute(part, axis, [((i + shift) % n, i) for i in range(n)])  319 us
    ppermute x180, starting transfers between devices, shifted(): return lax.ppermute(part, axis, [((i + shift) % n, i) for i in range(n)])  218 us
    unnamed x281, local copies, waits for them, and re-layouts  65.2 us
    dot_general x8, matrix products, project(): return jnp.dot(left, right, preferred_element_type=WIDE)  42.1 us
    broadcast_in_dim x63, local copies, waits for them, and re-layouts, gather_axis(): jnp.broadcast_to(jnp.expand_dims(part, dim), part.shape[:dim] + (n,) + pa...  41.8 us
    unnamed x1, blocking collectives  37.9 us
    dot_general x7, matrix products, project_back(): lax.dot_general(left, right, (((1,), (1,)), ((), ())), preferred_element_...  36.7 us
    dynamic_update_slice x96, local copies, waits for them, and re-layouts, gather_axis(): lax.dynamic_update_index_in_dim(whole, other, (mine + shift) % n, dim)  32.8 us
  transfers between devices with their start and end apart: 180, of which 75 were waited for; matrix products, arithmetic and copies ran while one was open for 32% of the time, Pallas kernels for 0%

profile of v1, /device:TPU:0, one launch (start us, length us, event | category | flops | bytes accessed | tf_op | source)
XLA Modules:
  0.0 1179.4 jit_solution(9949409970310823172)
XLA Ops:
  46.8 5.1 collective-permute-done.21
  69.5 6.2 collective-permute-done.51
  79.7 4.7 collective-permute-done.8
  84.5 8.6 collective-permute-done.9
  101.2 4.5 collective-permute-done.15
  117.6 5.6 collective-permute-done.34
  127.2 4.6 collective-permute-done.39
  133.5 6.1 collective-permute-done.40
  153.4 4.8 collective-permute-start.77
  171.9 16.3 %collective-permute-done.54 = bf16[4,32,512]{2,1,0:T(8,128)(2,1)S(1)} collective-permute-done((bf16[4,32,512]{2,1,0:T(8,128)(2,1)S(1)}, bf16[4,32,512]{2,1,0:T(8,128)(2,1)S(1)}, u32[]{:S(2)}, u32[]{:S(2)}) %collective-permute-start.54) | collective-permute-done | bytes 131104 | tf_op jit(solution)/shard_map/ppermute | solution.py:35
  189.7 4.8 collective-permute-done.23
  198.4 13.8 %collective-permute-done.24 = bf16[4,2,32,512]{3,2,1,0:T(8,128)(2,1)S(1)} collective-permute-done((bf16[4,2,32,512]{3,2,1,0:T(8,128)(2,1)S(1)}, bf16[4,2,32,512]{3,2,1,0:T(8,128)(2,1)S(1)}, u32[]{:S(2)}, u32[]{:S(2)}) %collective-permute-start.24) | collective-permute-done | bytes 262176 | tf_op jit(solution)/shard_map/ppermute | solution.py:35
  253.6 10.2 collective-permute-done.12
  268.0 12.6 %collective-permute-done.37 = bf16[4,2,32,1536]{3,2,1,0:T(8,128)(2,1)S(1)} collective-permute-done((bf16[4,2,32,1536]{3,2,1,0:T(8,128)(2,1)S(1)}, bf16[4,2,32,1536]{3,2,1,0:T(8,128)(2,1)S(1)}, u32[]{:S(2)}, u32[]{:S(2)}) %collective-permute-start.37) | collective-permute-done | bytes 786464 | tf_op jit(solution)/shard_map/ppermute | solution.py:35
  298.6 4.6 collective-permute-done.73
  313.9 14.5 %collective-permute-done.67 = bf16[4,2,32,2048]{3,2,1,0:T(8,128)(2,1)} collective-permute-done((bf16[4,2,32,2048]{3,2,1,0:T(8,128)(2,1)}, bf16[4,2,32,2048]{3,2,1,0:T(8,128)(2,1)}, u32[]{:S(2)}, u32[]{:S(2)}) %collective-permute-start.67) | collective-permute-done | bytes 1048608 | tf_op jit(solution)/shard_map/ppermute | solution.py:35
  345.7 6.1 convolution_convert_fusion.7
  351.8 8.5 reshape.719
  360.4 6.0 fusion.266
  381.0 6.0 fusion.77
  411.9 5.3 pad_maximum_fusion.3
  432.2 5.7 broadcast_in_dim.928
  441.1 8.0 pad_maximum_fusion.1
  449.1 7.9 pad_maximum_fusion
  470.2 6.6 convolution_convert_fusion.6
  476.8 6.2 reshape.720
  483.0 5.3 fusion.265
  490.3 5.0 fusion.56
  503.4 5.2 convert_bitcast_fusion.3
  519.6 12.4 %multiply_convert_fusion.1 = (bf16[512,4096]{1,0:T(8,128)(2,1)}, f32[512,4096]{1,0:T(8,128)}) fusion(bf16[512,1024]{1,0:T(8,128)(2,1)S(1)} %multiply_convert_fusion.5, bf16[1024,4096]{1,0:T(8,128)(2,1)} %bitcast.826), kind=kOutput, calls=%fused_computation.17 | convolution fusion | flops 4313841664 | bytes 22020096 | tf_op jit(solution)/shard_map/dot_general | solution.py:143
  532.0 7.9 reshape.706
  539.8 8.5 multiply_reduce_fusion.8
  563.1 13.4 %fusion.7 = bf16[512,4096]{1,0:T(8,128)(2,1)S(1)} fusion(f32[512,4096]{1,0:T(8,128)} %get-tuple-element.191, bf16[4096,1024]{1,0:T(8,128)(2,1)} %bitcast.831, f32[512,1024]{1,0:T(8,128)S(1)} %multiply_subtract_fusion.1), kind=kOutput, calls=%fused_computation.9 | convolution fusion | flops 4337434624 | bytes 23068672 | tf_op jit(solution)/shard_map/dot_general | solution.py:147
  576.6 6.1 multiply_reduce_fusion.4
  591.3 7.0 fusion.55
  602.9 5.3 copy.366
  608.2 6.0 convert_bitcast_fusion.2
  641.6 5.9 convert_bitcast_fusion
  651.1 4.5 copy.367
  663.2 7.1 fusion.53
  672.3 5.6 convolution_convert_fusion.2
  678.4 9.8 constant_dynamic-slice_fusion.17
  688.3 10.5 copy.457
  698.8 10.7 copy.458
  709.5 6.7 convolution_convert_fusion.8
  732.5 5.8 fusion.90
  738.3 14.9 %fusion.81 = bf16[2,256,16,64]{1,3,2,0:T(8,128)(2,1)} fusion(f32[2,16,256,256]{2,3,1,0:T(8,128)} %fusion.90, f32[2,16,256,256]{2,3,1,0:T(8,128)} %copy-done.3, f32[2,16,256]{2,1,0:T(8,128)S(1)} %copy-done.105, pred[256,256]{0,1:T(8,128)(4,1)S(1)} %copy-done.91, bf16[2,256,1,16,64]{1,4,3,0,2:T(8,128)(2,1)} %copy.420), kind=kOutput, calls=%fused_computation.163 | convolution fusion | flops 292036864 | bytes 18972672 | tf_op jit(solution)/shard_map/bhqk,bkhe->bqhe/dot_general | solution.py:198
  753.2 16.9 %fusion.78 = bf16[2,256,16,64]{1,3,2,0:T(8,128)(2,1)} fusion(f32[2,16,256,256]{2,3,1,0:T(8,128)} %fusion.90, f32[2,16,256,256]{2,3,1,0:T(8,128)} %copy-done.3, f32[2,16,256]{2,1,0:T(8,128)S(1)} %copy-done.105, pred[256,256]{0,1:T(8,128)(4,1)S(1)} %copy-done.91, bf16[2,256,1,16,64]{1,4,3,0,2:T(8,128)(2,1)} %copy-done.55), kind=kOutput, calls=%fused_computation.162 | convolution fusion | flops 292036864 | bytes 18972672 | tf_op jit(solution)/shard_map/bhqk,bqhe->bkhe/dot_general | solution.py:201
  770.1 5.4 fusion.74
  786.2 5.0 multiply_reduce_fusion.2
  794.6 5.7 convolution_convert_fusion.4
  855.7 4.7 collective-permute-done.177
  860.4 6.0 collective-permute-done.178
  889.8 5.6 collective-permute-done.162
  915.3 5.6 collective-permute-done.173
  929.1 5.5 collective-permute-done.175
  937.3 5.9 collective-permute-done.105
  944.6 10.2 collective-permute-done.100
  964.9 4.8 convert_add_fusion.1
  999.8 33.5 %collective-permute-done.94 = bf16[4,2,32,1536]{3,2,0,1:T(8,128)(2,1)S(1)} collective-permute-done((bf16[4,2,32,1536]{3,2,0,1:T(8,128)(2,1)S(1)}, bf16[4,2,32,1536]{3,2,0,1:T(8,128)(2,1)S(1)}, u32[]{:S(2)}, u32[]{:S(2)}) %collective-permute-start.94) | collective-permute-done | bytes 786464 | tf_op jit(solution)/shard_map/ppermute | solution.py:35
  1045.3 6.4 collective-permute-done.133
  1069.4 4.9 collective-permute-done.97
  1077.2 7.9 collective-permute-done.92
  1125.3 37.9 %all-reduce = f32[64]{0:T(128)S(1)} all-reduce(f32[64]{0:T(128)S(1)} %maximum_dynamic-update-slice_fusion), channel_id=2, replica_groups=mesh['z'=4,'r'=2,'m'=2,'h'=2] {'z','r','m','h'}, use_global_device_ids=true, to_apply=%add | all-reduce | flops 64 | bytes 512
  (1034 shorter events, 639.1 us)
Async XLA Ops:
  4.3 18.8 %collective-permute-start.83 = (f32[1,4]{1,0:T(1,128)S(1)}, f32[1,4]{1,0:T(1,128)S(1)}, u32[]{:S(2)}, u32[]{:S(2)}) collective-permute-start(f32[1,4]{1,0:T(1,128)S(1)} %bitcast.904), channel_id=1, source_target_pairs={{24,0},{0,8},{8,16},{16,24},{25,1},{1,9},{9,17},{17,25},{26,2},{2,... | collective-permute-start | bytes 56 | tf_op jit(solution)/shard_map/ppermute | solution.py:35
  22.5 46.7 %collective-permute-start.47 = (bf16[32,512]{1,0:T(8,128)(2,1)S(1)}, bf16[32,512]{1,0:T(8,128)(2,1)S(1)}, u32[]{:S(2)}, u32[]{:S(2)}) collective-permute-start(bf16[32,512]{1,0:T(8,128)(2,1)S(1)} %get-tuple-element.163), channel_id=1, source_target_pairs={{24,0},{0,8},{8,16},{16,24},{25,1},{1,9},{9,17},{17,25},{26,2},{2,... | collective-permute-start | bytes 98312 | tf_op jit(solution)/shard_map/ppermute | solution.py:35
  23.1 44.2 %collective-permute-start.46 = (bf16[32,512]{1,0:T(8,128)(2,1)S(1)}, bf16[32,512]{1,0:T(8,128)(2,1)S(1)}, u32[]{:S(2)}, u32[]{:S(2)}) collective-permute-start(bf16[32,512]{1,0:T(8,128)(2,1)S(1)} %get-tuple-element.163), channel_id=1, source_target_pairs={{16,0},{24,8},{0,16},{8,24},{17,1},{25,9},{1,17},{9,25},{18,2},{26... | collective-permute-start | bytes 98312 | tf_op jit(solution)/shard_map/ppermute | solution.py:35
  24.7 42.3 %collective-permute-start.45 = (bf16[32,512]{1,0:T(8,128)(2,1)S(1)}, bf16[32,512]{1,0:T(8,128)(2,1)S(1)}, u32[]{:S(2)}, u32[]{:S(2)}) collective-permute-start(bf16[32,512]{1,0:T(8,128)(2,1)S(1)} %get-tuple-element.163), channel_id=1, source_target_pairs={{8,0},{16,8},{24,16},{0,24},{9,1},{17,9},{25,17},{1,25},{10,2},{18... | collective-permute-start | bytes 98312 | tf_op jit(solution)/shard_map/ppermute | solution.py:35
  27.6 24.7 %collective-permute-start.22 = (bf16[32,512]{1,0:T(8,128)(2,1)S(1)}, bf16[32,512]{1,0:T(8,128)(2,1)S(1)}, u32[]{:S(2)}, u32[]{:S(2)}) collective-permute-start(bf16[32,512]{1,0:T(8,128)(2,1)S(1)} %get-tuple-element.165), channel_id=1, source_target_pairs={{24,0},{0,8},{8,16},{16,24},{25,1},{1,9},{9,17},{17,25},{26,2},{2,... | collective-permute-start | bytes 98312 | tf_op jit(solution)/shard_map/ppermute | solution.py:35
  67.3 78.6 %collective-permute-start.59 = (bf16[32,2048]{1,0:T(8,128)(2,1)S(1)}, bf16[32,2048]{1,0:T(8,128)(2,1)S(1)}, u32[]{:S(2)}, u32[]{:S(2)}) collective-permute-start(bf16[32,2048]{1,0:T(8,128)(2,1)S(1)} %get-tuple-element.146), channel_id=1, source_target_pairs={{24,0},{0,8},{8,16},{16,24},{25,1},{1,9},{9,17},{17,25},{26,2},{2,... | collective-permute-start | bytes 393224 | tf_op jit(solution)/shard_map/ppermute | solution.py:35
  69.2 74.6 %collective-permute-start.58 = (bf16[32,2048]{1,0:T(8,128)(2,1)S(1)}, bf16[32,2048]{1,0:T(8,128)(2,1)S(1)}, u32[]{:S(2)}, u32[]{:S(2)}) collective-permute-start(bf16[32,2048]{1,0:T(8,128)(2,1)S(1)} %get-tuple-element.146), channel_id=1, source_target_pairs={{16,0},{24,8},{0,16},{8,24},{17,1},{25,9},{1,17},{9,25},{18,2},{26... | collective-permute-start | bytes 393224 | tf_op jit(solution)/shard_map/ppermute | solution.py:35
  75.7 67.9 %collective-permute-start.57 = (bf16[32,2048]{1,0:T(8,128)(2,1)S(1)}, bf16[32,2048]{1,0:T(8,128)(2,1)S(1)}, u32[]{:S(2)}, u32[]{:S(2)}) collective-permute-start(bf16[32,2048]{1,0:T(8,128)(2,1)S(1)} %get-tuple-element.146), channel_id=1, source_target_pairs={{8,0},{16,8},{24,16},{0,24},{9,1},{17,9},{25,17},{1,25},{10,2},{18... | collective-permute-start | bytes 393224 | tf_op jit(solution)/shard_map/ppermute | solution.py:35
  105.7 17.8 %collective-permute-start.35 = (bf16[32,1536]{1,0:T(8,128)(2,1)S(1)}, bf16[32,1536]{1,0:T(8,128)(2,1)S(1)}, u32[]{:S(2)}, u32[]{:S(2)}) collective-permute-start(bf16[32,1536]{1,0:T(8,128)(2,1)S(1)} %get-tuple-element.148), channel_id=1, source_target_pairs={{24,0},{0,8},{8,16},{16,24},{25,1},{1,9},{9,17},{17,25},{26,2},{2,... | collective-permute-start | bytes 294920 | tf_op jit(solution)/shard_map/ppermute | solution.py:35
  139.6 18.6 %collective-permute-start.65 = (bf16[32,2048]{1,0:T(8,128)(2,1)S(1)}, bf16[32,2048]{1,0:T(8,128)(2,1)S(1)}, u32[]{:S(2)}, u32[]{:S(2)}) collective-permute-start(bf16[32,2048]{1,0:T(8,128)(2,1)S(1)} %get-tuple-element.147), channel_id=1, source_target_pairs={{24,0},{0,8},{8,16},{16,24},{25,1},{1,9},{9,17},{17,25},{26,2},{2,... | collective-permute-start | bytes 393224 | tf_op jit(solution)/shard_map/ppermute | solution.py:35
  143.8 20.9 %collective-permute-start.71 = (bf16[128,512]{1,0:T(8,128)(2,1)S(1)}, bf16[128,512]{1,0:T(8,128)(2,1)S(1)}, u32[]{:S(2)}, u32[]{:S(2)}) collective-permute-start(bf16[128,512]{1,0:T(8,128)(2,1)S(1)} %get-tuple-element.144), channel_id=1, source_target_pairs={{24,0},{0,8},{8,16},{16,24},{25,1},{1,9},{9,17},{17,25},{26,2},{2,... | collective-permute-start | bytes 393224 | tf_op jit(solution)/shard_map/ppermute | solution.py:35
  153.4 17.9 %collective-permute-start.77 = (bf16[128,512]{1,0:T(8,128)(2,1)S(1)}, bf16[128,512]{1,0:T(8,128)(2,1)S(1)}, u32[]{:S(2)}, u32[]{:S(2)}) collective-permute-start(bf16[128,512]{1,0:T(8,128)(2,1)S(1)} %get-tuple-element.145), channel_id=1, source_target_pairs={{24,0},{0,8},{8,16},{16,24},{25,1},{1,9},{9,17},{17,25},{26,2},{2,... | collective-permute-start | bytes 393224 | tf_op jit(solution)/shard_map/ppermute | solution.py:35
  163.1 69.3 %collective-permute-start.85 = (bf16[256,1024]{1,0:T(8,128)(2,1)S(1)}, bf16[256,1024]{1,0:T(8,128)(2,1)S(1)}, u32[]{:S(2)}, u32[]{:S(2)}) collective-permute-start(bf16[256,1024]{1,0:T(8,128)(2,1)S(1)} %get-tuple-element.80), channel_id=1, source_target_pairs={{2,0},{0,2},{3,1},{1,3},{6,4},{4,6},{7,5},{5,7},{10,8},{8,10},{11,... | collective-permute-start | bytes 1572872 | tf_op jit(solution)/shard_map/ppermute | solution.py:35
  164.7 69.5 %collective-permute-start.6 = (bf16[256,1024]{1,0:T(8,128)(2,1)S(1)}, bf16[256,1024]{1,0:T(8,128)(2,1)S(1)}, u32[]{:S(2)}, u32[]{:S(2)}) collective-permute-start(bf16[256,1024]{1,0:T(8,128)(2,1)S(1)} %get-tuple-element.81), channel_id=1, source_target_pairs={{2,0},{0,2},{3,1},{1,3},{6,4},{4,6},{7,5},{5,7},{10,8},{8,10},{11,... | collective-permute-start | bytes 1572872 | tf_op jit(solution)/shard_map/ppermute | solution.py:35
  168.1 20.1 %collective-permute-start.54 = (bf16[4,32,512]{2,1,0:T(8,128)(2,1)S(1)}, bf16[4,32,512]{2,1,0:T(8,128)(2,1)S(1)}, u32[]{:S(2)}, u32[]{:S(2)}) collective-permute-start(bf16[4,32,512]{2,1,0:T(8,128)(2,1)S(1)} %constant_dynamic-update-slice_fusion.4), channel_id=1, source_target_pairs={{2,0},{0,2},{3,1},{1,3},{6,4},{4,6},{7,5},{5,7},{10,8},{8,10},{11,... | collective-permute-start | bytes 393224 | tf_op jit(solution)/shard_map/ppermute | solution.py:35
  169.7 27.1 %collective-permute-start.48 = (bf16[4,32,512]{2,1,0:T(8,128)(2,1)S(1)}, bf16[4,32,512]{2,1,0:T(8,128)(2,1)S(1)}, u32[]{:S(2)}, u32[]{:S(2)}) collective-permute-start(bf16[4,32,512]{2,1,0:T(8,128)(2,1)S(1)} %constant_dynamic-update-slice_fusion.7), channel_id=1, source_target_pairs={{4,0},{0,4},{5,1},{1,5},{6,2},{2,6},{7,3},{3,7},{12,8},{8,12},{13,... | collective-permute-start | bytes 393224 | tf_op jit(solution)/shard_map/ppermute | solution.py:35
  171.3 24.9 %collective-permute-start.29 = (bf16[4,32,512]{2,1,0:T(8,128)(2,1)S(1)}, bf16[4,32,512]{2,1,0:T(8,128)(2,1)S(1)}, u32[]{:S(2)}, u32[]{:S(2)}) collective-permute-start(bf16[4,32,512]{2,1,0:T(8,128)(2,1)S(1)} %constant_dynamic-update-slice_fusion.10), channel_id=1, source_target_pairs={{2,0},{0,2},{3,1},{1,3},{6,4},{4,6},{7,5},{5,7},{10,8},{8,10},{11,... | collective-permute-start | bytes 393224 | tf_op jit(solution)/shard_map/ppermute | solution.py:35
  194.6 27.6 %collective-permute-start.42 = (bf16[4,32,1536]{2,1,0:T(8,128)(2,1)S(1)}, bf16[4,32,1536]{2,1,0:T(8,128)(2,1)S(1)}, u32[]{:S(2)}, u32[]{:S(2)}) collective-permute-start(bf16[4,32,1536]{2,1,0:T(8,128)(2,1)S(1)} %bitcast_dynamic-update-slice_fusion.59), channel_id=1, source_target_pairs={{2,0},{0,2},{3,1},{1,3},{6,4},{4,6},{7,5},{5,7},{10,8},{8,10},{11,... | collective-permute-start | bytes 1179656 | tf_op jit(solution)/shard_map/ppermute | solution.py:35
  243.4 20.4 %collective-permute-start.12 = (bf16[4,2,32,1536]{3,2,1,0:T(8,128)(2,1)S(1)}, bf16[4,2,32,1536]{3,2,1,0:T(8,128)(2,1)S(1)}, u32[]{:S(2)}, u32[]{:S(2)}) collective-permute-start(bf16[4,2,32,1536]{3,2,1,0:T(8,128)(2,1)S(1)} %bitcast_dynamic-update-slice_fusion.36), channel_id=1, source_target_pairs={{2,0},{0,2},{3,1},{1,3},{6,4},{4,6},{7,5},{5,7},{10,8},{8,10},{11,... | collective-permute-start | bytes 2359304 | tf_op jit(solution)/shard_map/ppermute | solution.py:35
  246.8 20.4 %collective-permute-start.18 = (bf16[4,2,32,1536]{3,2,1,0:T(8,128)(2,1)S(1)}, bf16[4,2,32,1536]{3,2,1,0:T(8,128)(2,1)S(1)}, u32[]{:S(2)}, u32[]{:S(2)}) collective-permute-start(bf16[4,2,32,1536]{3,2,1,0:T(8,128)(2,1)S(1)} %bitcast_dynamic-update-slice_fusion.35), channel_id=1, source_target_pairs={{4,0},{0,4},{5,1},{1,5},{6,2},{2,6},{7,3},{3,7},{12,8},{8,12},{13,... | collective-permute-start | bytes 2359304 | tf_op jit(solution)/shard_map/ppermute | solution.py:35
  248.5 32.2 %collective-permute-start.37 = (bf16[4,2,32,1536]{3,2,1,0:T(8,128)(2,1)S(1)}, bf16[4,2,32,1536]{3,2,1,0:T(8,128)(2,1)S(1)}, u32[]{:S(2)}, u32[]{:S(2)}) collective-permute-start(bf16[4,2,32,1536]{3,2,1,0:T(8,128)(2,1)S(1)} %bitcast_dynamic-update-slice_fusion.34), channel_id=1, source_target_pairs={{2,0},{0,2},{3,1},{1,3},{6,4},{4,6},{7,5},{5,7},{10,8},{8,10},{11,... | collective-permute-start | bytes 2359304 | tf_op jit(solution)/shard_map/ppermute | solution.py:35
  249.3 35.2 %collective-permute-start.43 = (bf16[4,2,32,1536]{3,2,1,0:T(8,128)(2,1)S(1)}, bf16[4,2,32,1536]{3,2,1,0:T(8,128)(2,1)S(1)}, u32[]{:S(2)}, u32[]{:S(2)}) collective-permute-start(bf16[4,2,32,1536]{3,2,1,0:T(8,128)(2,1)S(1)} %bitcast_dynamic-update-slice_fusion.33), channel_id=1, source_target_pairs={{4,0},{0,4},{5,1},{1,5},{6,2},{2,6},{7,3},{3,7},{12,8},{8,12},{13,... | collective-permute-start | bytes 2359304 | tf_op jit(solution)/shard_map/ppermute | solution.py:35
  250.1 38.1 %collective-permute-start.7 = (bf16[2,256,1024]{2,1,0:T(8,128)(2,1)S(1)}, bf16[2,256,1024]{2,1,0:T(8,128)(2,1)S(1)}, u32[]{:S(2)}, u32[]{:S(2)}) collective-permute-start(bf16[2,256,1024]{2,1,0:T(8,128)(2,1)S(1)} %bitcast_dynamic-update-slice_fusion.32), channel_id=1, source_target_pairs={{1,0},{0,1},{3,2},{2,3},{5,4},{4,5},{7,6},{6,7},{9,8},{8,9},{11,10... | collective-permute-start | bytes 3145736 | tf_op jit(solution)/shard_map/ppermute | solution.py:35
  263.8 24.9 %collective-permute-start.86 = (bf16[2,256,1024]{2,1,0:T(8,128)(2,1)S(1)}, bf16[2,256,1024]{2,1,0:T(8,128)(2,1)S(1)}, u32[]{:S(2)}, u32[]{:S(2)}) collective-permute-start(bf16[2,256,1024]{2,1,0:T(8,128)(2,1)S(1)} %bitcast_dynamic-update-slice_fusion.23), channel_id=1, source_target_pairs={{1,0},{0,1},{3,2},{2,3},{5,4},{4,5},{7,6},{6,7},{9,8},{8,9},{11,10... | collective-permute-start | bytes 3145736 | tf_op jit(solution)/shard_map/ppermute | solution.py:35
  267.2 36.0 %collective-permute-start.73 = (bf16[4,2,128,512]{3,2,1,0:T(8,128)(2,1)}, bf16[4,2,128,512]{3,2,1,0:T(8,128)(2,1)}, u32[]{:S(2)}, u32[]{:S(2)}) collective-permute-start(bf16[4,2,128,512]{3,2,1,0:T(8,128)(2,1)} %bitcast_dynamic-update-slice_fusion.25), channel_id=1, source_target_pairs={{2,0},{0,2},{3,1},{1,3},{6,4},{4,6},{7,5},{5,7},{10,8},{8,10},{11,... | collective-permute-start | bytes 3145736 | tf_op jit(solution)/shard_map/ppermute | solution.py:35
  280.6 27.7 %collective-permute-start.79 = (bf16[4,2,128,512]{3,2,1,0:T(8,128)(2,1)}, bf16[4,2,128,512]{3,2,1,0:T(8,128)(2,1)}, u32[]{:S(2)}, u32[]{:S(2)}) collective-permute-start(bf16[4,2,128,512]{3,2,1,0:T(8,128)(2,1)} %bitcast_dynamic-update-slice_fusion.24), channel_id=1, source_target_pairs={{4,0},{0,4},{5,1},{1,5},{6,2},{2,6},{7,3},{3,7},{12,8},{8,12},{13,... | collective-permute-start | bytes 3145736 | tf_op jit(solution)/shard_map/ppermute | solution.py:35
  284.5 49.0 %collective-permute-start.61 = (bf16[4,2,32,2048]{3,2,1,0:T(8,128)(2,1)}, bf16[4,2,32,2048]{3,2,1,0:T(8,128)(2,1)}, u32[]{:S(2)}, u32[]{:S(2)}) collective-permute-start(bf16[4,2,32,2048]{3,2,1,0:T(8,128)(2,1)} %bitcast_dynamic-update-slice_fusion.27), channel_id=1, source_target_pairs={{2,0},{0,2},{3,1},{1,3},{6,4},{4,6},{7,5},{5,7},{10,8},{8,10},{11,... | collective-permute-start | bytes 3145736 | tf_op jit(solution)/shard_map/ppermute | solution.py:35
  288.1 40.2 %collective-permute-start.67 = (bf16[4,2,32,2048]{3,2,1,0:T(8,128)(2,1)}, bf16[4,2,32,2048]{3,2,1,0:T(8,128)(2,1)}, u32[]{:S(2)}, u32[]{:S(2)}) collective-permute-start(bf16[4,2,32,2048]{3,2,1,0:T(8,128)(2,1)} %bitcast_dynamic-update-slice_fusion.26), channel_id=1, source_target_pairs={{4,0},{0,4},{5,1},{1,5},{6,2},{2,6},{7,3},{3,7},{12,8},{8,12},{13,... | collective-permute-start | bytes 3145736 | tf_op jit(solution)/shard_map/ppermute | solution.py:35
  288.7 50.5 %collective-permute-start.19 = (bf16[4,2,2,32,1536]{4,3,2,1,0:T(8,128)(2,1)S(1)}, bf16[4,2,2,32,1536]{4,3,2,1,0:T(8,128)(2,1)}, u32[]{:S(2)}, u32[]{:S(2)}) collective-permute-start(bf16[4,2,2,32,1536]{4,3,2,1,0:T(8,128)(2,1)S(1)} %bitcast_dynamic-update-slice_fusion.21), channel_id=1, source_target_pairs={{1,0},{0,1},{3,2},{2,3},{5,4},{4,5},{7,6},{6,7},{9,8},{8,9},{11,10... | collective-permute-start | bytes 4718600 | tf_op jit(solution)/shard_map/ppermute | solution.py:35
  303.2 97.2 %collective-permute-start.44 = (bf16[4,2,2,32,1536]{4,3,2,1,0:T(8,128)(2,1)}, bf16[4,2,2,32,1536]{4,3,2,1,0:T(8,128)(2,1)}, u32[]{:S(2)}, u32[]{:S(2)}) collective-permute-start(bf16[4,2,2,32,1536]{4,3,2,1,0:T(8,128)(2,1)} %bitcast_dynamic-update-slice_fusion.19), channel_id=1, source_target_pairs={{1,0},{0,1},{3,2},{2,3},{5,4},{4,5},{7,6},{6,7},{9,8},{8,9},{11,10... | collective-permute-start | bytes 4718600 | tf_op jit(solution)/shard_map/ppermute | solution.py:35
  308.3 32.8 %collective-permute-start.13 = (bf16[4,2,2,32,1536]{4,3,2,1,0:T(8,128)(2,1)S(1)}, bf16[4,2,2,32,1536]{4,3,2,1,0:T(8,128)(2,1)S(1)}, u32[]{:S(2)}, u32[]{:S(2)}) collective-permute-start(bf16[4,2,2,32,1536]{4,3,2,1,0:T(8,128)(2,1)S(1)} %bitcast_dynamic-update-slice_fusion.22), channel_id=1, source_target_pairs={{1,0},{0,1},{3,2},{2,3},{5,4},{4,5},{7,6},{6,7},{9,8},{8,9},{11,10... | collective-permute-start | bytes 4718600 | tf_op jit(solution)/shard_map/ppermute | solution.py:35
  328.4 58.7 %collective-permute-start.38 = (bf16[4,2,2,32,1536]{4,3,2,1,0:T(8,128)(2,1)}, bf16[4,2,2,32,1536]{4,3,2,1,0:T(8,128)(2,1)}, u32[]{:S(2)}, u32[]{:S(2)}) collective-permute-start(bf16[4,2,2,32,1536]{4,3,2,1,0:T(8,128)(2,1)} %bitcast_dynamic-update-slice_fusion.20), channel_id=1, source_target_pairs={{1,0},{0,1},{3,2},{2,3},{5,4},{4,5},{7,6},{6,7},{9,8},{8,9},{11,10... | collective-permute-start | bytes 4718600 | tf_op jit(solution)/shard_map/ppermute | solution.py:35
  333.5 87.7 %collective-permute-start.68 = (bf16[4,2,2,32,2048]{4,3,2,1,0:T(8,128)(2,1)}, bf16[4,2,2,32,2048]{4,3,2,1,0:T(8,128)(2,1)}, u32[]{:S(2)}, u32[]{:S(2)}) collective-permute-start(bf16[4,2,2,32,2048]{4,3,2,1,0:T(8,128)(2,1)} %bitcast_dynamic-update-slice_fusion.15), channel_id=1, source_target_pairs={{1,0},{0,1},{3,2},{2,3},{5,4},{4,5},{7,6},{6,7},{9,8},{8,9},{11,10... | collective-permute-start | bytes 6291464 | tf_op jit(solution)/shard_map/ppermute | solution.py:35
  339.2 87.6 %collective-permute-start.62 = (bf16[4,2,2,32,2048]{4,3,2,1,0:T(8,128)(2,1)}, bf16[4,2,2,32,2048]{4,3,2,1,0:T(8,128)(2,1)}, u32[]{:S(2)}, u32[]{:S(2)}) collective-permute-start(bf16[4,2,2,32,2048]{4,3,2,1,0:T(8,128)(2,1)} %bitcast_dynamic-update-slice_fusion.16), channel_id=1, source_target_pairs={{1,0},{0,1},{3,2},{2,3},{5,4},{4,5},{7,6},{6,7},{9,8},{8,9},{11,10... | collective-permute-start | bytes 6291464 | tf_op jit(solution)/shard_map/ppermute | solution.py:35
  341.1 76.1 %collective-permute-start.80 = (bf16[4,2,2,128,512]{4,3,2,1,0:T(8,128)(2,1)}, bf16[4,2,2,128,512]{4,3,2,1,0:T(8,128)(2,1)}, u32[]{:S(2)}, u32[]{:S(2)}) collective-permute-start(bf16[4,2,2,128,512]{4,3,2,1,0:T(8,128)(2,1)} %bitcast_dynamic-update-slice_fusion.13), channel_id=1, source_target_pairs={{1,0},{0,1},{3,2},{2,3},{5,4},{4,5},{7,6},{6,7},{9,8},{8,9},{11,10... | collective-permute-start | bytes 6291464 | tf_op jit(solution)/shard_map/ppermute | solution.py:35
  387.1 45.1 %collective-permute-start.74 = (bf16[4,2,2,128,512]{4,3,2,1,0:T(8,128)(2,1)}, bf16[4,2,2,128,512]{4,3,2,1,0:T(8,128)(2,1)}, u32[]{:S(2)}, u32[]{:S(2)}) collective-permute-start(bf16[4,2,2,128,512]{4,3,2,1,0:T(8,128)(2,1)} %bitcast_dynamic-update-slice_fusion.14), channel_id=1, source_target_pairs={{1,0},{0,1},{3,2},{2,3},{5,4},{4,5},{7,6},{6,7},{9,8},{8,9},{11,10... | collective-permute-start | bytes 6291464 | tf_op jit(solution)/shard_map/ppermute | solution.py:35
  400.5 56.6 %collective-permute-start.32 = (f32[2,128,1024]{1,0,2:T(2,128)}, f32[2,128,1024]{1,0,2:T(2,128)}, u32[]{:S(2)}, u32[]{:S(2)}) collective-permute-start(f32[2,128,1024]{1,0,2:T(2,128)} %bitcast.877), channel_id=1, source_target_pairs={{1,0},{0,1},{3,2},{2,3},{5,4},{4,5},{7,6},{6,7},{9,8},{8,9},{11,10... | collective-permute-start | bytes 3145736 | tf_op jit(solution)/shard_map/ppermute | solution.py:35
  636.7 163.6 %collective-permute-start.166 = (bf16[512,1024]{1,0:T(8,128)(2,1)}, bf16[512,1024]{1,0:T(8,128)(2,1)}, u32[]{:S(2)}, u32[]{:S(2)}) collective-permute-start(bf16[512,1024]{1,0:T(8,128)(2,1)} %convolution_convert_fusion.13), channel_id=1, source_target_pairs={{1,0},{0,1},{3,2},{2,3},{5,4},{4,5},{7,6},{6,7},{9,8},{8,9},{11,10... | collective-permute-start | bytes 3145736 | tf_op jit(solution)/shard_map/ppermute | solution.py:35
  636.7 138.8 %collective-permute-start.121 = (bf16[512,1024]{1,0:T(8,128)(2,1)}, bf16[512,1024]{1,0:T(8,128)(2,1)}, u32[]{:S(2)}, u32[]{:S(2)}) collective-permute-start(bf16[512,1024]{1,0:T(8,128)(2,1)} %convolution_convert_fusion.15), channel_id=1, source_target_pairs={{1,0},{0,1},{3,2},{2,3},{5,4},{4,5},{7,6},{6,7},{9,8},{8,9},{11,10... | collective-permute-start | bytes 3145736 | tf_op jit(solution)/shard_map/ppermute | solution.py:35
  672.2 48.2 %collective-permute-start.87 = (f32[2,128,1024]{2,1,0:T(8,128)}, f32[2,128,1024]{2,1,0:T(8,128)}, u32[]{:S(2)}, u32[]{:S(2)}) collective-permute-start(f32[2,128,1024]{2,1,0:T(8,128)} %get-tuple-element.78), channel_id=1, source_target_pairs={{1,0},{0,1},{3,2},{2,3},{5,4},{4,5},{7,6},{6,7},{9,8},{8,9},{11,10... | collective-permute-start | bytes 3145736 | tf_op jit(solution)/shard_map/ppermute | solution.py:35
  677.9 243.5 %collective-permute-start.99 = (bf16[512,3072]{1,0:T(8,128)(2,1)}, bf16[512,3072]{1,0:T(8,128)(2,1)}, u32[]{:S(2)}, u32[]{:S(2)}) collective-permute-start(bf16[512,3072]{1,0:T(8,128)(2,1)} %convolution_convert_fusion.2), channel_id=1, source_target_pairs={{1,0},{0,1},{3,2},{2,3},{5,4},{4,5},{7,6},{6,7},{9,8},{8,9},{11,10... | collective-permute-start | bytes 9437192 | tf_op jit(solution)/shard_map/ppermute | solution.py:35
  779.7 40.2 %collective-permute-start.127 = (bf16[4,2,32,512]{3,2,0,1:T(8,128)(2,1)}, bf16[4,2,32,512]{3,2,0,1:T(8,128)(2,1)S(1)}, u32[]{:S(2)}, u32[]{:S(2)}) collective-permute-start(bf16[4,2,32,512]{3,2,0,1:T(8,128)(2,1)} %fusion.136), channel_id=1, source_target_pairs={{2,0},{0,2},{3,1},{1,3},{6,4},{4,6},{7,5},{5,7},{10,8},{8,10},{11,... | collective-permute-start | bytes 786440 | tf_op jit(solution)/shard_map/ppermute | solution.py:35
  832.9 35.1 %collective-permute-start.110 = (bf16[512,1024]{1,0:T(8,128)(2,1)S(1)}, bf16[512,1024]{1,0:T(8,128)(2,1)S(1)}, u32[]{:S(2)}, u32[]{:S(2)}) collective-permute-start(bf16[512,1024]{1,0:T(8,128)(2,1)S(1)} %convolution_convert_fusion.17), channel_id=1, source_target_pairs={{1,0},{0,1},{3,2},{2,3},{5,4},{4,5},{7,6},{6,7},{9,8},{8,9},{11,10... | collective-permute-start | bytes 3145736 | tf_op jit(solution)/shard_map/ppermute | solution.py:35
  846.8 110.0 %collective-permute-start.143 = (bf16[2048,1024]{1,0:T(8,128)(2,1)S(1)}, bf16[2048,1024]{1,0:T(8,128)(2,1)S(1)}, u32[]{:S(2)}, u32[]{:S(2)}) collective-permute-start(bf16[2048,1024]{1,0:T(8,128)(2,1)S(1)} %copy-done.121), channel_id=1, source_target_pairs={{1,0},{0,1},{3,2},{2,3},{5,4},{4,5},{7,6},{6,7},{9,8},{8,9},{11,10... | collective-permute-start | bytes 12582920 | tf_op jit(solution)/shard_map/ppermute | solution.py:35
  846.8 23.3 %collective-permute-start.160 = (bf16[512,1024]{1,0:T(8,128)(2,1)S(1)}, bf16[512,1024]{1,0:T(8,128)(2,1)S(1)}, u32[]{:S(2)}, u32[]{:S(2)}) collective-permute-start(bf16[512,1024]{1,0:T(8,128)(2,1)S(1)} %convolution_convert_fusion.9), channel_id=1, source_target_pairs={{1,0},{0,1},{3,2},{2,3},{5,4},{4,5},{7,6},{6,7},{9,8},{8,9},{11,10... | collective-permute-start | bytes 3145736 | tf_op jit(solution)/shard_map/ppermute | solution.py:35
  907.8 56.1 %collective-permute-start.132 = (bf16[512,4096]{1,0:T(8,128)(2,1)}, bf16[512,4096]{1,0:T(8,128)(2,1)}, u32[]{:S(2)}, u32[]{:S(2)}) collective-permute-start(bf16[512,4096]{1,0:T(8,128)(2,1)} %convolution_convert_fusion), channel_id=1, source_target_pairs={{1,0},{0,1},{3,2},{2,3},{5,4},{4,5},{7,6},{6,7},{9,8},{8,9},{11,10... | collective-permute-start | bytes 12582920 | tf_op jit(solution)/shard_map/ppermute | solution.py:35
  907.8 66.8 %collective-permute-start.88 = (bf16[512,3072]{1,0:T(8,128)(2,1)}, bf16[512,3072]{1,0:T(8,128)(2,1)}, u32[]{:S(2)}, u32[]{:S(2)}) collective-permute-start(bf16[512,3072]{1,0:T(8,128)(2,1)} %convolution_convert_fusion.4), channel_id=1, source_target_pairs={{1,0},{0,1},{3,2},{2,3},{5,4},{4,5},{7,6},{6,7},{9,8},{8,9},{11,10... | collective-permute-start | bytes 9437192 | tf_op jit(solution)/shard_map/ppermute | solution.py:35
  934.6 20.1 %collective-permute-start.100 = (bf16[4,2,32,1536]{3,2,0,1:T(8,128)(2,1)S(1)}, bf16[4,2,32,1536]{3,2,0,1:T(8,128)(2,1)S(1)}, u32[]{:S(2)}, u32[]{:S(2)}) collective-permute-start(bf16[4,2,32,1536]{3,2,0,1:T(8,128)(2,1)S(1)} %fusion.104), channel_id=1, source_target_pairs={{4,0},{0,4},{5,1},{1,5},{6,2},{2,6},{7,3},{3,7},{12,8},{8,12},{13,... | collective-permute-start | bytes 2359304 | tf_op jit(solution)/shard_map/ppermute | solution.py:35
  944.3 35.6 %collective-permute-start.106 = (bf16[4,32,1536]{2,1,0:T(8,128)(2,1)}, bf16[4,32,1536]{2,1,0:T(8,128)(2,1)}, u32[]{:S(2)}, u32[]{:S(2)}) collective-permute-start(bf16[4,32,1536]{2,1,0:T(8,128)(2,1)} %fusion.129), channel_id=1, source_target_pairs={{4,0},{0,4},{5,1},{1,5},{6,2},{2,6},{7,3},{3,7},{12,8},{8,12},{13,... | collective-permute-start | bytes 1179656 | tf_op jit(solution)/shard_map/ppermute | solution.py:35
  955.7 30.7 %collective-permute-start.101 = (bf16[4,32,1536]{2,1,0:T(8,128)(2,1)}, bf16[4,32,1536]{2,1,0:T(8,128)(2,1)}, u32[]{:S(2)}, u32[]{:S(2)}) collective-permute-start(bf16[4,32,1536]{2,1,0:T(8,128)(2,1)} %fusion.128), channel_id=1, source_target_pairs={{2,0},{0,2},{3,1},{1,3},{6,4},{4,6},{7,5},{5,7},{10,8},{8,10},{11,... | collective-permute-start | bytes 1179656 | tf_op jit(solution)/shard_map/ppermute | solution.py:35
  961.8 74.2 %collective-permute-start.149 = (bf16[4,2,128,512]{3,2,0,1:T(8,128)(2,1)}, bf16[4,2,128,512]{3,2,0,1:T(8,128)(2,1)}, u32[]{:S(2)}, u32[]{:S(2)}) collective-permute-start(bf16[4,2,128,512]{3,2,0,1:T(8,128)(2,1)} %fusion.87), channel_id=1, source_target_pairs={{2,0},{0,2},{3,1},{1,3},{6,4},{4,6},{7,5},{5,7},{10,8},{8,10},{11,... | collective-permute-start | bytes 3145736 | tf_op jit(solution)/shard_map/ppermute | solution.py:35
  963.9 76.9 %collective-permute-start.144 = (bf16[4,2,128,512]{3,2,0,1:T(8,128)(2,1)}, bf16[4,2,128,512]{3,2,0,1:T(8,128)(2,1)}, u32[]{:S(2)}, u32[]{:S(2)}) collective-permute-start(bf16[4,2,128,512]{3,2,0,1:T(8,128)(2,1)} %fusion.86), channel_id=1, source_target_pairs={{4,0},{0,4},{5,1},{1,5},{6,2},{2,6},{7,3},{3,7},{12,8},{8,12},{13,... | collective-permute-start | bytes 3145736 | tf_op jit(solution)/shard_map/ppermute | solution.py:35
  995.3 48.6 %collective-permute-start.138 = (bf16[4,2,32,2048]{3,2,0,1:T(8,128)(2,1)S(1)}, bf16[4,2,32,2048]{3,2,0,1:T(8,128)(2,1)S(1)}, u32[]{:S(2)}, u32[]{:S(2)}) collective-permute-start(bf16[4,2,32,2048]{3,2,0,1:T(8,128)(2,1)S(1)} %fusion.85), channel_id=1, source_target_pairs={{2,0},{0,2},{3,1},{1,3},{6,4},{4,6},{7,5},{5,7},{10,8},{8,10},{11,... | collective-permute-start | bytes 3145736 | tf_op jit(solution)/shard_map/ppermute | solution.py:35
  996.3 37.0 %collective-permute-start.94 = (bf16[4,2,32,1536]{3,2,0,1:T(8,128)(2,1)S(1)}, bf16[4,2,32,1536]{3,2,0,1:T(8,128)(2,1)S(1)}, u32[]{:S(2)}, u32[]{:S(2)}) collective-permute-start(bf16[4,2,32,1536]{3,2,0,1:T(8,128)(2,1)S(1)} %fusion.103), channel_id=1, source_target_pairs={{2,0},{0,2},{3,1},{1,3},{6,4},{4,6},{7,5},{5,7},{10,8},{8,10},{11,... | collective-permute-start | bytes 2359304 | tf_op jit(solution)/shard_map/ppermute | solution.py:35
  998.7 36.2 %collective-permute-start.89 = (bf16[4,2,32,1536]{3,2,0,1:T(8,128)(2,1)S(1)}, bf16[4,2,32,1536]{3,2,0,1:T(8,128)(2,1)S(1)}, u32[]{:S(2)}, u32[]{:S(2)}) collective-permute-start(bf16[4,2,32,1536]{3,2,0,1:T(8,128)(2,1)S(1)} %fusion.102), channel_id=1, source_target_pairs={{4,0},{0,4},{5,1},{1,5},{6,2},{2,6},{7,3},{3,7},{12,8},{8,12},{13,... | collective-permute-start | bytes 2359304 | tf_op jit(solution)/shard_map/ppermute | solution.py:35
  1033.2 18.4 %collective-permute-start.133 = (bf16[4,2,32,2048]{3,2,0,1:T(8,128)(2,1)S(1)}, bf16[4,2,32,2048]{3,2,0,1:T(8,128)(2,1)S(1)}, u32[]{:S(2)}, u32[]{:S(2)}) collective-permute-start(bf16[4,2,32,2048]{3,2,0,1:T(8,128)(2,1)S(1)} %fusion.84), channel_id=1, source_target_pairs={{4,0},{0,4},{5,1},{1,5},{6,2},{2,6},{7,3},{3,7},{12,8},{8,12},{13,... | collective-permute-start | bytes 3145736 | tf_op jit(solution)/shard_map/ppermute | solution.py:35
  1034.9 23.0 %collective-permute-start.95 = (bf16[4,32,1536]{2,1,0:T(8,128)(2,1)S(1)}, bf16[4,32,1536]{2,1,0:T(8,128)(2,1)S(1)}, u32[]{:S(2)}, u32[]{:S(2)}) collective-permute-start(bf16[4,32,1536]{2,1,0:T(8,128)(2,1)S(1)} %fusion.127), channel_id=1, source_target_pairs={{4,0},{0,4},{5,1},{1,5},{6,2},{2,6},{7,3},{3,7},{12,8},{8,12},{13,... | collective-permute-start | bytes 1179656 | tf_op jit(solution)/shard_map/ppermute | solution.py:35
  1035.9 26.0 %collective-permute-start.90 = (bf16[4,32,1536]{2,1,0:T(8,128)(2,1)S(1)}, bf16[4,32,1536]{2,1,0:T(8,128)(2,1)S(1)}, u32[]{:S(2)}, u32[]{:S(2)}) collective-permute-start(bf16[4,32,1536]{2,1,0:T(8,128)(2,1)S(1)} %fusion.126), channel_id=1, source_target_pairs={{2,0},{0,2},{3,1},{1,3},{6,4},{4,6},{7,5},{5,7},{10,8},{8,10},{11,... | collective-permute-start | bytes 1179656 | tf_op jit(solution)/shard_map/ppermute | solution.py:35
  1040.8 46.5 %collective-permute-start.150 = (bf16[4,128,512]{2,1,0:T(8,128)(2,1)}, bf16[4,128,512]{2,1,0:T(8,128)(2,1)}, u32[]{:S(2)}, u32[]{:S(2)}) collective-permute-start(bf16[4,128,512]{2,1,0:T(8,128)(2,1)} %fusion.113), channel_id=1, source_target_pairs={{4,0},{0,4},{5,1},{1,5},{6,2},{2,6},{7,3},{3,7},{12,8},{8,12},{13,... | collective-permute-start | bytes 1572872 | tf_op jit(solution)/shard_map/ppermute | solution.py:35
  1043.8 50.5 %collective-permute-start.145 = (bf16[4,128,512]{2,1,0:T(8,128)(2,1)S(1)}, bf16[4,128,512]{2,1,0:T(8,128)(2,1)}, u32[]{:S(2)}, u32[]{:S(2)}) collective-permute-start(bf16[4,128,512]{2,1,0:T(8,128)(2,1)S(1)} %fusion.112), channel_id=1, source_target_pairs={{2,0},{0,2},{3,1},{1,3},{6,4},{4,6},{7,5},{5,7},{10,8},{8,10},{11,... | collective-permute-start | bytes 1572872 | tf_op jit(solution)/shard_map/ppermute | solution.py:35
  1074.4 18.7 %collective-permute-start.139 = (bf16[4,32,2048]{2,1,0:T(8,128)(2,1)}, bf16[4,32,2048]{2,1,0:T(8,128)(2,1)}, u32[]{:S(2)}, u32[]{:S(2)}) collective-permute-start(bf16[4,32,2048]{2,1,0:T(8,128)(2,1)} %fusion.111), channel_id=1, source_target_pairs={{4,0},{0,4},{5,1},{1,5},{6,2},{2,6},{7,3},{3,7},{12,8},{8,12},{13,... | collective-permute-start | bytes 1572872 | tf_op jit(solution)/shard_map/ppermute | solution.py:35
  1076.2 23.2 %collective-permute-start.134 = (bf16[4,32,2048]{2,1,0:T(8,128)(2,1)}, bf16[4,32,2048]{2,1,0:T(8,128)(2,1)}, u32[]{:S(2)}, u32[]{:S(2)}) collective-permute-start(bf16[4,32,2048]{2,1,0:T(8,128)(2,1)} %fusion.110), channel_id=1, source_target_pairs={{2,0},{0,2},{3,1},{1,3},{6,4},{4,6},{7,5},{5,7},{10,8},{8,10},{11,... | collective-permute-start | bytes 1572872 | tf_op jit(solution)/shard_map/ppermute | solution.py:35
  1089.1 18.7 %collective-permute-start.151 = (bf16[128,512]{1,0:T(8,128)(2,1)S(1)}, bf16[128,512]{1,0:T(8,128)(2,1)S(1)}, u32[]{:S(2)}, u32[]{:S(2)}) collective-permute-start(bf16[128,512]{1,0:T(8,128)(2,1)S(1)} %get-tuple-element.89), channel_id=1, source_target_pairs={{24,0},{0,8},{8,16},{16,24},{25,1},{1,9},{9,17},{17,25},{26,2},{2,... | collective-permute-start | bytes 393224 | tf_op jit(solution)/shard_map/ppermute | solution.py:35
  1089.2 18.7 %collective-permute-start.153 = (bf16[128,512]{1,0:T(8,128)(2,1)S(1)}, bf16[128,512]{1,0:T(8,128)(2,1)S(1)}, u32[]{:S(2)}, u32[]{:S(2)}) collective-permute-start(bf16[128,512]{1,0:T(8,128)(2,1)S(1)} %get-tuple-element.90), channel_id=1, source_target_pairs={{8,0},{16,8},{24,16},{0,24},{9,1},{17,9},{25,17},{1,25},{10,2},{18... | collective-permute-start | bytes 393224 | tf_op jit(solution)/shard_map/ppermute | solution.py:35
  (242 other events, 2653.3 us)

commit v2 on v1

v2 whole, which is shorter than its diff:
```python
import functools

import jax
import jax.numpy as jnp
from jax import lax
from jax.experimental import pallas as pl
from jax.experimental.pallas import tpu as pltpu
from jax.sharding import Mesh, PartitionSpec as P

D = 1024
HEADS = 16
HEAD = 64
FRAMES = 4
SLOTS = 256
SMALL_TOKENS = 64
CLIPS = 4
DOMAINS = 4
MICRO = 2
STEP = 10


EPS = 1e-05
NEG = -1e30
BETA_ONE = 0.9
BETA_TWO = 0.95
ADAM_EPS = 1e-08
DECAY = 0.1
RATE = 0.02
RATE_SMALL = 0.2
CLIP = 0.005
LOW = jnp.bfloat16
WIDE = jnp.float32
ALL = ("z", "r", "m", "h")
GROUP = 256
LANES = 128


def shifted(part, axis, shift):
    n = lax.axis_size(axis)
    return lax.ppermute(part, axis, [((i + shift) % n, i) for i in range(n)])


def at(array, index, dim):
    return lax.dynamic_index_in_dim(array, index, dim, keepdims=False)


def sent_around(part, axis):
    return [shifted(part, axis, shift) for shift in range(1, lax.axis_size(axis))]


def placed(part, others, axis, dim):
    n = lax.axis_size(axis)
    mine = lax.axis_index(axis)
    whole = jnp.broadcast_to(
        jnp.expand_dims(part, dim), part.shape[:dim] + (n,) + part.shape[dim:]
    )
    for shift, other in zip(range(1, n), others):
        whole = lax.dynamic_update_index_in_dim(whole, other, (mine + shift) % n, dim)
    return whole


def gather_axis(part, axis, dim):
    return placed(part, sent_around(part, axis), axis, dim)


def halves(array, dim):
    size = array.shape[dim] // lax.axis_size("h")
    half = lax.axis_index("h")
    return [
        lax.dynamic_slice_in_dim(array, start * size, size, dim) for start in (half, 1 - half)
    ]


class Job:
    def __init__(self, steps):
        self.steps = steps
        self.result = None
        self.flight = next(steps)

    def resume(self, arrived):
        try:
            self.flight = self.steps.send(arrived)
        except StopIteration as stop:
            self.flight, self.result = None, stop.value

    def finish(self):
        while self.flight is not None:
            self.resume(self.flight)
        return self.result


def advance(value, *jobs):
    jobs = [job for job in jobs if job.flight is not None]
    value, flights = lax.optimization_barrier((value, [job.flight for job in jobs]))
    for job, flight in zip(jobs, flights):
        job.resume(flight)
    return value


def gather_half(part):
    others = yield sent_around(part, "z")
    first, second = jnp.split(placed(part, others, "z", 0), 2, axis=-1)
    one = sent_around(first, "m")
    two = sent_around(second, "r")
    one, two = yield (one, two)
    first, second = placed(first, one, "m", 1), placed(second, two, "r", 1)
    one = sent_around(first, "r")
    two = sent_around(second, "m")
    one, two = yield (one, two)
    first, second = placed(first, one, "r", 1), placed(second, two, "m", 2)
    own = jnp.concatenate([first, second], axis=-1)
    own = own.reshape(-1, own.shape[-1])
    (other,) = yield [shifted(own, "h", 1)]
    return (own, other)


def by_owner(array, block):
    seen = array.reshape(array.shape[0], -1, 2, block)
    half = lax.axis_index("h")
    return [at(seen, which, 2).reshape(array.shape[0], -1) for which in (half, 1 - half)]


def gather_columns(part, block):
    mine, other = by_owner(part, block)
    (other,) = yield [shifted(other, "h", 1)]
    pair = placed(mine, [other], "h", 0)
    result = yield from gather_half(pair.reshape(-1, mine.shape[1]))
    return result


def reduce_rows(other, own, names, order):
    (arrived,) = yield [shifted(other, "h", 1)]
    total = (own() + arrived.astype(WIDE)).astype(LOW)
    names = list(names)
    total = total.reshape(
        tuple(lax.axis_size(name) for name in names) + (-1, total.shape[-1])
    )
    for axis in order:
        dim = names.index(axis)
        n = lax.axis_size(axis)
        mine = lax.axis_index(axis)
        pieces = [
            shifted(at(total, (mine + shift) % n, dim), axis, n - shift) for shift in range(1, n)
        ]
        pieces = yield pieces
        total = at(total, mine, dim).astype(WIDE)
        for piece in pieces:
            total = total + piece.astype(WIDE)
        names.pop(dim)
        if names:
            total = total.astype(LOW)
            if names == ["h"]:
                total = total.astype(WIDE)
    return total


def swap_rows(total):
    seen = total.reshape(2, -1, total.shape[-1])
    half = lax.axis_index("h")
    (other,) = yield [shifted(at(seen, 1 - half, 0), "h", 1)]
    return (at(seen, half, 0), other)


def reduce_layer(other, own, order, block=None):
    total = yield from reduce_rows(other, own, ("z", "r", "m"), order)
    total = total.reshape(-1, total.shape[-1])
    square = jnp.sum(total * total)
    mine, other = yield from swap_rows(total)
    rows = mine.shape[0]
    if block is None:
        return (placed(mine, [other], "h", 1).reshape(rows, -1), square)
    mine, other = (half.reshape(rows, -1, block) for half in (mine, other))
    return (placed(mine, [other], "h", 2).reshape(rows, -1), square)


def reduce_owned(other, own, order):
    total = yield from reduce_rows(other, own, ("z", "r", "m"), order)
    return (total.reshape(-1, total.shape[-1]), jnp.sum(total * total))


def reduce_table(other, own):
    total = yield from reduce_rows(other, own, ("m", "h", "r", "z"), ("m", "r", "z"))
    square = jnp.sum(total * total)
    total = total.astype(LOW)
    others = yield sent_around(total, "z")
    total = placed(total, others, "z", 1)
    others = yield sent_around(total, "r")
    total = placed(total, others, "r", 1)
    mine, other = yield from swap_rows(total.reshape(-1, total.shape[-1]))
    return (placed(mine, [other], "h", 1).reshape(mine.shape[0], -1).astype(WIDE), square)


def summed_over(part, axes):
    for axis in axes:
        shift = lax.axis_size(axis) // 2
        while shift:
            part = part + shifted(part, axis, shift)
            shift //= 2
    return part


def norm_forward(values, gain):
    return values * lax.rsqrt(jnp.mean(values * values, axis=-1, keepdims=True) + EPS) * gain


def norm_backward(values, gain, upstream):
    factor = lax.rsqrt(jnp.mean(values * values, axis=-1, keepdims=True) + EPS)
    scaled = upstream * gain
    inward = factor * scaled - values * factor**3 * jnp.mean(
        scaled * values, axis=-1, keepdims=True
    )
    gain_grad = jnp.sum(upstream * values * factor, axis=0)
    return (inward, gain_grad)


def dot_nt(left, right):
    return lax.dot_general(left, right, (((1,), (1,)), ((), ())), preferred_element_type=WIDE)


def dot_tn(left, right):
    return lax.dot_general(left, right, (((0,), (0,)), ((), ())), preferred_element_type=WIDE)


def dot_nn(left, right):
    return jnp.dot(left, right, preferred_element_type=WIDE)


def allowed_pairs(kind, scalar, count):
    row = lax.broadcasted_iota(jnp.int32, (count, count), 0)
    col = lax.broadcasted_iota(jnp.int32, (count, count), 1)
    if kind == "space":
        return (scalar == 0) | (row // SMALL_TOKENS == col // SMALL_TOKENS)
    lanes = count // FRAMES
    own = FRAMES // 2
    row_frame, col_frame = row // lanes, col // lanes
    row_at = row_frame + jnp.where(scalar == 0, 0, jnp.where(row_frame < own, own, -own))
    col_at = col_frame + jnp.where(scalar == 0, 0, jnp.where(col_frame < own, own, -own))
    return (row % lanes == col % lanes) & (col_at <= row_at)


def softmax_rows(query, key, allowed):
    scores = jnp.where(allowed, dot_nt(query, key) * HEAD ** (-0.5), NEG)
    expd = jnp.exp(scores - jnp.max(scores, axis=-1, keepdims=True))
    return expd / jnp.sum(expd, axis=-1, keepdims=True)


def block_of(ref, start, kind):
    if kind == "space":
        return ref[:, pl.ds(start, LANES)]
    part = ref[:, :, pl.ds(start, LANES)]
    return part.reshape(-1, LANES)


def store_to(ref, start, kind, value):
    if kind == "space":
        ref[:, pl.ds(start, LANES)] = value
    else:
        ref[:, :, pl.ds(start, LANES)] = value.reshape(FRAMES, -1, LANES)


def forward_body(kind, scalar_ref, packed_ref, mixed_ref):
    allowed = allowed_pairs(kind, scalar_ref[0], GROUP)
    first = lax.broadcasted_iota(jnp.int32, (GROUP, LANES), 1) < HEAD

    def turn(pair, _):
        start = pl.multiple_of(pair * LANES, LANES)
        query = block_of(packed_ref, start, kind)
        key = block_of(packed_ref, pl.multiple_of(D + start, LANES), kind)
        value = block_of(packed_ref, pl.multiple_of(2 * D + start, LANES), kind)
        zero = jnp.zeros_like(query)
        one = dot_nn(softmax_rows(jnp.where(first, query, zero), key, allowed).astype(LOW), value)
        two = dot_nn(softmax_rows(jnp.where(first, zero, query), key, allowed).astype(LOW), value)
        store_to(mixed_ref, start, kind, jnp.where(first, one, two).astype(LOW))
        return 0

    lax.fori_loop(0, D // LANES, turn, 0, unroll=4)


def backward_body(kind, scalar_ref, packed_ref, up_ref, out_ref):
    allowed = allowed_pairs(kind, scalar_ref[0], GROUP)
    first = lax.broadcasted_iota(jnp.int32, (GROUP, LANES), 1) < HEAD

    def turn(pair, _):
        start = pl.multiple_of(pair * LANES, LANES)
        key_at = pl.multiple_of(D + start, LANES)
        value_at = pl.multiple_of(2 * D + start, LANES)
        query = block_of(packed_ref, start, kind)
        key = block_of(packed_ref, key_at, kind)
        value = block_of(packed_ref, value_at, kind)
        up = block_of(up_ref, start, kind)
        zero = jnp.zeros_like(query)
        grads = []
        for mine in (first, ~first):
            probs = softmax_rows(jnp.where(mine, query, zero), key, allowed)
            inner = dot_nt(jnp.where(mine, up, zero), value)
            total = jnp.sum(probs * inner, axis=-1, keepdims=True)
            scores = (probs * (inner - total) * HEAD ** (-0.5)).astype(LOW)
            grads.append((dot_nn(scores, key), dot_tn(scores, query), dot_tn(probs.astype(LOW), up)))
        for place, one, two in zip((start, key_at, value_at), *grads):
            store_to(out_ref, place, kind, jnp.where(first, one, two).astype(LOW))
        return 0

    lax.fori_loop(0, D // LANES, turn, 0, unroll=2)


def attention(kind, scalar, packed, up=None):
    shape = packed.shape[:-1]
    if kind == "space":
        grid, block, where = (shape[0] // GROUP,), (GROUP,), lambda g, s: (g, 0)
    else:
        grid, block, where = (FRAMES * shape[1] // GROUP,), (FRAMES, GROUP // FRAMES), lambda g, s: (0, g, 0)
    wide = pl.BlockSpec(block + (3 * D,), where)
    narrow = pl.BlockSpec(block + (D,), where)
    body, last, ins = forward_body, D, (packed,)
    if up is not None:
        body, last, ins = backward_body, 3 * D, (packed, up.reshape(shape + (D,)))
    return pl.pallas_call(
        functools.partial(body, kind),
        out_shape=jax.ShapeDtypeStruct(shape + (last,), LOW),
        grid_spec=pltpu.PrefetchScalarGridSpec(
            num_scalar_prefetch=1,
            grid=grid,
            in_specs=[wide, narrow][: len(ins)],
            out_specs=narrow if up is None else wide,
        ),
    )(scalar.reshape(1).astype(jnp.int32), *ins)


def adamw(weight, grad, first, second, rate, decay):
    first_new = BETA_ONE * first + (1.0 - BETA_ONE) * grad
    second_new = BETA_TWO * second + (1.0 - BETA_TWO) * grad * grad
    unbiased_first = first_new / (1.0 - BETA_ONE**STEP)
    unbiased_second = second_new / (1.0 - BETA_TWO**STEP)
    updated = weight - rate * (
        unbiased_first / (jnp.sqrt(unbiased_second) + ADAM_EPS) + decay * weight
    )
    return (updated, first_new, second_new)


def gelu(values):
    return jax.nn.gelu(values, approximate=True)


def gelu_backward(values, upstream):
    return jax.vjp(gelu, values)[1](upstream)[0]


def swap_slots(values):
    mine, other = halves(values, 1)
    return jnp.concatenate([mine, shifted(other, "h", 1)], axis=0)


def swap_frames(values):
    half = lax.axis_index("h")
    mine, other = jnp.split(values, 2, axis=0)
    other = shifted(other, "h", 1)
    return jnp.where(
        half == 0,
        jnp.concatenate([mine, other], axis=1),
        jnp.concatenate([other, mine], axis=1),
    )


def on_device(
    tokens,
    masked,
    small_grid,
    domains,
    attend_in,
    attend_out,
    expand,
    contract,
    gains,
    tables,
    mean_in,
    mean_out,
    mean_expand,
    mean_contract,
    mean_gains,
    mean_tables,
    square_in,
    square_out,
    square_expand,
    square_contract,
    square_gains,
    square_tables,
):
    micro = lax.axis_index("m")
    half = lax.axis_index("h")
    frames = FRAMES // lax.axis_size("h")
    block = contract.shape[0]
    kinds = gains.shape[0]

    def of_micro(array):
        return at(array[:, 0], micro, 0)

    codes = of_micro(tokens)
    hidden_mask = of_micro(masked).astype(WIDE)
    small = of_micro(small_grid)
    doms = of_micro(domains)

    turned = jnp.pad(gains.T, ((0, 0), (0, LANES - kinds)))
    layer_one = jnp.concatenate([attend_in[0], attend_out[0], turned], axis=1).astype(LOW)
    layer_two = jnp.concatenate([attend_in[1], attend_out[1]], axis=1).astype(LOW)
    layer_one = lax.all_gather(layer_one, ALL, axis=0, tiled=True)
    layer_two = lax.all_gather(layer_two, ALL, axis=0, tiled=True)
    low_in, low_out = tables.astype(LOW)
    table_in = gather_axis(gather_axis(low_in, "m", 0), "h", 1).reshape(-1, D)
    up_job = Job(gather_columns(expand.astype(LOW), block))
    down_job = Job(gather_half(contract.astype(LOW)))
    table_out = gather_axis(gather_axis(low_out, "m", 0), "h", 1).reshape(-1, D)

    w_in = (layer_one[:, : 3 * D], layer_two[:, : 3 * D])
    w_out = (layer_one[:, 3 * D : 4 * D], layer_two[:, 3 * D :])
    gain_all = layer_one[:, 4 * D :].T[:kinds].astype(WIDE)

    slot_ids = jnp.arange(SLOTS)
    segment = jnp.where(small > 0, slot_ids // SMALL_TOKENS, 0)
    dom_slot = jnp.sum((segment[:, None] == jnp.arange(CLIPS)[None, :]) * doms[None, :], axis=-1)
    domain_hot = (dom_slot[:, None] == jnp.arange(DOMAINS)[None, :]).astype(WIDE)
    counts = jnp.sum(jnp.sum(hidden_mask, axis=0)[:, None] * domain_hot, axis=0)[None, :]
    counts = summed_over(counts, ("r", "z"))[0]
    scale = 1.0 / (MICRO * DOMAINS * jnp.maximum(counts, 1.0))
    slot_scale = jnp.sum(domain_hot * scale[None, :], axis=1)
    code_ids = jnp.arange(table_in.shape[0])

    def own_frames(array):
        return lax.dynamic_slice_in_dim(array, half * frames, frames, 0)

    def time_order(array):
        mine = halves(array, 1)[0]
        return jnp.concatenate(halves(mine, 0), axis=0).reshape(-1)

    space_codes = own_frames(codes).reshape(-1)
    space_mask = own_frames(hidden_mask).reshape(-1)
    time_codes = time_order(codes)
    time_weight = time_order(hidden_mask * slot_scale[None, :])

    picked = dot_nn((space_codes[:, None] == code_ids[None, :]).astype(LOW), table_in)
    start = jnp.where(space_mask[:, None] > 0, gain_all[4], picked)
    normed_space = norm_forward(start, gain_all[0]).astype(LOW)
    normed_space = advance(normed_space, up_job)
    normed_space = advance(normed_space, up_job, down_job)
    packed_space = dot_nn(normed_space, w_in[0]).astype(LOW)
    mixed_space = attention("space", small, packed_space)
    mixed_space = advance(mixed_space, up_job, down_job)
    after_space = start + dot_nn(mixed_space, w_out[0])
    after_space = swap_slots(after_space.reshape(frames, SLOTS, D)).reshape(-1, D)
    normed_time = norm_forward(after_space, gain_all[1]).astype(LOW)
    normed_time = advance(normed_time, up_job, down_job)
    packed_time = dot_nn(normed_time, w_in[1]).astype(LOW).reshape(FRAMES, -1, 3 * D)
    mixed_time = attention("time", half, packed_time).reshape(-1, D)
    after_time = after_space + dot_nn(mixed_time, w_out[1])
    normed_ffn = norm_forward(after_time, gain_all[2]).astype(LOW)
    ups, downs = up_job.finish(), down_job.finish()
    pres = [dot_nn(normed_ffn, up) for up in ups]
    activs = [gelu(pre).astype(LOW) for pre in pres]
    after_ffn = after_time + dot_nn(activs[0], downs[0]) + dot_nn(activs[1], downs[1])
    final = norm_forward(after_ffn, gain_all[3]).astype(LOW)
    logits = dot_nt(final, table_out)
    hits = time_codes[:, None] == code_ids[None, :]
    top = jnp.max(logits, axis=1, keepdims=True)
    log_total = top + jnp.log(jnp.sum(jnp.exp(logits - top), axis=1, keepdims=True))
    target = jnp.sum(jnp.where(hits, logits, 0.0), axis=1)
    loss_part = jnp.sum(time_weight * (log_total[:, 0] - target))
    grad_logits = (time_weight[:, None] * (jnp.exp(logits - log_total) - hits)).astype(LOW)

    def product(make, left, mine, other, *rest):
        return Job(make(dot_tn(left, other).astype(LOW), lambda: dot_tn(left, mine), *rest))

    head_job = product(reduce_table, grad_logits, *halves(final, 1))
    grad_final = dot_nn(grad_logits, table_out)
    grad_ffn, gain_three = norm_backward(after_ffn, gain_all[3], grad_final)
    up_low = grad_ffn.astype(LOW)
    contract_job = Job(
        reduce_owned(
            dot_tn(activs[1], up_low).astype(LOW),
            lambda: dot_tn(activs[0], up_low),
            ("m", "r", "z"),
        )
    )
    grad_activs = [dot_nt(up_low, down) for down in downs]
    grad_pres = [gelu_backward(pre, grad).astype(LOW) for pre, grad in zip(pres, grad_activs)]
    grad_pres = advance(grad_pres, head_job, contract_job)
    expand_job = product(
        reduce_layer, normed_ffn, grad_pres[0], grad_pres[1], ("r", "m", "z"), block
    )
    grad_normed = dot_nt(grad_pres[0], ups[0]) + dot_nt(grad_pres[1], ups[1])
    inward, gain_two = norm_backward(after_time, gain_all[2], grad_normed)
    grad_time = grad_ffn + inward
    up_low = grad_time.astype(LOW)
    up_low = advance(up_low, head_job, expand_job)
    out_job = product(reduce_layer, mixed_time, *halves(up_low, 1), ("m", "r", "z"))
    grad_mixed = dot_nt(up_low, w_out[1]).astype(LOW)
    grad_packed = attention("time", half, packed_time, grad_mixed).reshape(-1, 3 * D)
    grad_packed = advance(grad_packed, head_job, contract_job, out_job)
    in_job = product(reduce_layer, normed_time, *halves(grad_packed, 1), ("m", "r", "z"))
    grad_normed = dot_nt(grad_packed, w_in[1])
    inward, gain_one = norm_backward(after_space, gain_all[1], grad_normed)
    grad_space = swap_frames((grad_time + inward).reshape(FRAMES, -1, D)).reshape(-1, D)
    up_low = grad_space.astype(LOW)
    up_low = advance(up_low, head_job, contract_job, expand_job, out_job, in_job)
    first_out_job = product(reduce_layer, mixed_space, *halves(up_low, 1), ("r", "m", "z"))
    grad_mixed = dot_nt(up_low, w_out[0]).astype(LOW)
    grad_packed = attention("space", small, packed_space, grad_mixed)
    grad_packed = advance(
        grad_packed, head_job, contract_job, expand_job, out_job, first_out_job
    )
    first_in_job = product(reduce_layer, normed_space, *halves(grad_packed, 1), ("r", "m", "z"))
    grad_normed = dot_nt(grad_packed, w_in[0])
    inward, gain_zero = norm_backward(start, gain_all[0], grad_normed)
    grad_start = grad_space + inward
    mask_grad = jnp.sum(grad_start * space_mask[:, None], axis=0)
    chosen = (jnp.where(space_mask > 0, -1, space_codes)[:, None] == code_ids[None, :]).astype(LOW)
    start_low = grad_start.astype(LOW)
    embed_job = product(reduce_table, chosen, *halves(start_low, 1))

    gain_grads = jnp.stack([gain_zero, gain_one, gain_two, gain_three, mask_grad])
    gain_grads = summed_over(gain_grads, ("h", "r", "m", "z"))
    owner = jnp.int32(0)
    for axis in ALL:
        owner = owner * lax.axis_size(axis) + lax.axis_index(axis)
    width = gains.shape[1]
    gain_grads = lax.dynamic_slice_in_dim(gain_grads, owner * width, width, 1)

    jobs = (in_job, first_in_job, out_job, first_out_job, expand_job, contract_job)
    jobs = jobs + (embed_job, head_job)
    while any(job.flight is not None for job in jobs):
        for job in jobs:
            if job.flight is not None:
                job.resume(job.flight)
    results = [job.result for job in jobs]
    owned = sum(square for _, square in results) + jnp.sum(gain_grads * gain_grads)
    sums = summed_over(jnp.stack([owned, loss_part]).reshape(1, 2), ("h", "m", "r", "z"))
    square_sum, loss = sums[0, 0], sums[0, 1]
    norm = jnp.sqrt(square_sum)
    factor = jnp.minimum(1.0, CLIP / (norm + 1e-06))

    made = [grad for grad, _ in results]
    grads = (
        jnp.stack([made[1], made[0]]),
        jnp.stack([made[3], made[2]]),
        made[4],
        made[5],
        gain_grads,
        jnp.stack([made[6], made[7]]),
    )
    params = (attend_in, attend_out, expand, contract, gains, tables)
    firsts = (mean_in, mean_out, mean_expand, mean_contract, mean_gains, mean_tables)
    seconds = (square_in, square_out, square_expand, square_contract, square_gains, square_tables)
    rates = (RATE, RATE, RATE, RATE, RATE_SMALL, RATE)
    decays = (DECAY, DECAY, DECAY, DECAY, 0.0, DECAY)
    results = [
        adamw(p, factor * g, f, s, r, k)
        for p, g, f, s, r, k in zip(params, grads, firsts, seconds, rates, decays)
    ]
    return (loss, norm) + tuple(result[k] for k in range(3) for result in results)


def solution(mesh):
    dp, code = mesh.shape["dp"], mesh.shape["code"]
    deep = next(n for n in (4, 2, 1) if dp % n == 0)
    fine = Mesh(mesh.devices.reshape(deep, dp // deep, MICRO, code // MICRO), ALL)
    group = ("z", "r")
    weights = (
        P(None, ALL, None),
        P(None, ALL, None),
        P(ALL, None),
        P(ALL, None),
        P(None, ALL),
        P(None, ("m", "h"), None),
    )
    return jax.shard_map(
        on_device,
        mesh=fine,
        in_specs=(
            P(None, group, None, None),
            P(None, group, None, None),
            P(None, group),
            P(None, group, None),
        )
        + weights * 3,
        out_specs=(P(), P()) + weights * 3,
        check_vma=False,
    )
```

time: 1190 us -> 837 us (0.70)
  local copies, waits for them, and re-layouts: 297 us -> 93.5 us
  starting transfers between devices: 218 us -> 107 us
  matrix products: 213 us -> 149 us
  Pallas kernels: 0 us -> 62.7 us
  blocking collectives: 37.9 us -> 0 us
  between operations: 11.3 us -> 24.3 us
    ppermute x180 -> x99, starting transfers between devices: 218 us -> 107 us  [shifted(): return lax.ppermute(part, axis, [((i + shift) % n, i) for i in range(n)])]
    dot_general x43 -> x35, matrix products: 213 us -> 149 us  [the longest x9 51 us: dot_nt(): lax.dot_general(left, right, (((1,), (1,)), ((), ())), preferred_element_...]
    pallas_call x0 -> x4, Pallas kernels: none -> 62.7 us  [attention(): pl.pallas_call(functools.partial(body, kind), out_shape=jax.ShapeDtypeStr...]
    unnamed x281 -> x246, local copies, waits for them, and re-layouts: 65.2 us -> 11.8 us
    all_gather x0 -> x2, waiting for transfers between devices: none -> 48.6 us  [the longest x1 48.6 us: on_device(): layer_one = lax.all_gather(layer_one, ALL, axis=0, tiled=True)]
    ppermute x180 -> x99, waiting for transfers between devices: 319 us -> 273 us  [shifted(): return lax.ppermute(part, axis, [((i + shift) % n, i) for i in range(n)])]
    unnamed x1 -> x0, blocking collectives: 37.9 us -> none
    convert_element_type x54 -> x2, local copies, waits for them, and re-layouts: 38.7 us -> 1.53 us  [reduce_table(): placed(mine, [other], 'h', 1).reshape(mine.shape[0], -1).astype(WIDE)]
  transfers between devices with their start and end apart: 180 -> 101, of which waited for: 75 -> 36; matrix products, arithmetic and copies ran while one was open for 32% -> 32% of each run, Pallas kernels for 0% -> 8%
where the time goes in v2:
time: 837 us; the launch traced here: 830 us
  waiting for transfers between devices  321 us (38%)
  matrix products  149 us (18%)
  starting transfers between devices  107 us (13%)
  local copies, waits for them, and re-layouts  93.5 us (11%)
  other arithmetic  72.2 us (9%)
  Pallas kernels  62.7 us (7%)
  between operations  24.3 us (3%)
    ppermute x99, waiting for transfers between devices, shifted(): return lax.ppermute(part, axis, [((i + shift) % n, i) for i in range(n)])  273 us
    ppermute x99, starting transfers between devices, shifted(): return lax.ppermute(part, axis, [((i + shift) % n, i) for i in range(n)])  107 us
    pallas_call x4, Pallas kernels, attention(): pl.pallas_call(functools.partial(body, kind), out_shape=jax.ShapeDtypeStr...  62.7 us
    dot_general x9, matrix products, dot_nt(): lax.dot_general(left, right, (((1,), (1,)), ((), ())), preferred_element_...  51 us
    dot_general x16, matrix products, dot_tn(): lax.dot_general(left, right, (((0,), (0,)), ((), ())), preferred_element_...  49.8 us
    all_gather x1, waiting for transfers between devices, on_device(): layer_one = lax.all_gather(layer_one, ALL, axis=0, tiled=True)  48.6 us
    dot_general x10, matrix products, dot_nn(): return jnp.dot(left, right, preferred_element_type=WIDE)  47.9 us
    dynamic_update_slice x34, local copies, waits for them, and re-layouts, placed(): lax.dynamic_update_index_in_dim(whole, other, (mine + shift) % n, dim)  33.7 us
  transfers between devices with their start and end apart: 101, of which 36 were waited for; matrix products, arithmetic and copies ran while one was open for 32% of the time, Pallas kernels for 8%

profile of v2, /device:TPU:0, one launch (start us, length us, event | category | flops | bytes accessed | tf_op | source)
XLA Modules:
  0.0 829.6 jit_solution(1644716832759214929)
XLA Ops:
  16.1 3.7 collective-permute-start.6
  22.1 7.8 collective-permute-done
  38.5 9.1 %collective-permute-done.21 = f32[1,4]{1,0:T(1,128)S(1)} collective-permute-done((f32[1,4]{1,0:T(1,128)S(1)}, f32[1,4]{1,0:T(1,128)S(1)}, u32[]{:S(2)}, u32[]{:S(2)}) %collective-permute-start.21) | collective-permute-done | bytes 48 | tf_op jit(solution)/shard_map/ppermute | solution.py:40
  49.1 3.6 collective-permute-start.22
  54.1 48.6 %all-gather.3.cloned.1.call-done = bf16[1024,4224]{1,0:T(8,128)(2,1)} async-done(((bf16[32,4224]{1,0:T(8,128)(2,1)}), bf16[1024,4224]{1,0:T(8,128)(2,1)}) %all-gather.3.cloned.1.call-update) | async-done | bytes 8650768 | tf_op jit(solution)/shard_map/all_gather | solution.py:405
  116.8 6.2 collective-permute-done.3
  123.0 18.9 %collective-permute-done.4 = bf16[64,2048]{1,0:T(8,128)(2,1)S(1)} collective-permute-done((bf16[64,2048]{1,0:T(8,128)(2,1)S(1)}, bf16[64,2048]{1,0:T(8,128)(2,1)S(1)}, u32[]{:S(2)}, u32[]{:S(2)}) %collective-permute-start.4) | collective-permute-done | bytes 262176 | tf_op jit(solution)/shard_map/ppermute | solution.py:40
  151.2 4.8 fusion.8.packed_ref
  156.0 9.3 %shard_map.365 = bf16[512,1024]{1,0:T(8,128)(2,1)} custom-call(s32[1]{0:T(128)} %bitcast.8.scalar_ref, bf16[512,3072]{1,0:T(8,128)(2,1)} %fusion.8.packed_ref), custom_call_target="tpu_custom_call" | custom-call | tf_op jit(solution)/shard_map/pallas_call | solution.py:317
  165.3 5.5 collective-permute-done.11
  170.8 5.8 collective-permute-done.12
  176.6 3.2 fusion.61
  194.2 17.7 %collective-permute-done.14 = bf16[4,2,64,1024]{3,2,1,0:T(8,128)(2,1)S(1)} collective-permute-done((bf16[4,2,64,1024]{3,2,1,0:T(8,128)(2,1)S(1)}, bf16[4,2,64,1024]{3,2,1,0:T(8,128)(2,1)S(1)}, u32[]{:S(2)}, u32[]{:S(2)}) %collective-permute-start.14) | collective-permute-done | bytes 1048608 | tf_op jit(solution)/shard_map/ppermute | solution.py:40
  211.9 22.4 %collective-permute-done.16 = bf16[4,2,128,512]{3,2,1,0:T(8,128)(2,1)S(1)} collective-permute-done((bf16[4,2,128,512]{3,2,1,0:T(8,128)(2,1)S(1)}, bf16[4,2,128,512]{3,2,1,0:T(8,128)(2,1)S(1)}, u32[]{:S(2)}, u32[]{:S(2)}) %collective-permute-start.16) | collective-permute-done | bytes 1048608 | tf_op jit(solution)/shard_map/ppermute | solution.py:40
  244.1 7.6 fusion.11
  251.7 8.8 %shard_map.366 = bf16[4,128,1024]{2,1,0:T(8,128)(2,1)} custom-call(s32[1]{0:T(128)} %bitcast.26.scalar_ref, bf16[4,128,3072]{2,1,0:T(8,128)(2,1)} %bitcast.440), custom_call_target="tpu_custom_call" | custom-call | tf_op jit(solution)/shard_map/pallas_call | solution.py:317
  260.5 3.3 multiply_reduce_fusion.8
  264.0 5.4 fusion.167
  269.4 6.4 fusion.140
  275.9 4.5 fusion.168
  280.5 6.6 multiply_reduce_fusion.7
  287.4 3.9 fusion.165
  293.6 3.2 multiply_reduce_fusion.1
  298.6 4.9 convolution_convert_fusion.3
  306.0 8.7 %fusion.20 = bf16[512,2048]{1,0:T(8,128)(2,1)} fusion(f32[512,2048]{1,0:T(8,128)} %copy-done.110, bf16[512,1024]{1,0:T(8,128)(2,1)S(1)} %copy-done.48, bf16[2048,1024]{1,0:T(8,128)(2,1)} %bitcast.36), kind=kOutput, calls=%fused_computation.24 | convolution fusion | flops 2168455168 | bytes 11534336 | tf_op jit(solution)/shard_map/dot_general | solution.py:217
  314.7 7.5 fusion.27
  322.2 4.4 convolution_convert_fusion.2
  326.6 6.3 fusion.139
  335.8 6.3 add_convert_fusion.1
  346.4 4.9 fusion.169
  351.4 5.8 multiply_reduce_fusion.2
  359.3 5.5 fusion.70
  364.8 22.0 %shard_map.367 = bf16[4,128,3072]{2,1,0:T(8,128)(2,1)} custom-call(s32[1]{0:T(128)} %bitcast.26.scalar_ref, bf16[4,128,3072]{2,1,0:T(8,128)(2,1)} %bitcast.441, bf16[4,128,1024]{2,1,0:T(8,128)(2,1)} %bitcast.476), custom_call_target="tpu_custom_call" | custom-call | tf_op jit(solution)/shard_map/pallas_call | solution.py:317
  390.2 5.5 add_convert_fusion
  400.1 3.5 convolution_convert_fusion.1
  403.6 4.3 fusion.42
  428.5 4.0 collective-permute-done.35
  434.9 34.1 %collective-permute-done.36 = bf16[4,128,1024]{2,1,0:T(8,128)(2,1)} collective-permute-done((bf16[4,128,1024]{2,1,0:T(8,128)(2,1)}, bf16[4,128,1024]{2,1,0:T(8,128)(2,1)}, u32[]{:S(2)}, u32[]{:S(2)}) %collective-permute-start.36) | collective-permute-done | bytes 1048608 | tf_op jit(solution)/shard_map/ppermute | solution.py:40
  483.2 5.5 add_convert_fusion.3
  488.7 3.9 fusion.67.up_ref
  494.6 22.6 %shard_map.368 = bf16[512,3072]{1,0:T(8,128)(2,1)} custom-call(s32[1]{0:T(128)} %bitcast.8.scalar_ref, bf16[512,3072]{1,0:T(8,128)(2,1)} %fusion.8.packed_ref, bf16[512,1024]{1,0:T(8,128)(2,1)} %fusion.67.up_ref), custom_call_target="tpu_custom_call" | custom-call | tf_op jit(solution)/shard_map/pallas_call | solution.py:317
  528.1 7.0 collective-permute-done.49
  537.7 4.7 convolution_convert_fusion
  543.2 6.9 collective-permute-start.62
  557.4 6.5 multiply_reduce_fusion.3
  577.4 3.3 collective-permute-start.70
  585.5 19.4 %collective-permute-done.80 = f32[5,1024]{1,0:T(8,128)S(1)} collective-permute-done((f32[5,1024]{1,0:T(8,128)S(1)}, f32[5,1024]{1,0:T(8,128)S(1)}, u32[]{:S(2)}, u32[]{:S(2)}) %collective-permute-start.80) | collective-permute-done | bytes 20512 | tf_op jit(solution)/shard_map/ppermute | solution.py:40
  608.9 15.9 %collective-permute-done.97 = bf16[2,4,32,512]{3,2,1,0:T(8,128)(2,1)S(1)} collective-permute-done((bf16[2,4,32,512]{3,2,1,0:T(8,128)(2,1)S(1)}, bf16[2,4,32,512]{3,2,1,0:T(8,128)(2,1)S(1)}, u32[]{:S(2)}, u32[]{:S(2)}) %collective-permute-start.97) | collective-permute-done | bytes 262176 | tf_op jit(solution)/shard_map/ppermute | solution.py:40
  630.8 3.6 collective-permute-done.64
  637.3 7.9 collective-permute-done.72
  647.6 3.7 collective-permute-done.65
  652.6 17.7 %collective-permute-done.73 = bf16[2,4,32,512]{3,2,0,1:T(8,128)(2,1)S(1)} collective-permute-done((bf16[2,4,32,512]{3,2,0,1:T(8,128)(2,1)S(1)}, bf16[2,4,32,512]{3,2,0,1:T(8,128)(2,1)S(1)}, u32[]{:S(2)}, u32[]{:S(2)}) %collective-permute-start.73) | collective-permute-done | bytes 262176 | tf_op jit(solution)/shard_map/ppermute | solution.py:40
  670.4 3.6 collective-permute-start.76
  687.9 4.4 collective-permute-done.93
  692.8 6.3 collective-permute-done.94
  699.2 12.3 %collective-permute-done.55 = bf16[4,2,64,1536]{3,2,1,0:T(8,128)(2,1)S(1)} collective-permute-done((bf16[4,2,64,1536]{3,2,1,0:T(8,128)(2,1)S(1)}, bf16[4,2,64,1536]{3,2,1,0:T(8,128)(2,1)S(1)}, u32[]{:S(2)}, u32[]{:S(2)}) %collective-permute-start.55) | collective-permute-done | bytes 1572896 | tf_op jit(solution)/shard_map/ppermute | solution.py:40
  715.8 3.4 collective-permute-done.42
  724.1 11.3 %collective-permute-done.56 = bf16[4,64,1536]{2,1,0:T(8,128)(2,1)S(1)} collective-permute-done((bf16[4,64,1536]{2,1,0:T(8,128)(2,1)S(1)}, bf16[4,64,1536]{2,1,0:T(8,128)(2,1)S(1)}, u32[]{:S(2)}, u32[]{:S(2)}) %collective-permute-start.56) | collective-permute-done | bytes 786464 | tf_op jit(solution)/shard_map/ppermute | solution.py:40
  745.6 4.5 dynamic_update_slice.152
  752.1 5.2 dynamic_update_slice.142
  761.0 3.0 dynamic_update_slice.139
  767.7 4.5 dynamic_update_slice.147
  809.1 3.9 multiply_subtract_fusion
  814.9 3.0 dynamic_update_slice.138
  (641 shorter events, 267.1 us)
Async XLA Ops:
  7.2 95.5 %all-gather.3.cloned.1.call-start = ((), (), s32[]{:S(2)}) async-start(), calls=%async_computation | async-start | bytes 8921088 | tf_op jit(solution)/shard_map/all_gather | solution.py:405
  11.2 232.9 %all-gather.5.cloned.1.call-start = ((), (), s32[]{:S(2)}) async-start(), calls=%async_computation.1 | async-start | bytes 8650752 | tf_op jit(solution)/shard_map/all_gather | solution.py:406
  13.0 16.8 %collective-permute-start = (bf16[256,1024]{1,0:T(8,128)(2,1)S(1)}, bf16[256,1024]{1,0:T(8,128)(2,1)S(1)}, u32[]{:S(2)}, u32[]{:S(2)}) collective-permute-start(bf16[256,1024]{1,0:T(8,128)(2,1)S(1)} %get-tuple-element.198), channel_id=1, source_target_pairs={{2,0},{0,2},{3,1},{1,3},{6,4},{4,6},{7,5},{5,7},{10,8},{8,10},{11,... | collective-permute-start | bytes 1572872 | tf_op jit(solution)/shard_map/ppermute | solution.py:40
  16.1 97.0 %collective-permute-start.6 = (bf16[128,1024]{1,0:T(8,128)(2,1)S(1)}, bf16[128,1024]{1,0:T(8,128)(2,1)}, u32[]{:S(2)}, u32[]{:S(2)}) collective-permute-start(bf16[128,1024]{1,0:T(8,128)(2,1)S(1)} %convert_element_type.505), channel_id=1, source_target_pairs={{8,0},{16,8},{24,16},{0,24},{9,1},{17,9},{25,17},{1,25},{10,2},{18... | collective-permute-start | bytes 786440 | tf_op jit(solution)/shard_map/ppermute | solution.py:40
  19.7 95.5 %collective-permute-start.7 = (bf16[128,1024]{1,0:T(8,128)(2,1)S(1)}, bf16[128,1024]{1,0:T(8,128)(2,1)}, u32[]{:S(2)}, u32[]{:S(2)}) collective-permute-start(bf16[128,1024]{1,0:T(8,128)(2,1)S(1)} %convert_element_type.505), channel_id=1, source_target_pairs={{16,0},{24,8},{0,16},{8,24},{17,1},{25,9},{1,17},{9,25},{18,2},{26... | collective-permute-start | bytes 786440 | tf_op jit(solution)/shard_map/ppermute | solution.py:40
  19.7 97.1 %collective-permute-start.8 = (bf16[128,1024]{1,0:T(8,128)(2,1)S(1)}, bf16[128,1024]{1,0:T(8,128)(2,1)}, u32[]{:S(2)}, u32[]{:S(2)}) collective-permute-start(bf16[128,1024]{1,0:T(8,128)(2,1)S(1)} %convert_element_type.505), channel_id=1, source_target_pairs={{24,0},{0,8},{8,16},{16,24},{25,1},{1,9},{9,17},{17,25},{26,2},{2,... | collective-permute-start | bytes 786440 | tf_op jit(solution)/shard_map/ppermute | solution.py:40
  30.1 18.1 %collective-permute-start.1 = (bf16[2,256,1024]{2,1,0:T(8,128)(2,1)S(1)}, bf16[2,256,1024]{2,1,0:T(8,128)(2,1)S(1)}, u32[]{:S(2)}, u32[]{:S(2)}) collective-permute-start(bf16[2,256,1024]{2,1,0:T(8,128)(2,1)S(1)} %bitcast_dynamic-update-slice_fusion.11), channel_id=1, source_target_pairs={{1,0},{0,1},{3,2},{2,3},{5,4},{4,5},{7,6},{6,7},{9,8},{8,9},{11,10... | collective-permute-start | bytes 3145736 | tf_op jit(solution)/shard_map/ppermute | solution.py:40
  47.7 61.3 %collective-permute-start.2 = (bf16[32,2048]{1,0:T(8,128)(2,1)}, bf16[32,2048]{1,0:T(8,128)(2,1)}, u32[]{:S(2)}, u32[]{:S(2)}) collective-permute-start(bf16[32,2048]{1,0:T(8,128)(2,1)} %bitcast.436), channel_id=1, source_target_pairs={{1,0},{0,1},{3,2},{2,3},{5,4},{4,5},{7,6},{6,7},{9,8},{8,9},{11,10... | collective-permute-start | bytes 393224 | tf_op jit(solution)/shard_map/ppermute | solution.py:40
  49.1 62.9 %collective-permute-start.22 = (f32[1,4]{1,0:T(1,128)}, f32[1,4]{1,0:T(1,128)}, u32[]{:S(2)}, u32[]{:S(2)}) collective-permute-start(f32[1,4]{1,0:T(1,128)} %add.874), channel_id=1, source_target_pairs={{8,0},{16,8},{24,16},{0,24},{9,1},{17,9},{25,17},{1,25},{10,2},{18... | collective-permute-start | bytes 56 | tf_op jit(solution)/shard_map/ppermute | solution.py:40
  112.1 29.9 %collective-permute-start.4 = (bf16[64,2048]{1,0:T(8,128)(2,1)S(1)}, bf16[64,2048]{1,0:T(8,128)(2,1)S(1)}, u32[]{:S(2)}, u32[]{:S(2)}) collective-permute-start(bf16[64,2048]{1,0:T(8,128)(2,1)S(1)} %bitcast.467), channel_id=1, source_target_pairs={{16,0},{24,8},{0,16},{8,24},{17,1},{25,9},{1,17},{9,25},{18,2},{26... | collective-permute-start | bytes 786440 | tf_op jit(solution)/shard_map/ppermute | solution.py:40
  113.1 28.9 %collective-permute-start.5 = (bf16[64,2048]{1,0:T(8,128)(2,1)S(1)}, bf16[64,2048]{1,0:T(8,128)(2,1)S(1)}, u32[]{:S(2)}, u32[]{:S(2)}) collective-permute-start(bf16[64,2048]{1,0:T(8,128)(2,1)S(1)} %bitcast.468), channel_id=1, source_target_pairs={{24,0},{0,8},{8,16},{16,24},{25,1},{1,9},{9,17},{17,25},{26,2},{2,... | collective-permute-start | bytes 786440 | tf_op jit(solution)/shard_map/ppermute | solution.py:40
  115.3 76.5 %collective-permute-start.23 = (bf16[256,1024]{1,0:T(8,128)(2,1)S(1)}, bf16[256,1024]{1,0:T(8,128)(2,1)}, u32[]{:S(2)}, u32[]{:S(2)}) collective-permute-start(bf16[256,1024]{1,0:T(8,128)(2,1)S(1)} %copy-done.32), channel_id=1, source_target_pairs={{2,0},{0,2},{3,1},{1,3},{6,4},{4,6},{7,5},{5,7},{10,8},{8,10},{11,... | collective-permute-start | bytes 1572872 | tf_op jit(solution)/shard_map/ppermute | solution.py:40
  143.1 22.3 %collective-permute-start.9 = (bf16[4,64,1024]{2,1,0:T(8,128)(2,1)}, bf16[4,64,1024]{2,1,0:T(8,128)(2,1)}, u32[]{:S(2)}, u32[]{:S(2)}) collective-permute-start(bf16[4,64,1024]{2,1,0:T(8,128)(2,1)} %get-tuple-element.202), channel_id=1, source_target_pairs={{2,0},{0,2},{3,1},{1,3},{6,4},{4,6},{7,5},{5,7},{10,8},{8,10},{11,... | collective-permute-start | bytes 1572872 | tf_op jit(solution)/shard_map/ppermute | solution.py:40
  144.5 20.8 %collective-permute-start.10 = (bf16[4,64,1024]{2,1,0:T(8,128)(2,1)S(1)}, bf16[4,64,1024]{2,1,0:T(8,128)(2,1)}, u32[]{:S(2)}, u32[]{:S(2)}) collective-permute-start(bf16[4,64,1024]{2,1,0:T(8,128)(2,1)S(1)} %get-tuple-element.201), channel_id=1, source_target_pairs={{4,0},{0,4},{5,1},{1,5},{6,2},{2,6},{7,3},{3,7},{12,8},{8,12},{13,... | collective-permute-start | bytes 1572872 | tf_op jit(solution)/shard_map/ppermute | solution.py:40
  149.2 21.6 %collective-permute-start.11 = (bf16[4,128,512]{2,1,0:T(8,128)(2,1)}, bf16[4,128,512]{2,1,0:T(8,128)(2,1)}, u32[]{:S(2)}, u32[]{:S(2)}) collective-permute-start(bf16[4,128,512]{2,1,0:T(8,128)(2,1)} %get-tuple-element.200), channel_id=1, source_target_pairs={{2,0},{0,2},{3,1},{1,3},{6,4},{4,6},{7,5},{5,7},{10,8},{8,10},{11,... | collective-permute-start | bytes 1572872 | tf_op jit(solution)/shard_map/ppermute | solution.py:40
  150.6 25.9 %collective-permute-start.12 = (bf16[4,128,512]{2,1,0:T(8,128)(2,1)}, bf16[4,128,512]{2,1,0:T(8,128)(2,1)}, u32[]{:S(2)}, u32[]{:S(2)}) collective-permute-start(bf16[4,128,512]{2,1,0:T(8,128)(2,1)} %get-tuple-element.199), channel_id=1, source_target_pairs={{4,0},{0,4},{5,1},{1,5},{6,2},{2,6},{7,3},{3,7},{12,8},{8,12},{13,... | collective-permute-start | bytes 1572872 | tf_op jit(solution)/shard_map/ppermute | solution.py:40
  182.3 29.6 %collective-permute-start.14 = (bf16[4,2,64,1024]{3,2,1,0:T(8,128)(2,1)S(1)}, bf16[4,2,64,1024]{3,2,1,0:T(8,128)(2,1)S(1)}, u32[]{:S(2)}, u32[]{:S(2)}) collective-permute-start(bf16[4,2,64,1024]{3,2,1,0:T(8,128)(2,1)S(1)} %bitcast_dynamic-update-slice_fusion.7), channel_id=1, source_target_pairs={{4,0},{0,4},{5,1},{1,5},{6,2},{2,6},{7,3},{3,7},{12,8},{8,12},{13,... | collective-permute-start | bytes 3145736 | tf_op jit(solution)/shard_map/ppermute | solution.py:40
  184.0 27.9 %collective-permute-start.15 = (bf16[4,2,64,1024]{3,2,1,0:T(8,128)(2,1)S(1)}, bf16[4,2,64,1024]{3,2,1,0:T(8,128)(2,1)S(1)}, u32[]{:S(2)}, u32[]{:S(2)}) collective-permute-start(bf16[4,2,64,1024]{3,2,1,0:T(8,128)(2,1)S(1)} %bitcast_dynamic-update-slice_fusion.10), channel_id=1, source_target_pairs={{2,0},{0,2},{3,1},{1,3},{6,4},{4,6},{7,5},{5,7},{10,8},{8,10},{11,... | collective-permute-start | bytes 3145736 | tf_op jit(solution)/shard_map/ppermute | solution.py:40
  187.9 46.3 %collective-permute-start.16 = (bf16[4,2,128,512]{3,2,1,0:T(8,128)(2,1)S(1)}, bf16[4,2,128,512]{3,2,1,0:T(8,128)(2,1)S(1)}, u32[]{:S(2)}, u32[]{:S(2)}) collective-permute-start(bf16[4,2,128,512]{3,2,1,0:T(8,128)(2,1)S(1)} %bitcast_dynamic-update-slice_fusion.6), channel_id=1, source_target_pairs={{4,0},{0,4},{5,1},{1,5},{6,2},{2,6},{7,3},{3,7},{12,8},{8,12},{13,... | collective-permute-start | bytes 3145736 | tf_op jit(solution)/shard_map/ppermute | solution.py:40
  191.8 42.5 %collective-permute-start.17 = (bf16[4,2,128,512]{3,2,1,0:T(8,128)(2,1)S(1)}, bf16[4,2,128,512]{3,2,1,0:T(8,128)(2,1)S(1)}, u32[]{:S(2)}, u32[]{:S(2)}) collective-permute-start(bf16[4,2,128,512]{3,2,1,0:T(8,128)(2,1)S(1)} %bitcast_dynamic-update-slice_fusion.9), channel_id=1, source_target_pairs={{2,0},{0,2},{3,1},{1,3},{6,4},{4,6},{7,5},{5,7},{10,8},{8,10},{11,... | collective-permute-start | bytes 3145736 | tf_op jit(solution)/shard_map/ppermute | solution.py:40
  193.5 47.9 %collective-permute-start.24 = (bf16[2,256,1024]{2,1,0:T(8,128)(2,1)S(1)}, bf16[2,256,1024]{2,1,0:T(8,128)(2,1)S(1)}, u32[]{:S(2)}, u32[]{:S(2)}) collective-permute-start(bf16[2,256,1024]{2,1,0:T(8,128)(2,1)S(1)} %bitcast_dynamic-update-slice_fusion.8), channel_id=1, source_target_pairs={{1,0},{0,1},{3,2},{2,3},{5,4},{4,5},{7,6},{6,7},{9,8},{8,9},{11,10... | collective-permute-start | bytes 3145736 | tf_op jit(solution)/shard_map/ppermute | solution.py:40
  237.5 38.4 %collective-permute-start.18 = (bf16[1024,2048]{1,0:T(8,128)(2,1)}, bf16[1024,2048]{1,0:T(8,128)(2,1)}, u32[]{:S(2)}, u32[]{:S(2)}) collective-permute-start(bf16[1024,2048]{1,0:T(8,128)(2,1)} %bitcast.33), channel_id=1, source_target_pairs={{1,0},{0,1},{3,2},{2,3},{5,4},{4,5},{7,6},{6,7},{9,8},{8,9},{11,10... | collective-permute-start | bytes 12582920 | tf_op jit(solution)/shard_map/ppermute | solution.py:40
  240.8 39.6 %collective-permute-start.19 = (bf16[2048,1024]{1,0:T(8,128)(2,1)}, bf16[2048,1024]{1,0:T(8,128)(2,1)}, u32[]{:S(2)}, u32[]{:S(2)}) collective-permute-start(bf16[2048,1024]{1,0:T(8,128)(2,1)} %bitcast.36), channel_id=1, source_target_pairs={{1,0},{0,1},{3,2},{2,3},{5,4},{4,5},{7,6},{6,7},{9,8},{8,9},{11,10... | collective-permute-start | bytes 12582920 | tf_op jit(solution)/shard_map/ppermute | solution.py:40
  303.5 18.7 %collective-permute-start.26 = (bf16[2048,1024]{1,0:T(8,128)(2,1)}, bf16[2048,1024]{1,0:T(8,128)(2,1)}, u32[]{:S(2)}, u32[]{:S(2)}) collective-permute-start(bf16[2048,1024]{1,0:T(8,128)(2,1)} %convolution_convert_fusion.3), channel_id=1, source_target_pairs={{1,0},{0,1},{3,2},{2,3},{5,4},{4,5},{7,6},{6,7},{9,8},{8,9},{11,10... | collective-permute-start | bytes 12582920 | tf_op jit(solution)/shard_map/ppermute | solution.py:40
  305.4 16.8 %collective-permute-start.25 = (bf16[1024,512]{1,0:T(8,128)(2,1)S(1)}, bf16[1024,512]{1,0:T(8,128)(2,1)S(1)}, u32[]{:S(2)}, u32[]{:S(2)}) collective-permute-start(bf16[1024,512]{1,0:T(8,128)(2,1)S(1)} %convolution_convert_fusion.6), channel_id=1, source_target_pairs={{1,0},{0,1},{3,2},{2,3},{5,4},{4,5},{7,6},{6,7},{9,8},{8,9},{11,10... | collective-permute-start | bytes 3145736 | tf_op jit(solution)/shard_map/ppermute | solution.py:40
  326.6 32.7 %collective-permute-start.28 = (bf16[1024,2048]{1,0:T(8,128)(2,1)}, bf16[1024,2048]{1,0:T(8,128)(2,1)S(1)}, u32[]{:S(2)}, u32[]{:S(2)}) collective-permute-start(bf16[1024,2048]{1,0:T(8,128)(2,1)} %convolution_convert_fusion.2), channel_id=1, source_target_pairs={{1,0},{0,1},{3,2},{2,3},{5,4},{4,5},{7,6},{6,7},{9,8},{8,9},{11,10... | collective-permute-start | bytes 12582920 | tf_op jit(solution)/shard_map/ppermute | solution.py:40
  334.2 25.1 %collective-permute-start.27 = (bf16[2,2,4,32,512]{4,3,0,2,1:T(8,128)(2,1)S(1)}, bf16[2,2,4,32,512]{4,3,0,2,1:T(8,128)(2,1)S(1)}, u32[]{:S(2)}, u32[]{:S(2)}) collective-permute-start(bf16[2,2,4,32,512]{4,3,0,2,1:T(8,128)(2,1)S(1)} %bitcast.480), channel_id=1, source_target_pairs={{2,0},{0,2},{3,1},{1,3},{6,4},{4,6},{7,5},{5,7},{10,8},{8,10},{11,... | collective-permute-start | bytes 1572872 | tf_op jit(solution)/shard_map/ppermute | solution.py:40
  345.7 54.3 %collective-permute-start.30 = (bf16[4,2,128,1024]{3,2,0,1:T(8,128)(2,1)}, bf16[4,2,128,1024]{3,2,0,1:T(8,128)(2,1)}, u32[]{:S(2)}, u32[]{:S(2)}) collective-permute-start(bf16[4,2,128,1024]{3,2,0,1:T(8,128)(2,1)} %bitcast.432), channel_id=1, source_target_pairs={{2,0},{0,2},{3,1},{1,3},{6,4},{4,6},{7,5},{5,7},{10,8},{8,10},{11,... | collective-permute-start | bytes 6291464 | tf_op jit(solution)/shard_map/ppermute | solution.py:40
  398.8 70.2 %collective-permute-start.37 = (bf16[4,2,64,2048]{3,2,1,0:T(8,128)(2,1)}, bf16[4,2,64,2048]{3,2,1,0:T(8,128)(2,1)}, u32[]{:S(2)}, u32[]{:S(2)}) collective-permute-start(bf16[4,2,64,2048]{3,2,1,0:T(8,128)(2,1)} %dynamic-slice_bitcast_fusion), channel_id=1, source_target_pairs={{4,0},{0,4},{5,1},{1,5},{6,2},{2,6},{7,3},{3,7},{12,8},{8,12},{13,... | collective-permute-start | bytes 6291464 | tf_op jit(solution)/shard_map/ppermute | solution.py:40
  403.5 65.5 %collective-permute-start.39 = (bf16[1024,1536]{1,0:T(8,128)(2,1)}, bf16[1024,1536]{1,0:T(8,128)(2,1)}, u32[]{:S(2)}, u32[]{:S(2)}) collective-permute-start(bf16[1024,1536]{1,0:T(8,128)(2,1)} %convolution_convert_fusion.1), channel_id=1, source_target_pairs={{1,0},{0,1},{3,2},{2,3},{5,4},{4,5},{7,6},{6,7},{9,8},{8,9},{11,10... | collective-permute-start | bytes 9437192 | tf_op jit(solution)/shard_map/ppermute | solution.py:40
  413.6 55.4 %collective-permute-start.36 = (bf16[4,128,1024]{2,1,0:T(8,128)(2,1)}, bf16[4,128,1024]{2,1,0:T(8,128)(2,1)}, u32[]{:S(2)}, u32[]{:S(2)}) collective-permute-start(bf16[4,128,1024]{2,1,0:T(8,128)(2,1)} %dynamic-slice_bitcast_fusion.4), channel_id=1, source_target_pairs={{4,0},{0,4},{5,1},{1,5},{6,2},{2,6},{7,3},{3,7},{12,8},{8,12},{13,... | collective-permute-start | bytes 3145736 | tf_op jit(solution)/shard_map/ppermute | solution.py:40
  469.7 47.5 %collective-permute-start.45 = (bf16[2,32,512]{2,1,0:T(8,128)(2,1)S(1)}, bf16[2,32,512]{2,1,0:T(8,128)(2,1)S(1)}, u32[]{:S(2)}, u32[]{:S(2)}) collective-permute-start(bf16[2,32,512]{2,1,0:T(8,128)(2,1)S(1)} %get-tuple-element.156), channel_id=1, source_target_pairs={{8,0},{16,8},{24,16},{0,24},{9,1},{17,9},{25,17},{1,25},{10,2},{18... | collective-permute-start | bytes 196616 | tf_op jit(solution)/shard_map/ppermute | solution.py:40
  472.5 47.3 %collective-permute-start.46 = (bf16[2,32,512]{2,1,0:T(8,128)(2,1)S(1)}, bf16[2,32,512]{2,1,0:T(8,128)(2,1)}, u32[]{:S(2)}, u32[]{:S(2)}) collective-permute-start(bf16[2,32,512]{2,1,0:T(8,128)(2,1)S(1)} %get-tuple-element.156), channel_id=1, source_target_pairs={{16,0},{24,8},{0,16},{8,24},{17,1},{25,9},{1,17},{9,25},{18,2},{26... | collective-permute-start | bytes 196616 | tf_op jit(solution)/shard_map/ppermute | solution.py:40
  475.4 48.7 %collective-permute-start.48 = (bf16[128,1024]{1,0:T(8,128)(2,1)}, bf16[128,1024]{1,0:T(8,128)(2,1)}, u32[]{:S(2)}, u32[]{:S(2)}) collective-permute-start(bf16[128,1024]{1,0:T(8,128)(2,1)} %get-tuple-element.194), channel_id=1, source_target_pairs={{24,0},{0,8},{8,16},{16,24},{25,1},{1,9},{9,17},{17,25},{26,2},{2,... | collective-permute-start | bytes 786440 | tf_op jit(solution)/shard_map/ppermute | solution.py:40
  480.4 56.6 %collective-permute-start.51 = (bf16[4,64,2048]{2,1,0:T(8,128)(2,1)}, bf16[4,64,2048]{2,1,0:T(8,128)(2,1)}, u32[]{:S(2)}, u32[]{:S(2)}) collective-permute-start(bf16[4,64,2048]{2,1,0:T(8,128)(2,1)} %dynamic-slice_bitcast_fusion.3), channel_id=1, source_target_pairs={{2,0},{0,2},{3,1},{1,3},{6,4},{4,6},{7,5},{5,7},{10,8},{8,10},{11,... | collective-permute-start | bytes 3145736 | tf_op jit(solution)/shard_map/ppermute | solution.py:40
  483.2 54.5 %collective-permute-start.53 = (bf16[1024,512]{1,0:T(8,128)(2,1)}, bf16[1024,512]{1,0:T(8,128)(2,1)}, u32[]{:S(2)}, u32[]{:S(2)}) collective-permute-start(bf16[1024,512]{1,0:T(8,128)(2,1)} %convolution_convert_fusion.4), channel_id=1, source_target_pairs={{1,0},{0,1},{3,2},{2,3},{5,4},{4,5},{7,6},{6,7},{9,8},{8,9},{11,10... | collective-permute-start | bytes 3145736 | tf_op jit(solution)/shard_map/ppermute | solution.py:40
  535.0 91.3 %collective-permute-start.40 = (bf16[4,2,64,1536]{3,2,1,0:T(8,128)(2,1)}, bf16[4,2,64,1536]{3,2,1,0:T(8,128)(2,1)}, u32[]{:S(2)}, u32[]{:S(2)}) collective-permute-start(bf16[4,2,64,1536]{3,2,1,0:T(8,128)(2,1)} %dynamic-slice_bitcast_fusion.2), channel_id=1, source_target_pairs={{2,0},{0,2},{3,1},{1,3},{6,4},{4,6},{7,5},{5,7},{10,8},{8,10},{11,... | collective-permute-start | bytes 4718600 | tf_op jit(solution)/shard_map/ppermute | solution.py:40
  543.2 37.6 %collective-permute-start.62 = (bf16[64,512]{1,0:T(8,128)(2,1)}, bf16[64,512]{1,0:T(8,128)(2,1)}, u32[]{:S(2)}, u32[]{:S(2)}) collective-permute-start(bf16[64,512]{1,0:T(8,128)(2,1)} %get-tuple-element.228), channel_id=1, source_target_pairs={{8,0},{16,8},{24,16},{0,24},{9,1},{17,9},{25,17},{1,25},{10,2},{18... | collective-permute-start | bytes 196616 | tf_op jit(solution)/shard_map/ppermute | solution.py:40
  550.1 31.8 %collective-permute-start.61 = (bf16[64,512]{1,0:T(8,128)(2,1)}, bf16[64,512]{1,0:T(8,128)(2,1)}, u32[]{:S(2)}, u32[]{:S(2)}) collective-permute-start(bf16[64,512]{1,0:T(8,128)(2,1)} %get-tuple-element.229), channel_id=1, source_target_pairs={{16,0},{24,8},{0,16},{8,24},{17,1},{25,9},{1,17},{9,25},{18,2},{26... | collective-permute-start | bytes 196616 | tf_op jit(solution)/shard_map/ppermute | solution.py:40
  550.1 31.9 %collective-permute-start.60 = (bf16[64,512]{1,0:T(8,128)(2,1)}, bf16[64,512]{1,0:T(8,128)(2,1)}, u32[]{:S(2)}, u32[]{:S(2)}) collective-permute-start(bf16[64,512]{1,0:T(8,128)(2,1)} %get-tuple-element.227), channel_id=1, source_target_pairs={{24,0},{0,8},{8,16},{16,24},{25,1},{1,9},{9,17},{17,25},{26,2},{2,... | collective-permute-start | bytes 196616 | tf_op jit(solution)/shard_map/ppermute | solution.py:40
  577.4 27.4 %collective-permute-start.70 = (bf16[64,2048]{1,0:T(8,128)(2,1)S(1)}, bf16[64,2048]{1,0:T(8,128)(2,1)S(1)}, u32[]{:S(2)}, u32[]{:S(2)}) collective-permute-start(bf16[64,2048]{1,0:T(8,128)(2,1)S(1)} %copy-done.74), channel_id=1, source_target_pairs={{8,0},{16,8},{24,16},{0,24},{9,1},{17,9},{25,17},{1,25},{10,2},{18... | collective-permute-start | bytes 786440 | tf_op jit(solution)/shard_map/ppermute | solution.py:40
  580.8 25.5 %collective-permute-start.69 = (bf16[64,2048]{1,0:T(8,128)(2,1)S(1)}, bf16[64,2048]{1,0:T(8,128)(2,1)S(1)}, u32[]{:S(2)}, u32[]{:S(2)}) collective-permute-start(bf16[64,2048]{1,0:T(8,128)(2,1)S(1)} %copy-done.73), channel_id=1, source_target_pairs={{16,0},{24,8},{0,16},{8,24},{17,1},{25,9},{1,17},{9,25},{18,2},{26... | collective-permute-start | bytes 786440 | tf_op jit(solution)/shard_map/ppermute | solution.py:40
  581.9 24.6 %collective-permute-start.68 = (bf16[64,2048]{1,0:T(8,128)(2,1)S(1)}, bf16[64,2048]{1,0:T(8,128)(2,1)S(1)}, u32[]{:S(2)}, u32[]{:S(2)}) collective-permute-start(bf16[64,2048]{1,0:T(8,128)(2,1)S(1)} %copy-done.72), channel_id=1, source_target_pairs={{24,0},{0,8},{8,16},{16,24},{25,1},{1,9},{9,17},{17,25},{26,2},{2,... | collective-permute-start | bytes 786440 | tf_op jit(solution)/shard_map/ppermute | solution.py:40
  582.1 22.8 %collective-permute-start.80 = (f32[5,1024]{1,0:T(8,128)S(1)}, f32[5,1024]{1,0:T(8,128)S(1)}, u32[]{:S(2)}, u32[]{:S(2)}) collective-permute-start(f32[5,1024]{1,0:T(8,128)S(1)} %add.945), channel_id=1, source_target_pairs={{16,0},{24,8},{0,16},{8,24},{17,1},{25,9},{1,17},{9,25},{18,2},{26... | collective-permute-start | bytes 61448 | tf_op jit(solution)/shard_map/ppermute | solution.py:40
  604.8 69.1 %collective-permute-start.54 = (bf16[1024,1536]{1,0:T(8,128)(2,1)S(1)}, bf16[1024,1536]{1,0:T(8,128)(2,1)S(1)}, u32[]{:S(2)}, u32[]{:S(2)}) collective-permute-start(bf16[1024,1536]{1,0:T(8,128)(2,1)S(1)} %copy-done.109), channel_id=1, source_target_pairs={{1,0},{0,1},{3,2},{2,3},{5,4},{4,5},{7,6},{6,7},{9,8},{8,9},{11,10... | collective-permute-start | bytes 9437192 | tf_op jit(solution)/shard_map/ppermute | solution.py:40
  604.8 20.2 %collective-permute-start.63 = (bf16[4,2,64,512]{3,2,1,0:T(8,128)(2,1)S(1)}, bf16[4,2,64,512]{3,2,1,0:T(8,128)(2,1)S(1)}, u32[]{:S(2)}, u32[]{:S(2)}) collective-permute-start(bf16[4,2,64,512]{3,2,1,0:T(8,128)(2,1)S(1)} %dynamic-slice_bitcast_fusion.7), channel_id=1, source_target_pairs={{4,0},{0,4},{5,1},{1,5},{6,2},{2,6},{7,3},{3,7},{12,8},{8,12},{13,... | collective-permute-start | bytes 1572872 | tf_op jit(solution)/shard_map/ppermute | solution.py:40
  606.2 22.4 %collective-permute-start.71 = (bf16[1024,512]{1,0:T(8,128)(2,1)S(1)}, bf16[1024,512]{1,0:T(8,128)(2,1)S(1)}, u32[]{:S(2)}, u32[]{:S(2)}) collective-permute-start(bf16[1024,512]{1,0:T(8,128)(2,1)S(1)} %fusion.66), channel_id=1, source_target_pairs={{1,0},{0,1},{3,2},{2,3},{5,4},{4,5},{7,6},{6,7},{9,8},{8,9},{11,10... | collective-permute-start | bytes 3145736 | tf_op jit(solution)/shard_map/ppermute | solution.py:40
  606.5 18.4 %collective-permute-start.97 = (bf16[2,4,32,512]{3,2,1,0:T(8,128)(2,1)S(1)}, bf16[2,4,32,512]{3,2,1,0:T(8,128)(2,1)S(1)}, u32[]{:S(2)}, u32[]{:S(2)}) collective-permute-start(bf16[2,4,32,512]{3,2,1,0:T(8,128)(2,1)S(1)} %bitcast_dynamic-update-slice_fusion.25), channel_id=1, source_target_pairs={{4,0},{0,4},{5,1},{1,5},{6,2},{2,6},{7,3},{3,7},{12,8},{8,12},{13,... | collective-permute-start | bytes 786440 | tf_op jit(solution)/shard_map/ppermute | solution.py:40
  624.9 112.1 %collective-permute-start.90 = (f32[32,512]{1,0:T(8,128)S(1)}, f32[32,512]{1,0:T(8,128)S(1)}, u32[]{:S(2)}, u32[]{:S(2)}) collective-permute-start(f32[32,512]{1,0:T(8,128)S(1)} %get-tuple-element.235), channel_id=1, source_target_pairs={{1,0},{0,1},{3,2},{2,3},{5,4},{4,5},{7,6},{6,7},{9,8},{8,9},{11,10... | collective-permute-start | bytes 196616 | tf_op jit(solution)/shard_map/ppermute | solution.py:40
  629.7 15.6 %collective-permute-start.72 = (bf16[2,2,4,32,512]{4,3,0,2,1:T(8,128)(2,1)S(1)}, bf16[2,2,4,32,512]{4,3,0,2,1:T(8,128)(2,1)S(1)}, u32[]{:S(2)}, u32[]{:S(2)}) collective-permute-start(bf16[2,2,4,32,512]{4,3,0,2,1:T(8,128)(2,1)S(1)} %bitcast.481), channel_id=1, source_target_pairs={{2,0},{0,2},{3,1},{1,3},{6,4},{4,6},{7,5},{5,7},{10,8},{8,10},{11,... | collective-permute-start | bytes 1572872 | tf_op jit(solution)/shard_map/ppermute | solution.py:40
  645.5 32.0 %collective-permute-start.41 = (bf16[4,64,1536]{2,1,0:T(8,128)(2,1)S(1)}, bf16[4,64,1536]{2,1,0:T(8,128)(2,1)S(1)}, u32[]{:S(2)}, u32[]{:S(2)}) collective-permute-start(bf16[4,64,1536]{2,1,0:T(8,128)(2,1)S(1)} %dynamic-slice_bitcast_fusion.6), channel_id=1, source_target_pairs={{4,0},{0,4},{5,1},{1,5},{6,2},{2,6},{7,3},{3,7},{12,8},{8,12},{13,... | collective-permute-start | bytes 2359304 | tf_op jit(solution)/shard_map/ppermute | solution.py:40
  646.9 23.4 %collective-permute-start.73 = (bf16[2,4,32,512]{3,2,0,1:T(8,128)(2,1)S(1)}, bf16[2,4,32,512]{3,2,0,1:T(8,128)(2,1)S(1)}, u32[]{:S(2)}, u32[]{:S(2)}) collective-permute-start(bf16[2,4,32,512]{3,2,0,1:T(8,128)(2,1)S(1)} %dynamic-slice_bitcast_fusion.15), channel_id=1, source_target_pairs={{4,0},{0,4},{5,1},{1,5},{6,2},{2,6},{7,3},{3,7},{12,8},{8,12},{13,... | collective-permute-start | bytes 786440 | tf_op jit(solution)/shard_map/ppermute | solution.py:40
  677.5 34.1 %collective-permute-start.55 = (bf16[4,2,64,1536]{3,2,1,0:T(8,128)(2,1)S(1)}, bf16[4,2,64,1536]{3,2,1,0:T(8,128)(2,1)S(1)}, u32[]{:S(2)}, u32[]{:S(2)}) collective-permute-start(bf16[4,2,64,1536]{3,2,1,0:T(8,128)(2,1)S(1)} %dynamic-slice_bitcast_fusion.1), channel_id=1, source_target_pairs={{4,0},{0,4},{5,1},{1,5},{6,2},{2,6},{7,3},{3,7},{12,8},{8,12},{13,... | collective-permute-start | bytes 4718600 | tf_op jit(solution)/shard_map/ppermute | solution.py:40
  679.0 57.5 %collective-permute-start.81 = (f32[5,1024]{1,0:T(8,128)S(1)}, f32[5,1024]{1,0:T(8,128)S(1)}, u32[]{:S(2)}, u32[]{:S(2)}) collective-permute-start(f32[5,1024]{1,0:T(8,128)S(1)} %add.946), channel_id=1, source_target_pairs={{8,0},{16,8},{24,16},{0,24},{9,1},{17,9},{25,17},{1,25},{10,2},{18... | collective-permute-start | bytes 61448 | tf_op jit(solution)/shard_map/ppermute | solution.py:40
  682.8 31.5 %collective-permute-start.44 = (bf16[64,1536]{1,0:T(8,128)(2,1)S(1)}, bf16[64,1536]{1,0:T(8,128)(2,1)S(1)}, u32[]{:S(2)}, u32[]{:S(2)}) collective-permute-start(bf16[64,1536]{1,0:T(8,128)(2,1)S(1)} %get-tuple-element.207), channel_id=1, source_target_pairs={{8,0},{16,8},{24,16},{0,24},{9,1},{17,9},{25,17},{1,25},{10,2},{18... | collective-permute-start | bytes 589832 | tf_op jit(solution)/shard_map/ppermute | solution.py:40
  714.3 22.8 %collective-permute-start.91 = (f32[32,2048]{1,0:T(8,128)S(1)}, f32[32,2048]{1,0:T(8,128)S(1)}, u32[]{:S(2)}, u32[]{:S(2)}) collective-permute-start(f32[32,2048]{1,0:T(8,128)S(1)} %get-tuple-element.213), channel_id=1, source_target_pairs={{1,0},{0,1},{3,2},{2,3},{5,4},{4,5},{7,6},{6,7},{9,8},{8,9},{11,10... | collective-permute-start | bytes 786440 | tf_op jit(solution)/shard_map/ppermute | solution.py:40
  719.2 16.2 %collective-permute-start.56 = (bf16[4,64,1536]{2,1,0:T(8,128)(2,1)S(1)}, bf16[4,64,1536]{2,1,0:T(8,128)(2,1)S(1)}, u32[]{:S(2)}, u32[]{:S(2)}) collective-permute-start(bf16[4,64,1536]{2,1,0:T(8,128)(2,1)S(1)} %dynamic-slice_bitcast_fusion.5), channel_id=1, source_target_pairs={{2,0},{0,2},{3,1},{1,3},{6,4},{4,6},{7,5},{5,7},{10,8},{8,10},{11,... | collective-permute-start | bytes 2359304 | tf_op jit(solution)/shard_map/ppermute | solution.py:40
  723.1 15.7 %collective-permute-start.98 = (bf16[256,512]{1,0:T(8,128)(2,1)S(1)}, bf16[256,512]{1,0:T(8,128)(2,1)S(1)}, u32[]{:S(2)}, u32[]{:S(2)}) collective-permute-start(bf16[256,512]{1,0:T(8,128)(2,1)S(1)} %get-tuple-element.211), channel_id=1, source_target_pairs={{1,0},{0,1},{3,2},{2,3},{5,4},{4,5},{7,6},{6,7},{9,8},{8,9},{11,10... | collective-permute-start | bytes 786440 | tf_op jit(solution)/shard_map/ppermute | solution.py:40
  736.5 22.4 %collective-permute-start.88 = (f32[32,1536]{1,0:T(8,128)}, f32[32,1536]{1,0:T(8,128)}, u32[]{:S(2)}, u32[]{:S(2)}) collective-permute-start(f32[32,1536]{1,0:T(8,128)} %get-tuple-element.217), channel_id=1, source_target_pairs={{1,0},{0,1},{3,2},{2,3},{5,4},{4,5},{7,6},{6,7},{9,8},{8,9},{11,10... | collective-permute-start | bytes 589832 | tf_op jit(solution)/shard_map/ppermute | solution.py:40
  737.0 28.2 %collective-permute-start.96 = (bf16[256,512]{1,0:T(8,128)(2,1)}, bf16[256,512]{1,0:T(8,128)(2,1)}, u32[]{:S(2)}, u32[]{:S(2)}) collective-permute-start(bf16[256,512]{1,0:T(8,128)(2,1)} %get-tuple-element.209), channel_id=1, source_target_pairs={{1,0},{0,1},{3,2},{2,3},{5,4},{4,5},{7,6},{6,7},{9,8},{8,9},{11,10... | collective-permute-start | bytes 786440 | tf_op jit(solution)/shard_map/ppermute | solution.py:40
  737.1 36.4 %collective-permute-start.59 = (bf16[64,1536]{1,0:T(8,128)(2,1)}, bf16[64,1536]{1,0:T(8,128)(2,1)}, u32[]{:S(2)}, u32[]{:S(2)}) collective-permute-start(bf16[64,1536]{1,0:T(8,128)(2,1)} %get-tuple-element.204), channel_id=1, source_target_pairs={{8,0},{16,8},{24,16},{0,24},{9,1},{17,9},{25,17},{1,25},{10,2},{18... | collective-permute-start | bytes 589832 | tf_op jit(solution)/shard_map/ppermute | solution.py:40
  738.8 34.7 %collective-permute-start.58 = (bf16[64,1536]{1,0:T(8,128)(2,1)}, bf16[64,1536]{1,0:T(8,128)(2,1)}, u32[]{:S(2)}, u32[]{:S(2)}) collective-permute-start(bf16[64,1536]{1,0:T(8,128)(2,1)} %get-tuple-element.205), channel_id=1, source_target_pairs={{16,0},{24,8},{0,16},{8,24},{17,1},{25,9},{1,17},{9,25},{18,2},{26... | collective-permute-start | bytes 589832 | tf_op jit(solution)/shard_map/ppermute | solution.py:40
  739.5 34.0 %collective-permute-start.57 = (bf16[64,1536]{1,0:T(8,128)(2,1)}, bf16[64,1536]{1,0:T(8,128)(2,1)}, u32[]{:S(2)}, u32[]{:S(2)}) collective-permute-start(bf16[64,1536]{1,0:T(8,128)(2,1)} %get-tuple-element.203), channel_id=1, source_target_pairs={{24,0},{0,8},{8,16},{16,24},{25,1},{1,9},{9,17},{17,25},{26,2},{2,... | collective-permute-start | bytes 589832 | tf_op jit(solution)/shard_map/ppermute | solution.py:40
  782.7 30.9 %collective-permute-start.87 = (f32[32,1536]{1,0:T(8,128)}, f32[32,1536]{1,0:T(8,128)}, u32[]{:S(2)}, u32[]{:S(2)}) collective-permute-start(f32[32,1536]{1,0:T(8,128)} %get-tuple-element.215), channel_id=1, source_target_pairs={{1,0},{0,1},{3,2},{2,3},{5,4},{4,5},{7,6},{6,7},{9,8},{8,9},{11,10... | collective-permute-start | bytes 589832 | tf_op jit(solution)/shard_map/ppermute | solution.py:40
  (156 other events, 1515.4 us)
Sparse Core Ops, SparseCore 0:
  11.5 91.1 all-gather.2
  106.1 99.4 all-gather.4

commit v3 on v2

--- a/solution.py
+++ b/solution.py
@@ -128,30 +128,42 @@
     return result
 
 
-def reduce_rows(other, own, names, order):
+def pieces_of(total, dim, axis):
+    n = lax.axis_size(axis)
+    mine = lax.axis_index(axis)
+    return [
+        shifted(at(total, (mine + shift) % n, dim), axis, n - shift) for shift in range(1, n)
+    ]
+
+
+def added(total, dim, axis, pieces):
+    total = at(total, lax.axis_index(axis), dim).astype(WIDE)
+    for piece in pieces:
+        total = total + piece.astype(WIDE)
+    return total
+
+
+def reduce_rows(other, own, names, order, parts=1):
     (arrived,) = yield [shifted(other, "h", 1)]
     total = (own() + arrived.astype(WIDE)).astype(LOW)
     names = list(names)
     total = total.reshape(
         tuple(lax.axis_size(name) for name in names) + (-1, total.shape[-1])
     )
-    for axis in order:
-        dim = names.index(axis)
-        n = lax.axis_size(axis)
-        mine = lax.axis_index(axis)
-        pieces = [
-            shifted(at(total, (mine + shift) % n, dim), axis, n - shift) for shift in range(1, n)
-        ]
-        pieces = yield pieces
-        total = at(total, mine, dim).astype(WIDE)
-        for piece in pieces:
-            total = total + piece.astype(WIDE)
-        names.pop(dim)
-        if names:
-            total = total.astype(LOW)
-            if names == ["h"]:
-                total = total.astype(WIDE)
-    return total
+    totals = jnp.split(total, parts, axis=-1)
+    orders = [list(order), [order[1], order[0]] + list(order[2:])][:parts]
+    left = [list(names) for _ in totals]
+    for step in range(2):
+        dims = [names.index(axes[step]) for names, axes in zip(left, orders)]
+        steps = list(zip(totals, dims, [axes[step] for axes in orders]))
+        pieces = yield [pieces_of(*each) for each in steps]
+        totals = [added(*each, arrived).astype(LOW) for each, arrived in zip(steps, pieces)]
+        for names, dim in zip(left, dims):
+            names.pop(dim)
+    total = totals[0] if parts == 1 else jnp.concatenate(totals, axis=-1)
+    dim = left[0].index(order[2])
+    pieces = yield pieces_of(total, dim, order[2])
+    return added(total, dim, order[2], pieces)
 
 
 def swap_rows(total):
@@ -161,16 +173,23 @@
     return (at(seen, half, 0), other)
 
 
-def reduce_layer(other, own, order, block=None):
-    total = yield from reduce_rows(other, own, ("z", "r", "m"), order)
+def in_order(mine, other, dim):
+    first = lax.axis_index("h") == 0
+    return jnp.concatenate(
+        [jnp.where(first, mine, other), jnp.where(first, other, mine)], axis=dim
+    )
+
+
+def reduce_layer(other, own, order, block=None, parts=1):
+    total = yield from reduce_rows(other, own, ("z", "r", "m"), order, parts)
     total = total.reshape(-1, total.shape[-1])
     square = jnp.sum(total * total)
     mine, other = yield from swap_rows(total)
+    if block is None:
+        return (in_order(mine, other, 1), square)
     rows = mine.shape[0]
-    if block is None:
-        return (placed(mine, [other], "h", 1).reshape(rows, -1), square)
-    mine, other = (half.reshape(rows, -1, block) for half in (mine, other))
-    return (placed(mine, [other], "h", 2).reshape(rows, -1), square)
+    mine, other = (half.reshape(rows, -1, 1, block) for half in (mine, other))
+    return (in_order(mine, other, 2).reshape(rows, -1), square)
 
 
 def reduce_owned(other, own, order):
@@ -187,14 +206,20 @@
     others = yield sent_around(total, "r")
     total = placed(total, others, "r", 1)
     mine, other = yield from swap_rows(total.reshape(-1, total.shape[-1]))
-    return (placed(mine, [other], "h", 1).reshape(mine.shape[0], -1).astype(WIDE), square)
-
-
-def summed_over(part, axes):
+    return (in_order(mine, other, 1).astype(WIDE), square)
+
+
+def sum_over(part, axes):
     for axis in axes:
-        shift = lax.axis_size(axis) // 2
+        n = lax.axis_size(axis)
+        if n == 4:
+            others = yield sent_around(part, axis)
+            part = jnp.sum(placed(part, others, axis, 0), axis=0)
+            continue
+        shift = n // 2
         while shift:
-            part = part + shifted(part, axis, shift)
+            (other,) = yield [shifted(part, axis, shift)]
+            part = part + other
             shift //= 2
     return part
 
@@ -408,8 +433,18 @@
     table_in = gather_axis(gather_axis(low_in, "m", 0), "h", 1).reshape(-1, D)
     up_job = Job(gather_columns(expand.astype(LOW), block))
     down_job = Job(gather_half(contract.astype(LOW)))
+    table_in = advance(table_in, up_job)
     table_out = gather_axis(gather_axis(low_out, "m", 0), "h", 1).reshape(-1, D)
 
+    code_ids = jnp.arange(table_in.shape[0])
+
+    def own_frames(array):
+        return lax.dynamic_slice_in_dim(array, half * frames, frames, 0)
+
+    space_codes = own_frames(codes).reshape(-1)
+    picked = dot_nn((space_codes[:, None] == code_ids[None, :]).astype(LOW), table_in)
+    picked = advance(picked, up_job, down_job)
+    layer_one = advance(layer_one, up_job, down_job)
     w_in = (layer_one[:, : 3 * D], layer_two[:, : 3 * D])
     w_out = (layer_one[:, 3 * D : 4 * D], layer_two[:, 3 * D :])
     gain_all = layer_one[:, 4 * D :].T[:kinds].astype(WIDE)
@@ -419,31 +454,22 @@
     dom_slot = jnp.sum((segment[:, None] == jnp.arange(CLIPS)[None, :]) * doms[None, :], axis=-1)
     domain_hot = (dom_slot[:, None] == jnp.arange(DOMAINS)[None, :]).astype(WIDE)
     counts = jnp.sum(jnp.sum(hidden_mask, axis=0)[:, None] * domain_hot, axis=0)[None, :]
-    counts = summed_over(counts, ("r", "z"))[0]
+    counts = Job(sum_over(counts, ("r", "z"))).finish()[0]
     scale = 1.0 / (MICRO * DOMAINS * jnp.maximum(counts, 1.0))
     slot_scale = jnp.sum(domain_hot * scale[None, :], axis=1)
-    code_ids = jnp.arange(table_in.shape[0])
-
-    def own_frames(array):
-        return lax.dynamic_slice_in_dim(array, half * frames, frames, 0)
 
     def time_order(array):
         mine = halves(array, 1)[0]
         return jnp.concatenate(halves(mine, 0), axis=0).reshape(-1)
 
-    space_codes = own_frames(codes).reshape(-1)
     space_mask = own_frames(hidden_mask).reshape(-1)
     time_codes = time_order(codes)
     time_weight = time_order(hidden_mask * slot_scale[None, :])
 
-    picked = dot_nn((space_codes[:, None] == code_ids[None, :]).astype(LOW), table_in)
     start = jnp.where(space_mask[:, None] > 0, gain_all[4], picked)
     normed_space = norm_forward(start, gain_all[0]).astype(LOW)
-    normed_space = advance(normed_space, up_job)
-    normed_space = advance(normed_space, up_job, down_job)
     packed_space = dot_nn(normed_space, w_in[0]).astype(LOW)
     mixed_space = attention("space", small, packed_space)
-    mixed_space = advance(mixed_space, up_job, down_job)
     after_space = start + dot_nn(mixed_space, w_out[0])
     after_space = swap_slots(after_space.reshape(frames, SLOTS, D)).reshape(-1, D)
     normed_time = norm_forward(after_space, gain_all[1]).astype(LOW)
@@ -499,15 +525,18 @@
     inward, gain_one = norm_backward(after_space, gain_all[1], grad_normed)
     grad_space = swap_frames((grad_time + inward).reshape(FRAMES, -1, D)).reshape(-1, D)
     up_low = grad_space.astype(LOW)
-    up_low = advance(up_low, head_job, contract_job, expand_job, out_job, in_job)
+    up_low = advance(up_low, head_job, out_job, in_job)
     first_out_job = product(reduce_layer, mixed_space, *halves(up_low, 1), ("r", "m", "z"))
     grad_mixed = dot_nt(up_low, w_out[0]).astype(LOW)
     grad_packed = attention("space", small, packed_space, grad_mixed)
     grad_packed = advance(
-        grad_packed, head_job, contract_job, expand_job, out_job, first_out_job
-    )
-    first_in_job = product(reduce_layer, normed_space, *halves(grad_packed, 1), ("r", "m", "z"))
+        grad_packed, head_job, contract_job, expand_job, out_job, in_job, first_out_job
+    )
+    first_in_job = product(
+        reduce_layer, normed_space, *halves(grad_packed, 1), ("r", "m", "z"), None, 2
+    )
     grad_normed = dot_nt(grad_packed, w_in[0])
+    grad_normed = advance(grad_normed, first_in_job, head_job, out_job)
     inward, gain_zero = norm_backward(start, gain_all[0], grad_normed)
     grad_start = grad_space + inward
     mask_grad = jnp.sum(grad_start * space_mask[:, None], axis=0)
@@ -516,22 +545,27 @@
     embed_job = product(reduce_table, chosen, *halves(start_low, 1))
 
     gain_grads = jnp.stack([gain_zero, gain_one, gain_two, gain_three, mask_grad])
-    gain_grads = summed_over(gain_grads, ("h", "r", "m", "z"))
+    gain_job = Job(sum_over(gain_grads, ("h", "m", "r", "z")))
+    token = jnp.zeros((), WIDE)
+    late = (expand_job, contract_job, in_job, first_out_job)
+    token = advance(token, embed_job, gain_job, head_job, out_job, *late)
+    token = advance(token, first_in_job)
+    token = advance(token, embed_job, gain_job, first_out_job)
+    token = advance(token, first_in_job)
+    token = advance(token, embed_job, gain_job, expand_job, in_job, first_out_job)
+    token = advance(token, first_in_job, embed_job, gain_job)
+
+    jobs = (in_job, first_in_job, out_job, first_out_job, expand_job, contract_job)
+    jobs = jobs + (embed_job, head_job)
     owner = jnp.int32(0)
     for axis in ALL:
         owner = owner * lax.axis_size(axis) + lax.axis_index(axis)
     width = gains.shape[1]
-    gain_grads = lax.dynamic_slice_in_dim(gain_grads, owner * width, width, 1)
-
-    jobs = (in_job, first_in_job, out_job, first_out_job, expand_job, contract_job)
-    jobs = jobs + (embed_job, head_job)
-    while any(job.flight is not None for job in jobs):
-        for job in jobs:
-            if job.flight is not None:
-                job.resume(job.flight)
-    results = [job.result for job in jobs]
+    gain_grads = lax.dynamic_slice_in_dim(gain_job.finish(), owner * width, width, 1)
+    results = [job.finish() for job in jobs]
     owned = sum(square for _, square in results) + jnp.sum(gain_grads * gain_grads)
-    sums = summed_over(jnp.stack([owned, loss_part]).reshape(1, 2), ("h", "m", "r", "z"))
+    sums = jnp.stack([owned, loss_part]).reshape(1, 2)
+    sums = Job(sum_over(sums, ("h", "m", "r", "z"))).finish()
     square_sum, loss = sums[0, 0], sums[0, 1]
     norm = jnp.sqrt(square_sum)
     factor = jnp.minimum(1.0, CLIP / (norm + 1e-06))

time: 837 us -> 794 us (0.949)
  local copies, waits for them, and re-layouts: 93.5 us -> 63.3 us
  waiting for transfers between devices: 321 us -> 294 us
  starting transfers between devices: 107 us -> 116 us
    all_gather x1, waiting for transfers between devices: 48.6 us -> 5.57 us  [on_device(): layer_one = lax.all_gather(layer_one, ALL, axis=0, tiled=True)]
    dynamic_update_slice x34 -> x36, local copies, waits for them, and re-layouts: 33.7 us -> 14.3 us  [placed(): lax.dynamic_update_index_in_dim(whole, other, (mine + shift) % n, dim)]
    ppermute x99 -> x104, waiting for transfers between devices: 273 us -> 288 us  [shifted(): return lax.ppermute(part, axis, [((i + shift) % n, i) for i in range(n)])]
    ppermute x99 -> x104, starting transfers between devices: 107 us -> 116 us  [shifted(): return lax.ppermute(part, axis, [((i + shift) % n, i) for i in range(n)])]
    convert_element_type x16 -> x19, other arithmetic: 13.7 us -> 19.1 us  [the longest x18 17 us: reduce_rows(): added(*each, arrived).astype(LOW)]
  transfers between devices with their start and end apart: 101 -> 106, of which waited for: 36 -> 33; matrix products, arithmetic and copies ran while one was open for 32% -> 30% of each run, Pallas kernels for 8% -> 8%
where the time goes in v3:
time: 794 us; the launch traced here: 785 us
  waiting for transfers between devices  294 us (37%)
  matrix products  146 us (18%)
  starting transfers between devices  116 us (15%)
  other arithmetic  78.3 us (10%)
  local copies, waits for them, and re-layouts  63.3 us (8%)
  Pallas kernels  63.1 us (8%)
  between operations  24.7 us (3%)
    ppermute x104, waiting for transfers between devices, shifted(): return lax.ppermute(part, axis, [((i + shift) % n, i) for i in range(n)])  288 us
    ppermute x104, starting transfers between devices, shifted(): return lax.ppermute(part, axis, [((i + shift) % n, i) for i in range(n)])  116 us
    pallas_call x4, Pallas kernels, attention(): pl.pallas_call(functools.partial(body, kind), out_shape=jax.ShapeDtypeStr...  63.1 us
    dot_general x9, matrix products, dot_nt(): lax.dot_general(left, right, (((1,), (1,)), ((), ())), preferred_element_...  51.4 us
    dot_general x16, matrix products, dot_tn(): lax.dot_general(left, right, (((0,), (0,)), ((), ())), preferred_element_...  47.7 us
    dot_general x10, matrix products, dot_nn(): return jnp.dot(left, right, preferred_element_type=WIDE)  46.6 us
    convert_element_type x18, other arithmetic, reduce_rows(): added(*each, arrived).astype(LOW)  17 us
  transfers between devices with their start and end apart: 106, of which 33 were waited for; matrix products, arithmetic and copies ran while one was open for 30% of the time, Pallas kernels for 8%

profile of v3, /device:TPU:0, one launch (start us, length us, event | category | flops | bytes accessed | tf_op | source)
XLA Modules:
  0.0 784.7 jit_solution(6356825562704237380)
XLA Ops:
  12.1 5.1 collective-permute-start.6
  23.5 9.9 %collective-permute-done = bf16[256,1024]{1,0:T(8,128)(2,1)} collective-permute-done((bf16[256,1024]{1,0:T(8,128)(2,1)S(1)}, bf16[256,1024]{1,0:T(8,128)(2,1)}, u32[]{:S(2)}, u32[]{:S(2)}) %collective-permute-start) | collective-permute-done | bytes 524320 | tf_op jit(solution)/shard_map/ppermute | solution.py:40
  37.0 3.1 collective-permute-start.21
  40.2 4.0 collective-permute-done.21
  44.9 3.7 collective-permute-done.22
  57.9 8.1 %collective-permute-done.3 = bf16[64,2048]{1,0:T(8,128)(2,1)S(1)} collective-permute-done((bf16[64,2048]{1,0:T(8,128)(2,1)S(1)}, bf16[64,2048]{1,0:T(8,128)(2,1)S(1)}, u32[]{:S(2)}, u32[]{:S(2)}) %collective-permute-start.3) | collective-permute-done | bytes 262176 | tf_op jit(solution)/shard_map/ppermute | solution.py:40
  65.9 21.2 %collective-permute-done.4 = bf16[64,2048]{1,0:T(8,128)(2,1)S(1)} collective-permute-done((bf16[64,2048]{1,0:T(8,128)(2,1)S(1)}, bf16[64,2048]{1,0:T(8,128)(2,1)S(1)}, u32[]{:S(2)}, u32[]{:S(2)}) %collective-permute-start.4) | collective-permute-done | bytes 262176 | tf_op jit(solution)/shard_map/ppermute | solution.py:40
  96.6 18.0 %collective-permute-done.9 = bf16[4,64,1024]{2,1,0:T(8,128)(2,1)} collective-permute-done((bf16[4,64,1024]{2,1,0:T(8,128)(2,1)}, bf16[4,64,1024]{2,1,0:T(8,128)(2,1)}, u32[]{:S(2)}, u32[]{:S(2)}) %collective-permute-start.9) | collective-permute-done | bytes 524320 | tf_op jit(solution)/shard_map/ppermute | solution.py:40
  115.7 11.1 %collective-permute-done.11 = bf16[4,128,512]{2,1,0:T(8,128)(2,1)} collective-permute-done((bf16[4,128,512]{2,1,0:T(8,128)(2,1)}, bf16[4,128,512]{2,1,0:T(8,128)(2,1)}, u32[]{:S(2)}, u32[]{:S(2)}) %collective-permute-start.11) | collective-permute-done | bytes 524320 | tf_op jit(solution)/shard_map/ppermute | solution.py:40
  126.8 5.6 all-gather.3.cloned.1.call-done
  136.8 5.0 fusion.8.packed_ref
  141.8 9.3 %shard_map.365 = bf16[512,1024]{1,0:T(8,128)(2,1)} custom-call(s32[1]{0:T(128)} %bitcast.16.scalar_ref, bf16[512,3072]{1,0:T(8,128)(2,1)} %fusion.8.packed_ref), custom_call_target="tpu_custom_call" | custom-call | tf_op jit(solution)/shard_map/pallas_call | solution.py:342
  151.2 3.2 fusion.60
  169.2 21.5 %collective-permute-done.14 = bf16[4,2,64,1024]{3,2,1,0:T(8,128)(2,1)S(1)} collective-permute-done((bf16[4,2,64,1024]{3,2,1,0:T(8,128)(2,1)S(1)}, bf16[4,2,64,1024]{3,2,1,0:T(8,128)(2,1)S(1)}, u32[]{:S(2)}, u32[]{:S(2)}) %collective-permute-start.14) | collective-permute-done | bytes 1048608 | tf_op jit(solution)/shard_map/ppermute | solution.py:40
  190.7 36.7 %collective-permute-done.16 = bf16[4,2,128,512]{3,2,1,0:T(8,128)(2,1)S(1)} collective-permute-done((bf16[4,2,128,512]{3,2,1,0:T(8,128)(2,1)S(1)}, bf16[4,2,128,512]{3,2,1,0:T(8,128)(2,1)S(1)}, u32[]{:S(2)}, u32[]{:S(2)}) %collective-permute-start.16) | collective-permute-done | bytes 1048608 | tf_op jit(solution)/shard_map/ppermute | solution.py:40
  237.1 7.7 fusion.11
  244.8 9.1 %shard_map.366 = bf16[4,128,1024]{2,1,0:T(8,128)(2,1)} custom-call(s32[1]{0:T(128)} %bitcast.26.scalar_ref, bf16[4,128,3072]{2,1,0:T(8,128)(2,1)} %bitcast.502), custom_call_target="tpu_custom_call" | custom-call | tf_op jit(solution)/shard_map/pallas_call | solution.py:342
  253.9 3.3 multiply_reduce_fusion.8
  257.4 5.4 fusion.177
  262.8 6.4 fusion.152
  269.2 4.5 fusion.178
  273.8 6.6 multiply_reduce_fusion.7
  280.7 3.9 fusion.175
  286.9 3.2 multiply_reduce_fusion.1
  291.9 4.9 convolution_convert_fusion.3
  299.3 8.7 %fusion.20 = bf16[512,2048]{1,0:T(8,128)(2,1)} fusion(f32[512,2048]{1,0:T(8,128)} %copy-done.98, bf16[512,1024]{1,0:T(8,128)(2,1)S(1)} %copy-done.52, bf16[2048,1024]{1,0:T(8,128)(2,1)} %bitcast.36), kind=kOutput, calls=%fused_computation.24 | convolution fusion | flops 2168455168 | bytes 11534336 | tf_op jit(solution)/shard_map/dot_general | solution.py:242
  308.0 7.2 fusion.27
  315.3 4.4 convolution_convert_fusion.2
  319.8 6.3 fusion.151
  328.6 6.4 add_convert_fusion.1
  339.5 4.9 fusion.179
  344.5 6.1 multiply_reduce_fusion.2
  356.0 6.7 add_convert_fusion
  362.7 3.9 fusion.69
  366.6 22.1 %shard_map.367 = bf16[4,128,3072]{2,1,0:T(8,128)(2,1)} custom-call(s32[1]{0:T(128)} %bitcast.26.scalar_ref, bf16[4,128,3072]{2,1,0:T(8,128)(2,1)} %bitcast.503, bf16[4,128,1024]{2,1,0:T(8,128)(2,1)} %bitcast.542), custom_call_target="tpu_custom_call" | custom-call | tf_op jit(solution)/shard_map/pallas_call | solution.py:342
  388.7 3.7 convolution_convert_fusion.1
  392.9 6.8 fusion.41
  410.4 2.8 collective-permute-start.36
  416.8 4.0 collective-permute-done.37
  425.9 2.6 fusion.29
  436.0 47.2 %collective-permute-done.42 = bf16[4,128,1024]{2,1,0:T(8,128)(2,1)} collective-permute-done((bf16[4,128,1024]{2,1,0:T(8,128)(2,1)}, bf16[4,128,1024]{2,1,0:T(8,128)(2,1)}, u32[]{:S(2)}, u32[]{:S(2)}) %collective-permute-start.42) | collective-permute-done | bytes 1048608 | tf_op jit(solution)/shard_map/ppermute | solution.py:40
  485.9 3.9 fusion.66.up_ref
  489.8 22.6 %shard_map.368 = bf16[512,3072]{1,0:T(8,128)(2,1)} custom-call(s32[1]{0:T(128)} %bitcast.16.scalar_ref, bf16[512,3072]{1,0:T(8,128)(2,1)} %fusion.8.packed_ref, bf16[512,1024]{1,0:T(8,128)(2,1)} %fusion.66.up_ref), custom_call_target="tpu_custom_call" | custom-call | tf_op jit(solution)/shard_map/pallas_call | solution.py:342
  512.4 3.7 convolution_convert_fusion
  534.1 6.2 fusion.4
  556.2 12.7 %collective-permute-done.76 = bf16[4,2,64,768]{3,2,0,1:T(8,128)(2,1)S(1)} collective-permute-done((bf16[4,2,64,768]{3,2,0,1:T(8,128)(2,1)S(1)}, bf16[4,2,64,768]{3,2,0,1:T(8,128)(2,1)S(1)}, u32[]{:S(2)}, u32[]{:S(2)}) %collective-permute-start.76) | collective-permute-done | bytes 786464 | tf_op jit(solution)/shard_map/ppermute | solution.py:40
  569.6 15.0 %collective-permute-done.77 = bf16[4,2,64,768]{3,2,1,0:T(8,128)(2,1)} collective-permute-done((bf16[4,2,64,768]{3,2,1,0:T(8,128)(2,1)S(1)}, bf16[4,2,64,768]{3,2,1,0:T(8,128)(2,1)}, u32[]{:S(2)}, u32[]{:S(2)}) %collective-permute-start.77) | collective-permute-done | bytes 786464 | tf_op jit(solution)/shard_map/ppermute | solution.py:40
  596.0 18.1 %collective-permute-done.61 = bf16[4,2,64,512]{3,2,1,0:T(8,128)(2,1)S(1)} collective-permute-done((bf16[4,2,64,512]{3,2,1,0:T(8,128)(2,1)}, bf16[4,2,64,512]{3,2,1,0:T(8,128)(2,1)S(1)}, u32[]{:S(2)}, u32[]{:S(2)}) %collective-permute-start.61) | collective-permute-done | bytes 524320 | tf_op jit(solution)/shard_map/ppermute | solution.py:40
  625.7 2.6 multiply_reduce_fusion.11
  631.4 7.3 collective-permute-done.63
  640.3 3.1 collective-permute-done.64
  645.8 9.3 %collective-permute-done.70 = bf16[64,1536]{1,0:T(8,128)(2,1)S(1)} collective-permute-done((bf16[64,1536]{1,0:T(8,128)(2,1)S(1)}, bf16[64,1536]{1,0:T(8,128)(2,1)S(1)}, u32[]{:S(2)}, u32[]{:S(2)}) %collective-permute-start.70) | collective-permute-done | bytes 196640 | tf_op jit(solution)/shard_map/ppermute | solution.py:40
  656.8 10.5 %collective-permute-done.71 = bf16[64,1536]{1,0:T(8,128)(2,1)S(1)} collective-permute-done((bf16[64,1536]{1,0:T(8,128)(2,1)S(1)}, bf16[64,1536]{1,0:T(8,128)(2,1)S(1)}, u32[]{:S(2)}, u32[]{:S(2)}) %collective-permute-start.71) | collective-permute-done | bytes 196640 | tf_op jit(solution)/shard_map/ppermute | solution.py:40
  676.5 2.9 collective-permute-start.75
  680.7 4.1 collective-permute-done.74
  684.9 3.5 collective-permute-start.82
  695.7 3.4 collective-permute-start.83
  699.1 4.3 collective-permute-start.84
  710.1 2.6 collective-permute-start.99
  738.6 2.9 collective-permute-start.93
  744.6 3.9 collective-permute-done.94
  750.2 2.7 multiply_subtract_fusion.3
  763.6 2.6 multiply_subtract_fusion.4
  772.7 3.5 multiply_subtract_fusion
  (627 shorter events, 244.6 us)
Async XLA Ops:
  7.2 125.1 %all-gather.3.cloned.1.call-start = ((), (), s32[]{:S(2)}) async-start(), calls=%async_computation | async-start | bytes 8921088 | tf_op jit(solution)/shard_map/all_gather | solution.py:430
  11.2 225.9 %all-gather.5.cloned.1.call-start = ((), (), s32[]{:S(2)}) async-start(), calls=%async_computation.1 | async-start | bytes 8650752 | tf_op jit(solution)/shard_map/all_gather | solution.py:431
  12.1 41.2 %collective-permute-start.6 = (bf16[128,1024]{1,0:T(8,128)(2,1)S(1)}, bf16[128,1024]{1,0:T(8,128)(2,1)}, u32[]{:S(2)}, u32[]{:S(2)}) collective-permute-start(bf16[128,1024]{1,0:T(8,128)(2,1)S(1)} %convert_element_type.513), channel_id=1, source_target_pairs={{8,0},{16,8},{24,16},{0,24},{9,1},{17,9},{25,17},{1,25},{10,2},{18... | collective-permute-start | bytes 786440 | tf_op jit(solution)/shard_map/ppermute | solution.py:40
  17.2 37.4 %collective-permute-start.7 = (bf16[128,1024]{1,0:T(8,128)(2,1)S(1)}, bf16[128,1024]{1,0:T(8,128)(2,1)}, u32[]{:S(2)}, u32[]{:S(2)}) collective-permute-start(bf16[128,1024]{1,0:T(8,128)(2,1)S(1)} %convert_element_type.513), channel_id=1, source_target_pairs={{16,0},{24,8},{0,16},{8,24},{17,1},{25,9},{1,17},{9,25},{18,2},{26... | collective-permute-start | bytes 786440 | tf_op jit(solution)/shard_map/ppermute | solution.py:40
  17.2 39.0 %collective-permute-start.8 = (bf16[128,1024]{1,0:T(8,128)(2,1)S(1)}, bf16[128,1024]{1,0:T(8,128)(2,1)}, u32[]{:S(2)}, u32[]{:S(2)}) collective-permute-start(bf16[128,1024]{1,0:T(8,128)(2,1)S(1)} %convert_element_type.513), channel_id=1, source_target_pairs={{24,0},{0,8},{8,16},{16,24},{25,1},{1,9},{9,17},{17,25},{26,2},{2,... | collective-permute-start | bytes 786440 | tf_op jit(solution)/shard_map/ppermute | solution.py:40
  51.5 35.7 %collective-permute-start.4 = (bf16[64,2048]{1,0:T(8,128)(2,1)S(1)}, bf16[64,2048]{1,0:T(8,128)(2,1)S(1)}, u32[]{:S(2)}, u32[]{:S(2)}) collective-permute-start(bf16[64,2048]{1,0:T(8,128)(2,1)S(1)} %bitcast.529), channel_id=1, source_target_pairs={{16,0},{24,8},{0,16},{8,24},{17,1},{25,9},{1,17},{9,25},{18,2},{26... | collective-permute-start | bytes 786440 | tf_op jit(solution)/shard_map/ppermute | solution.py:40
  53.3 33.9 %collective-permute-start.5 = (bf16[64,2048]{1,0:T(8,128)(2,1)S(1)}, bf16[64,2048]{1,0:T(8,128)(2,1)S(1)}, u32[]{:S(2)}, u32[]{:S(2)}) collective-permute-start(bf16[64,2048]{1,0:T(8,128)(2,1)S(1)} %bitcast.530), channel_id=1, source_target_pairs={{24,0},{0,8},{8,16},{16,24},{25,1},{1,9},{9,17},{17,25},{26,2},{2,... | collective-permute-start | bytes 786440 | tf_op jit(solution)/shard_map/ppermute | solution.py:40
  54.6 111.7 %collective-permute-start.24 = (bf16[256,1024]{1,0:T(8,128)(2,1)S(1)}, bf16[256,1024]{1,0:T(8,128)(2,1)}, u32[]{:S(2)}, u32[]{:S(2)}) collective-permute-start(bf16[256,1024]{1,0:T(8,128)(2,1)S(1)} %get-tuple-element.275), channel_id=1, source_target_pairs={{2,0},{0,2},{3,1},{1,3},{6,4},{4,6},{7,5},{5,7},{10,8},{8,10},{11,... | collective-permute-start | bytes 1572872 | tf_op jit(solution)/shard_map/ppermute | solution.py:40
  56.2 39.6 %collective-permute-start.23 = (f32[1,4]{1,0:T(1,128)S(1)}, f32[1,4]{1,0:T(1,128)S(1)}, u32[]{:S(2)}, u32[]{:S(2)}) collective-permute-start(f32[1,4]{1,0:T(1,128)S(1)} %bitcast_add_fusion.2), channel_id=1, source_target_pairs={{24,0},{0,8},{8,16},{16,24},{25,1},{1,9},{9,17},{17,25},{26,2},{2,... | collective-permute-start | bytes 56 | tf_op jit(solution)/shard_map/ppermute | solution.py:40
  88.2 26.3 %collective-permute-start.9 = (bf16[4,64,1024]{2,1,0:T(8,128)(2,1)}, bf16[4,64,1024]{2,1,0:T(8,128)(2,1)}, u32[]{:S(2)}, u32[]{:S(2)}) collective-permute-start(bf16[4,64,1024]{2,1,0:T(8,128)(2,1)} %get-tuple-element.280), channel_id=1, source_target_pairs={{2,0},{0,2},{3,1},{1,3},{6,4},{4,6},{7,5},{5,7},{10,8},{8,10},{11,... | collective-permute-start | bytes 1572872 | tf_op jit(solution)/shard_map/ppermute | solution.py:40
  89.7 26.0 %collective-permute-start.10 = (bf16[4,64,1024]{2,1,0:T(8,128)(2,1)S(1)}, bf16[4,64,1024]{2,1,0:T(8,128)(2,1)}, u32[]{:S(2)}, u32[]{:S(2)}) collective-permute-start(bf16[4,64,1024]{2,1,0:T(8,128)(2,1)S(1)} %get-tuple-element.279), channel_id=1, source_target_pairs={{4,0},{0,4},{5,1},{1,5},{6,2},{2,6},{7,3},{3,7},{12,8},{8,12},{13,... | collective-permute-start | bytes 1572872 | tf_op jit(solution)/shard_map/ppermute | solution.py:40
  95.3 31.5 %collective-permute-start.11 = (bf16[4,128,512]{2,1,0:T(8,128)(2,1)}, bf16[4,128,512]{2,1,0:T(8,128)(2,1)}, u32[]{:S(2)}, u32[]{:S(2)}) collective-permute-start(bf16[4,128,512]{2,1,0:T(8,128)(2,1)} %get-tuple-element.278), channel_id=1, source_target_pairs={{2,0},{0,2},{3,1},{1,3},{6,4},{4,6},{7,5},{5,7},{10,8},{8,10},{11,... | collective-permute-start | bytes 1572872 | tf_op jit(solution)/shard_map/ppermute | solution.py:40
  95.9 30.9 %collective-permute-start.12 = (bf16[4,128,512]{2,1,0:T(8,128)(2,1)}, bf16[4,128,512]{2,1,0:T(8,128)(2,1)}, u32[]{:S(2)}, u32[]{:S(2)}) collective-permute-start(bf16[4,128,512]{2,1,0:T(8,128)(2,1)} %get-tuple-element.277), channel_id=1, source_target_pairs={{4,0},{0,4},{5,1},{1,5},{6,2},{2,6},{7,3},{3,7},{12,8},{8,12},{13,... | collective-permute-start | bytes 1572872 | tf_op jit(solution)/shard_map/ppermute | solution.py:40
  157.2 33.6 %collective-permute-start.14 = (bf16[4,2,64,1024]{3,2,1,0:T(8,128)(2,1)S(1)}, bf16[4,2,64,1024]{3,2,1,0:T(8,128)(2,1)S(1)}, u32[]{:S(2)}, u32[]{:S(2)}) collective-permute-start(bf16[4,2,64,1024]{3,2,1,0:T(8,128)(2,1)S(1)} %bitcast_dynamic-update-slice_fusion.7), channel_id=1, source_target_pairs={{4,0},{0,4},{5,1},{1,5},{6,2},{2,6},{7,3},{3,7},{12,8},{8,12},{13,... | collective-permute-start | bytes 3145736 | tf_op jit(solution)/shard_map/ppermute | solution.py:40
  159.7 31.0 %collective-permute-start.15 = (bf16[4,2,64,1024]{3,2,1,0:T(8,128)(2,1)S(1)}, bf16[4,2,64,1024]{3,2,1,0:T(8,128)(2,1)S(1)}, u32[]{:S(2)}, u32[]{:S(2)}) collective-permute-start(bf16[4,2,64,1024]{3,2,1,0:T(8,128)(2,1)S(1)} %bitcast_dynamic-update-slice_fusion.10), channel_id=1, source_target_pairs={{2,0},{0,2},{3,1},{1,3},{6,4},{4,6},{7,5},{5,7},{10,8},{8,10},{11,... | collective-permute-start | bytes 3145736 | tf_op jit(solution)/shard_map/ppermute | solution.py:40
  162.0 65.4 %collective-permute-start.16 = (bf16[4,2,128,512]{3,2,1,0:T(8,128)(2,1)S(1)}, bf16[4,2,128,512]{3,2,1,0:T(8,128)(2,1)S(1)}, u32[]{:S(2)}, u32[]{:S(2)}) collective-permute-start(bf16[4,2,128,512]{3,2,1,0:T(8,128)(2,1)S(1)} %bitcast_dynamic-update-slice_fusion.6), channel_id=1, source_target_pairs={{4,0},{0,4},{5,1},{1,5},{6,2},{2,6},{7,3},{3,7},{12,8},{8,12},{13,... | collective-permute-start | bytes 3145736 | tf_op jit(solution)/shard_map/ppermute | solution.py:40
  166.3 61.1 %collective-permute-start.17 = (bf16[4,2,128,512]{3,2,1,0:T(8,128)(2,1)S(1)}, bf16[4,2,128,512]{3,2,1,0:T(8,128)(2,1)S(1)}, u32[]{:S(2)}, u32[]{:S(2)}) collective-permute-start(bf16[4,2,128,512]{3,2,1,0:T(8,128)(2,1)S(1)} %bitcast_dynamic-update-slice_fusion.9), channel_id=1, source_target_pairs={{2,0},{0,2},{3,1},{1,3},{6,4},{4,6},{7,5},{5,7},{10,8},{8,10},{11,... | collective-permute-start | bytes 3145736 | tf_op jit(solution)/shard_map/ppermute | solution.py:40
  168.5 66.0 %collective-permute-start.25 = (bf16[2,256,1024]{2,1,0:T(8,128)(2,1)S(1)}, bf16[2,256,1024]{2,1,0:T(8,128)(2,1)S(1)}, u32[]{:S(2)}, u32[]{:S(2)}) collective-permute-start(bf16[2,256,1024]{2,1,0:T(8,128)(2,1)S(1)} %bitcast_dynamic-update-slice_fusion.8), channel_id=1, source_target_pairs={{1,0},{0,1},{3,2},{2,3},{5,4},{4,5},{7,6},{6,7},{9,8},{8,9},{11,10... | collective-permute-start | bytes 3145736 | tf_op jit(solution)/shard_map/ppermute | solution.py:40
  230.7 38.6 %collective-permute-start.18 = (bf16[1024,2048]{1,0:T(8,128)(2,1)}, bf16[1024,2048]{1,0:T(8,128)(2,1)}, u32[]{:S(2)}, u32[]{:S(2)}) collective-permute-start(bf16[1024,2048]{1,0:T(8,128)(2,1)} %bitcast.33), channel_id=1, source_target_pairs={{1,0},{0,1},{3,2},{2,3},{5,4},{4,5},{7,6},{6,7},{9,8},{8,9},{11,10... | collective-permute-start | bytes 12582920 | tf_op jit(solution)/shard_map/ppermute | solution.py:40
  233.9 39.9 %collective-permute-start.19 = (bf16[2048,1024]{1,0:T(8,128)(2,1)}, bf16[2048,1024]{1,0:T(8,128)(2,1)}, u32[]{:S(2)}, u32[]{:S(2)}) collective-permute-start(bf16[2048,1024]{1,0:T(8,128)(2,1)} %bitcast.36), channel_id=1, source_target_pairs={{1,0},{0,1},{3,2},{2,3},{5,4},{4,5},{7,6},{6,7},{9,8},{8,9},{11,10... | collective-permute-start | bytes 12582920 | tf_op jit(solution)/shard_map/ppermute | solution.py:40
  296.8 18.5 %collective-permute-start.27 = (bf16[2048,1024]{1,0:T(8,128)(2,1)}, bf16[2048,1024]{1,0:T(8,128)(2,1)}, u32[]{:S(2)}, u32[]{:S(2)}) collective-permute-start(bf16[2048,1024]{1,0:T(8,128)(2,1)} %convolution_convert_fusion.3), channel_id=1, source_target_pairs={{1,0},{0,1},{3,2},{2,3},{5,4},{4,5},{7,6},{6,7},{9,8},{8,9},{11,10... | collective-permute-start | bytes 12582920 | tf_op jit(solution)/shard_map/ppermute | solution.py:40
  298.7 16.6 %collective-permute-start.26 = (bf16[1024,512]{1,0:T(8,128)(2,1)S(1)}, bf16[1024,512]{1,0:T(8,128)(2,1)S(1)}, u32[]{:S(2)}, u32[]{:S(2)}) collective-permute-start(bf16[1024,512]{1,0:T(8,128)(2,1)S(1)} %convolution_convert_fusion.6), channel_id=1, source_target_pairs={{1,0},{0,1},{3,2},{2,3},{5,4},{4,5},{7,6},{6,7},{9,8},{8,9},{11,10... | collective-permute-start | bytes 3145736 | tf_op jit(solution)/shard_map/ppermute | solution.py:40
  319.8 32.9 %collective-permute-start.29 = (bf16[1024,2048]{1,0:T(8,128)(2,1)}, bf16[1024,2048]{1,0:T(8,128)(2,1)}, u32[]{:S(2)}, u32[]{:S(2)}) collective-permute-start(bf16[1024,2048]{1,0:T(8,128)(2,1)} %convolution_convert_fusion.2), channel_id=1, source_target_pairs={{1,0},{0,1},{3,2},{2,3},{5,4},{4,5},{7,6},{6,7},{9,8},{8,9},{11,10... | collective-permute-start | bytes 12582920 | tf_op jit(solution)/shard_map/ppermute | solution.py:40
  327.4 25.3 %collective-permute-start.28 = (bf16[2,2,4,32,512]{4,3,0,2,1:T(8,128)(2,1)S(1)}, bf16[2,2,4,32,512]{4,3,0,2,1:T(8,128)(2,1)S(1)}, u32[]{:S(2)}, u32[]{:S(2)}) collective-permute-start(bf16[2,2,4,32,512]{4,3,0,2,1:T(8,128)(2,1)S(1)} %bitcast.550), channel_id=1, source_target_pairs={{2,0},{0,2},{3,1},{1,3},{6,4},{4,6},{7,5},{5,7},{10,8},{8,10},{11,... | collective-permute-start | bytes 1572872 | tf_op jit(solution)/shard_map/ppermute | solution.py:40
  338.7 50.0 %collective-permute-start.31 = (bf16[4,2,128,1024]{3,2,0,1:T(8,128)(2,1)}, bf16[4,2,128,1024]{3,2,0,1:T(8,128)(2,1)}, u32[]{:S(2)}, u32[]{:S(2)}) collective-permute-start(bf16[4,2,128,1024]{3,2,0,1:T(8,128)(2,1)} %bitcast.491), channel_id=1, source_target_pairs={{2,0},{0,2},{3,1},{1,3},{6,4},{4,6},{7,5},{5,7},{10,8},{8,10},{11,... | collective-permute-start | bytes 6291464 | tf_op jit(solution)/shard_map/ppermute | solution.py:40
  352.9 35.8 %collective-permute-start.30 = (bf16[2,4,32,512]{3,2,0,1:T(8,128)(2,1)S(1)}, bf16[2,4,32,512]{3,2,0,1:T(8,128)(2,1)S(1)}, u32[]{:S(2)}, u32[]{:S(2)}) collective-permute-start(bf16[2,4,32,512]{3,2,0,1:T(8,128)(2,1)S(1)} %dynamic-slice_bitcast_fusion.22), channel_id=1, source_target_pairs={{4,0},{0,4},{5,1},{1,5},{6,2},{2,6},{7,3},{3,7},{12,8},{8,12},{13,... | collective-permute-start | bytes 786440 | tf_op jit(solution)/shard_map/ppermute | solution.py:40
  356.0 32.7 %collective-permute-start.32 = (bf16[1024,512]{1,0:T(8,128)(2,1)}, bf16[1024,512]{1,0:T(8,128)(2,1)}, u32[]{:S(2)}, u32[]{:S(2)}) collective-permute-start(bf16[1024,512]{1,0:T(8,128)(2,1)} %convolution_convert_fusion.5), channel_id=1, source_target_pairs={{1,0},{0,1},{3,2},{2,3},{5,4},{4,5},{7,6},{6,7},{9,8},{8,9},{11,10... | collective-permute-start | bytes 3145736 | tf_op jit(solution)/shard_map/ppermute | solution.py:40
  392.4 28.4 %collective-permute-start.38 = (bf16[1024,1536]{1,0:T(8,128)(2,1)S(1)}, bf16[1024,1536]{1,0:T(8,128)(2,1)S(1)}, u32[]{:S(2)}, u32[]{:S(2)}) collective-permute-start(bf16[1024,1536]{1,0:T(8,128)(2,1)S(1)} %convolution_convert_fusion.1), channel_id=1, source_target_pairs={{1,0},{0,1},{3,2},{2,3},{5,4},{4,5},{7,6},{6,7},{9,8},{8,9},{11,10... | collective-permute-start | bytes 9437192 | tf_op jit(solution)/shard_map/ppermute | solution.py:40
  414.7 69.2 %collective-permute-start.43 = (bf16[4,2,64,2048]{3,2,1,0:T(8,128)(2,1)}, bf16[4,2,64,2048]{3,2,1,0:T(8,128)(2,1)}, u32[]{:S(2)}, u32[]{:S(2)}) collective-permute-start(bf16[4,2,64,2048]{3,2,1,0:T(8,128)(2,1)} %dynamic-slice_bitcast_fusion), channel_id=1, source_target_pairs={{4,0},{0,4},{5,1},{1,5},{6,2},{2,6},{7,3},{3,7},{12,8},{8,12},{13,... | collective-permute-start | bytes 6291464 | tf_op jit(solution)/shard_map/ppermute | solution.py:40
  424.1 88.3 %collective-permute-start.45 = (bf16[4,2,64,1536]{3,2,1,0:T(8,128)(2,1)}, bf16[4,2,64,1536]{3,2,1,0:T(8,128)(2,1)}, u32[]{:S(2)}, u32[]{:S(2)}) collective-permute-start(bf16[4,2,64,1536]{3,2,1,0:T(8,128)(2,1)} %dynamic-slice_bitcast_fusion.1), channel_id=1, source_target_pairs={{2,0},{0,2},{3,1},{1,3},{6,4},{4,6},{7,5},{5,7},{10,8},{8,10},{11,... | collective-permute-start | bytes 4718600 | tf_op jit(solution)/shard_map/ppermute | solution.py:40
  429.6 53.6 %collective-permute-start.42 = (bf16[4,128,1024]{2,1,0:T(8,128)(2,1)}, bf16[4,128,1024]{2,1,0:T(8,128)(2,1)}, u32[]{:S(2)}, u32[]{:S(2)}) collective-permute-start(bf16[4,128,1024]{2,1,0:T(8,128)(2,1)} %dynamic-slice_bitcast_fusion.3), channel_id=1, source_target_pairs={{4,0},{0,4},{5,1},{1,5},{6,2},{2,6},{7,3},{3,7},{12,8},{8,12},{13,... | collective-permute-start | bytes 3145736 | tf_op jit(solution)/shard_map/ppermute | solution.py:40
  432.3 80.2 %collective-permute-start.46 = (bf16[1024,512]{1,0:T(8,128)(2,1)}, bf16[1024,512]{1,0:T(8,128)(2,1)}, u32[]{:S(2)}, u32[]{:S(2)}) collective-permute-start(bf16[1024,512]{1,0:T(8,128)(2,1)} %convolution_convert_fusion.4), channel_id=1, source_target_pairs={{1,0},{0,1},{3,2},{2,3},{5,4},{4,5},{7,6},{6,7},{9,8},{8,9},{11,10... | collective-permute-start | bytes 3145736 | tf_op jit(solution)/shard_map/ppermute | solution.py:40
  432.9 51.8 %collective-permute-start.39 = (bf16[2,32,512]{2,1,0:T(8,128)(2,1)S(1)}, bf16[2,32,512]{2,1,0:T(8,128)(2,1)S(1)}, u32[]{:S(2)}, u32[]{:S(2)}) collective-permute-start(bf16[2,32,512]{2,1,0:T(8,128)(2,1)S(1)} %get-tuple-element.302), channel_id=1, source_target_pairs={{8,0},{16,8},{24,16},{0,24},{9,1},{17,9},{25,17},{1,25},{10,2},{18... | collective-permute-start | bytes 196616 | tf_op jit(solution)/shard_map/ppermute | solution.py:40
  483.2 29.2 %collective-permute-start.40 = (bf16[2,32,512]{2,1,0:T(8,128)(2,1)S(1)}, bf16[2,32,512]{2,1,0:T(8,128)(2,1)S(1)}, u32[]{:S(2)}, u32[]{:S(2)}) collective-permute-start(bf16[2,32,512]{2,1,0:T(8,128)(2,1)S(1)} %get-tuple-element.302), channel_id=1, source_target_pairs={{16,0},{24,8},{0,16},{8,24},{17,1},{25,9},{1,17},{9,25},{18,2},{26... | collective-permute-start | bytes 196616 | tf_op jit(solution)/shard_map/ppermute | solution.py:40
  483.9 28.5 %collective-permute-start.41 = (bf16[2,32,512]{2,1,0:T(8,128)(2,1)S(1)}, bf16[2,32,512]{2,1,0:T(8,128)(2,1)S(1)}, u32[]{:S(2)}, u32[]{:S(2)}) collective-permute-start(bf16[2,32,512]{2,1,0:T(8,128)(2,1)S(1)} %get-tuple-element.302), channel_id=1, source_target_pairs={{24,0},{0,8},{8,16},{16,24},{25,1},{1,9},{9,17},{17,25},{26,2},{2,... | collective-permute-start | bytes 196616 | tf_op jit(solution)/shard_map/ppermute | solution.py:40
  484.7 27.7 %collective-permute-start.44 = (bf16[4,64,512]{2,1,0:T(8,128)(2,1)S(1)}, bf16[4,64,512]{2,1,0:T(8,128)(2,1)S(1)}, u32[]{:S(2)}, u32[]{:S(2)}) collective-permute-start(bf16[4,64,512]{2,1,0:T(8,128)(2,1)S(1)} %dynamic-slice_bitcast_fusion.21), channel_id=1, source_target_pairs={{4,0},{0,4},{5,1},{1,5},{6,2},{2,6},{7,3},{3,7},{12,8},{8,12},{13,... | collective-permute-start | bytes 786440 | tf_op jit(solution)/shard_map/ppermute | solution.py:40
  516.2 30.4 %collective-permute-start.47 = (bf16[1024,1536]{1,0:T(8,128)(2,1)S(1)}, bf16[1024,1536]{1,0:T(8,128)(2,1)S(1)}, u32[]{:S(2)}, u32[]{:S(2)}) collective-permute-start(bf16[1024,1536]{1,0:T(8,128)(2,1)S(1)} %convolution_convert_fusion), channel_id=1, source_target_pairs={{1,0},{0,1},{3,2},{2,3},{5,4},{4,5},{7,6},{6,7},{9,8},{8,9},{11,10... | collective-permute-start | bytes 9437192 | tf_op jit(solution)/shard_map/ppermute | solution.py:40
  516.3 30.2 %collective-permute-start.48 = (bf16[2,4,32,512]{3,2,1,0:T(8,128)(2,1)S(1)}, bf16[2,4,32,512]{3,2,1,0:T(8,128)(2,1)S(1)}, u32[]{:S(2)}, u32[]{:S(2)}) collective-permute-start(bf16[2,4,32,512]{3,2,1,0:T(8,128)(2,1)S(1)} %bitcast_dynamic-update-slice_fusion.26), channel_id=1, source_target_pairs={{4,0},{0,4},{5,1},{1,5},{6,2},{2,6},{7,3},{3,7},{12,8},{8,12},{13,... | collective-permute-start | bytes 786440 | tf_op jit(solution)/shard_map/ppermute | solution.py:40
  517.3 25.7 %collective-permute-start.49 = (bf16[64,512]{1,0:T(8,128)(2,1)S(1)}, bf16[64,512]{1,0:T(8,128)(2,1)S(1)}, u32[]{:S(2)}, u32[]{:S(2)}) collective-permute-start(bf16[64,512]{1,0:T(8,128)(2,1)S(1)} %get-tuple-element.313), channel_id=1, source_target_pairs={{24,0},{0,8},{8,16},{16,24},{25,1},{1,9},{9,17},{17,25},{26,2},{2,... | collective-permute-start | bytes 196616 | tf_op jit(solution)/shard_map/ppermute | solution.py:40
  519.3 25.0 %collective-permute-start.50 = (bf16[64,512]{1,0:T(8,128)(2,1)S(1)}, bf16[64,512]{1,0:T(8,128)(2,1)S(1)}, u32[]{:S(2)}, u32[]{:S(2)}) collective-permute-start(bf16[64,512]{1,0:T(8,128)(2,1)S(1)} %get-tuple-element.312), channel_id=1, source_target_pairs={{16,0},{24,8},{0,16},{8,24},{17,1},{25,9},{1,17},{9,25},{18,2},{26... | collective-permute-start | bytes 196616 | tf_op jit(solution)/shard_map/ppermute | solution.py:40
  520.9 24.3 %collective-permute-start.51 = (bf16[64,512]{1,0:T(8,128)(2,1)S(1)}, bf16[64,512]{1,0:T(8,128)(2,1)S(1)}, u32[]{:S(2)}, u32[]{:S(2)}) collective-permute-start(bf16[64,512]{1,0:T(8,128)(2,1)S(1)} %get-tuple-element.311), channel_id=1, source_target_pairs={{8,0},{16,8},{24,16},{0,24},{9,1},{17,9},{25,17},{1,25},{10,2},{18... | collective-permute-start | bytes 196616 | tf_op jit(solution)/shard_map/ppermute | solution.py:40
  543.0 71.7 %collective-permute-start.56 = (bf16[4,64,2048]{2,1,0:T(8,128)(2,1)}, bf16[4,64,2048]{2,1,0:T(8,128)(2,1)}, u32[]{:S(2)}, u32[]{:S(2)}) collective-permute-start(bf16[4,64,2048]{2,1,0:T(8,128)(2,1)} %dynamic-slice_bitcast_fusion.2), channel_id=1, source_target_pairs={{2,0},{0,2},{3,1},{1,3},{6,4},{4,6},{7,5},{5,7},{10,8},{8,10},{11,... | collective-permute-start | bytes 3145736 | tf_op jit(solution)/shard_map/ppermute | solution.py:40
  544.3 43.6 %collective-permute-start.57 = (bf16[128,1024]{1,0:T(8,128)(2,1)}, bf16[128,1024]{1,0:T(8,128)(2,1)}, u32[]{:S(2)}, u32[]{:S(2)}) collective-permute-start(bf16[128,1024]{1,0:T(8,128)(2,1)} %get-tuple-element.272), channel_id=1, source_target_pairs={{24,0},{0,8},{8,16},{16,24},{25,1},{1,9},{9,17},{17,25},{26,2},{2,... | collective-permute-start | bytes 786440 | tf_op jit(solution)/shard_map/ppermute | solution.py:40
  545.3 44.6 %collective-permute-start.58 = (bf16[128,1024]{1,0:T(8,128)(2,1)}, bf16[128,1024]{1,0:T(8,128)(2,1)}, u32[]{:S(2)}, u32[]{:S(2)}) collective-permute-start(bf16[128,1024]{1,0:T(8,128)(2,1)} %get-tuple-element.271), channel_id=1, source_target_pairs={{16,0},{24,8},{0,16},{8,24},{17,1},{25,9},{1,17},{9,25},{18,2},{26... | collective-permute-start | bytes 786440 | tf_op jit(solution)/shard_map/ppermute | solution.py:40
  550.8 18.0 %collective-permute-start.76 = (bf16[4,2,64,768]{3,2,0,1:T(8,128)(2,1)S(1)}, bf16[4,2,64,768]{3,2,0,1:T(8,128)(2,1)S(1)}, u32[]{:S(2)}, u32[]{:S(2)}) collective-permute-start(bf16[4,2,64,768]{3,2,0,1:T(8,128)(2,1)S(1)} %bitcast.543), channel_id=1, source_target_pairs={{4,0},{0,4},{5,1},{1,5},{6,2},{2,6},{7,3},{3,7},{12,8},{8,12},{13,... | collective-permute-start | bytes 2359304 | tf_op jit(solution)/shard_map/ppermute | solution.py:40
  551.6 33.0 %collective-permute-start.77 = (bf16[4,2,64,768]{3,2,1,0:T(8,128)(2,1)S(1)}, bf16[4,2,64,768]{3,2,1,0:T(8,128)(2,1)}, u32[]{:S(2)}, u32[]{:S(2)}) collective-permute-start(bf16[4,2,64,768]{3,2,1,0:T(8,128)(2,1)S(1)} %dynamic-slice_bitcast_fusion.4), channel_id=1, source_target_pairs={{2,0},{0,2},{3,1},{1,3},{6,4},{4,6},{7,5},{5,7},{10,8},{8,10},{11,... | collective-permute-start | bytes 2359304 | tf_op jit(solution)/shard_map/ppermute | solution.py:40
  568.9 47.8 %collective-permute-start.52 = (bf16[1024,512]{1,0:T(8,128)(2,1)}, bf16[1024,512]{1,0:T(8,128)(2,1)}, u32[]{:S(2)}, u32[]{:S(2)}) collective-permute-start(bf16[1024,512]{1,0:T(8,128)(2,1)} %fusion.65), channel_id=1, source_target_pairs={{1,0},{0,1},{3,2},{2,3},{5,4},{4,5},{7,6},{6,7},{9,8},{8,9},{11,10... | collective-permute-start | bytes 3145736 | tf_op jit(solution)/shard_map/ppermute | solution.py:40
  584.7 29.5 %collective-permute-start.60 = (bf16[4,64,1536]{2,1,0:T(8,128)(2,1)}, bf16[4,64,1536]{2,1,0:T(8,128)(2,1)}, u32[]{:S(2)}, u32[]{:S(2)}) collective-permute-start(bf16[4,64,1536]{2,1,0:T(8,128)(2,1)} %dynamic-slice_bitcast_fusion.5), channel_id=1, source_target_pairs={{4,0},{0,4},{5,1},{1,5},{6,2},{2,6},{7,3},{3,7},{12,8},{8,12},{13,... | collective-permute-start | bytes 2359304 | tf_op jit(solution)/shard_map/ppermute | solution.py:40
  589.9 24.3 %collective-permute-start.61 = (bf16[4,2,64,512]{3,2,1,0:T(8,128)(2,1)}, bf16[4,2,64,512]{3,2,1,0:T(8,128)(2,1)S(1)}, u32[]{:S(2)}, u32[]{:S(2)}) collective-permute-start(bf16[4,2,64,512]{3,2,1,0:T(8,128)(2,1)} %dynamic-slice_bitcast_fusion.6), channel_id=1, source_target_pairs={{4,0},{0,4},{5,1},{1,5},{6,2},{2,6},{7,3},{3,7},{12,8},{8,12},{13,... | collective-permute-start | bytes 1572872 | tf_op jit(solution)/shard_map/ppermute | solution.py:40
  594.7 22.0 %collective-permute-start.54 = (bf16[256,512]{1,0:T(8,128)(2,1)S(1)}, bf16[256,512]{1,0:T(8,128)(2,1)S(1)}, u32[]{:S(2)}, u32[]{:S(2)}) collective-permute-start(bf16[256,512]{1,0:T(8,128)(2,1)S(1)} %copy-done.67), channel_id=1, source_target_pairs={{1,0},{0,1},{3,2},{2,3},{5,4},{4,5},{7,6},{6,7},{9,8},{8,9},{11,10... | collective-permute-start | bytes 786440 | tf_op jit(solution)/shard_map/ppermute | solution.py:40
  618.9 25.3 %collective-permute-start.62 = (bf16[2,2,4,32,512]{4,3,0,2,1:T(8,128)(2,1)S(1)}, bf16[2,2,4,32,512]{4,3,0,2,1:T(8,128)(2,1)S(1)}, u32[]{:S(2)}, u32[]{:S(2)}) collective-permute-start(bf16[2,2,4,32,512]{4,3,0,2,1:T(8,128)(2,1)S(1)} %bitcast.549), channel_id=1, source_target_pairs={{2,0},{0,2},{3,1},{1,3},{6,4},{4,6},{7,5},{5,7},{10,8},{8,10},{11,... | collective-permute-start | bytes 1572872 | tf_op jit(solution)/shard_map/ppermute | solution.py:40
  620.3 18.4 %collective-permute-start.63 = (f32[5,1024]{1,0:T(8,128)S(1)}, f32[5,1024]{1,0:T(8,128)S(1)}, u32[]{:S(2)}, u32[]{:S(2)}) collective-permute-start(f32[5,1024]{1,0:T(8,128)S(1)} %add.911), channel_id=1, source_target_pairs={{2,0},{0,2},{3,1},{1,3},{6,4},{4,6},{7,5},{5,7},{10,8},{8,10},{11,... | collective-permute-start | bytes 61448 | tf_op jit(solution)/shard_map/ppermute | solution.py:40
  621.2 22.2 %collective-permute-start.64 = (bf16[4,64,512]{2,1,0:T(8,128)(2,1)S(1)}, bf16[4,64,512]{2,1,0:T(8,128)(2,1)S(1)}, u32[]{:S(2)}, u32[]{:S(2)}) collective-permute-start(bf16[4,64,512]{2,1,0:T(8,128)(2,1)S(1)} %dynamic-slice_bitcast_fusion.16), channel_id=1, source_target_pairs={{2,0},{0,2},{3,1},{1,3},{6,4},{4,6},{7,5},{5,7},{10,8},{8,10},{11,... | collective-permute-start | bytes 786440 | tf_op jit(solution)/shard_map/ppermute | solution.py:40
  629.0 42.5 %collective-permute-start.67 = (bf16[64,2048]{1,0:T(8,128)(2,1)S(1)}, bf16[64,2048]{1,0:T(8,128)(2,1)S(1)}, u32[]{:S(2)}, u32[]{:S(2)}) collective-permute-start(bf16[64,2048]{1,0:T(8,128)(2,1)S(1)} %get-tuple-element.267), channel_id=1, source_target_pairs={{24,0},{0,8},{8,16},{16,24},{25,1},{1,9},{9,17},{17,25},{26,2},{2,... | collective-permute-start | bytes 786440 | tf_op jit(solution)/shard_map/ppermute | solution.py:40
  630.0 44.0 %collective-permute-start.68 = (bf16[64,2048]{1,0:T(8,128)(2,1)S(1)}, bf16[64,2048]{1,0:T(8,128)(2,1)S(1)}, u32[]{:S(2)}, u32[]{:S(2)}) collective-permute-start(bf16[64,2048]{1,0:T(8,128)(2,1)S(1)} %get-tuple-element.266), channel_id=1, source_target_pairs={{16,0},{24,8},{0,16},{8,24},{17,1},{25,9},{1,17},{9,25},{18,2},{26... | collective-permute-start | bytes 786440 | tf_op jit(solution)/shard_map/ppermute | solution.py:40
  638.7 37.8 %collective-permute-start.69 = (bf16[64,2048]{1,0:T(8,128)(2,1)S(1)}, bf16[64,2048]{1,0:T(8,128)(2,1)S(1)}, u32[]{:S(2)}, u32[]{:S(2)}) collective-permute-start(bf16[64,2048]{1,0:T(8,128)(2,1)S(1)} %get-tuple-element.265), channel_id=1, source_target_pairs={{8,0},{16,8},{24,16},{0,24},{9,1},{17,9},{25,17},{1,25},{10,2},{18... | collective-permute-start | bytes 786440 | tf_op jit(solution)/shard_map/ppermute | solution.py:40
  644.3 23.0 %collective-permute-start.71 = (bf16[64,1536]{1,0:T(8,128)(2,1)S(1)}, bf16[64,1536]{1,0:T(8,128)(2,1)S(1)}, u32[]{:S(2)}, u32[]{:S(2)}) collective-permute-start(bf16[64,1536]{1,0:T(8,128)(2,1)S(1)} %get-tuple-element.289), channel_id=1, source_target_pairs={{16,0},{24,8},{0,16},{8,24},{17,1},{25,9},{1,17},{9,25},{18,2},{26... | collective-permute-start | bytes 589832 | tf_op jit(solution)/shard_map/ppermute | solution.py:40
  667.3 21.1 %collective-permute-start.65 = (bf16[2,4,32,512]{3,2,0,1:T(8,128)(2,1)S(1)}, bf16[2,4,32,512]{3,2,0,1:T(8,128)(2,1)S(1)}, u32[]{:S(2)}, u32[]{:S(2)}) collective-permute-start(bf16[2,4,32,512]{3,2,0,1:T(8,128)(2,1)S(1)} %dynamic-slice_bitcast_fusion.15), channel_id=1, source_target_pairs={{4,0},{0,4},{5,1},{1,5},{6,2},{2,6},{7,3},{3,7},{12,8},{8,12},{13,... | collective-permute-start | bytes 786440 | tf_op jit(solution)/shard_map/ppermute | solution.py:40
  688.4 17.4 %collective-permute-start.87 = (f32[5,1024]{1,0:T(8,128)S(1)}, f32[5,1024]{1,0:T(8,128)}, u32[]{:S(2)}, u32[]{:S(2)}) collective-permute-start(f32[5,1024]{1,0:T(8,128)S(1)} %add.926), channel_id=1, source_target_pairs={{16,0},{24,8},{0,16},{8,24},{17,1},{25,9},{1,17},{9,25},{18,2},{26... | collective-permute-start | bytes 61448 | tf_op jit(solution)/shard_map/ppermute | solution.py:40
  705.8 54.5 %collective-permute-start.96 = (f32[32,1536]{1,0:T(8,128)}, f32[32,1536]{1,0:T(8,128)}, u32[]{:S(2)}, u32[]{:S(2)}) collective-permute-start(f32[32,1536]{1,0:T(8,128)} %dynamic-slice_bitcast_fusion.23), channel_id=1, source_target_pairs={{1,0},{0,1},{3,2},{2,3},{5,4},{4,5},{7,6},{6,7},{9,8},{8,9},{11,10... | collective-permute-start | bytes 589832 | tf_op jit(solution)/shard_map/ppermute | solution.py:40
  705.8 18.7 %collective-permute-start.97 = (f32[32,512]{1,0:T(8,128)}, f32[32,512]{1,0:T(8,128)}, u32[]{:S(2)}, u32[]{:S(2)}) collective-permute-start(f32[32,512]{1,0:T(8,128)} %dynamic-slice_bitcast_fusion.28), channel_id=1, source_target_pairs={{1,0},{0,1},{3,2},{2,3},{5,4},{4,5},{7,6},{6,7},{9,8},{8,9},{11,10... | collective-permute-start | bytes 196616 | tf_op jit(solution)/shard_map/ppermute | solution.py:40
  706.3 55.0 %collective-permute-start.98 = (f32[32,2048]{1,0:T(8,128)}, f32[32,2048]{1,0:T(8,128)}, u32[]{:S(2)}, u32[]{:S(2)}) collective-permute-start(f32[32,2048]{1,0:T(8,128)} %get-tuple-element.298), channel_id=1, source_target_pairs={{1,0},{0,1},{3,2},{2,3},{5,4},{4,5},{7,6},{6,7},{9,8},{8,9},{11,10... | collective-permute-start | bytes 786440 | tf_op jit(solution)/shard_map/ppermute | solution.py:40
  710.1 46.2 %collective-permute-start.99 = (bf16[2,32,512]{2,1,0:T(8,128)(2,1)}, bf16[2,32,512]{2,1,0:T(8,128)(2,1)}, u32[]{:S(2)}, u32[]{:S(2)}) collective-permute-start(bf16[2,32,512]{2,1,0:T(8,128)(2,1)} %get-tuple-element.299), channel_id=1, source_target_pairs={{8,0},{16,8},{24,16},{0,24},{9,1},{17,9},{25,17},{1,25},{10,2},{18... | collective-permute-start | bytes 196616 | tf_op jit(solution)/shard_map/ppermute | solution.py:40
  712.6 45.4 %collective-permute-start.100 = (bf16[2,32,512]{2,1,0:T(8,128)(2,1)}, bf16[2,32,512]{2,1,0:T(8,128)(2,1)}, u32[]{:S(2)}, u32[]{:S(2)}) collective-permute-start(bf16[2,32,512]{2,1,0:T(8,128)(2,1)} %get-tuple-element.299), channel_id=1, source_target_pairs={{16,0},{24,8},{0,16},{8,24},{17,1},{25,9},{1,17},{9,25},{18,2},{26... | collective-permute-start | bytes 196616 | tf_op jit(solution)/shard_map/ppermute | solution.py:40
  (147 other events, 1561.4 us)
Sparse Core Ops, SparseCore 0:
  11.5 120.8 all-gather.2
  135.8 99.1 all-gather.4

commit v4 on v3

--- a/solution.py
+++ b/solution.py
@@ -33,6 +33,7 @@
 ALL = ("z", "r", "m", "h")
 GROUP = 256
 LANES = 128
+HALF = D // 2
 
 
 def shifted(part, axis, shift):
@@ -97,21 +98,54 @@
     return value
 
 
-def gather_half(part):
-    others = yield sent_around(part, "z")
-    first, second = jnp.split(placed(part, others, "z", 0), 2, axis=-1)
-    one = sent_around(first, "m")
-    two = sent_around(second, "r")
-    one, two = yield (one, two)
-    first, second = placed(first, one, "m", 1), placed(second, two, "r", 1)
-    one = sent_around(first, "r")
-    two = sent_around(second, "m")
-    one, two = yield (one, two)
-    first, second = placed(first, one, "r", 1), placed(second, two, "m", 2)
-    own = jnp.concatenate([first, second], axis=-1)
+def split_columns(array):
+    cut = array.shape[-1] // (2 * LANES) * LANES
+    return array[..., :cut], array[..., cut:]
+
+
+def gather_deep(part):
+    if lax.axis_size("z") != 4:
+        others = yield sent_around(part, "z")
+        return placed(part, others, "z", 0)
+    above, below = yield [shifted(part, "z", 1), shifted(part, "z", 3)]
+    first, second = split_columns(above)[0], split_columns(below)[1]
+    first, second = yield [shifted(first, "z", 1), shifted(second, "z", 3)]
+    mine = lax.axis_index("z")
+    whole = jnp.broadcast_to(part[None], (4,) + part.shape)
+    whole = lax.dynamic_update_index_in_dim(whole, above, (mine + 1) % 4, 0)
+    whole = lax.dynamic_update_index_in_dim(whole, below, (mine + 3) % 4, 0)
+    zero = jnp.int32(0)
+    place = [(mine + 2) % 4] + [zero] * part.ndim
+    whole = lax.dynamic_update_slice(whole, first[None], place)
+    place[-1] = jnp.int32(first.shape[-1])
+    return lax.dynamic_update_slice(whole, second[None], place)
+
+
+def gather_flat(part, dim):
+    first, second = split_columns(part)
+    one, two = yield (sent_around(first, "m"), sent_around(second, "r"))
+    first, second = placed(first, one, "m", dim), placed(second, two, "r", dim)
+    one, two = yield (sent_around(first, "r"), sent_around(second, "m"))
+    first, second = placed(first, one, "r", dim), placed(second, two, "m", dim + 1)
+    return jnp.concatenate([first, second], axis=-1)
+
+
+def exchanged(own):
     own = own.reshape(-1, own.shape[-1])
     (other,) = yield [shifted(own, "h", 1)]
     return (own, other)
+
+
+def gather_half(part):
+    whole = yield from gather_deep(part)
+    whole = yield from gather_flat(whole, 1)
+    return (yield from exchanged(whole))
+
+
+def gather_pair(mine, other):
+    (other,) = yield [shifted(other, "h", 1)]
+    pair = placed(mine, [other], "h", 0)
+    return pair.reshape(-1, mine.shape[1])
 
 
 def by_owner(array, block):
@@ -121,11 +155,24 @@
 
 
 def gather_columns(part, block):
-    mine, other = by_owner(part, block)
-    (other,) = yield [shifted(other, "h", 1)]
-    pair = placed(mine, [other], "h", 0)
-    result = yield from gather_half(pair.reshape(-1, mine.shape[1]))
-    return result
+    pair = yield from gather_pair(*by_owner(part, block))
+    return (yield from gather_half(pair))
+
+
+def gather_layer(w_in, w_out, *rest):
+    parts = [by_owner(array, HALF) for array in (w_in, w_out)]
+    mine, other = (jnp.concatenate(part + rest, axis=1).astype(LOW) for part in zip(*parts))
+    pair = yield from gather_pair(mine, other)
+    whole = yield from gather_flat(pair, 0)
+    whole = yield from gather_deep(whole)
+    return (yield from exchanged(whole))
+
+
+def gather_table(part):
+    others = yield sent_around(part, "m")
+    part = placed(part, others, "m", 0)
+    others = yield sent_around(part, "h")
+    return placed(part, others, "h", 1).reshape(-1, part.shape[-1])
 
 
 def pieces_of(total, dim, axis):
@@ -283,72 +330,91 @@
         ref[:, :, pl.ds(start, LANES)] = value.reshape(FRAMES, -1, LANES)
 
 
-def forward_body(kind, scalar_ref, packed_ref, mixed_ref):
+def forward_body(kind, scalar_ref, own_ref, other_ref, mixed_ref):
     allowed = allowed_pairs(kind, scalar_ref[0], GROUP)
     first = lax.broadcasted_iota(jnp.int32, (GROUP, LANES), 1) < HEAD
+    half = scalar_ref[1]
 
     def turn(pair, _):
         start = pl.multiple_of(pair * LANES, LANES)
-        query = block_of(packed_ref, start, kind)
-        key = block_of(packed_ref, pl.multiple_of(D + start, LANES), kind)
-        value = block_of(packed_ref, pl.multiple_of(2 * D + start, LANES), kind)
-        zero = jnp.zeros_like(query)
-        one = dot_nn(softmax_rows(jnp.where(first, query, zero), key, allowed).astype(LOW), value)
-        two = dot_nn(softmax_rows(jnp.where(first, zero, query), key, allowed).astype(LOW), value)
-        store_to(mixed_ref, start, kind, jnp.where(first, one, two).astype(LOW))
+        for ref, which in ((own_ref, half), (other_ref, 1 - half)):
+            query, key, value = (
+                block_of(ref, pl.multiple_of(part * HALF + start, LANES), kind)
+                for part in range(3)
+            )
+            zero = jnp.zeros_like(query)
+            one = softmax_rows(jnp.where(first, query, zero), key, allowed).astype(LOW)
+            two = softmax_rows(jnp.where(first, zero, query), key, allowed).astype(LOW)
+            mixed = jnp.where(first, dot_nn(one, value), dot_nn(two, value)).astype(LOW)
+            store_to(mixed_ref, pl.multiple_of(which * HALF + start, LANES), kind, mixed)
         return 0
 
-    lax.fori_loop(0, D // LANES, turn, 0, unroll=4)
-
-
-def backward_body(kind, scalar_ref, packed_ref, up_ref, out_ref):
+    lax.fori_loop(0, HALF // LANES, turn, 0, unroll=2)
+
+
+def backward_body(kind, scalar_ref, own_ref, other_ref, up_ref, own_out_ref, other_out_ref):
     allowed = allowed_pairs(kind, scalar_ref[0], GROUP)
     first = lax.broadcasted_iota(jnp.int32, (GROUP, LANES), 1) < HEAD
+    half = scalar_ref[1]
 
     def turn(pair, _):
         start = pl.multiple_of(pair * LANES, LANES)
-        key_at = pl.multiple_of(D + start, LANES)
-        value_at = pl.multiple_of(2 * D + start, LANES)
-        query = block_of(packed_ref, start, kind)
-        key = block_of(packed_ref, key_at, kind)
-        value = block_of(packed_ref, value_at, kind)
-        up = block_of(up_ref, start, kind)
-        zero = jnp.zeros_like(query)
-        grads = []
-        for mine in (first, ~first):
-            probs = softmax_rows(jnp.where(mine, query, zero), key, allowed)
-            inner = dot_nt(jnp.where(mine, up, zero), value)
-            total = jnp.sum(probs * inner, axis=-1, keepdims=True)
-            scores = (probs * (inner - total) * HEAD ** (-0.5)).astype(LOW)
-            grads.append((dot_nn(scores, key), dot_tn(scores, query), dot_tn(probs.astype(LOW), up)))
-        for place, one, two in zip((start, key_at, value_at), *grads):
-            store_to(out_ref, place, kind, jnp.where(first, one, two).astype(LOW))
+        for ref, out_ref, which in (
+            (own_ref, own_out_ref, half),
+            (other_ref, other_out_ref, 1 - half),
+        ):
+            starts = [pl.multiple_of(part * HALF + start, LANES) for part in range(3)]
+            query, key, value = (block_of(ref, place, kind) for place in starts)
+            up = block_of(up_ref, pl.multiple_of(which * HALF + start, LANES), kind)
+            zero = jnp.zeros_like(query)
+            grads = []
+            for mine in (first, ~first):
+                probs = softmax_rows(jnp.where(mine, query, zero), key, allowed)
+                inner = dot_nt(jnp.where(mine, up, zero), value)
+                total = jnp.sum(probs * inner, axis=-1, keepdims=True)
+                scores = (probs * (inner - total) * HEAD ** (-0.5)).astype(LOW)
+                grads.append(
+                    (dot_nn(scores, key), dot_tn(scores, query), dot_tn(probs.astype(LOW), up))
+                )
+            for place, one, two in zip(starts, *grads):
+                store_to(out_ref, place, kind, jnp.where(first, one, two).astype(LOW))
         return 0
 
-    lax.fori_loop(0, D // LANES, turn, 0, unroll=2)
-
-
-def attention(kind, scalar, packed, up=None):
-    shape = packed.shape[:-1]
+    lax.fori_loop(0, HALF // LANES, turn, 0)
+
+
+def attention(kind, scalars, packed, up=None):
+    shape = packed[0].shape[:-1]
     if kind == "space":
         grid, block, where = (shape[0] // GROUP,), (GROUP,), lambda g, s: (g, 0)
     else:
-        grid, block, where = (FRAMES * shape[1] // GROUP,), (FRAMES, GROUP // FRAMES), lambda g, s: (0, g, 0)
-    wide = pl.BlockSpec(block + (3 * D,), where)
-    narrow = pl.BlockSpec(block + (D,), where)
-    body, last, ins = forward_body, D, (packed,)
-    if up is not None:
-        body, last, ins = backward_body, 3 * D, (packed, up.reshape(shape + (D,)))
+        grid, block, where = (
+            (FRAMES * shape[1] // GROUP,),
+            (FRAMES, GROUP // FRAMES),
+            lambda g, s: (0, g, 0),
+        )
+    third = pl.BlockSpec(block + (3 * HALF,), where)
+    whole = pl.BlockSpec(block + (D,), where)
+    if up is None:
+        body, ins, flops = forward_body, (*packed,), 9e9
+        outs, shapes = whole, jax.ShapeDtypeStruct(shape + (D,), LOW)
+    else:
+        body, ins, flops = backward_body, (*packed, up.reshape(shape + (D,))), 22e9
+        outs = (third, third)
+        shapes = (jax.ShapeDtypeStruct(shape + (3 * HALF,), LOW),) * 2
     return pl.pallas_call(
         functools.partial(body, kind),
-        out_shape=jax.ShapeDtypeStruct(shape + (last,), LOW),
+        out_shape=shapes,
         grid_spec=pltpu.PrefetchScalarGridSpec(
             num_scalar_prefetch=1,
             grid=grid,
-            in_specs=[wide, narrow][: len(ins)],
-            out_specs=narrow if up is None else wide,
+            in_specs=[third, third, whole][: len(ins)],
+            out_specs=outs,
         ),
-    )(scalar.reshape(1).astype(jnp.int32), *ins)
+        cost_estimate=pl.CostEstimate(
+            flops=int(flops), transcendentals=4 * HEADS * GROUP * GROUP, bytes_accessed=8 << 20
+        ),
+    )(jnp.stack(scalars).astype(jnp.int32), *ins)
 
 
 def adamw(weight, grad, first, second, rate, decay):
@@ -425,17 +491,20 @@
     doms = of_micro(domains)
 
     turned = jnp.pad(gains.T, ((0, 0), (0, LANES - kinds)))
-    layer_one = jnp.concatenate([attend_in[0], attend_out[0], turned], axis=1).astype(LOW)
-    layer_two = jnp.concatenate([attend_in[1], attend_out[1]], axis=1).astype(LOW)
-    layer_one = lax.all_gather(layer_one, ALL, axis=0, tiled=True)
-    layer_two = lax.all_gather(layer_two, ALL, axis=0, tiled=True)
     low_in, low_out = tables.astype(LOW)
-    table_in = gather_axis(gather_axis(low_in, "m", 0), "h", 1).reshape(-1, D)
+    one_job = Job(gather_layer(attend_in[0], attend_out[0], turned))
+    down_job = Job(gather_half(contract.astype(LOW)))
     up_job = Job(gather_columns(expand.astype(LOW), block))
-    down_job = Job(gather_half(contract.astype(LOW)))
-    table_in = advance(table_in, up_job)
-    table_out = gather_axis(gather_axis(low_out, "m", 0), "h", 1).reshape(-1, D)
-
+    in_table_job = Job(gather_table(low_in))
+    token = advance(jnp.zeros((), WIDE), one_job, down_job, up_job)
+    two_job = Job(gather_layer(attend_in[1], attend_out[1]))
+    token = advance(token, one_job, down_job, up_job, two_job)
+    token = advance(token, one_job, in_table_job, up_job)
+    token = advance(token, one_job, in_table_job, two_job, down_job, up_job)
+    out_table_job = Job(gather_table(low_out))
+    token = advance(token, one_job, two_job, down_job, up_job)
+    token = advance(token, one_job)
+    layer_one, table_in = one_job.result, in_table_job.result
     code_ids = jnp.arange(table_in.shape[0])
 
     def own_frames(array):
@@ -443,11 +512,17 @@
 
     space_codes = own_frames(codes).reshape(-1)
     picked = dot_nn((space_codes[:, None] == code_ids[None, :]).astype(LOW), table_in)
-    picked = advance(picked, up_job, down_job)
-    layer_one = advance(layer_one, up_job, down_job)
-    w_in = (layer_one[:, : 3 * D], layer_two[:, : 3 * D])
-    w_out = (layer_one[:, 3 * D : 4 * D], layer_two[:, 3 * D :])
-    gain_all = layer_one[:, 4 * D :].T[:kinds].astype(WIDE)
+    gain_all = layer_one[0][:, 4 * HALF :].T[:kinds].astype(WIDE)
+
+    def layer_weights(layer):
+        return [part[:, : 3 * HALF] for part in layer], [
+            part[:, 3 * HALF : 4 * HALF] for part in layer
+        ]
+
+    def project_out(mixed, w_out):
+        return in_order(*(dot_nn(mixed, part) for part in w_out), 1)
+
+    w_in, w_out = layer_weights(layer_one)
 
     slot_ids = jnp.arange(SLOTS)
     segment = jnp.where(small > 0, slot_ids // SMALL_TOKENS, 0)
@@ -468,17 +543,23 @@
 
     start = jnp.where(space_mask[:, None] > 0, gain_all[4], picked)
     normed_space = norm_forward(start, gain_all[0]).astype(LOW)
-    packed_space = dot_nn(normed_space, w_in[0]).astype(LOW)
-    mixed_space = attention("space", small, packed_space)
-    after_space = start + dot_nn(mixed_space, w_out[0])
+    packed_space = [dot_nn(normed_space, part).astype(LOW) for part in w_in]
+    mixed_space = attention("space", (small, half), packed_space)
+    mixed_space = advance(mixed_space, two_job)
+    after_space = start + project_out(mixed_space, w_out)
     after_space = swap_slots(after_space.reshape(frames, SLOTS, D)).reshape(-1, D)
+    after_space = advance(after_space, two_job, out_table_job)
     normed_time = norm_forward(after_space, gain_all[1]).astype(LOW)
-    normed_time = advance(normed_time, up_job, down_job)
-    packed_time = dot_nn(normed_time, w_in[1]).astype(LOW).reshape(FRAMES, -1, 3 * D)
-    mixed_time = attention("time", half, packed_time).reshape(-1, D)
-    after_time = after_space + dot_nn(mixed_time, w_out[1])
+    normed_time = advance(normed_time, two_job, down_job, up_job, out_table_job)
+    next_in, next_out = layer_weights(two_job.finish())
+    packed_time = [
+        dot_nn(normed_time, part).astype(LOW).reshape(FRAMES, -1, 3 * HALF) for part in next_in
+    ]
+    mixed_time = attention("time", (half, half), packed_time).reshape(-1, D)
+    after_time = after_space + project_out(mixed_time, next_out)
     normed_ffn = norm_forward(after_time, gain_all[2]).astype(LOW)
     ups, downs = up_job.finish(), down_job.finish()
+    table_out = out_table_job.finish()
     pres = [dot_nn(normed_ffn, up) for up in ups]
     activs = [gelu(pre).astype(LOW) for pre in pres]
     after_ffn = after_time + dot_nn(activs[0], downs[0]) + dot_nn(activs[1], downs[1])
@@ -509,33 +590,37 @@
     grad_pres = [gelu_backward(pre, grad).astype(LOW) for pre, grad in zip(pres, grad_activs)]
     grad_pres = advance(grad_pres, head_job, contract_job)
     expand_job = product(
-        reduce_layer, normed_ffn, grad_pres[0], grad_pres[1], ("r", "m", "z"), block
+        reduce_layer, normed_ffn, grad_pres[0], grad_pres[1], ("m", "r", "z"), block
     )
     grad_normed = dot_nt(grad_pres[0], ups[0]) + dot_nt(grad_pres[1], ups[1])
     inward, gain_two = norm_backward(after_time, gain_all[2], grad_normed)
     grad_time = grad_ffn + inward
     up_low = grad_time.astype(LOW)
     up_low = advance(up_low, head_job, expand_job)
-    out_job = product(reduce_layer, mixed_time, *halves(up_low, 1), ("m", "r", "z"))
-    grad_mixed = dot_nt(up_low, w_out[1]).astype(LOW)
-    grad_packed = attention("time", half, packed_time, grad_mixed).reshape(-1, 3 * D)
+    mine, other = halves(up_low, 1)
+    out_job = product(reduce_layer, mixed_time, mine, other, ("r", "m", "z"))
+    grad_mixed = (dot_nt(mine, next_out[0]) + dot_nt(other, next_out[1])).astype(LOW)
+    grad_packed = attention("time", (half, half), packed_time, grad_mixed)
+    grad_packed = [part.reshape(-1, 3 * HALF) for part in grad_packed]
     grad_packed = advance(grad_packed, head_job, contract_job, out_job)
-    in_job = product(reduce_layer, normed_time, *halves(grad_packed, 1), ("m", "r", "z"))
-    grad_normed = dot_nt(grad_packed, w_in[1])
+    in_job = product(reduce_layer, normed_time, *grad_packed, ("r", "m", "z"), HALF)
+    grad_normed = dot_nt(grad_packed[0], next_in[0]) + dot_nt(grad_packed[1], next_in[1])
     inward, gain_one = norm_backward(after_space, gain_all[1], grad_normed)
     grad_space = swap_frames((grad_time + inward).reshape(FRAMES, -1, D)).reshape(-1, D)
     up_low = grad_space.astype(LOW)
     up_low = advance(up_low, head_job, out_job, in_job)
-    first_out_job = product(reduce_layer, mixed_space, *halves(up_low, 1), ("r", "m", "z"))
-    grad_mixed = dot_nt(up_low, w_out[0]).astype(LOW)
-    grad_packed = attention("space", small, packed_space, grad_mixed)
+    mine, other = halves(up_low, 1)
+    first_out_job = product(reduce_layer, mixed_space, mine, other, ("r", "m", "z"))
+    grad_mixed = (dot_nt(mine, w_out[0]) + dot_nt(other, w_out[1])).astype(LOW)
+    grad_mixed = advance(grad_mixed, contract_job)
+    grad_packed = attention("space", (small, half), packed_space, grad_mixed)
     grad_packed = advance(
         grad_packed, head_job, contract_job, expand_job, out_job, in_job, first_out_job
     )
     first_in_job = product(
-        reduce_layer, normed_space, *halves(grad_packed, 1), ("r", "m", "z"), None, 2
-    )
-    grad_normed = dot_nt(grad_packed, w_in[0])
+        reduce_layer, normed_space, *grad_packed, ("r", "m", "z"), HALF, 2
+    )
+    grad_normed = dot_nt(grad_packed[0], w_in[0]) + dot_nt(grad_packed[1], w_in[1])
     grad_normed = advance(grad_normed, first_in_job, head_job, out_job)
     inward, gain_zero = norm_backward(start, gain_all[0], grad_normed)
     grad_start = grad_space + inward

time: 794 us -> 815 us (1.026)
  waiting for transfers between devices: 294 us -> 250 us
  local copies, waits for them, and re-layouts: 63.3 us -> 102 us
  starting transfers between devices: 116 us -> 141 us
  between operations: 24.7 us -> 12 us
  Pallas kernels: 63.1 us -> 73.1 us
    ppermute x104 -> x126, waiting for transfers between devices: 288 us -> 250 us  [shifted(): return lax.ppermute(part, axis, [((i + shift) % n, i) for i in range(n)])]
    ppermute x104 -> x126, starting transfers between devices: 116 us -> 141 us  [shifted(): return lax.ppermute(part, axis, [((i + shift) % n, i) for i in range(n)])]
    dynamic_update_slice x0 -> x16, local copies, waits for them, and re-layouts: none -> 13.8 us  [the longest x4 5.72 us: gather_deep(): whole = lax.dynamic_update_index_in_dim(whole, above, (mine + 1) % 4, 0)]
    unnamed x218 -> x312, local copies, waits for them, and re-layouts: 11.1 us -> 21.5 us
    pallas_call x4, Pallas kernels: 63.1 us -> 73.1 us  [attention(): pl.pallas_call(functools.partial(body, kind), out_shape=shapes, grid_spec...]
    dot_general x10 -> x14, matrix products: 46.6 us -> 55.2 us  [dot_nn(): return jnp.dot(left, right, preferred_element_type=WIDE)]
    dot_general x9 -> x13, matrix products: 51.4 us -> 54.2 us  [dot_nt(): lax.dot_general(left, right, (((1,), (1,)), ((), ())), preferred_element_...]
  transfers between devices with their start and end apart: 106 -> 126, of which waited for: 33 -> 40; matrix products, arithmetic and copies ran while one was open for 30% -> 30% of each run, Pallas kernels for 8% -> 7%
where the time goes in v4:
time: 815 us; the launch traced here: 804 us
  waiting for transfers between devices  250 us (31%)
  matrix products  152 us (19%)
  starting transfers between devices  141 us (17%)
  local copies, waits for them, and re-layouts  102 us (13%)
  other arithmetic  73.7 us (9%)
  Pallas kernels  73.1 us (9%)
  between operations  12 us (1%)
    ppermute x126, waiting for transfers between devices, shifted(): return lax.ppermute(part, axis, [((i + shift) % n, i) for i in range(n)])  250 us
    ppermute x126, starting transfers between devices, shifted(): return lax.ppermute(part, axis, [((i + shift) % n, i) for i in range(n)])  141 us
    pallas_call x4, Pallas kernels, attention(): pl.pallas_call(functools.partial(body, kind), out_shape=shapes, grid_spec...  73.1 us
    dot_general x14, matrix products, dot_nn(): return jnp.dot(left, right, preferred_element_type=WIDE)  55.2 us
    dot_general x13, matrix products, dot_nt(): lax.dot_general(left, right, (((1,), (1,)), ((), ())), preferred_element_...  54.2 us
    dot_general x16, matrix products, dot_tn(): lax.dot_general(left, right, (((0,), (0,)), ((), ())), preferred_element_...  42.6 us
    unnamed x312, local copies, waits for them, and re-layouts  21.5 us
  transfers between devices with their start and end apart: 126, of which 40 were waited for; matrix products, arithmetic and copies ran while one was open for 30% of the time, Pallas kernels for 7%

profile of v4, /device:TPU:0, one launch (start us, length us, event | category | flops | bytes accessed | tf_op | source)
XLA Modules:
  0.0 803.7 jit_solution(14049105767010760482)
XLA Ops:
  1.8 5.1 collective-permute-start.1
  23.1 3.9 collective-permute-start.8
  33.0 3.9 collective-permute-start.6
  37.8 4.9 collective-permute-done.6
  52.0 5.5 collective-permute-done.13
  64.1 3.8 collective-permute-start.16
  69.4 7.4 collective-permute-done.21
  80.3 9.8 %collective-permute-done.23 = bf16[4,64,1024]{2,1,0:T(8,128)(2,1)} collective-permute-done((bf16[4,64,1024]{2,1,0:T(8,128)(2,1)}, bf16[4,64,1024]{2,1,0:T(8,128)(2,1)}, u32[]{:S(2)}, u32[]{:S(2)}) %collective-permute-start.23) | collective-permute-done | bytes 524320 | tf_op jit(solution)/shard_map/ppermute | solution.py:41
  92.9 20.2 %collective-permute-done.17 = bf16[2,2,64,2176]{3,2,1,0:T(8,128)(2,1)S(1)} collective-permute-done((bf16[2,2,64,2176]{3,2,1,0:T(8,128)(2,1)S(1)}, bf16[2,2,64,2176]{3,2,1,0:T(8,128)(2,1)S(1)}, u32[]{:S(2)}, u32[]{:S(2)}) %collective-permute-start.17) | collective-permute-done | bytes 1114144 | tf_op jit(solution)/shard_map/ppermute | solution.py:41
  114.1 3.7 collective-permute-start.25
  140.2 14.0 %collective-permute-done.26 = bf16[2,2,64,1152]{3,2,1,0:T(8,128)(2,1)S(1)} collective-permute-done((bf16[2,2,64,1152]{3,2,1,0:T(8,128)(2,1)S(1)}, bf16[2,2,64,1152]{3,2,1,0:T(8,128)(2,1)S(1)}, u32[]{:S(2)}, u32[]{:S(2)}) %collective-permute-start.26) | collective-permute-done | bytes 589856 | tf_op jit(solution)/shard_map/ppermute | solution.py:41
  154.8 17.8 %collective-permute-done.31 = bf16[4,2,64,1024]{3,2,1,0:T(8,128)(2,1)S(1)} collective-permute-done((bf16[4,2,64,1024]{3,2,1,0:T(8,128)(2,1)S(1)}, bf16[4,2,64,1024]{3,2,1,0:T(8,128)(2,1)S(1)}, u32[]{:S(2)}, u32[]{:S(2)}) %collective-permute-start.31) | collective-permute-done | bytes 1048608 | tf_op jit(solution)/shard_map/ppermute | solution.py:41
  172.6 3.8 collective-permute-done.32
  198.7 5.6 convolution_convert_fusion.7.own_ref
  204.4 4.9 convolution_convert_fusion.6.other_ref
  209.3 9.7 %shard_map.365 = bf16[512,1024]{1,0:T(8,128)(2,1)} custom-call(s32[2]{0:T(128)} %pad_add_fusion.scalar_ref, bf16[512,1536]{1,0:T(8,128)(2,1)} %convolution_convert_fusion.7.own_ref, bf16[512,1536]{1,0:T(8,128)(2,1)} %convolution_convert_fusion.6.other_ref), custom_call_target="tpu_custom_call" | custom-call | flops 8999999488 | bytes 8388608 | tf_op jit(solution)/shard_map/pallas_call | solution.py:405
  219.0 12.9 %collective-permute-done.34 = bf16[2,2,64,2048]{3,2,1,0:T(8,128)(2,1)} collective-permute-done((bf16[2,2,64,2048]{3,2,1,0:T(8,128)(2,1)S(1)}, bf16[2,2,64,2048]{3,2,1,0:T(8,128)(2,1)}, u32[]{:S(2)}, u32[]{:S(2)}) %collective-permute-start.34) | collective-permute-done | bytes 1048608 | tf_op jit(solution)/shard_map/ppermute | solution.py:41
  252.9 2.9 collective-permute-done.37
  255.7 12.3 %collective-permute-done.38 = bf16[2,2,64,1024]{3,2,1,0:T(8,128)(2,1)S(1)} collective-permute-done((bf16[2,2,64,1024]{3,2,1,0:T(8,128)(2,1)S(1)}, bf16[2,2,64,1024]{3,2,1,0:T(8,128)(2,1)S(1)}, u32[]{:S(2)}, u32[]{:S(2)}) %collective-permute-start.38) | collective-permute-done | bytes 524320 | tf_op jit(solution)/shard_map/ppermute | solution.py:41
  280.2 2.9 collective-permute-done.47
  289.3 4.8 convolution_convert_fusion.5
  294.1 4.9 convolution_convert_fusion.4
  299.0 18.3 %shard_map.366 = bf16[4,128,1024]{2,1,0:T(8,128)(2,1)} custom-call(s32[2]{0:T(128)} %pad_add_fusion.1.scalar_ref, bf16[4,128,1536]{2,1,0:T(8,128)(2,1)} %bitcast.621, bf16[4,128,1536]{2,1,0:T(8,128)(2,1)} %bitcast.623), custom_call_target="tpu_custom_call" | custom-call | flops 8999999488 | bytes 8388608 | tf_op jit(solution)/shard_map/pallas_call | solution.py:405
  322.2 5.4 fusion.170
  327.6 6.0 fusion.171
  333.6 6.4 fusion.142
  340.0 5.2 multiply_reduce_fusion.9
  355.2 4.9 convolution_convert_fusion.3
  362.6 7.7 fusion.6
  370.3 8.2 %fusion.13 = bf16[512,2048]{1,0:T(8,128)(2,1)S(1)} fusion(f32[512,2048]{1,0:T(8,128)S(1)} %copy-done.142, bf16[512,1024]{1,0:T(8,128)(2,1)S(1)} %copy-done.57, bf16[2048,1024]{1,0:T(8,128)(2,1)} %collective-permute-done.41), kind=kOutput, calls=%fused_computation.21 | convolution fusion | flops 2168455168 | bytes 11534336 | tf_op jit(solution)/shard_map/dot_general | solution.py:289
  378.6 4.3 convolution_convert_fusion.2
  383.0 6.2 fusion.141
  392.8 6.2 add_convert_fusion.1
  403.3 4.6 fusion.172
  407.9 5.3 multiply_reduce_fusion.2
  417.5 3.0 add_convert_fusion.8
  420.5 22.6 %shard_map.367 = (bf16[4,128,1536]{2,1,0:T(8,128)(2,1)}, bf16[4,128,1536]{2,1,0:T(8,128)(2,1)}) custom-call(s32[2]{0:T(128)} %pad_add_fusion.1.scalar_ref, bf16[4,128,1536]{2,1,0:T(8,128)(2,1)} %bitcast.622, bf16[4,128,1536]{2,1,0:T(8,128)(2,1)} %bitcast.624, bf16[4,128,1024]{2,1,0:T(8,128)(2,1)} %bitcast.565), custom_call_target="tpu_custom_call" | custom-call | flops 22000001024 | bytes 8388608 | tf_op jit(solution)/shard_map/pallas_call | solution.py:405
  446.3 4.6 add_convert_fusion
  454.3 3.8 fusion.26
  460.2 4.8 multiply_reduce_fusion.3
  477.7 6.4 collective-permute-done.59
  490.9 3.0 add_convert_fusion.6.up_ref
  493.8 11.3 %collective-permute-done.61 = bf16[4,128,1024]{2,1,0:T(8,128)(2,1)S(1)} collective-permute-done((bf16[4,128,1024]{2,1,0:T(8,128)(2,1)S(1)}, bf16[4,128,1024]{2,1,0:T(8,128)(2,1)S(1)}, u32[]{:S(2)}, u32[]{:S(2)}) %collective-permute-start.61) | collective-permute-done | bytes 1048608 | tf_op jit(solution)/shard_map/ppermute | solution.py:41
  516.2 6.8 collective-permute-done.68
  528.7 22.5 %shard_map.368 = (bf16[512,1536]{1,0:T(8,128)(2,1)}, bf16[512,1536]{1,0:T(8,128)(2,1)}) custom-call(s32[2]{0:T(128)} %pad_add_fusion.scalar_ref, bf16[512,1536]{1,0:T(8,128)(2,1)} %convolution_convert_fusion.7.own_ref, bf16[512,1536]{1,0:T(8,128)(2,1)} %convolution_convert_fusion.6.other_ref, bf16[512,1024]{1,0:T(8,128)(2,1)} %add_convert_fusion.6.up_ref), custom_call_target="tpu_custom_call" | custom-call | flops 22000001024 | bytes 8388608 | tf_op jit(solution)/shard_map/pallas_call | solution.py:405
  551.2 10.0 %collective-permute-done.70 = bf16[4,2,64,1536]{3,2,1,0:T(8,128)(2,1)} collective-permute-done((bf16[4,2,64,1536]{3,2,1,0:T(8,128)(2,1)}, bf16[4,2,64,1536]{3,2,1,0:T(8,128)(2,1)}, u32[]{:S(2)}, u32[]{:S(2)}) %collective-permute-start.70) | collective-permute-done | bytes 1572896 | tf_op jit(solution)/shard_map/ppermute | solution.py:41
  561.3 3.7 convolution_convert_fusion
  574.5 3.0 multiply_reduce_fusion.13
  579.7 4.1 fusion.20
  585.8 4.3 fusion.38
  605.0 28.0 %collective-permute-done.98 = bf16[4,2,64,768]{3,2,0,1:T(8,128)(2,1)} collective-permute-done((bf16[4,2,64,768]{3,2,0,1:T(8,128)(2,1)}, bf16[4,2,64,768]{3,2,0,1:T(8,128)(2,1)}, u32[]{:S(2)}, u32[]{:S(2)}) %collective-permute-start.98) | collective-permute-done | bytes 786464 | tf_op jit(solution)/shard_map/ppermute | solution.py:41
  637.3 8.3 %collective-permute-done.83 = bf16[4,2,64,512]{3,2,1,0:T(8,128)(2,1)S(1)} collective-permute-done((bf16[4,2,64,512]{3,2,1,0:T(8,128)(2,1)S(1)}, bf16[4,2,64,512]{3,2,1,0:T(8,128)(2,1)S(1)}, u32[]{:S(2)}, u32[]{:S(2)}) %collective-permute-start.83) | collective-permute-done | bytes 524320 | tf_op jit(solution)/shard_map/ppermute | solution.py:41
  660.1 10.0 %collective-permute-done.85 = f32[5,1024]{1,0:T(8,128)S(1)} collective-permute-done((f32[5,1024]{1,0:T(8,128)S(1)}, f32[5,1024]{1,0:T(8,128)S(1)}, u32[]{:S(2)}, u32[]{:S(2)}) %collective-permute-start.85) | collective-permute-done | bytes 20512 | tf_op jit(solution)/shard_map/ppermute | solution.py:41
  670.7 4.1 collective-permute-done.86
  676.6 7.8 collective-permute-done.92
  686.0 10.7 %collective-permute-done.93 = bf16[64,1536]{1,0:T(8,128)(2,1)S(1)} collective-permute-done((bf16[64,1536]{1,0:T(8,128)(2,1)S(1)}, bf16[64,1536]{1,0:T(8,128)(2,1)S(1)}, u32[]{:S(2)}, u32[]{:S(2)}) %collective-permute-start.93) | collective-permute-done | bytes 196640 | tf_op jit(solution)/shard_map/ppermute | solution.py:41
  709.3 7.3 collective-permute-start.103
  728.1 3.4 collective-permute-start.106
  736.4 3.6 collective-permute-start.121
  753.7 3.0 collective-permute-done.112
  764.8 2.9 collective-permute-start.115
  770.7 3.9 collective-permute-done.116
  795.0 3.4 multiply_subtract_fusion.2
  798.6 3.6 multiply_subtract_fusion
  (828 shorter events, 324.5 us)
Async XLA Ops:
  1.8 19.3 %collective-permute-start.1 = (bf16[128,1024]{1,0:T(8,128)(2,1)S(1)}, bf16[128,1024]{1,0:T(8,128)(2,1)}, u32[]{:S(2)}, u32[]{:S(2)}) collective-permute-start(bf16[128,1024]{1,0:T(8,128)(2,1)S(1)} %convert_element_type.527), channel_id=1, source_target_pairs={{8,0},{16,8},{24,16},{0,24},{9,1},{17,9},{25,17},{1,25},{10,2},{18... | collective-permute-start | bytes 786440 | tf_op jit(solution)/shard_map/ppermute | solution.py:41
  23.1 22.2 %collective-permute-start.8 = (bf16[64,2048]{1,0:T(8,128)(2,1)S(1)}, bf16[64,2048]{1,0:T(8,128)(2,1)S(1)}, u32[]{:S(2)}, u32[]{:S(2)}) collective-permute-start(bf16[64,2048]{1,0:T(8,128)(2,1)S(1)} %bitcast.566), channel_id=1, source_target_pairs={{8,0},{16,8},{24,16},{0,24},{9,1},{17,9},{25,17},{1,25},{10,2},{18... | collective-permute-start | bytes 786440 | tf_op jit(solution)/shard_map/ppermute | solution.py:41
  27.0 18.3 %collective-permute-start.9 = (bf16[64,2048]{1,0:T(8,128)(2,1)S(1)}, bf16[64,2048]{1,0:T(8,128)(2,1)S(1)}, u32[]{:S(2)}, u32[]{:S(2)}) collective-permute-start(bf16[64,2048]{1,0:T(8,128)(2,1)S(1)} %bitcast.567), channel_id=1, source_target_pairs={{24,0},{0,8},{8,16},{16,24},{25,1},{1,9},{9,17},{17,25},{26,2},{2,... | collective-permute-start | bytes 786440 | tf_op jit(solution)/shard_map/ppermute | solution.py:41
  28.5 16.8 %collective-permute-start.5 = (bf16[64,1152]{1,0:T(8,128)(2,1)S(1)}, bf16[64,1152]{1,0:T(8,128)(2,1)S(1)}, u32[]{:S(2)}, u32[]{:S(2)}) collective-permute-start(bf16[64,1152]{1,0:T(8,128)(2,1)S(1)} %slice.155), channel_id=1, source_target_pairs={{4,0},{0,4},{5,1},{1,5},{6,2},{2,6},{7,3},{3,7},{12,8},{8,12},{13,... | collective-permute-start | bytes 442376 | tf_op jit(solution)/shard_map/ppermute | solution.py:41
  47.0 16.8 %collective-permute-start.12 = (bf16[2,64,1152]{2,1,0:T(8,128)(2,1)S(1)}, bf16[2,64,1152]{2,1,0:T(8,128)(2,1)S(1)}, u32[]{:S(2)}, u32[]{:S(2)}) collective-permute-start(bf16[2,64,1152]{2,1,0:T(8,128)(2,1)S(1)} %bitcast_dynamic-update-slice_fusion.30), channel_id=1, source_target_pairs={{2,0},{0,2},{3,1},{1,3},{6,4},{4,6},{7,5},{5,7},{10,8},{8,10},{11,... | collective-permute-start | bytes 884744 | tf_op jit(solution)/shard_map/ppermute | solution.py:41
  60.0 16.8 %collective-permute-start.21 = (bf16[4,128,512]{2,1,0:T(8,128)(2,1)S(1)}, bf16[4,128,512]{2,1,0:T(8,128)(2,1)S(1)}, u32[]{:S(2)}, u32[]{:S(2)}) collective-permute-start(bf16[4,128,512]{2,1,0:T(8,128)(2,1)S(1)} %get-tuple-element.350), channel_id=1, source_target_pairs={{2,0},{0,2},{3,1},{1,3},{6,4},{4,6},{7,5},{5,7},{10,8},{8,10},{11,... | collective-permute-start | bytes 1572872 | tf_op jit(solution)/shard_map/ppermute | solution.py:41
  61.0 17.2 %collective-permute-start.22 = (bf16[4,128,512]{2,1,0:T(8,128)(2,1)S(1)}, bf16[4,128,512]{2,1,0:T(8,128)(2,1)S(1)}, u32[]{:S(2)}, u32[]{:S(2)}) collective-permute-start(bf16[4,128,512]{2,1,0:T(8,128)(2,1)S(1)} %get-tuple-element.349), channel_id=1, source_target_pairs={{4,0},{0,4},{5,1},{1,5},{6,2},{2,6},{7,3},{3,7},{12,8},{8,12},{13,... | collective-permute-start | bytes 1572872 | tf_op jit(solution)/shard_map/ppermute | solution.py:41
  64.1 28.8 %collective-permute-start.16 = (bf16[2,2,64,2176]{3,2,1,0:T(8,128)(2,1)S(1)}, bf16[2,2,64,2176]{3,2,1,0:T(8,128)(2,1)}, u32[]{:S(2)}, u32[]{:S(2)}) collective-permute-start(bf16[2,2,64,2176]{3,2,1,0:T(8,128)(2,1)S(1)} %pad_maximum_fusion.3), channel_id=1, source_target_pairs={{8,0},{16,8},{24,16},{0,24},{9,1},{17,9},{25,17},{1,25},{10,2},{18... | collective-permute-start | bytes 3342344 | tf_op jit(solution)/shard_map/ppermute | solution.py:41
  68.1 44.9 %collective-permute-start.17 = (bf16[2,2,64,2176]{3,2,1,0:T(8,128)(2,1)S(1)}, bf16[2,2,64,2176]{3,2,1,0:T(8,128)(2,1)S(1)}, u32[]{:S(2)}, u32[]{:S(2)}) collective-permute-start(bf16[2,2,64,2176]{3,2,1,0:T(8,128)(2,1)S(1)} %pad_maximum_fusion.3), channel_id=1, source_target_pairs={{24,0},{0,8},{8,16},{16,24},{25,1},{1,9},{9,17},{17,25},{26,2},{2,... | collective-permute-start | bytes 3342344 | tf_op jit(solution)/shard_map/ppermute | solution.py:41
  68.2 23.9 %collective-permute-start.18 = (bf16[2,256,1024]{2,1,0:T(8,128)(2,1)S(1)}, bf16[2,256,1024]{2,1,0:T(8,128)(2,1)}, u32[]{:S(2)}, u32[]{:S(2)}) collective-permute-start(bf16[2,256,1024]{2,1,0:T(8,128)(2,1)S(1)} %bitcast_dynamic-update-slice_fusion.19), channel_id=1, source_target_pairs={{1,0},{0,1},{3,2},{2,3},{5,4},{4,5},{7,6},{6,7},{9,8},{8,9},{11,10... | collective-permute-start | bytes 3145736 | tf_op jit(solution)/shard_map/ppermute | solution.py:41
  114.1 24.9 %collective-permute-start.25 = (bf16[2,2,64,1024]{3,2,1,0:T(8,128)(2,1)S(1)}, bf16[2,2,64,1024]{3,2,1,0:T(8,128)(2,1)S(1)}, u32[]{:S(2)}, u32[]{:S(2)}) collective-permute-start(bf16[2,2,64,1024]{3,2,1,0:T(8,128)(2,1)S(1)} %slice.133), channel_id=1, source_target_pairs={{8,0},{16,8},{24,16},{0,24},{9,1},{17,9},{25,17},{1,25},{10,2},{18... | collective-permute-start | bytes 1572872 | tf_op jit(solution)/shard_map/ppermute | solution.py:41
  124.0 30.8 %collective-permute-start.29 = (bf16[4,2,128,512]{3,2,1,0:T(8,128)(2,1)S(1)}, bf16[4,2,128,512]{3,2,1,0:T(8,128)(2,1)S(1)}, u32[]{:S(2)}, u32[]{:S(2)}) collective-permute-start(bf16[4,2,128,512]{3,2,1,0:T(8,128)(2,1)S(1)} %bitcast_dynamic-update-slice_fusion.12), channel_id=1, source_target_pairs={{4,0},{0,4},{5,1},{1,5},{6,2},{2,6},{7,3},{3,7},{12,8},{8,12},{13,... | collective-permute-start | bytes 3145736 | tf_op jit(solution)/shard_map/ppermute | solution.py:41
  124.8 30.1 %collective-permute-start.30 = (bf16[4,2,128,512]{3,2,1,0:T(8,128)(2,1)S(1)}, bf16[4,2,128,512]{3,2,1,0:T(8,128)(2,1)S(1)}, u32[]{:S(2)}, u32[]{:S(2)}) collective-permute-start(bf16[4,2,128,512]{3,2,1,0:T(8,128)(2,1)S(1)} %bitcast_dynamic-update-slice_fusion.18), channel_id=1, source_target_pairs={{2,0},{0,2},{3,1},{1,3},{6,4},{4,6},{7,5},{5,7},{10,8},{8,10},{11,... | collective-permute-start | bytes 3145736 | tf_op jit(solution)/shard_map/ppermute | solution.py:41
  130.3 42.4 %collective-permute-start.31 = (bf16[4,2,64,1024]{3,2,1,0:T(8,128)(2,1)S(1)}, bf16[4,2,64,1024]{3,2,1,0:T(8,128)(2,1)S(1)}, u32[]{:S(2)}, u32[]{:S(2)}) collective-permute-start(bf16[4,2,64,1024]{3,2,1,0:T(8,128)(2,1)S(1)} %bitcast_dynamic-update-slice_fusion.11), channel_id=1, source_target_pairs={{4,0},{0,4},{5,1},{1,5},{6,2},{2,6},{7,3},{3,7},{12,8},{8,12},{13,... | collective-permute-start | bytes 3145736 | tf_op jit(solution)/shard_map/ppermute | solution.py:41
  132.5 43.9 %collective-permute-start.32 = (bf16[4,2,64,1024]{3,2,1,0:T(8,128)(2,1)S(1)}, bf16[4,2,64,1024]{3,2,1,0:T(8,128)(2,1)S(1)}, u32[]{:S(2)}, u32[]{:S(2)}) collective-permute-start(bf16[4,2,64,1024]{3,2,1,0:T(8,128)(2,1)S(1)} %bitcast_dynamic-update-slice_fusion.17), channel_id=1, source_target_pairs={{2,0},{0,2},{3,1},{1,3},{6,4},{4,6},{7,5},{5,7},{10,8},{8,10},{11,... | collective-permute-start | bytes 3145736 | tf_op jit(solution)/shard_map/ppermute | solution.py:41
  154.2 98.6 %collective-permute-start.39 = (bf16[256,1024]{1,0:T(8,128)(2,1)}, bf16[256,1024]{1,0:T(8,128)(2,1)}, u32[]{:S(2)}, u32[]{:S(2)}) collective-permute-start(bf16[256,1024]{1,0:T(8,128)(2,1)} %get-tuple-element.345), channel_id=1, source_target_pairs={{2,0},{0,2},{3,1},{1,3},{6,4},{4,6},{7,5},{5,7},{10,8},{8,10},{11,... | collective-permute-start | bytes 1572872 | tf_op jit(solution)/shard_map/ppermute | solution.py:41
  178.2 26.1 %collective-permute-start.33 = (bf16[1024,2176]{1,0:T(8,128)(2,1)}, bf16[1024,2176]{1,0:T(8,128)(2,1)}, u32[]{:S(2)}, u32[]{:S(2)}) collective-permute-start(bf16[1024,2176]{1,0:T(8,128)(2,1)} %bitcast.33), channel_id=1, source_target_pairs={{1,0},{0,1},{3,2},{2,3},{5,4},{4,5},{7,6},{6,7},{9,8},{8,9},{11,10... | collective-permute-start | bytes 13369352 | tf_op jit(solution)/shard_map/ppermute | solution.py:41
  183.7 48.2 %collective-permute-start.34 = (bf16[2,2,64,2048]{3,2,1,0:T(8,128)(2,1)S(1)}, bf16[2,2,64,2048]{3,2,1,0:T(8,128)(2,1)}, u32[]{:S(2)}, u32[]{:S(2)}) collective-permute-start(bf16[2,2,64,2048]{3,2,1,0:T(8,128)(2,1)S(1)} %pad_maximum_fusion.4), channel_id=1, source_target_pairs={{8,0},{16,8},{24,16},{0,24},{9,1},{17,9},{25,17},{1,25},{10,2},{18... | collective-permute-start | bytes 3145736 | tf_op jit(solution)/shard_map/ppermute | solution.py:41
  183.8 48.1 %collective-permute-start.35 = (bf16[2,2,64,2048]{3,2,1,0:T(8,128)(2,1)S(1)}, bf16[2,2,64,2048]{3,2,1,0:T(8,128)(2,1)}, u32[]{:S(2)}, u32[]{:S(2)}) collective-permute-start(bf16[2,2,64,2048]{3,2,1,0:T(8,128)(2,1)S(1)} %pad_maximum_fusion.4), channel_id=1, source_target_pairs={{24,0},{0,8},{8,16},{16,24},{25,1},{1,9},{9,17},{17,25},{26,2},{2,... | collective-permute-start | bytes 3145736 | tf_op jit(solution)/shard_map/ppermute | solution.py:41
  190.3 96.6 %collective-permute-start.41 = (bf16[2048,1024]{1,0:T(8,128)(2,1)}, bf16[2048,1024]{1,0:T(8,128)(2,1)}, u32[]{:S(2)}, u32[]{:S(2)}) collective-permute-start(bf16[2048,1024]{1,0:T(8,128)(2,1)} %bitcast.51), channel_id=1, source_target_pairs={{1,0},{0,1},{3,2},{2,3},{5,4},{4,5},{7,6},{6,7},{9,8},{8,9},{11,10... | collective-permute-start | bytes 12582920 | tf_op jit(solution)/shard_map/ppermute | solution.py:41
  244.4 23.6 %collective-permute-start.38 = (bf16[2,2,64,1024]{3,2,1,0:T(8,128)(2,1)S(1)}, bf16[2,2,64,1024]{3,2,1,0:T(8,128)(2,1)S(1)}, u32[]{:S(2)}, u32[]{:S(2)}) collective-permute-start(bf16[2,2,64,1024]{3,2,1,0:T(8,128)(2,1)S(1)} %slice.144), channel_id=1, source_target_pairs={{24,0},{0,8},{8,16},{16,24},{25,1},{1,9},{9,17},{17,25},{26,2},{2,... | collective-permute-start | bytes 1572872 | tf_op jit(solution)/shard_map/ppermute | solution.py:41
  252.7 34.1 %collective-permute-start.42 = (bf16[1024,2048]{1,0:T(8,128)(2,1)}, bf16[1024,2048]{1,0:T(8,128)(2,1)}, u32[]{:S(2)}, u32[]{:S(2)}) collective-permute-start(bf16[1024,2048]{1,0:T(8,128)(2,1)} %bitcast.54), channel_id=1, source_target_pairs={{1,0},{0,1},{3,2},{2,3},{5,4},{4,5},{7,6},{6,7},{9,8},{8,9},{11,10... | collective-permute-start | bytes 12582920 | tf_op jit(solution)/shard_map/ppermute | solution.py:41
  269.7 19.5 %collective-permute-start.40 = (bf16[1024,2048]{1,0:T(8,128)(2,1)}, bf16[1024,2048]{1,0:T(8,128)(2,1)}, u32[]{:S(2)}, u32[]{:S(2)}) collective-permute-start(bf16[1024,2048]{1,0:T(8,128)(2,1)} %bitcast.48), channel_id=1, source_target_pairs={{1,0},{0,1},{3,2},{2,3},{5,4},{4,5},{7,6},{6,7},{9,8},{8,9},{11,10... | collective-permute-start | bytes 12582920 | tf_op jit(solution)/shard_map/ppermute | solution.py:41
  360.1 18.4 %collective-permute-start.49 = (bf16[2048,1024]{1,0:T(8,128)(2,1)}, bf16[2048,1024]{1,0:T(8,128)(2,1)}, u32[]{:S(2)}, u32[]{:S(2)}) collective-permute-start(bf16[2048,1024]{1,0:T(8,128)(2,1)} %convolution_convert_fusion.3), channel_id=1, source_target_pairs={{1,0},{0,1},{3,2},{2,3},{5,4},{4,5},{7,6},{6,7},{9,8},{8,9},{11,10... | collective-permute-start | bytes 12582920 | tf_op jit(solution)/shard_map/ppermute | solution.py:41
  362.2 16.4 %collective-permute-start.48 = (bf16[1024,512]{1,0:T(8,128)(2,1)S(1)}, bf16[1024,512]{1,0:T(8,128)(2,1)S(1)}, u32[]{:S(2)}, u32[]{:S(2)}) collective-permute-start(bf16[1024,512]{1,0:T(8,128)(2,1)S(1)} %convolution_convert_fusion.10), channel_id=1, source_target_pairs={{1,0},{0,1},{3,2},{2,3},{5,4},{4,5},{7,6},{6,7},{9,8},{8,9},{11,10... | collective-permute-start | bytes 3145736 | tf_op jit(solution)/shard_map/ppermute | solution.py:41
  382.9 32.4 %collective-permute-start.51 = (bf16[1024,2048]{1,0:T(8,128)(2,1)}, bf16[1024,2048]{1,0:T(8,128)(2,1)}, u32[]{:S(2)}, u32[]{:S(2)}) collective-permute-start(bf16[1024,2048]{1,0:T(8,128)(2,1)} %convolution_convert_fusion.2), channel_id=1, source_target_pairs={{1,0},{0,1},{3,2},{2,3},{5,4},{4,5},{7,6},{6,7},{9,8},{8,9},{11,10... | collective-permute-start | bytes 12582920 | tf_op jit(solution)/shard_map/ppermute | solution.py:41
  391.3 24.1 %collective-permute-start.50 = (bf16[2,2,4,32,512]{4,3,0,2,1:T(8,128)(2,1)S(1)}, bf16[2,2,4,32,512]{4,3,0,2,1:T(8,128)(2,1)S(1)}, u32[]{:S(2)}, u32[]{:S(2)}) collective-permute-start(bf16[2,2,4,32,512]{4,3,0,2,1:T(8,128)(2,1)S(1)} %bitcast.594), channel_id=1, source_target_pairs={{2,0},{0,2},{3,1},{1,3},{6,4},{4,6},{7,5},{5,7},{10,8},{8,10},{11,... | collective-permute-start | bytes 1572872 | tf_op jit(solution)/shard_map/ppermute | solution.py:41
  402.6 50.3 %collective-permute-start.53 = (bf16[4,2,128,1024]{3,2,0,1:T(8,128)(2,1)}, bf16[4,2,128,1024]{3,2,0,1:T(8,128)(2,1)}, u32[]{:S(2)}, u32[]{:S(2)}) collective-permute-start(bf16[4,2,128,1024]{3,2,0,1:T(8,128)(2,1)} %bitcast.525), channel_id=1, source_target_pairs={{2,0},{0,2},{3,1},{1,3},{6,4},{4,6},{7,5},{5,7},{10,8},{8,10},{11,... | collective-permute-start | bytes 6291464 | tf_op jit(solution)/shard_map/ppermute | solution.py:41
  460.1 24.0 %collective-permute-start.60 = (bf16[1024,1536]{1,0:T(8,128)(2,1)S(1)}, bf16[1024,1536]{1,0:T(8,128)(2,1)S(1)}, u32[]{:S(2)}, u32[]{:S(2)}) collective-permute-start(bf16[1024,1536]{1,0:T(8,128)(2,1)S(1)} %convolution_convert_fusion.1), channel_id=1, source_target_pairs={{1,0},{0,1},{3,2},{2,3},{5,4},{4,5},{7,6},{6,7},{9,8},{8,9},{11,10... | collective-permute-start | bytes 9437192 | tf_op jit(solution)/shard_map/ppermute | solution.py:41
  474.8 30.4 %collective-permute-start.61 = (bf16[4,128,1024]{2,1,0:T(8,128)(2,1)S(1)}, bf16[4,128,1024]{2,1,0:T(8,128)(2,1)S(1)}, u32[]{:S(2)}, u32[]{:S(2)}) collective-permute-start(bf16[4,128,1024]{2,1,0:T(8,128)(2,1)S(1)} %dynamic-slice_bitcast_fusion.3), channel_id=1, source_target_pairs={{4,0},{0,4},{5,1},{1,5},{6,2},{2,6},{7,3},{3,7},{12,8},{8,12},{13,... | collective-permute-start | bytes 3145736 | tf_op jit(solution)/shard_map/ppermute | solution.py:41
  476.3 46.8 %collective-permute-start.68 = (bf16[4,2,64,2048]{3,2,1,0:T(8,128)(2,1)S(1)}, bf16[4,2,64,2048]{3,2,1,0:T(8,128)(2,1)}, u32[]{:S(2)}, u32[]{:S(2)}) collective-permute-start(bf16[4,2,64,2048]{3,2,1,0:T(8,128)(2,1)S(1)} %dynamic-slice_bitcast_fusion), channel_id=1, source_target_pairs={{2,0},{0,2},{3,1},{1,3},{6,4},{4,6},{7,5},{5,7},{10,8},{8,10},{11,... | collective-permute-start | bytes 6291464 | tf_op jit(solution)/shard_map/ppermute | solution.py:41
  484.7 40.1 %collective-permute-start.62 = (bf16[2,32,512]{2,1,0:T(8,128)(2,1)S(1)}, bf16[2,32,512]{2,1,0:T(8,128)(2,1)S(1)}, u32[]{:S(2)}, u32[]{:S(2)}) collective-permute-start(bf16[2,32,512]{2,1,0:T(8,128)(2,1)S(1)} %get-tuple-element.370), channel_id=1, source_target_pairs={{8,0},{16,8},{24,16},{0,24},{9,1},{17,9},{25,17},{1,25},{10,2},{18... | collective-permute-start | bytes 196616 | tf_op jit(solution)/shard_map/ppermute | solution.py:41
  486.5 39.5 %collective-permute-start.63 = (bf16[2,32,512]{2,1,0:T(8,128)(2,1)S(1)}, bf16[2,32,512]{2,1,0:T(8,128)(2,1)S(1)}, u32[]{:S(2)}, u32[]{:S(2)}) collective-permute-start(bf16[2,32,512]{2,1,0:T(8,128)(2,1)S(1)} %get-tuple-element.370), channel_id=1, source_target_pairs={{16,0},{24,8},{0,16},{8,24},{17,1},{25,9},{1,17},{9,25},{18,2},{26... | collective-permute-start | bytes 196616 | tf_op jit(solution)/shard_map/ppermute | solution.py:41
  488.5 38.8 %collective-permute-start.64 = (bf16[2,32,512]{2,1,0:T(8,128)(2,1)S(1)}, bf16[2,32,512]{2,1,0:T(8,128)(2,1)S(1)}, u32[]{:S(2)}, u32[]{:S(2)}) collective-permute-start(bf16[2,32,512]{2,1,0:T(8,128)(2,1)S(1)} %get-tuple-element.370), channel_id=1, source_target_pairs={{24,0},{0,8},{8,16},{16,24},{25,1},{1,9},{9,17},{17,25},{26,2},{2,... | collective-permute-start | bytes 196616 | tf_op jit(solution)/shard_map/ppermute | solution.py:41
  507.3 20.6 %collective-permute-start.65 = (bf16[128,1024]{1,0:T(8,128)(2,1)S(1)}, bf16[128,1024]{1,0:T(8,128)(2,1)S(1)}, u32[]{:S(2)}, u32[]{:S(2)}) collective-permute-start(bf16[128,1024]{1,0:T(8,128)(2,1)S(1)} %get-tuple-element.342), channel_id=1, source_target_pairs={{24,0},{0,8},{8,16},{16,24},{25,1},{1,9},{9,17},{17,25},{26,2},{2,... | collective-permute-start | bytes 786440 | tf_op jit(solution)/shard_map/ppermute | solution.py:41
  523.0 28.2 %collective-permute-start.66 = (bf16[128,1024]{1,0:T(8,128)(2,1)}, bf16[128,1024]{1,0:T(8,128)(2,1)}, u32[]{:S(2)}, u32[]{:S(2)}) collective-permute-start(bf16[128,1024]{1,0:T(8,128)(2,1)} %get-tuple-element.341), channel_id=1, source_target_pairs={{16,0},{24,8},{0,16},{8,24},{17,1},{25,9},{1,17},{9,25},{18,2},{26... | collective-permute-start | bytes 786440 | tf_op jit(solution)/shard_map/ppermute | solution.py:41
  524.8 26.4 %collective-permute-start.67 = (bf16[128,1024]{1,0:T(8,128)(2,1)S(1)}, bf16[128,1024]{1,0:T(8,128)(2,1)}, u32[]{:S(2)}, u32[]{:S(2)}) collective-permute-start(bf16[128,1024]{1,0:T(8,128)(2,1)S(1)} %get-tuple-element.340), channel_id=1, source_target_pairs={{8,0},{16,8},{24,16},{0,24},{9,1},{17,9},{25,17},{1,25},{10,2},{18... | collective-permute-start | bytes 786440 | tf_op jit(solution)/shard_map/ppermute | solution.py:41
  526.0 25.2 %collective-permute-start.69 = (bf16[4,64,512]{2,1,0:T(8,128)(2,1)}, bf16[4,64,512]{2,1,0:T(8,128)(2,1)}, u32[]{:S(2)}, u32[]{:S(2)}) collective-permute-start(bf16[4,64,512]{2,1,0:T(8,128)(2,1)} %dynamic-slice_bitcast_fusion.18), channel_id=1, source_target_pairs={{2,0},{0,2},{3,1},{1,3},{6,4},{4,6},{7,5},{5,7},{10,8},{8,10},{11,... | collective-permute-start | bytes 786440 | tf_op jit(solution)/shard_map/ppermute | solution.py:41
  527.3 34.0 %collective-permute-start.70 = (bf16[4,2,64,1536]{3,2,1,0:T(8,128)(2,1)}, bf16[4,2,64,1536]{3,2,1,0:T(8,128)(2,1)}, u32[]{:S(2)}, u32[]{:S(2)}) collective-permute-start(bf16[4,2,64,1536]{3,2,1,0:T(8,128)(2,1)} %dynamic-slice_bitcast_fusion.1), channel_id=1, source_target_pairs={{4,0},{0,4},{5,1},{1,5},{6,2},{2,6},{7,3},{3,7},{12,8},{8,12},{13,... | collective-permute-start | bytes 4718600 | tf_op jit(solution)/shard_map/ppermute | solution.py:41
  528.7 22.6 %collective-permute-start.71 = (bf16[1024,512]{1,0:T(8,128)(2,1)}, bf16[1024,512]{1,0:T(8,128)(2,1)}, u32[]{:S(2)}, u32[]{:S(2)}) collective-permute-start(bf16[1024,512]{1,0:T(8,128)(2,1)} %convolution_convert_fusion.8), channel_id=1, source_target_pairs={{1,0},{0,1},{3,2},{2,3},{5,4},{4,5},{7,6},{6,7},{9,8},{8,9},{11,10... | collective-permute-start | bytes 3145736 | tf_op jit(solution)/shard_map/ppermute | solution.py:41
  565.0 28.3 %collective-permute-start.72 = (bf16[1024,1536]{1,0:T(8,128)(2,1)S(1)}, bf16[1024,1536]{1,0:T(8,128)(2,1)S(1)}, u32[]{:S(2)}, u32[]{:S(2)}) collective-permute-start(bf16[1024,1536]{1,0:T(8,128)(2,1)S(1)} %convolution_convert_fusion), channel_id=1, source_target_pairs={{1,0},{0,1},{3,2},{2,3},{5,4},{4,5},{7,6},{6,7},{9,8},{8,9},{11,10... | collective-permute-start | bytes 9437192 | tf_op jit(solution)/shard_map/ppermute | solution.py:41
  565.2 28.1 %collective-permute-start.73 = (bf16[2,4,32,512]{3,2,1,0:T(8,128)(2,1)S(1)}, bf16[2,4,32,512]{3,2,1,0:T(8,128)(2,1)S(1)}, u32[]{:S(2)}, u32[]{:S(2)}) collective-permute-start(bf16[2,4,32,512]{3,2,1,0:T(8,128)(2,1)S(1)} %bitcast_dynamic-update-slice_fusion.46), channel_id=1, source_target_pairs={{4,0},{0,4},{5,1},{1,5},{6,2},{2,6},{7,3},{3,7},{12,8},{8,12},{13,... | collective-permute-start | bytes 786440 | tf_op jit(solution)/shard_map/ppermute | solution.py:41
  566.9 24.2 %collective-permute-start.74 = (bf16[64,512]{1,0:T(8,128)(2,1)S(1)}, bf16[64,512]{1,0:T(8,128)(2,1)S(1)}, u32[]{:S(2)}, u32[]{:S(2)}) collective-permute-start(bf16[64,512]{1,0:T(8,128)(2,1)S(1)} %get-tuple-element.387), channel_id=1, source_target_pairs={{24,0},{0,8},{8,16},{16,24},{25,1},{1,9},{9,17},{17,25},{26,2},{2,... | collective-permute-start | bytes 196616 | tf_op jit(solution)/shard_map/ppermute | solution.py:41
  567.5 25.1 %collective-permute-start.75 = (bf16[64,512]{1,0:T(8,128)(2,1)S(1)}, bf16[64,512]{1,0:T(8,128)(2,1)S(1)}, u32[]{:S(2)}, u32[]{:S(2)}) collective-permute-start(bf16[64,512]{1,0:T(8,128)(2,1)S(1)} %get-tuple-element.386), channel_id=1, source_target_pairs={{16,0},{24,8},{0,16},{8,24},{17,1},{25,9},{1,17},{9,25},{18,2},{26... | collective-permute-start | bytes 196616 | tf_op jit(solution)/shard_map/ppermute | solution.py:41
  569.6 23.7 %collective-permute-start.76 = (bf16[64,512]{1,0:T(8,128)(2,1)S(1)}, bf16[64,512]{1,0:T(8,128)(2,1)S(1)}, u32[]{:S(2)}, u32[]{:S(2)}) collective-permute-start(bf16[64,512]{1,0:T(8,128)(2,1)S(1)} %get-tuple-element.385), channel_id=1, source_target_pairs={{8,0},{16,8},{24,16},{0,24},{9,1},{17,9},{25,17},{1,25},{10,2},{18... | collective-permute-start | bytes 196616 | tf_op jit(solution)/shard_map/ppermute | solution.py:41
  591.1 55.0 %collective-permute-start.81 = (bf16[4,64,2048]{2,1,0:T(8,128)(2,1)}, bf16[4,64,2048]{2,1,0:T(8,128)(2,1)}, u32[]{:S(2)}, u32[]{:S(2)}) collective-permute-start(bf16[4,64,2048]{2,1,0:T(8,128)(2,1)} %dynamic-slice_bitcast_fusion.2), channel_id=1, source_target_pairs={{4,0},{0,4},{5,1},{1,5},{6,2},{2,6},{7,3},{3,7},{12,8},{8,12},{13,... | collective-permute-start | bytes 3145736 | tf_op jit(solution)/shard_map/ppermute | solution.py:41
  592.6 53.0 %collective-permute-start.82 = (bf16[4,64,1536]{2,1,0:T(8,128)(2,1)}, bf16[4,64,1536]{2,1,0:T(8,128)(2,1)}, u32[]{:S(2)}, u32[]{:S(2)}) collective-permute-start(bf16[4,64,1536]{2,1,0:T(8,128)(2,1)} %dynamic-slice_bitcast_fusion.5), channel_id=1, source_target_pairs={{2,0},{0,2},{3,1},{1,3},{6,4},{4,6},{7,5},{5,7},{10,8},{8,10},{11,... | collective-permute-start | bytes 2359304 | tf_op jit(solution)/shard_map/ppermute | solution.py:41
  597.3 35.7 %collective-permute-start.98 = (bf16[4,2,64,768]{3,2,0,1:T(8,128)(2,1)}, bf16[4,2,64,768]{3,2,0,1:T(8,128)(2,1)}, u32[]{:S(2)}, u32[]{:S(2)}) collective-permute-start(bf16[4,2,64,768]{3,2,0,1:T(8,128)(2,1)} %bitcast.526), channel_id=1, source_target_pairs={{4,0},{0,4},{5,1},{1,5},{6,2},{2,6},{7,3},{3,7},{12,8},{8,12},{13,... | collective-permute-start | bytes 2359304 | tf_op jit(solution)/shard_map/ppermute | solution.py:41
  598.9 35.5 %collective-permute-start.99 = (bf16[4,2,64,768]{3,2,1,0:T(8,128)(2,1)}, bf16[4,2,64,768]{3,2,1,0:T(8,128)(2,1)}, u32[]{:S(2)}, u32[]{:S(2)}) collective-permute-start(bf16[4,2,64,768]{3,2,1,0:T(8,128)(2,1)} %dynamic-slice_bitcast_fusion.4), channel_id=1, source_target_pairs={{2,0},{0,2},{3,1},{1,3},{6,4},{4,6},{7,5},{5,7},{10,8},{8,10},{11,... | collective-permute-start | bytes 2359304 | tf_op jit(solution)/shard_map/ppermute | solution.py:41
  602.8 45.6 %collective-permute-start.77 = (bf16[1024,512]{1,0:T(8,128)(2,1)}, bf16[1024,512]{1,0:T(8,128)(2,1)}, u32[]{:S(2)}, u32[]{:S(2)}) collective-permute-start(bf16[1024,512]{1,0:T(8,128)(2,1)} %fusion.45), channel_id=1, source_target_pairs={{1,0},{0,1},{3,2},{2,3},{5,4},{4,5},{7,6},{6,7},{9,8},{8,9},{11,10... | collective-permute-start | bytes 3145736 | tf_op jit(solution)/shard_map/ppermute | solution.py:41
  650.7 24.5 %collective-permute-start.84 = (bf16[2,2,4,32,512]{4,3,0,2,1:T(8,128)(2,1)S(1)}, bf16[2,2,4,32,512]{4,3,0,2,1:T(8,128)(2,1)S(1)}, u32[]{:S(2)}, u32[]{:S(2)}) collective-permute-start(bf16[2,2,4,32,512]{4,3,0,2,1:T(8,128)(2,1)S(1)} %bitcast.593), channel_id=1, source_target_pairs={{2,0},{0,2},{3,1},{1,3},{6,4},{4,6},{7,5},{5,7},{10,8},{8,10},{11,... | collective-permute-start | bytes 1572872 | tf_op jit(solution)/shard_map/ppermute | solution.py:41
  652.1 18.0 %collective-permute-start.85 = (f32[5,1024]{1,0:T(8,128)S(1)}, f32[5,1024]{1,0:T(8,128)S(1)}, u32[]{:S(2)}, u32[]{:S(2)}) collective-permute-start(f32[5,1024]{1,0:T(8,128)S(1)} %add.985), channel_id=1, source_target_pairs={{2,0},{0,2},{3,1},{1,3},{6,4},{4,6},{7,5},{5,7},{10,8},{8,10},{11,... | collective-permute-start | bytes 61448 | tf_op jit(solution)/shard_map/ppermute | solution.py:41
  653.0 21.8 %collective-permute-start.86 = (bf16[4,64,512]{2,1,0:T(8,128)(2,1)S(1)}, bf16[4,64,512]{2,1,0:T(8,128)(2,1)S(1)}, u32[]{:S(2)}, u32[]{:S(2)}) collective-permute-start(bf16[4,64,512]{2,1,0:T(8,128)(2,1)S(1)} %dynamic-slice_bitcast_fusion.16), channel_id=1, source_target_pairs={{2,0},{0,2},{3,1},{1,3},{6,4},{4,6},{7,5},{5,7},{10,8},{8,10},{11,... | collective-permute-start | bytes 786440 | tf_op jit(solution)/shard_map/ppermute | solution.py:41
  658.3 42.7 %collective-permute-start.89 = (bf16[64,2048]{1,0:T(8,128)(2,1)S(1)}, bf16[64,2048]{1,0:T(8,128)(2,1)S(1)}, u32[]{:S(2)}, u32[]{:S(2)}) collective-permute-start(bf16[64,2048]{1,0:T(8,128)(2,1)S(1)} %get-tuple-element.337), channel_id=1, source_target_pairs={{24,0},{0,8},{8,16},{16,24},{25,1},{1,9},{9,17},{17,25},{26,2},{2,... | collective-permute-start | bytes 786440 | tf_op jit(solution)/shard_map/ppermute | solution.py:41
  658.9 44.6 %collective-permute-start.90 = (bf16[64,2048]{1,0:T(8,128)(2,1)S(1)}, bf16[64,2048]{1,0:T(8,128)(2,1)S(1)}, u32[]{:S(2)}, u32[]{:S(2)}) collective-permute-start(bf16[64,2048]{1,0:T(8,128)(2,1)S(1)} %get-tuple-element.336), channel_id=1, source_target_pairs={{16,0},{24,8},{0,16},{8,24},{17,1},{25,9},{1,17},{9,25},{18,2},{26... | collective-permute-start | bytes 786440 | tf_op jit(solution)/shard_map/ppermute | solution.py:41
  670.1 36.2 %collective-permute-start.91 = (bf16[64,2048]{1,0:T(8,128)(2,1)S(1)}, bf16[64,2048]{1,0:T(8,128)(2,1)S(1)}, u32[]{:S(2)}, u32[]{:S(2)}) collective-permute-start(bf16[64,2048]{1,0:T(8,128)(2,1)S(1)} %get-tuple-element.335), channel_id=1, source_target_pairs={{8,0},{16,8},{24,16},{0,24},{9,1},{17,9},{25,17},{1,25},{10,2},{18... | collective-permute-start | bytes 786440 | tf_op jit(solution)/shard_map/ppermute | solution.py:41
  675.2 21.4 %collective-permute-start.93 = (bf16[64,1536]{1,0:T(8,128)(2,1)S(1)}, bf16[64,1536]{1,0:T(8,128)(2,1)S(1)}, u32[]{:S(2)}, u32[]{:S(2)}) collective-permute-start(bf16[64,1536]{1,0:T(8,128)(2,1)S(1)} %get-tuple-element.359), channel_id=1, source_target_pairs={{16,0},{24,8},{0,16},{8,24},{17,1},{25,9},{1,17},{9,25},{18,2},{26... | collective-permute-start | bytes 589832 | tf_op jit(solution)/shard_map/ppermute | solution.py:41
  696.6 22.3 %collective-permute-start.87 = (bf16[2,4,32,512]{3,2,0,1:T(8,128)(2,1)S(1)}, bf16[2,4,32,512]{3,2,0,1:T(8,128)(2,1)S(1)}, u32[]{:S(2)}, u32[]{:S(2)}) collective-permute-start(bf16[2,4,32,512]{3,2,0,1:T(8,128)(2,1)S(1)} %dynamic-slice_bitcast_fusion.15), channel_id=1, source_target_pairs={{4,0},{0,4},{5,1},{1,5},{6,2},{2,6},{7,3},{3,7},{12,8},{8,12},{13,... | collective-permute-start | bytes 786440 | tf_op jit(solution)/shard_map/ppermute | solution.py:41
  709.3 16.4 %collective-permute-start.103 = (bf16[64,1536]{1,0:T(8,128)(2,1)S(1)}, bf16[64,1536]{1,0:T(8,128)(2,1)S(1)}, u32[]{:S(2)}, u32[]{:S(2)}) collective-permute-start(bf16[64,1536]{1,0:T(8,128)(2,1)S(1)} %get-tuple-element.357), channel_id=1, source_target_pairs={{16,0},{24,8},{0,16},{8,24},{17,1},{25,9},{1,17},{9,25},{18,2},{26... | collective-permute-start | bytes 589832 | tf_op jit(solution)/shard_map/ppermute | solution.py:41
  734.5 50.8 %collective-permute-start.118 = (f32[32,1536]{1,0:T(8,128)}, f32[32,1536]{1,0:T(8,128)}, u32[]{:S(2)}, u32[]{:S(2)}) collective-permute-start(f32[32,1536]{1,0:T(8,128)} %get-tuple-element.378), channel_id=1, source_target_pairs={{1,0},{0,1},{3,2},{2,3},{5,4},{4,5},{7,6},{6,7},{9,8},{8,9},{11,10... | collective-permute-start | bytes 589832 | tf_op jit(solution)/shard_map/ppermute | solution.py:41
  734.6 16.6 %collective-permute-start.119 = (f32[32,512]{1,0:T(8,128)}, f32[32,512]{1,0:T(8,128)}, u32[]{:S(2)}, u32[]{:S(2)}) collective-permute-start(f32[32,512]{1,0:T(8,128)} %dynamic-slice_bitcast_fusion.28), channel_id=1, source_target_pairs={{1,0},{0,1},{3,2},{2,3},{5,4},{4,5},{7,6},{6,7},{9,8},{8,9},{11,10... | collective-permute-start | bytes 196616 | tf_op jit(solution)/shard_map/ppermute | solution.py:41
  735.1 52.4 %collective-permute-start.120 = (f32[32,2048]{1,0:T(8,128)}, f32[32,2048]{1,0:T(8,128)}, u32[]{:S(2)}, u32[]{:S(2)}) collective-permute-start(f32[32,2048]{1,0:T(8,128)} %get-tuple-element.366), channel_id=1, source_target_pairs={{1,0},{0,1},{3,2},{2,3},{5,4},{4,5},{7,6},{6,7},{9,8},{8,9},{11,10... | collective-permute-start | bytes 786440 | tf_op jit(solution)/shard_map/ppermute | solution.py:41
  736.4 44.3 %collective-permute-start.121 = (bf16[2,32,512]{2,1,0:T(8,128)(2,1)S(1)}, bf16[2,32,512]{2,1,0:T(8,128)(2,1)}, u32[]{:S(2)}, u32[]{:S(2)}) collective-permute-start(bf16[2,32,512]{2,1,0:T(8,128)(2,1)S(1)} %get-tuple-element.367), channel_id=1, source_target_pairs={{8,0},{16,8},{24,16},{0,24},{9,1},{17,9},{25,17},{1,25},{10,2},{18... | collective-permute-start | bytes 196616 | tf_op jit(solution)/shard_map/ppermute | solution.py:41
  740.0 41.6 %collective-permute-start.122 = (bf16[2,32,512]{2,1,0:T(8,128)(2,1)S(1)}, bf16[2,32,512]{2,1,0:T(8,128)(2,1)}, u32[]{:S(2)}, u32[]{:S(2)}) collective-permute-start(bf16[2,32,512]{2,1,0:T(8,128)(2,1)S(1)} %get-tuple-element.367), channel_id=1, source_target_pairs={{16,0},{24,8},{0,16},{8,24},{17,1},{25,9},{1,17},{9,25},{18,2},{26... | collective-permute-start | bytes 196616 | tf_op jit(solution)/shard_map/ppermute | solution.py:41
  (208 other events, 2181.4 us)

commit v5 on v3

--- a/solution.py
+++ b/solution.py
@@ -1,4 +1,5 @@
 import functools
+from typing import NamedTuple
 
 import jax
 import jax.numpy as jnp
@@ -71,10 +72,15 @@
     ]
 
 
+class Squared(NamedTuple):
+    square: jax.Array
+    flight: list
+
+
 class Job:
     def __init__(self, steps):
         self.steps = steps
-        self.result = None
+        self.result = self.square = None
         self.flight = next(steps)
 
     def resume(self, arrived):
@@ -82,6 +88,8 @@
             self.flight = self.steps.send(arrived)
         except StopIteration as stop:
             self.flight, self.result = None, stop.value
+        if isinstance(self.flight, Squared):
+            self.square, self.flight = self.flight
 
     def finish(self):
         while self.flight is not None:
@@ -98,20 +106,19 @@
 
 
 def gather_half(part):
-    others = yield sent_around(part, "z")
-    first, second = jnp.split(placed(part, others, "z", 0), 2, axis=-1)
-    one = sent_around(first, "m")
-    two = sent_around(second, "r")
-    one, two = yield (one, two)
-    first, second = placed(first, one, "m", 1), placed(second, two, "r", 1)
-    one = sent_around(first, "r")
-    two = sent_around(second, "m")
-    one, two = yield (one, two)
-    first, second = placed(first, one, "r", 1), placed(second, two, "m", 2)
-    own = jnp.concatenate([first, second], axis=-1)
-    own = own.reshape(-1, own.shape[-1])
+    for axis, dim in (("r", 0), ("z", 0), ("m", 2)):
+        others = yield sent_around(part, axis)
+        part = placed(part, others, axis, dim)
+    own = part.reshape(-1, part.shape[-1])
     (other,) = yield [shifted(own, "h", 1)]
     return (own, other)
+
+
+def gather_table(part):
+    others = yield sent_around(part, "m")
+    part = placed(part, others, "m", 0)
+    others = yield sent_around(part, "h")
+    return placed(part, others, "h", 1).reshape(-1, part.shape[-1])
 
 
 def by_owner(array, block):
@@ -166,10 +173,11 @@
     return added(total, dim, order[2], pieces)
 
 
-def swap_rows(total):
+def swap_rows(total, square=None):
     seen = total.reshape(2, -1, total.shape[-1])
     half = lax.axis_index("h")
-    (other,) = yield [shifted(at(seen, 1 - half, 0), "h", 1)]
+    flight = [shifted(at(seen, 1 - half, 0), "h", 1)]
+    (other,) = yield flight if square is None else Squared(square, flight)
     return (at(seen, half, 0), other)
 
 
@@ -183,30 +191,31 @@
 def reduce_layer(other, own, order, block=None, parts=1):
     total = yield from reduce_rows(other, own, ("z", "r", "m"), order, parts)
     total = total.reshape(-1, total.shape[-1])
-    square = jnp.sum(total * total)
-    mine, other = yield from swap_rows(total)
+    mine, other = yield from swap_rows(total, jnp.sum(total * total))
     if block is None:
-        return (in_order(mine, other, 1), square)
+        return in_order(mine, other, 1)
     rows = mine.shape[0]
     mine, other = (half.reshape(rows, -1, 1, block) for half in (mine, other))
-    return (in_order(mine, other, 2).reshape(rows, -1), square)
-
-
-def reduce_owned(other, own, order):
-    total = yield from reduce_rows(other, own, ("z", "r", "m"), order)
-    return (total.reshape(-1, total.shape[-1]), jnp.sum(total * total))
+    return in_order(mine, other, 2).reshape(rows, -1)
+
+
+def reduce_owned(other, own, order, parts):
+    total = yield from reduce_rows(other, own, ("z", "r", "m"), order, parts)
+    total = total.reshape(-1, total.shape[-1])
+    yield Squared(jnp.sum(total * total), [])
+    return total
 
 
 def reduce_table(other, own):
     total = yield from reduce_rows(other, own, ("m", "h", "r", "z"), ("m", "r", "z"))
     square = jnp.sum(total * total)
     total = total.astype(LOW)
-    others = yield sent_around(total, "z")
+    others = yield Squared(square, sent_around(total, "z"))
     total = placed(total, others, "z", 1)
     others = yield sent_around(total, "r")
     total = placed(total, others, "r", 1)
     mine, other = yield from swap_rows(total.reshape(-1, total.shape[-1]))
-    return (in_order(mine, other, 1).astype(WIDE), square)
+    return in_order(mine, other, 1).astype(WIDE)
 
 
 def sum_over(part, axes):
@@ -336,9 +345,10 @@
         grid, block, where = (FRAMES * shape[1] // GROUP,), (FRAMES, GROUP // FRAMES), lambda g, s: (0, g, 0)
     wide = pl.BlockSpec(block + (3 * D,), where)
     narrow = pl.BlockSpec(block + (D,), where)
-    body, last, ins = forward_body, D, (packed,)
+    body, last, ins, flops = forward_body, D, (packed,), 9e9
     if up is not None:
-        body, last, ins = backward_body, 3 * D, (packed, up.reshape(shape + (D,)))
+        body, last, flops = backward_body, 3 * D, 22e9
+        ins = (packed, up.reshape(shape + (D,)))
     return pl.pallas_call(
         functools.partial(body, kind),
         out_shape=jax.ShapeDtypeStruct(shape + (last,), LOW),
@@ -347,6 +357,9 @@
             grid=grid,
             in_specs=[wide, narrow][: len(ins)],
             out_specs=narrow if up is None else wide,
+        ),
+        cost_estimate=pl.CostEstimate(
+            flops=int(flops), transcendentals=4 * HEADS * GROUP * GROUP, bytes_accessed=8 << 20
         ),
     )(scalar.reshape(1).astype(jnp.int32), *ins)
 
@@ -425,17 +438,19 @@
     doms = of_micro(domains)
 
     turned = jnp.pad(gains.T, ((0, 0), (0, LANES - kinds)))
-    layer_one = jnp.concatenate([attend_in[0], attend_out[0], turned], axis=1).astype(LOW)
-    layer_two = jnp.concatenate([attend_in[1], attend_out[1]], axis=1).astype(LOW)
-    layer_one = lax.all_gather(layer_one, ALL, axis=0, tiled=True)
-    layer_two = lax.all_gather(layer_two, ALL, axis=0, tiled=True)
+    layers = [attend_in[0], attend_out[0], turned, attend_in[1], attend_out[1]]
+    ends = [0]
+    for array in layers:
+        ends.append(ends[-1] + array.shape[1])
+    gathered = jnp.concatenate(layers, axis=1).astype(LOW)
+    gathered = lax.all_gather(gathered, ALL, axis=0, tiled=True)
     low_in, low_out = tables.astype(LOW)
-    table_in = gather_axis(gather_axis(low_in, "m", 0), "h", 1).reshape(-1, D)
     up_job = Job(gather_columns(expand.astype(LOW), block))
     down_job = Job(gather_half(contract.astype(LOW)))
-    table_in = advance(table_in, up_job)
-    table_out = gather_axis(gather_axis(low_out, "m", 0), "h", 1).reshape(-1, D)
-
+    in_table_job = Job(gather_table(low_in))
+    token = advance(jnp.zeros((), WIDE), up_job, down_job)
+    token = advance(token, in_table_job, up_job)
+    table_in = in_table_job.finish()
     code_ids = jnp.arange(table_in.shape[0])
 
     def own_frames(array):
@@ -443,11 +458,16 @@
 
     space_codes = own_frames(codes).reshape(-1)
     picked = dot_nn((space_codes[:, None] == code_ids[None, :]).astype(LOW), table_in)
-    picked = advance(picked, up_job, down_job)
-    layer_one = advance(layer_one, up_job, down_job)
-    w_in = (layer_one[:, : 3 * D], layer_two[:, : 3 * D])
-    w_out = (layer_one[:, 3 * D : 4 * D], layer_two[:, 3 * D :])
-    gain_all = layer_one[:, 4 * D :].T[:kinds].astype(WIDE)
+    token = advance(token, down_job)
+    out_table_job = Job(gather_table(low_out))
+    token = advance(token, up_job)
+    picked, token = lax.optimization_barrier((picked, token))
+    gathered = advance(gathered, out_table_job)
+    first_in, first_out, turned, next_in, next_out = (
+        gathered[:, start:end] for start, end in zip(ends, ends[1:])
+    )
+    w_in, w_out = (first_in, next_in), (first_out, next_out)
+    gain_all = turned.T[:kinds].astype(WIDE)
 
     slot_ids = jnp.arange(SLOTS)
     segment = jnp.where(small > 0, slot_ids // SMALL_TOKENS, 0)
@@ -473,7 +493,8 @@
     after_space = start + dot_nn(mixed_space, w_out[0])
     after_space = swap_slots(after_space.reshape(frames, SLOTS, D)).reshape(-1, D)
     normed_time = norm_forward(after_space, gain_all[1]).astype(LOW)
-    normed_time = advance(normed_time, up_job, down_job)
+    normed_time = advance(normed_time, up_job, down_job, out_table_job)
+    table_out = out_table_job.finish()
     packed_time = dot_nn(normed_time, w_in[1]).astype(LOW).reshape(FRAMES, -1, 3 * D)
     mixed_time = attention("time", half, packed_time).reshape(-1, D)
     after_time = after_space + dot_nn(mixed_time, w_out[1])
@@ -503,13 +524,14 @@
             dot_tn(activs[1], up_low).astype(LOW),
             lambda: dot_tn(activs[0], up_low),
             ("m", "r", "z"),
+            2,
         )
     )
     grad_activs = [dot_nt(up_low, down) for down in downs]
     grad_pres = [gelu_backward(pre, grad).astype(LOW) for pre, grad in zip(pres, grad_activs)]
     grad_pres = advance(grad_pres, head_job, contract_job)
     expand_job = product(
-        reduce_layer, normed_ffn, grad_pres[0], grad_pres[1], ("r", "m", "z"), block
+        reduce_layer, normed_ffn, grad_pres[0], grad_pres[1], ("r", "m", "z"), block, 2
     )
     grad_normed = dot_nt(grad_pres[0], ups[0]) + dot_nt(grad_pres[1], ups[1])
     inward, gain_two = norm_backward(after_time, gain_all[2], grad_normed)
@@ -520,23 +542,26 @@
     grad_mixed = dot_nt(up_low, w_out[1]).astype(LOW)
     grad_packed = attention("time", half, packed_time, grad_mixed).reshape(-1, 3 * D)
     grad_packed = advance(grad_packed, head_job, contract_job, out_job)
-    in_job = product(reduce_layer, normed_time, *halves(grad_packed, 1), ("m", "r", "z"))
+    in_job = product(
+        reduce_layer, normed_time, *halves(grad_packed, 1), ("m", "r", "z"), None, 2
+    )
     grad_normed = dot_nt(grad_packed, w_in[1])
     inward, gain_one = norm_backward(after_space, gain_all[1], grad_normed)
     grad_space = swap_frames((grad_time + inward).reshape(FRAMES, -1, D)).reshape(-1, D)
     up_low = grad_space.astype(LOW)
-    up_low = advance(up_low, head_job, out_job, in_job)
+    up_low = advance(up_low, head_job, contract_job, out_job, in_job)
     first_out_job = product(reduce_layer, mixed_space, *halves(up_low, 1), ("r", "m", "z"))
     grad_mixed = dot_nt(up_low, w_out[0]).astype(LOW)
+    grad_mixed = advance(grad_mixed, contract_job, expand_job, first_out_job)
     grad_packed = attention("space", small, packed_space, grad_mixed)
     grad_packed = advance(
-        grad_packed, head_job, contract_job, expand_job, out_job, in_job, first_out_job
+        grad_packed, head_job, expand_job, out_job, in_job, first_out_job
     )
     first_in_job = product(
         reduce_layer, normed_space, *halves(grad_packed, 1), ("r", "m", "z"), None, 2
     )
     grad_normed = dot_nt(grad_packed, w_in[0])
-    grad_normed = advance(grad_normed, first_in_job, head_job, out_job)
+    grad_normed = advance(grad_normed, first_in_job, head_job, out_job, in_job, first_out_job)
     inward, gain_zero = norm_backward(start, gain_all[0], grad_normed)
     grad_start = grad_space + inward
     mask_grad = jnp.sum(grad_start * space_mask[:, None], axis=0)
@@ -547,26 +572,27 @@
     gain_grads = jnp.stack([gain_zero, gain_one, gain_two, gain_three, mask_grad])
     gain_job = Job(sum_over(gain_grads, ("h", "m", "r", "z")))
     token = jnp.zeros((), WIDE)
-    late = (expand_job, contract_job, in_job, first_out_job)
-    token = advance(token, embed_job, gain_job, head_job, out_job, *late)
+    token = advance(token, embed_job, gain_job, head_job, out_job, expand_job)
     token = advance(token, first_in_job)
-    token = advance(token, embed_job, gain_job, first_out_job)
+    token = advance(token, embed_job, gain_job, in_job, first_out_job)
     token = advance(token, first_in_job)
-    token = advance(token, embed_job, gain_job, expand_job, in_job, first_out_job)
-    token = advance(token, first_in_job, embed_job, gain_job)
-
-    jobs = (in_job, first_in_job, out_job, first_out_job, expand_job, contract_job)
-    jobs = jobs + (embed_job, head_job)
+    token = advance(token, embed_job, gain_job, expand_job)
+    token = advance(token, first_in_job, embed_job, gain_job, in_job, first_out_job)
+
     owner = jnp.int32(0)
     for axis in ALL:
         owner = owner * lax.axis_size(axis) + lax.axis_index(axis)
     width = gains.shape[1]
     gain_grads = lax.dynamic_slice_in_dim(gain_job.finish(), owner * width, width, 1)
-    results = [job.finish() for job in jobs]
-    owned = sum(square for _, square in results) + jnp.sum(gain_grads * gain_grads)
+    jobs = (in_job, first_in_job, out_job, first_out_job, expand_job, contract_job)
+    jobs = jobs + (embed_job, head_job)
+    owned = sum(job.square for job in jobs) + jnp.sum(gain_grads * gain_grads)
     sums = jnp.stack([owned, loss_part]).reshape(1, 2)
-    sums = Job(sum_over(sums, ("h", "m", "r", "z"))).finish()
-    square_sum, loss = sums[0, 0], sums[0, 1]
+    norm_job = Job(sum_over(sums, ("h", "m", "r", "z")))
+    while norm_job.flight is not None:
+        token = advance(token, norm_job, *jobs)
+    results = [(job.finish(), None) for job in jobs]
+    square_sum, loss = norm_job.result[0, 0], norm_job.result[0, 1]
     norm = jnp.sqrt(square_sum)
     factor = jnp.minimum(1.0, CLIP / (norm + 1e-06))
 

time: 794 us -> 781 us (0.984)
  waiting for transfers between devices: 294 us -> 275 us
  local copies, waits for them, and re-layouts: 63.3 us -> 77.1 us
  matrix products: 146 us -> 136 us
    ppermute x104 -> x106, waiting for transfers between devices: 288 us -> 272 us  [shifted(): return lax.ppermute(part, axis, [((i + shift) % n, i) for i in range(n)])]
    unnamed x218 -> x284, local copies, waits for them, and re-layouts: 11.1 us -> 17.1 us
    dynamic_update_slice x36 -> x32, local copies, waits for them, and re-layouts: 14.3 us -> 17.7 us  [placed(): lax.dynamic_update_index_in_dim(whole, other, (mine + shift) % n, dim)]
    ppermute x104 -> x106, starting transfers between devices: 116 us -> 119 us  [shifted(): return lax.ppermute(part, axis, [((i + shift) % n, i) for i in range(n)])]
    convert_element_type x18 -> x24, other arithmetic: 17 us -> 18.8 us  [reduce_rows(): added(*each, arrived).astype(LOW)]
  transfers between devices with their start and end apart: 106 -> 107, of which waited for: 33 -> 34; matrix products, arithmetic and copies ran while one was open for 30% -> 28% of each run, Pallas kernels for 8% -> 8%
where the time goes in v5:
time: 781 us; the launch traced here: 772 us
  waiting for transfers between devices  275 us (35%)
  matrix products  136 us (17%)
  starting transfers between devices  119 us (15%)
  other arithmetic  77.7 us (10%)
  local copies, waits for them, and re-layouts  77.1 us (10%)
  Pallas kernels  63.2 us (8%)
  between operations  24.4 us (3%)
    ppermute x106, waiting for transfers between devices, shifted(): return lax.ppermute(part, axis, [((i + shift) % n, i) for i in range(n)])  272 us
    ppermute x106, starting transfers between devices, shifted(): return lax.ppermute(part, axis, [((i + shift) % n, i) for i in range(n)])  119 us
    pallas_call x4, Pallas kernels, attention(): pl.pallas_call(functools.partial(body, kind), out_shape=jax.ShapeDtypeStr...  63.2 us
    dot_general x10, matrix products, dot_nn(): return jnp.dot(left, right, preferred_element_type=WIDE)  47.9 us
    dot_general x9, matrix products, dot_nt(): lax.dot_general(left, right, (((1,), (1,)), ((), ())), preferred_element_...  47.6 us
    dot_general x16, matrix products, dot_tn(): lax.dot_general(left, right, (((0,), (0,)), ((), ())), preferred_element_...  40.2 us
    convert_element_type x24, other arithmetic, reduce_rows(): added(*each, arrived).astype(LOW)  18.8 us
    dynamic_update_slice x32, local copies, waits for them, and re-layouts, placed(): lax.dynamic_update_index_in_dim(whole, other, (mine + shift) % n, dim)  17.7 us
  transfers between devices with their start and end apart: 107, of which 34 were waited for; matrix products, arithmetic and copies ran while one was open for 28% of the time, Pallas kernels for 8%

profile of v5, /device:TPU:0, one launch (start us, length us, event | category | flops | bytes accessed | tf_op | source)
XLA Modules:
  0.0 772.4 jit_solution(13852726086659478353)
XLA Ops:
  17.5 2.5 collective-permute-start.3
  25.0 2.6 collective-permute-done.18
  27.6 3.6 collective-permute-start.19
  33.9 3.3 collective-permute-start.21
  45.6 9.7 %collective-permute-done.11 = bf16[2,128,1024]{2,1,0:T(8,128)(2,1)S(1)} collective-permute-done((bf16[2,128,1024]{2,1,0:T(8,128)(2,1)S(1)}, bf16[2,128,1024]{2,1,0:T(8,128)(2,1)S(1)}, u32[]{:S(2)}, u32[]{:S(2)}) %collective-permute-start.11) | collective-permute-done | bytes 524320 | tf_op jit(solution)/shard_map/ppermute | solution.py:41
  55.3 3.6 collective-permute-start.7
  58.8 64.0 %collective-permute-done.12 = bf16[2,128,1024]{2,1,0:T(8,128)(2,1)S(1)} collective-permute-done((bf16[2,128,1024]{2,1,0:T(8,128)(2,1)S(1)}, bf16[2,128,1024]{2,1,0:T(8,128)(2,1)S(1)}, u32[]{:S(2)}, u32[]{:S(2)}) %collective-permute-start.12) | collective-permute-done | bytes 524320 | tf_op jit(solution)/shard_map/ppermute | solution.py:41
  122.8 11.0 %collective-permute-start.9 = (bf16[2,64,2048]{2,1,0:T(8,128)(2,1)S(1)}, bf16[2,64,2048]{2,1,0:T(8,128)(2,1)S(1)}, u32[]{:S(2)}, u32[]{:S(2)}) collective-permute-start(bf16[2,64,2048]{2,1,0:T(8,128)(2,1)S(1)} %bitcast_dynamic-update-slice_fusion.15), channel_id=1, source_target_pairs={{24,0},{0,8},{8,16},{16,24},{25,1},{1,9},{9,17},{17,25},{26,2},{2,... | collective-permute-start | bytes 1572872 | tf_op jit(solution)/shard_map/ppermute | solution.py:41
  137.9 57.5 %collective-permute-done.8 = bf16[2,64,2048]{2,1,0:T(8,128)(2,1)S(1)} collective-permute-done((bf16[2,64,2048]{2,1,0:T(8,128)(2,1)S(1)}, bf16[2,64,2048]{2,1,0:T(8,128)(2,1)S(1)}, u32[]{:S(2)}, u32[]{:S(2)}) %collective-permute-start.8) | collective-permute-done | bytes 524320 | tf_op jit(solution)/shard_map/ppermute | solution.py:41
  203.3 3.1 all-gather.2.cloned.1.call-done
  210.6 8.0 %fusion.8.packed_ref = bf16[512,3072]{1,0:T(8,128)(2,1)} fusion(bf16[512,1024]{1,0:T(8,128)(2,1)S(1)} %multiply_convert_fusion.5, bf16[1024,8320]{1,0:T(8,128)(2,1)} %all-gather.2.cloned.1.call-done), kind=kOutput, calls=%fused_computation.16 | convolution fusion | flops 3222798336 | bytes 10485760 | tf_op jit(solution)/shard_map/dot_general | solution.py:259
  218.6 9.3 %shard_map.365 = bf16[512,1024]{1,0:T(8,128)(2,1)} custom-call(s32[1]{0:T(128)} %bitcast.13.scalar_ref, bf16[512,3072]{1,0:T(8,128)(2,1)} %fusion.8.packed_ref), custom_call_target="tpu_custom_call" | custom-call | flops 8999999488 | bytes 8388608 | tf_op jit(solution)/shard_map/pallas_call | solution.py:352
  227.9 3.2 fusion.60
  236.9 7.4 collective-permute-done.14
  244.3 37.9 %collective-permute-done.10 = bf16[4,2,64,2048]{3,2,1,0:T(8,128)(2,1)} collective-permute-done((bf16[4,2,64,2048]{3,2,1,0:T(8,128)(2,1)}, bf16[4,2,64,2048]{3,2,1,0:T(8,128)(2,1)}, u32[]{:S(2)}, u32[]{:S(2)}) %collective-permute-start.10) | collective-permute-done | bytes 2097184 | tf_op jit(solution)/shard_map/ppermute | solution.py:41
  282.2 4.1 broadcast_in_dim.299
  286.3 3.1 bitcast_dynamic-update-slice_fusion
  289.4 4.1 broadcast_in_dim.297
  293.5 3.1 bitcast_dynamic-update-slice_fusion.1
  297.1 7.6 fusion.11
  304.7 9.2 %shard_map.366 = bf16[4,128,1024]{2,1,0:T(8,128)(2,1)} custom-call(s32[1]{0:T(128)} %bitcast.26.scalar_ref, bf16[4,128,3072]{2,1,0:T(8,128)(2,1)} %bitcast.598), custom_call_target="tpu_custom_call" | custom-call | flops 8999999488 | bytes 8388608 | tf_op jit(solution)/shard_map/pallas_call | solution.py:352
  313.9 3.3 multiply_reduce_fusion.8
  319.5 4.9 fusion.210
  324.4 6.4 fusion.184
  330.9 4.5 fusion.211
  335.5 6.6 multiply_reduce_fusion.7
  349.9 4.9 convolution_convert_fusion.3
  359.3 6.2 fusion.183
  365.5 8.1 %fusion.20 = bf16[512,2048]{1,0:T(8,128)(2,1)} fusion(f32[512,2048]{1,0:T(8,128)S(1)} %copy-done.128, bf16[512,1024]{1,0:T(8,128)(2,1)S(1)} %copy-done.48, bf16[2048,1024]{1,0:T(8,128)(2,1)} %bitcast.32), kind=kOutput, calls=%fused_computation.24 | convolution fusion | flops 2168455168 | bytes 11534336 | tf_op jit(solution)/shard_map/dot_general | solution.py:251
  373.6 7.2 fusion.27
  380.9 4.4 convolution_convert_fusion.2
  387.5 6.2 add_convert_fusion.1
  400.4 4.9 fusion.212
  405.4 5.1 multiply_reduce_fusion.2
  413.0 4.4 fusion.69
  419.2 22.0 %shard_map.367 = bf16[4,128,3072]{2,1,0:T(8,128)(2,1)} custom-call(s32[1]{0:T(128)} %bitcast.26.scalar_ref, bf16[4,128,3072]{2,1,0:T(8,128)(2,1)} %bitcast.599, bf16[4,128,1024]{2,1,0:T(8,128)(2,1)} %bitcast.606), custom_call_target="tpu_custom_call" | custom-call | flops 22000001024 | bytes 8388608 | tf_op jit(solution)/shard_map/pallas_call | solution.py:352
  443.6 5.2 add_convert_fusion
  451.2 6.7 fusion.40
  469.7 5.2 collective-permute-done.32
  474.9 3.5 collective-permute-start.33
  481.5 10.8 %collective-permute-done.36 = bf16[4,2,64,512]{3,2,1,0:T(8,128)(2,1)S(1)} collective-permute-done((bf16[4,2,64,512]{3,2,1,0:T(8,128)(2,1)S(1)}, bf16[4,2,64,512]{3,2,1,0:T(8,128)(2,1)S(1)}, u32[]{:S(2)}, u32[]{:S(2)}) %collective-permute-start.36) | collective-permute-done | bytes 524320 | tf_op jit(solution)/shard_map/ppermute | solution.py:41
  492.8 4.4 collective-permute-start.39
  502.5 4.1 fusion.66.up_ref
  508.5 5.5 collective-permute-done.42
  514.0 3.5 collective-permute-start.44
  530.2 22.7 %shard_map.368 = bf16[512,3072]{1,0:T(8,128)(2,1)} custom-call(s32[1]{0:T(128)} %bitcast.13.scalar_ref, bf16[512,3072]{1,0:T(8,128)(2,1)} %fusion.8.packed_ref, bf16[512,1024]{1,0:T(8,128)(2,1)} %fusion.66.up_ref), custom_call_target="tpu_custom_call" | custom-call | flops 22000001024 | bytes 8388608 | tf_op jit(solution)/shard_map/pallas_call | solution.py:352
  552.9 2.7 multiply_reduce_fusion.11
  556.4 9.7 %collective-permute-done.52 = bf16[4,2,64,512]{3,2,1,0:T(8,128)(2,1)} collective-permute-done((bf16[4,2,64,512]{3,2,1,0:T(8,128)(2,1)}, bf16[4,2,64,512]{3,2,1,0:T(8,128)(2,1)}, u32[]{:S(2)}, u32[]{:S(2)}) %collective-permute-start.52) | collective-permute-done | bytes 524320 | tf_op jit(solution)/shard_map/ppermute | solution.py:41
  566.1 3.3 convolution_convert_fusion
  580.6 5.7 fusion.4
  592.3 10.8 %collective-permute-done.60 = bf16[4,64,512]{2,1,0:T(8,128)(2,1)S(1)} collective-permute-done((bf16[4,64,512]{2,1,0:T(8,128)(2,1)S(1)}, bf16[4,64,512]{2,1,0:T(8,128)(2,1)S(1)}, u32[]{:S(2)}, u32[]{:S(2)}) %collective-permute-start.60) | collective-permute-done | bytes 262176 | tf_op jit(solution)/shard_map/ppermute | solution.py:41
  622.3 12.8 %collective-permute-done.76 = bf16[4,2,64,768]{3,2,0,1:T(8,128)(2,1)} collective-permute-done((bf16[4,2,64,768]{3,2,0,1:T(8,128)(2,1)}, bf16[4,2,64,768]{3,2,0,1:T(8,128)(2,1)}, u32[]{:S(2)}, u32[]{:S(2)}) %collective-permute-start.76) | collective-permute-done | bytes 786464 | tf_op jit(solution)/shard_map/ppermute | solution.py:41
  645.0 2.6 collective-permute-start.74
  670.0 6.0 collective-permute-done.71
  677.6 3.4 collective-permute-start.81
  692.9 3.1 collective-permute-done.82
  696.1 2.7 collective-permute-start.91
  706.8 2.6 collective-permute-start.96
  727.1 6.4 collective-permute-done.100
  735.6 2.5 collective-permute-done.101
  738.2 3.4 collective-permute-start.103
  742.9 3.2 collective-permute-done.104
  751.8 2.6 multiply_subtract_fusion.4
  760.7 3.5 multiply_subtract_fusion
  (694 shorter events, 232.0 us)
Async XLA Ops:
  7.2 199.1 %all-gather.2.cloned.1.call-start = ((), (), s32[]{:S(2)}) async-start(), calls=%async_computation | async-start | bytes 17571840 | tf_op jit(solution)/shard_map/all_gather | solution.py:446
  17.0 17.0 %collective-permute-start.2 = (bf16[32,2048]{1,0:T(8,128)(2,1)}, bf16[32,2048]{1,0:T(8,128)(2,1)}, u32[]{:S(2)}, u32[]{:S(2)}) collective-permute-start(bf16[32,2048]{1,0:T(8,128)(2,1)} %bitcast.536), channel_id=1, source_target_pairs={{1,0},{0,1},{3,2},{2,3},{5,4},{4,5},{7,6},{6,7},{9,8},{8,9},{11,10... | collective-permute-start | bytes 393224 | tf_op jit(solution)/shard_map/ppermute | solution.py:41
  17.5 19.7 %collective-permute-start.3 = (bf16[128,1024]{1,0:T(8,128)(2,1)S(1)}, bf16[128,1024]{1,0:T(8,128)(2,1)S(1)}, u32[]{:S(2)}, u32[]{:S(2)}) collective-permute-start(bf16[128,1024]{1,0:T(8,128)(2,1)S(1)} %convert_element_type.585), channel_id=1, source_target_pairs={{4,0},{0,4},{5,1},{1,5},{6,2},{2,6},{7,3},{3,7},{12,8},{8,12},{13,... | collective-permute-start | bytes 786440 | tf_op jit(solution)/shard_map/ppermute | solution.py:41
  20.3 21.8 %collective-permute-start.1 = (bf16[256,1024]{1,0:T(8,128)(2,1)S(1)}, bf16[256,1024]{1,0:T(8,128)(2,1)S(1)}, u32[]{:S(2)}, u32[]{:S(2)}) collective-permute-start(bf16[256,1024]{1,0:T(8,128)(2,1)S(1)} %get-tuple-element.326), channel_id=1, source_target_pairs={{2,0},{0,2},{3,1},{1,3},{6,4},{4,6},{7,5},{5,7},{10,8},{8,10},{11,... | collective-permute-start | bytes 1572872 | tf_op jit(solution)/shard_map/ppermute | solution.py:41
  21.9 181.3 %collective-permute-start = (bf16[256,1024]{1,0:T(8,128)(2,1)S(1)}, bf16[256,1024]{1,0:T(8,128)(2,1)}, u32[]{:S(2)}, u32[]{:S(2)}) collective-permute-start(bf16[256,1024]{1,0:T(8,128)(2,1)S(1)} %get-tuple-element.325), channel_id=1, source_target_pairs={{2,0},{0,2},{3,1},{1,3},{6,4},{4,6},{7,5},{5,7},{10,8},{8,10},{11,... | collective-permute-start | bytes 1572872 | tf_op jit(solution)/shard_map/ppermute | solution.py:41
  33.9 198.6 %collective-permute-start.21 = (f32[1,4]{1,0:T(1,128)S(1)}, f32[1,4]{1,0:T(1,128)S(1)}, u32[]{:S(2)}, u32[]{:S(2)}) collective-permute-start(f32[1,4]{1,0:T(1,128)S(1)} %bitcast_add_fusion.2), channel_id=1, source_target_pairs={{24,0},{0,8},{8,16},{16,24},{25,1},{1,9},{9,17},{17,25},{26,2},{2,... | collective-permute-start | bytes 56 | tf_op jit(solution)/shard_map/ppermute | solution.py:41
  41.3 14.0 %collective-permute-start.11 = (bf16[2,128,1024]{2,1,0:T(8,128)(2,1)S(1)}, bf16[2,128,1024]{2,1,0:T(8,128)(2,1)S(1)}, u32[]{:S(2)}, u32[]{:S(2)}) collective-permute-start(bf16[2,128,1024]{2,1,0:T(8,128)(2,1)S(1)} %bitcast_dynamic-update-slice_fusion.14), channel_id=1, source_target_pairs={{8,0},{16,8},{24,16},{0,24},{9,1},{17,9},{25,17},{1,25},{10,2},{18... | collective-permute-start | bytes 1572872 | tf_op jit(solution)/shard_map/ppermute | solution.py:41
  42.2 80.7 %collective-permute-start.12 = (bf16[2,128,1024]{2,1,0:T(8,128)(2,1)S(1)}, bf16[2,128,1024]{2,1,0:T(8,128)(2,1)S(1)}, u32[]{:S(2)}, u32[]{:S(2)}) collective-permute-start(bf16[2,128,1024]{2,1,0:T(8,128)(2,1)S(1)} %bitcast_dynamic-update-slice_fusion.14), channel_id=1, source_target_pairs={{16,0},{24,8},{0,16},{8,24},{17,1},{25,9},{1,17},{9,25},{18,2},{26... | collective-permute-start | bytes 1572872 | tf_op jit(solution)/shard_map/ppermute | solution.py:41
  45.3 77.5 %collective-permute-start.13 = (bf16[2,128,1024]{2,1,0:T(8,128)(2,1)S(1)}, bf16[2,128,1024]{2,1,0:T(8,128)(2,1)S(1)}, u32[]{:S(2)}, u32[]{:S(2)}) collective-permute-start(bf16[2,128,1024]{2,1,0:T(8,128)(2,1)S(1)} %bitcast_dynamic-update-slice_fusion.14), channel_id=1, source_target_pairs={{24,0},{0,8},{8,16},{16,24},{25,1},{1,9},{9,17},{17,25},{26,2},{2,... | collective-permute-start | bytes 1572872 | tf_op jit(solution)/shard_map/ppermute | solution.py:41
  55.3 82.7 %collective-permute-start.7 = (bf16[2,64,2048]{2,1,0:T(8,128)(2,1)S(1)}, bf16[2,64,2048]{2,1,0:T(8,128)(2,1)S(1)}, u32[]{:S(2)}, u32[]{:S(2)}) collective-permute-start(bf16[2,64,2048]{2,1,0:T(8,128)(2,1)S(1)} %bitcast_dynamic-update-slice_fusion.15), channel_id=1, source_target_pairs={{8,0},{16,8},{24,16},{0,24},{9,1},{17,9},{25,17},{1,25},{10,2},{18... | collective-permute-start | bytes 1572872 | tf_op jit(solution)/shard_map/ppermute | solution.py:41
  122.8 72.6 %collective-permute-start.8 = (bf16[2,64,2048]{2,1,0:T(8,128)(2,1)S(1)}, bf16[2,64,2048]{2,1,0:T(8,128)(2,1)S(1)}, u32[]{:S(2)}, u32[]{:S(2)}) collective-permute-start(bf16[2,64,2048]{2,1,0:T(8,128)(2,1)S(1)} %bitcast_dynamic-update-slice_fusion.15), channel_id=1, source_target_pairs={{16,0},{24,8},{0,16},{8,24},{17,1},{25,9},{1,17},{9,25},{18,2},{26... | collective-permute-start | bytes 1572872 | tf_op jit(solution)/shard_map/ppermute | solution.py:41
  122.8 72.6 %collective-permute-start.9 = (bf16[2,64,2048]{2,1,0:T(8,128)(2,1)S(1)}, bf16[2,64,2048]{2,1,0:T(8,128)(2,1)S(1)}, u32[]{:S(2)}, u32[]{:S(2)}) collective-permute-start(bf16[2,64,2048]{2,1,0:T(8,128)(2,1)S(1)} %bitcast_dynamic-update-slice_fusion.15), channel_id=1, source_target_pairs={{24,0},{0,8},{8,16},{16,24},{25,1},{1,9},{9,17},{17,25},{26,2},{2,... | collective-permute-start | bytes 1572872 | tf_op jit(solution)/shard_map/ppermute | solution.py:41
  137.9 63.6 %collective-permute-start.5 = (bf16[2,256,1024]{2,1,0:T(8,128)(2,1)S(1)}, bf16[2,256,1024]{2,1,0:T(8,128)(2,1)S(1)}, u32[]{:S(2)}, u32[]{:S(2)}) collective-permute-start(bf16[2,256,1024]{2,1,0:T(8,128)(2,1)S(1)} %bitcast_dynamic-update-slice_fusion.11), channel_id=1, source_target_pairs={{1,0},{0,1},{3,2},{2,3},{5,4},{4,5},{7,6},{6,7},{9,8},{8,9},{11,10... | collective-permute-start | bytes 3145736 | tf_op jit(solution)/shard_map/ppermute | solution.py:41
  195.5 48.8 %collective-permute-start.14 = (bf16[4,2,128,1024]{3,2,1,0:T(8,128)(2,1)}, bf16[4,2,128,1024]{3,2,1,0:T(8,128)(2,1)}, u32[]{:S(2)}, u32[]{:S(2)}) collective-permute-start(bf16[4,2,128,1024]{3,2,1,0:T(8,128)(2,1)} %bitcast_dynamic-update-slice_fusion.5), channel_id=1, source_target_pairs={{2,0},{0,2},{3,1},{1,3},{6,4},{4,6},{7,5},{5,7},{10,8},{8,10},{11,... | collective-permute-start | bytes 6291464 | tf_op jit(solution)/shard_map/ppermute | solution.py:41
  199.5 82.6 %collective-permute-start.10 = (bf16[4,2,64,2048]{3,2,1,0:T(8,128)(2,1)}, bf16[4,2,64,2048]{3,2,1,0:T(8,128)(2,1)}, u32[]{:S(2)}, u32[]{:S(2)}) collective-permute-start(bf16[4,2,64,2048]{3,2,1,0:T(8,128)(2,1)} %bitcast_dynamic-update-slice_fusion.8), channel_id=1, source_target_pairs={{2,0},{0,2},{3,1},{1,3},{6,4},{4,6},{7,5},{5,7},{10,8},{8,10},{11,... | collective-permute-start | bytes 6291464 | tf_op jit(solution)/shard_map/ppermute | solution.py:41
  234.0 48.2 %collective-permute-start.15 = (bf16[2,256,1024]{2,1,0:T(8,128)(2,1)S(1)}, bf16[2,256,1024]{2,1,0:T(8,128)(2,1)}, u32[]{:S(2)}, u32[]{:S(2)}) collective-permute-start(bf16[2,256,1024]{2,1,0:T(8,128)(2,1)S(1)} %bitcast_dynamic-update-slice_fusion.4), channel_id=1, source_target_pairs={{1,0},{0,1},{3,2},{2,3},{5,4},{4,5},{7,6},{6,7},{9,8},{8,9},{11,10... | collective-permute-start | bytes 3145736 | tf_op jit(solution)/shard_map/ppermute | solution.py:41
  289.4 46.1 %collective-permute-start.17 = (bf16[2048,1024]{1,0:T(8,128)(2,1)}, bf16[2048,1024]{1,0:T(8,128)(2,1)}, u32[]{:S(2)}, u32[]{:S(2)}) collective-permute-start(bf16[2048,1024]{1,0:T(8,128)(2,1)} %bitcast.32), channel_id=1, source_target_pairs={{1,0},{0,1},{3,2},{2,3},{5,4},{4,5},{7,6},{6,7},{9,8},{8,9},{11,10... | collective-permute-start | bytes 12582920 | tf_op jit(solution)/shard_map/ppermute | solution.py:41
  296.6 34.2 %collective-permute-start.16 = (bf16[1024,2048]{1,0:T(8,128)(2,1)}, bf16[1024,2048]{1,0:T(8,128)(2,1)}, u32[]{:S(2)}, u32[]{:S(2)}) collective-permute-start(bf16[1024,2048]{1,0:T(8,128)(2,1)} %bitcast.30), channel_id=1, source_target_pairs={{1,0},{0,1},{3,2},{2,3},{5,4},{4,5},{7,6},{6,7},{9,8},{8,9},{11,10... | collective-permute-start | bytes 12582920 | tf_op jit(solution)/shard_map/ppermute | solution.py:41
  354.9 26.0 %collective-permute-start.23 = (bf16[2048,1024]{1,0:T(8,128)(2,1)}, bf16[2048,1024]{1,0:T(8,128)(2,1)}, u32[]{:S(2)}, u32[]{:S(2)}) collective-permute-start(bf16[2048,1024]{1,0:T(8,128)(2,1)} %convolution_convert_fusion.3), channel_id=1, source_target_pairs={{1,0},{0,1},{3,2},{2,3},{5,4},{4,5},{7,6},{6,7},{9,8},{8,9},{11,10... | collective-permute-start | bytes 12582920 | tf_op jit(solution)/shard_map/ppermute | solution.py:41
  356.8 24.1 %collective-permute-start.22 = (bf16[1024,512]{1,0:T(8,128)(2,1)S(1)}, bf16[1024,512]{1,0:T(8,128)(2,1)S(1)}, u32[]{:S(2)}, u32[]{:S(2)}) collective-permute-start(bf16[1024,512]{1,0:T(8,128)(2,1)S(1)} %convolution_convert_fusion.6), channel_id=1, source_target_pairs={{1,0},{0,1},{3,2},{2,3},{5,4},{4,5},{7,6},{6,7},{9,8},{8,9},{11,10... | collective-permute-start | bytes 3145736 | tf_op jit(solution)/shard_map/ppermute | solution.py:41
  385.3 27.7 %collective-permute-start.25 = (bf16[1024,2048]{1,0:T(8,128)(2,1)}, bf16[1024,2048]{1,0:T(8,128)(2,1)}, u32[]{:S(2)}, u32[]{:S(2)}) collective-permute-start(bf16[1024,2048]{1,0:T(8,128)(2,1)} %convolution_convert_fusion.2), channel_id=1, source_target_pairs={{1,0},{0,1},{3,2},{2,3},{5,4},{4,5},{7,6},{6,7},{9,8},{8,9},{11,10... | collective-permute-start | bytes 12582920 | tf_op jit(solution)/shard_map/ppermute | solution.py:41
  387.1 25.9 %collective-permute-start.24 = (bf16[2,2,4,32,512]{4,3,0,2,1:T(8,128)(2,1)S(1)}, bf16[2,2,4,32,512]{4,3,0,2,1:T(8,128)(2,1)S(1)}, u32[]{:S(2)}, u32[]{:S(2)}) collective-permute-start(bf16[2,2,4,32,512]{4,3,0,2,1:T(8,128)(2,1)S(1)} %bitcast.580), channel_id=1, source_target_pairs={{2,0},{0,2},{3,1},{1,3},{6,4},{4,6},{7,5},{5,7},{10,8},{8,10},{11,... | collective-permute-start | bytes 1572872 | tf_op jit(solution)/shard_map/ppermute | solution.py:41
  395.5 54.0 %collective-permute-start.27 = (bf16[4,2,128,512]{3,2,0,1:T(8,128)(2,1)}, bf16[4,2,128,512]{3,2,0,1:T(8,128)(2,1)}, u32[]{:S(2)}, u32[]{:S(2)}) collective-permute-start(bf16[4,2,128,512]{3,2,0,1:T(8,128)(2,1)} %bitcast.531), channel_id=1, source_target_pairs={{2,0},{0,2},{3,1},{1,3},{6,4},{4,6},{7,5},{5,7},{10,8},{8,10},{11,... | collective-permute-start | bytes 3145736 | tf_op jit(solution)/shard_map/ppermute | solution.py:41
  399.6 50.0 %collective-permute-start.28 = (bf16[4,2,128,512]{3,2,0,1:T(8,128)(2,1)}, bf16[4,2,128,512]{3,2,0,1:T(8,128)(2,1)}, u32[]{:S(2)}, u32[]{:S(2)}) collective-permute-start(bf16[4,2,128,512]{3,2,0,1:T(8,128)(2,1)} %bitcast.530), channel_id=1, source_target_pairs={{4,0},{0,4},{5,1},{1,5},{6,2},{2,6},{7,3},{3,7},{12,8},{8,12},{13,... | collective-permute-start | bytes 3145736 | tf_op jit(solution)/shard_map/ppermute | solution.py:41
  459.8 32.5 %collective-permute-start.37 = (bf16[1024,1536]{1,0:T(8,128)(2,1)S(1)}, bf16[1024,1536]{1,0:T(8,128)(2,1)S(1)}, u32[]{:S(2)}, u32[]{:S(2)}) collective-permute-start(bf16[1024,1536]{1,0:T(8,128)(2,1)S(1)} %convolution_convert_fusion.1), channel_id=1, source_target_pairs={{1,0},{0,1},{3,2},{2,3},{5,4},{4,5},{7,6},{6,7},{9,8},{8,9},{11,10... | collective-permute-start | bytes 9437192 | tf_op jit(solution)/shard_map/ppermute | solution.py:41
  463.2 17.9 %collective-permute-start.34 = (bf16[4,128,512]{2,1,0:T(8,128)(2,1)S(1)}, bf16[4,128,512]{2,1,0:T(8,128)(2,1)S(1)}, u32[]{:S(2)}, u32[]{:S(2)}) collective-permute-start(bf16[4,128,512]{2,1,0:T(8,128)(2,1)S(1)} %dynamic-slice_bitcast_fusion.8), channel_id=1, source_target_pairs={{4,0},{0,4},{5,1},{1,5},{6,2},{2,6},{7,3},{3,7},{12,8},{8,12},{13,... | collective-permute-start | bytes 1572872 | tf_op jit(solution)/shard_map/ppermute | solution.py:41
  466.2 15.3 %collective-permute-start.35 = (bf16[4,128,512]{2,1,0:T(8,128)(2,1)S(1)}, bf16[4,128,512]{2,1,0:T(8,128)(2,1)S(1)}, u32[]{:S(2)}, u32[]{:S(2)}) collective-permute-start(bf16[4,128,512]{2,1,0:T(8,128)(2,1)S(1)} %dynamic-slice_bitcast_fusion.7), channel_id=1, source_target_pairs={{2,0},{0,2},{3,1},{1,3},{6,4},{4,6},{7,5},{5,7},{10,8},{8,10},{11,... | collective-permute-start | bytes 1572872 | tf_op jit(solution)/shard_map/ppermute | solution.py:41
  467.8 24.5 %collective-permute-start.36 = (bf16[4,2,64,512]{3,2,1,0:T(8,128)(2,1)S(1)}, bf16[4,2,64,512]{3,2,1,0:T(8,128)(2,1)S(1)}, u32[]{:S(2)}, u32[]{:S(2)}) collective-permute-start(bf16[4,2,64,512]{3,2,1,0:T(8,128)(2,1)S(1)} %dynamic-slice_bitcast_fusion.6), channel_id=1, source_target_pairs={{2,0},{0,2},{3,1},{1,3},{6,4},{4,6},{7,5},{5,7},{10,8},{8,10},{11,... | collective-permute-start | bytes 1572872 | tf_op jit(solution)/shard_map/ppermute | solution.py:41
  480.4 26.2 %collective-permute-start.41 = (bf16[4,2,64,1024]{3,2,0,1:T(8,128)(2,1)S(1)}, bf16[4,2,64,1024]{3,2,0,1:T(8,128)(2,1)S(1)}, u32[]{:S(2)}, u32[]{:S(2)}) collective-permute-start(bf16[4,2,64,1024]{3,2,0,1:T(8,128)(2,1)S(1)} %bitcast.563), channel_id=1, source_target_pairs={{4,0},{0,4},{5,1},{1,5},{6,2},{2,6},{7,3},{3,7},{12,8},{8,12},{13,... | collective-permute-start | bytes 3145736 | tf_op jit(solution)/shard_map/ppermute | solution.py:41
  481.2 32.8 %collective-permute-start.42 = (bf16[4,2,64,1024]{3,2,1,0:T(8,128)(2,1)S(1)}, bf16[4,2,64,1024]{3,2,1,0:T(8,128)(2,1)S(1)}, u32[]{:S(2)}, u32[]{:S(2)}) collective-permute-start(bf16[4,2,64,1024]{3,2,1,0:T(8,128)(2,1)S(1)} %dynamic-slice_bitcast_fusion), channel_id=1, source_target_pairs={{2,0},{0,2},{3,1},{1,3},{6,4},{4,6},{7,5},{5,7},{10,8},{8,10},{11,... | collective-permute-start | bytes 3145736 | tf_op jit(solution)/shard_map/ppermute | solution.py:41
  492.7 24.8 %collective-permute-start.38 = (bf16[128,1024]{1,0:T(8,128)(2,1)S(1)}, bf16[128,1024]{1,0:T(8,128)(2,1)S(1)}, u32[]{:S(2)}, u32[]{:S(2)}) collective-permute-start(bf16[128,1024]{1,0:T(8,128)(2,1)S(1)} %get-tuple-element.321), channel_id=1, source_target_pairs={{24,0},{0,8},{8,16},{16,24},{25,1},{1,9},{9,17},{17,25},{26,2},{2,... | collective-permute-start | bytes 786440 | tf_op jit(solution)/shard_map/ppermute | solution.py:41
  492.8 24.8 %collective-permute-start.39 = (bf16[128,1024]{1,0:T(8,128)(2,1)S(1)}, bf16[128,1024]{1,0:T(8,128)(2,1)S(1)}, u32[]{:S(2)}, u32[]{:S(2)}) collective-permute-start(bf16[128,1024]{1,0:T(8,128)(2,1)S(1)} %get-tuple-element.322), channel_id=1, source_target_pairs={{16,0},{24,8},{0,16},{8,24},{17,1},{25,9},{1,17},{9,25},{18,2},{26... | collective-permute-start | bytes 786440 | tf_op jit(solution)/shard_map/ppermute | solution.py:41
  497.9 21.2 %collective-permute-start.43 = (bf16[1024,512]{1,0:T(8,128)(2,1)S(1)}, bf16[1024,512]{1,0:T(8,128)(2,1)S(1)}, u32[]{:S(2)}, u32[]{:S(2)}) collective-permute-start(bf16[1024,512]{1,0:T(8,128)(2,1)S(1)} %convolution_convert_fusion.4), channel_id=1, source_target_pairs={{1,0},{0,1},{3,2},{2,3},{5,4},{4,5},{7,6},{6,7},{9,8},{8,9},{11,10... | collective-permute-start | bytes 3145736 | tf_op jit(solution)/shard_map/ppermute | solution.py:41
  519.1 36.5 %collective-permute-start.50 = (bf16[4,2,64,768]{3,2,0,1:T(8,128)(2,1)}, bf16[4,2,64,768]{3,2,0,1:T(8,128)(2,1)}, u32[]{:S(2)}, u32[]{:S(2)}) collective-permute-start(bf16[4,2,64,768]{3,2,0,1:T(8,128)(2,1)} %bitcast.533), channel_id=1, source_target_pairs={{2,0},{0,2},{3,1},{1,3},{6,4},{4,6},{7,5},{5,7},{10,8},{8,10},{11,... | collective-permute-start | bytes 2359304 | tf_op jit(solution)/shard_map/ppermute | solution.py:41
  524.5 31.1 %collective-permute-start.51 = (bf16[4,2,64,768]{3,2,1,0:T(8,128)(2,1)}, bf16[4,2,64,768]{3,2,1,0:T(8,128)(2,1)}, u32[]{:S(2)}, u32[]{:S(2)}) collective-permute-start(bf16[4,2,64,768]{3,2,1,0:T(8,128)(2,1)} %dynamic-slice_bitcast_fusion.2), channel_id=1, source_target_pairs={{4,0},{0,4},{5,1},{1,5},{6,2},{2,6},{7,3},{3,7},{12,8},{8,12},{13,... | collective-permute-start | bytes 2359304 | tf_op jit(solution)/shard_map/ppermute | solution.py:41
  525.7 29.9 %collective-permute-start.47 = (bf16[4,64,1024]{2,1,0:T(8,128)(2,1)}, bf16[4,64,1024]{2,1,0:T(8,128)(2,1)}, u32[]{:S(2)}, u32[]{:S(2)}) collective-permute-start(bf16[4,64,1024]{2,1,0:T(8,128)(2,1)} %dynamic-slice_bitcast_fusion.5), channel_id=1, source_target_pairs={{2,0},{0,2},{3,1},{1,3},{6,4},{4,6},{7,5},{5,7},{10,8},{8,10},{11,... | collective-permute-start | bytes 1572872 | tf_op jit(solution)/shard_map/ppermute | solution.py:41
  527.4 29.0 %collective-permute-start.48 = (bf16[4,64,1024]{2,1,0:T(8,128)(2,1)}, bf16[4,64,1024]{2,1,0:T(8,128)(2,1)}, u32[]{:S(2)}, u32[]{:S(2)}) collective-permute-start(bf16[4,64,1024]{2,1,0:T(8,128)(2,1)} %dynamic-slice_bitcast_fusion.4), channel_id=1, source_target_pairs={{4,0},{0,4},{5,1},{1,5},{6,2},{2,6},{7,3},{3,7},{12,8},{8,12},{13,... | collective-permute-start | bytes 1572872 | tf_op jit(solution)/shard_map/ppermute | solution.py:41
  529.0 37.1 %collective-permute-start.52 = (bf16[4,2,64,512]{3,2,1,0:T(8,128)(2,1)}, bf16[4,2,64,512]{3,2,1,0:T(8,128)(2,1)}, u32[]{:S(2)}, u32[]{:S(2)}) collective-permute-start(bf16[4,2,64,512]{3,2,1,0:T(8,128)(2,1)} %dynamic-slice_bitcast_fusion.3), channel_id=1, source_target_pairs={{4,0},{0,4},{5,1},{1,5},{6,2},{2,6},{7,3},{3,7},{12,8},{8,12},{13,... | collective-permute-start | bytes 1572872 | tf_op jit(solution)/shard_map/ppermute | solution.py:41
  569.4 35.5 %collective-permute-start.53 = (bf16[1024,1536]{1,0:T(8,128)(2,1)S(1)}, bf16[1024,1536]{1,0:T(8,128)(2,1)S(1)}, u32[]{:S(2)}, u32[]{:S(2)}) collective-permute-start(bf16[1024,1536]{1,0:T(8,128)(2,1)S(1)} %convolution_convert_fusion), channel_id=1, source_target_pairs={{1,0},{0,1},{3,2},{2,3},{5,4},{4,5},{7,6},{6,7},{9,8},{8,9},{11,10... | collective-permute-start | bytes 9437192 | tf_op jit(solution)/shard_map/ppermute | solution.py:41
  569.6 21.8 %collective-permute-start.54 = (bf16[2,4,32,512]{3,2,1,0:T(8,128)(2,1)S(1)}, bf16[2,4,32,512]{3,2,1,0:T(8,128)(2,1)S(1)}, u32[]{:S(2)}, u32[]{:S(2)}) collective-permute-start(bf16[2,4,32,512]{3,2,1,0:T(8,128)(2,1)S(1)} %bitcast_dynamic-update-slice_fusion.22), channel_id=1, source_target_pairs={{4,0},{0,4},{5,1},{1,5},{6,2},{2,6},{7,3},{3,7},{12,8},{8,12},{13,... | collective-permute-start | bytes 786440 | tf_op jit(solution)/shard_map/ppermute | solution.py:41
  571.0 15.4 %collective-permute-start.55 = (bf16[64,512]{1,0:T(8,128)(2,1)S(1)}, bf16[64,512]{1,0:T(8,128)(2,1)S(1)}, u32[]{:S(2)}, u32[]{:S(2)}) collective-permute-start(bf16[64,512]{1,0:T(8,128)(2,1)S(1)} %get-tuple-element.357), channel_id=1, source_target_pairs={{24,0},{0,8},{8,16},{16,24},{25,1},{1,9},{9,17},{17,25},{26,2},{2,... | collective-permute-start | bytes 196616 | tf_op jit(solution)/shard_map/ppermute | solution.py:41
  572.2 15.0 %collective-permute-start.56 = (bf16[64,512]{1,0:T(8,128)(2,1)S(1)}, bf16[64,512]{1,0:T(8,128)(2,1)S(1)}, u32[]{:S(2)}, u32[]{:S(2)}) collective-permute-start(bf16[64,512]{1,0:T(8,128)(2,1)S(1)} %get-tuple-element.356), channel_id=1, source_target_pairs={{16,0},{24,8},{0,16},{8,24},{17,1},{25,9},{1,17},{9,25},{18,2},{26... | collective-permute-start | bytes 196616 | tf_op jit(solution)/shard_map/ppermute | solution.py:41
  573.5 15.5 %collective-permute-start.57 = (bf16[64,512]{1,0:T(8,128)(2,1)S(1)}, bf16[64,512]{1,0:T(8,128)(2,1)S(1)}, u32[]{:S(2)}, u32[]{:S(2)}) collective-permute-start(bf16[64,512]{1,0:T(8,128)(2,1)S(1)} %get-tuple-element.355), channel_id=1, source_target_pairs={{8,0},{16,8},{24,16},{0,24},{9,1},{17,9},{25,17},{1,25},{10,2},{18... | collective-permute-start | bytes 196616 | tf_op jit(solution)/shard_map/ppermute | solution.py:41
  586.4 18.5 %collective-permute-start.58 = (bf16[4,64,768]{2,1,0:T(8,128)(2,1)S(1)}, bf16[4,64,768]{2,1,0:T(8,128)(2,1)S(1)}, u32[]{:S(2)}, u32[]{:S(2)}) collective-permute-start(bf16[4,64,768]{2,1,0:T(8,128)(2,1)S(1)} %dynamic-slice_bitcast_fusion.12), channel_id=1, source_target_pairs={{4,0},{0,4},{5,1},{1,5},{6,2},{2,6},{7,3},{3,7},{12,8},{8,12},{13,... | collective-permute-start | bytes 1179656 | tf_op jit(solution)/shard_map/ppermute | solution.py:41
  587.2 17.7 %collective-permute-start.59 = (bf16[4,64,768]{2,1,0:T(8,128)(2,1)S(1)}, bf16[4,64,768]{2,1,0:T(8,128)(2,1)S(1)}, u32[]{:S(2)}, u32[]{:S(2)}) collective-permute-start(bf16[4,64,768]{2,1,0:T(8,128)(2,1)S(1)} %dynamic-slice_bitcast_fusion.11), channel_id=1, source_target_pairs={{2,0},{0,2},{3,1},{1,3},{6,4},{4,6},{7,5},{5,7},{10,8},{8,10},{11,... | collective-permute-start | bytes 1179656 | tf_op jit(solution)/shard_map/ppermute | solution.py:41
  589.0 14.2 %collective-permute-start.60 = (bf16[4,64,512]{2,1,0:T(8,128)(2,1)S(1)}, bf16[4,64,512]{2,1,0:T(8,128)(2,1)S(1)}, u32[]{:S(2)}, u32[]{:S(2)}) collective-permute-start(bf16[4,64,512]{2,1,0:T(8,128)(2,1)S(1)} %dynamic-slice_bitcast_fusion.17), channel_id=1, source_target_pairs={{2,0},{0,2},{3,1},{1,3},{6,4},{4,6},{7,5},{5,7},{10,8},{8,10},{11,... | collective-permute-start | bytes 786440 | tf_op jit(solution)/shard_map/ppermute | solution.py:41
  591.4 49.8 %collective-permute-start.65 = (bf16[64,2048]{1,0:T(8,128)(2,1)}, bf16[64,2048]{1,0:T(8,128)(2,1)}, u32[]{:S(2)}, u32[]{:S(2)}) collective-permute-start(bf16[64,2048]{1,0:T(8,128)(2,1)} %get-tuple-element.318), channel_id=1, source_target_pairs={{24,0},{0,8},{8,16},{16,24},{25,1},{1,9},{9,17},{17,25},{26,2},{2,... | collective-permute-start | bytes 786440 | tf_op jit(solution)/shard_map/ppermute | solution.py:41
  603.1 38.5 %collective-permute-start.66 = (bf16[64,2048]{1,0:T(8,128)(2,1)}, bf16[64,2048]{1,0:T(8,128)(2,1)}, u32[]{:S(2)}, u32[]{:S(2)}) collective-permute-start(bf16[64,2048]{1,0:T(8,128)(2,1)} %get-tuple-element.319), channel_id=1, source_target_pairs={{16,0},{24,8},{0,16},{8,24},{17,1},{25,9},{1,17},{9,25},{18,2},{26... | collective-permute-start | bytes 786440 | tf_op jit(solution)/shard_map/ppermute | solution.py:41
  608.8 40.5 %collective-permute-start.61 = (bf16[1024,512]{1,0:T(8,128)(2,1)}, bf16[1024,512]{1,0:T(8,128)(2,1)}, u32[]{:S(2)}, u32[]{:S(2)}) collective-permute-start(bf16[1024,512]{1,0:T(8,128)(2,1)} %fusion.65), channel_id=1, source_target_pairs={{1,0},{0,1},{3,2},{2,3},{5,4},{4,5},{7,6},{6,7},{9,8},{8,9},{11,10... | collective-permute-start | bytes 3145736 | tf_op jit(solution)/shard_map/ppermute | solution.py:41
  614.8 20.3 %collective-permute-start.76 = (bf16[4,2,64,768]{3,2,0,1:T(8,128)(2,1)}, bf16[4,2,64,768]{3,2,0,1:T(8,128)(2,1)}, u32[]{:S(2)}, u32[]{:S(2)}) collective-permute-start(bf16[4,2,64,768]{3,2,0,1:T(8,128)(2,1)} %bitcast.532), channel_id=1, source_target_pairs={{4,0},{0,4},{5,1},{1,5},{6,2},{2,6},{7,3},{3,7},{12,8},{8,12},{13,... | collective-permute-start | bytes 2359304 | tf_op jit(solution)/shard_map/ppermute | solution.py:41
  617.0 20.0 %collective-permute-start.77 = (bf16[4,2,64,768]{3,2,1,0:T(8,128)(2,1)}, bf16[4,2,64,768]{3,2,1,0:T(8,128)(2,1)}, u32[]{:S(2)}, u32[]{:S(2)}) collective-permute-start(bf16[4,2,64,768]{3,2,1,0:T(8,128)(2,1)} %dynamic-slice_bitcast_fusion.1), channel_id=1, source_target_pairs={{2,0},{0,2},{3,1},{1,3},{6,4},{4,6},{7,5},{5,7},{10,8},{8,10},{11,... | collective-permute-start | bytes 2359304 | tf_op jit(solution)/shard_map/ppermute | solution.py:41
  643.2 26.8 %collective-permute-start.70 = (bf16[64,1536]{1,0:T(8,128)(2,1)}, bf16[64,1536]{1,0:T(8,128)(2,1)}, u32[]{:S(2)}, u32[]{:S(2)}) collective-permute-start(bf16[64,1536]{1,0:T(8,128)(2,1)} %get-tuple-element.335), channel_id=1, source_target_pairs={{24,0},{0,8},{8,16},{16,24},{25,1},{1,9},{9,17},{17,25},{26,2},{2,... | collective-permute-start | bytes 589832 | tf_op jit(solution)/shard_map/ppermute | solution.py:41
  643.5 21.9 %collective-permute-start.73 = (bf16[64,512]{1,0:T(8,128)(2,1)}, bf16[64,512]{1,0:T(8,128)(2,1)}, u32[]{:S(2)}, u32[]{:S(2)}) collective-permute-start(bf16[64,512]{1,0:T(8,128)(2,1)} %get-tuple-element.354), channel_id=1, source_target_pairs={{24,0},{0,8},{8,16},{16,24},{25,1},{1,9},{9,17},{17,25},{26,2},{2,... | collective-permute-start | bytes 196616 | tf_op jit(solution)/shard_map/ppermute | solution.py:41
  645.0 20.6 %collective-permute-start.74 = (bf16[64,512]{1,0:T(8,128)(2,1)}, bf16[64,512]{1,0:T(8,128)(2,1)}, u32[]{:S(2)}, u32[]{:S(2)}) collective-permute-start(bf16[64,512]{1,0:T(8,128)(2,1)} %get-tuple-element.353), channel_id=1, source_target_pairs={{16,0},{24,8},{0,16},{8,24},{17,1},{25,9},{1,17},{9,25},{18,2},{26... | collective-permute-start | bytes 196616 | tf_op jit(solution)/shard_map/ppermute | solution.py:41
  647.6 12.8 %collective-permute-start.78 = (bf16[4,64,768]{2,1,0:T(8,128)(2,1)}, bf16[4,64,768]{2,1,0:T(8,128)(2,1)}, u32[]{:S(2)}, u32[]{:S(2)}) collective-permute-start(bf16[4,64,768]{2,1,0:T(8,128)(2,1)} %dynamic-slice_bitcast_fusion.10), channel_id=1, source_target_pairs={{2,0},{0,2},{3,1},{1,3},{6,4},{4,6},{7,5},{5,7},{10,8},{8,10},{11,... | collective-permute-start | bytes 1179656 | tf_op jit(solution)/shard_map/ppermute | solution.py:41
  649.4 13.2 %collective-permute-start.79 = (bf16[4,64,768]{2,1,0:T(8,128)(2,1)}, bf16[4,64,768]{2,1,0:T(8,128)(2,1)}, u32[]{:S(2)}, u32[]{:S(2)}) collective-permute-start(bf16[4,64,768]{2,1,0:T(8,128)(2,1)} %dynamic-slice_bitcast_fusion.9), channel_id=1, source_target_pairs={{4,0},{0,4},{5,1},{1,5},{6,2},{2,6},{7,3},{3,7},{12,8},{8,12},{13,... | collective-permute-start | bytes 1179656 | tf_op jit(solution)/shard_map/ppermute | solution.py:41
  662.5 18.5 %collective-permute-start.68 = (bf16[2,2,4,32,512]{4,3,0,2,1:T(8,128)(2,1)}, bf16[2,2,4,32,512]{4,3,0,2,1:T(8,128)(2,1)S(1)}, u32[]{:S(2)}, u32[]{:S(2)}) collective-permute-start(bf16[2,2,4,32,512]{4,3,0,2,1:T(8,128)(2,1)} %bitcast.579), channel_id=1, source_target_pairs={{2,0},{0,2},{3,1},{1,3},{6,4},{4,6},{7,5},{5,7},{10,8},{8,10},{11,... | collective-permute-start | bytes 1572872 | tf_op jit(solution)/shard_map/ppermute | solution.py:41
  667.8 13.2 %collective-permute-start.69 = (f32[5,1024]{1,0:T(8,128)S(1)}, f32[5,1024]{1,0:T(8,128)S(1)}, u32[]{:S(2)}, u32[]{:S(2)}) collective-permute-start(f32[5,1024]{1,0:T(8,128)S(1)} %add.947), channel_id=1, source_target_pairs={{2,0},{0,2},{3,1},{1,3},{6,4},{4,6},{7,5},{5,7},{10,8},{8,10},{11,... | collective-permute-start | bytes 61448 | tf_op jit(solution)/shard_map/ppermute | solution.py:41
  670.0 17.3 %collective-permute-start.85 = (f32[32,2048]{1,0:T(8,128)S(1)}, f32[32,2048]{1,0:T(8,128)S(1)}, u32[]{:S(2)}, u32[]{:S(2)}) collective-permute-start(f32[32,2048]{1,0:T(8,128)S(1)} %copy-done.72), channel_id=1, source_target_pairs={{1,0},{0,1},{3,2},{2,3},{5,4},{4,5},{7,6},{6,7},{9,8},{8,9},{11,10... | collective-permute-start | bytes 786440 | tf_op jit(solution)/shard_map/ppermute | solution.py:41
  676.0 12.7 %collective-permute-start.80 = (bf16[64,1536]{1,0:T(8,128)(2,1)S(1)}, bf16[64,1536]{1,0:T(8,128)(2,1)S(1)}, u32[]{:S(2)}, u32[]{:S(2)}) collective-permute-start(bf16[64,1536]{1,0:T(8,128)(2,1)S(1)} %get-tuple-element.332), channel_id=1, source_target_pairs={{24,0},{0,8},{8,16},{16,24},{25,1},{1,9},{9,17},{17,25},{26,2},{2,... | collective-permute-start | bytes 589832 | tf_op jit(solution)/shard_map/ppermute | solution.py:41
  677.6 15.0 %collective-permute-start.81 = (bf16[64,1536]{1,0:T(8,128)(2,1)}, bf16[64,1536]{1,0:T(8,128)(2,1)}, u32[]{:S(2)}, u32[]{:S(2)}) collective-permute-start(bf16[64,1536]{1,0:T(8,128)(2,1)} %get-tuple-element.333), channel_id=1, source_target_pairs={{16,0},{24,8},{0,16},{8,24},{17,1},{25,9},{1,17},{9,25},{18,2},{26... | collective-permute-start | bytes 589832 | tf_op jit(solution)/shard_map/ppermute | solution.py:41
  706.8 16.0 %collective-permute-start.96 = (bf16[2,32,512]{2,1,0:T(8,128)(2,1)S(1)}, bf16[2,32,512]{2,1,0:T(8,128)(2,1)S(1)}, u32[]{:S(2)}, u32[]{:S(2)}) collective-permute-start(bf16[2,32,512]{2,1,0:T(8,128)(2,1)S(1)} %get-tuple-element.345), channel_id=1, source_target_pairs={{8,0},{16,8},{24,16},{0,24},{9,1},{17,9},{25,17},{1,25},{10,2},{18... | collective-permute-start | bytes 196616 | tf_op jit(solution)/shard_map/ppermute | solution.py:41
  709.4 13.4 %collective-permute-start.97 = (bf16[2,32,512]{2,1,0:T(8,128)(2,1)S(1)}, bf16[2,32,512]{2,1,0:T(8,128)(2,1)S(1)}, u32[]{:S(2)}, u32[]{:S(2)}) collective-permute-start(bf16[2,32,512]{2,1,0:T(8,128)(2,1)S(1)} %get-tuple-element.345), channel_id=1, source_target_pairs={{16,0},{24,8},{0,16},{8,24},{17,1},{25,9},{1,17},{9,25},{18,2},{26... | collective-permute-start | bytes 196616 | tf_op jit(solution)/shard_map/ppermute | solution.py:41
  709.6 13.2 %collective-permute-start.98 = (bf16[2,32,512]{2,1,0:T(8,128)(2,1)S(1)}, bf16[2,32,512]{2,1,0:T(8,128)(2,1)}, u32[]{:S(2)}, u32[]{:S(2)}) collective-permute-start(bf16[2,32,512]{2,1,0:T(8,128)(2,1)S(1)} %get-tuple-element.345), channel_id=1, source_target_pairs={{24,0},{0,8},{8,16},{16,24},{25,1},{1,9},{9,17},{17,25},{26,2},{2,... | collective-permute-start | bytes 196616 | tf_op jit(solution)/shard_map/ppermute | solution.py:41
  (177 other events, 1597.2 us)
Sparse Core Ops, SparseCore 0:
  14.6 191.6 all-gather.1

commit v6 on v5

--- a/solution.py
+++ b/solution.py
@@ -105,13 +105,48 @@
     return value
 
 
-def gather_half(part):
-    for axis, dim in (("r", 0), ("z", 0), ("m", 2)):
-        others = yield sent_around(part, axis)
-        part = placed(part, others, axis, dim)
-    own = part.reshape(-1, part.shape[-1])
+def split_columns(array):
+    cut = array.shape[-1] // (2 * LANES) * LANES
+    return array[..., :cut], array[..., cut:]
+
+
+def gather_deep(part):
+    if lax.axis_size("z") != 4:
+        others = yield sent_around(part, "z")
+        return placed(part, others, "z", 0)
+    above, below = yield [shifted(part, "z", 1), shifted(part, "z", 3)]
+    first, second = split_columns(above)[0], split_columns(below)[1]
+    first, second = yield [shifted(first, "z", 1), shifted(second, "z", 3)]
+    mine = lax.axis_index("z")
+    whole = jnp.broadcast_to(part[None], (4,) + part.shape)
+    whole = lax.dynamic_update_index_in_dim(whole, above, (mine + 1) % 4, 0)
+    whole = lax.dynamic_update_index_in_dim(whole, below, (mine + 3) % 4, 0)
+    zero = jnp.int32(0)
+    place = [(mine + 2) % 4] + [zero] * part.ndim
+    whole = lax.dynamic_update_slice(whole, first[None], place)
+    place[-1] = jnp.int32(first.shape[-1])
+    return lax.dynamic_update_slice(whole, second[None], place)
+
+
+def gather_flat(part, dim):
+    first, second = split_columns(part)
+    one, two = yield (sent_around(first, "m"), sent_around(second, "r"))
+    first, second = placed(first, one, "m", dim), placed(second, two, "r", dim)
+    one, two = yield (sent_around(first, "r"), sent_around(second, "m"))
+    first, second = placed(first, one, "r", dim), placed(second, two, "m", dim + 1)
+    return jnp.concatenate([first, second], axis=-1)
+
+
+def exchanged(own):
+    own = own.reshape(-1, own.shape[-1])
     (other,) = yield [shifted(own, "h", 1)]
     return (own, other)
+
+
+def gather_half(part):
+    whole = yield from gather_deep(part)
+    whole = yield from gather_flat(whole, 1)
+    return (yield from exchanged(whole))
 
 
 def gather_table(part):
@@ -173,6 +208,11 @@
     return added(total, dim, order[2], pieces)
 
 
+def squares(total):
+    total = total.reshape(-1, total.shape[-1] // LANES, LANES)
+    return jnp.sum(total * total, axis=(0, 1))
+
+
 def swap_rows(total, square=None):
     seen = total.reshape(2, -1, total.shape[-1])
     half = lax.axis_index("h")
@@ -191,7 +231,7 @@
 def reduce_layer(other, own, order, block=None, parts=1):
     total = yield from reduce_rows(other, own, ("z", "r", "m"), order, parts)
     total = total.reshape(-1, total.shape[-1])
-    mine, other = yield from swap_rows(total, jnp.sum(total * total))
+    mine, other = yield from swap_rows(total, squares(total))
     if block is None:
         return in_order(mine, other, 1)
     rows = mine.shape[0]
@@ -202,13 +242,13 @@
 def reduce_owned(other, own, order, parts):
     total = yield from reduce_rows(other, own, ("z", "r", "m"), order, parts)
     total = total.reshape(-1, total.shape[-1])
-    yield Squared(jnp.sum(total * total), [])
+    yield Squared(squares(total), [])
     return total
 
 
 def reduce_table(other, own):
     total = yield from reduce_rows(other, own, ("m", "h", "r", "z"), ("m", "r", "z"))
-    square = jnp.sum(total * total)
+    square = squares(total)
     total = total.astype(LOW)
     others = yield Squared(square, sent_around(total, "z"))
     total = placed(total, others, "z", 1)
@@ -449,6 +489,7 @@
     down_job = Job(gather_half(contract.astype(LOW)))
     in_table_job = Job(gather_table(low_in))
     token = advance(jnp.zeros((), WIDE), up_job, down_job)
+    token = advance(token, in_table_job, up_job, down_job)
     token = advance(token, in_table_job, up_job)
     table_in = in_table_job.finish()
     code_ids = jnp.arange(table_in.shape[0])
@@ -458,9 +499,9 @@
 
     space_codes = own_frames(codes).reshape(-1)
     picked = dot_nn((space_codes[:, None] == code_ids[None, :]).astype(LOW), table_in)
-    token = advance(token, down_job)
+    token = advance(token, down_job, up_job)
     out_table_job = Job(gather_table(low_out))
-    token = advance(token, up_job)
+    token = advance(token, down_job, up_job)
     picked, token = lax.optimization_barrier((picked, token))
     gathered = advance(gathered, out_table_job)
     first_in, first_out, turned, next_in, next_out = (
@@ -493,7 +534,7 @@
     after_space = start + dot_nn(mixed_space, w_out[0])
     after_space = swap_slots(after_space.reshape(frames, SLOTS, D)).reshape(-1, D)
     normed_time = norm_forward(after_space, gain_all[1]).astype(LOW)
-    normed_time = advance(normed_time, up_job, down_job, out_table_job)
+    normed_time = advance(normed_time, out_table_job)
     table_out = out_table_job.finish()
     packed_time = dot_nn(normed_time, w_in[1]).astype(LOW).reshape(FRAMES, -1, 3 * D)
     mixed_time = attention("time", half, packed_time).reshape(-1, D)
@@ -549,13 +590,13 @@
     inward, gain_one = norm_backward(after_space, gain_all[1], grad_normed)
     grad_space = swap_frames((grad_time + inward).reshape(FRAMES, -1, D)).reshape(-1, D)
     up_low = grad_space.astype(LOW)
-    up_low = advance(up_low, head_job, contract_job, out_job, in_job)
+    up_low = advance(up_low, head_job, contract_job, in_job)
     first_out_job = product(reduce_layer, mixed_space, *halves(up_low, 1), ("r", "m", "z"))
     grad_mixed = dot_nt(up_low, w_out[0]).astype(LOW)
-    grad_mixed = advance(grad_mixed, contract_job, expand_job, first_out_job)
+    grad_mixed = advance(grad_mixed, contract_job, expand_job, out_job, first_out_job)
     grad_packed = attention("space", small, packed_space, grad_mixed)
     grad_packed = advance(
-        grad_packed, head_job, expand_job, out_job, in_job, first_out_job
+        grad_packed, head_job, expand_job, out_job, in_job
     )
     first_in_job = product(
         reduce_layer, normed_space, *halves(grad_packed, 1), ("r", "m", "z"), None, 2
@@ -572,12 +613,12 @@
     gain_grads = jnp.stack([gain_zero, gain_one, gain_two, gain_three, mask_grad])
     gain_job = Job(sum_over(gain_grads, ("h", "m", "r", "z")))
     token = jnp.zeros((), WIDE)
-    token = advance(token, embed_job, gain_job, head_job, out_job, expand_job)
+    token = advance(token, embed_job, gain_job, head_job, out_job, expand_job, first_out_job)
     token = advance(token, first_in_job)
     token = advance(token, embed_job, gain_job, in_job, first_out_job)
     token = advance(token, first_in_job)
-    token = advance(token, embed_job, gain_job, expand_job)
-    token = advance(token, first_in_job, embed_job, gain_job, in_job, first_out_job)
+    token = advance(token, embed_job, gain_job, expand_job, in_job, first_out_job)
+    token = advance(token, first_in_job, embed_job, gain_job, first_out_job)
 
     owner = jnp.int32(0)
     for axis in ALL:
@@ -586,13 +627,15 @@
     gain_grads = lax.dynamic_slice_in_dim(gain_job.finish(), owner * width, width, 1)
     jobs = (in_job, first_in_job, out_job, first_out_job, expand_job, contract_job)
     jobs = jobs + (embed_job, head_job)
-    owned = sum(job.square for job in jobs) + jnp.sum(gain_grads * gain_grads)
-    sums = jnp.stack([owned, loss_part]).reshape(1, 2)
+    lane = jnp.arange(LANES)
+    small_square = jnp.pad(jnp.sum(gain_grads * gain_grads, axis=0), (0, LANES - width))
+    owned = sum(job.square for job in jobs) + small_square
+    sums = jnp.stack([owned, jnp.where(lane == 0, loss_part, 0.0)])
     norm_job = Job(sum_over(sums, ("h", "m", "r", "z")))
     while norm_job.flight is not None:
         token = advance(token, norm_job, *jobs)
     results = [(job.finish(), None) for job in jobs]
-    square_sum, loss = norm_job.result[0, 0], norm_job.result[0, 1]
+    square_sum, loss = jnp.sum(norm_job.result, axis=1)
     norm = jnp.sqrt(square_sum)
     factor = jnp.minimum(1.0, CLIP / (norm + 1e-06))
 

time: 781 us -> 712 us (0.912)
  waiting for transfers between devices: 275 us -> 210 us
  starting transfers between devices: 119 us -> 132 us
  local copies, waits for them, and re-layouts: 77.1 us -> 68.5 us
    ppermute x106 -> x112, waiting for transfers between devices: 272 us -> 210 us  [shifted(): return lax.ppermute(part, axis, [((i + shift) % n, i) for i in range(n)])]
    ppermute x106 -> x112, starting transfers between devices: 119 us -> 132 us  [shifted(): return lax.ppermute(part, axis, [((i + shift) % n, i) for i in range(n)])]
    dynamic_update_slice x32 -> x30, local copies, waits for them, and re-layouts: 17.7 us -> 9.81 us  [placed(): lax.dynamic_update_index_in_dim(whole, other, (mine + shift) % n, dim)]
    unnamed x284 -> x306, local copies, waits for them, and re-layouts: 17.1 us -> 23.6 us
  transfers between devices with their start and end apart: 107 -> 113, of which waited for: 34 -> 39; matrix products, arithmetic and copies ran while one was open for 28% -> 29% of each run, Pallas kernels for 8% -> 8%
where the time goes in v6:
time: 712 us; the launch traced here: 703 us
  waiting for transfers between devices  210 us (29%)
  matrix products  135 us (19%)
  starting transfers between devices  132 us (19%)
  other arithmetic  75.4 us (11%)
  local copies, waits for them, and re-layouts  68.5 us (10%)
  Pallas kernels  63 us (9%)
  between operations  19.3 us (3%)
    ppermute x112, waiting for transfers between devices, shifted(): return lax.ppermute(part, axis, [((i + shift) % n, i) for i in range(n)])  210 us
    ppermute x112, starting transfers between devices, shifted(): return lax.ppermute(part, axis, [((i + shift) % n, i) for i in range(n)])  132 us
    pallas_call x4, Pallas kernels, attention(): pl.pallas_call(functools.partial(body, kind), out_shape=jax.ShapeDtypeStr...  63 us
    dot_general x10, matrix products, dot_nn(): return jnp.dot(left, right, preferred_element_type=WIDE)  48.8 us
    dot_general x9, matrix products, dot_nt(): lax.dot_general(left, right, (((1,), (1,)), ((), ())), preferred_element_...  46.5 us
    dot_general x16, matrix products, dot_tn(): lax.dot_general(left, right, (((0,), (0,)), ((), ())), preferred_element_...  40.1 us
    unnamed x306, local copies, waits for them, and re-layouts  23.6 us
    convert_element_type x24, other arithmetic, reduce_rows(): added(*each, arrived).astype(LOW)  17.4 us
  transfers between devices with their start and end apart: 113, of which 39 were waited for; matrix products, arithmetic and copies ran while one was open for 29% of the time, Pallas kernels for 8%

profile of v6, /device:TPU:0, one launch (start us, length us, event | category | flops | bytes accessed | tf_op | source)
XLA Modules:
  0.0 703.3 jit_solution(9043893502663083625)
XLA Ops:
  14.5 5.1 collective-permute-start.3
  29.9 3.9 collective-permute-start.25
  36.1 4.5 collective-permute-done.26
  40.7 4.2 collective-permute-start.5
  46.9 3.9 collective-permute-start.7
  50.9 13.9 %collective-permute-done.7 = bf16[128,512]{1,0:T(8,128)(2,1)S(1)} collective-permute-done((bf16[128,512]{1,0:T(8,128)(2,1)S(1)}, bf16[128,512]{1,0:T(8,128)(2,1)S(1)}, u32[]{:S(2)}, u32[]{:S(2)}) %collective-permute-start.7) | collective-permute-done | bytes 131104 | tf_op jit(solution)/shard_map/ppermute | solution.py:41
  66.0 3.7 collective-permute-done.8
  74.3 12.7 %collective-permute-done.10 = bf16[64,1024]{1,0:T(8,128)(2,1)S(1)} collective-permute-done((bf16[64,1024]{1,0:T(8,128)(2,1)S(1)}, bf16[64,1024]{1,0:T(8,128)(2,1)S(1)}, u32[]{:S(2)}, u32[]{:S(2)}) %collective-permute-start.10) | collective-permute-done | bytes 131104 | tf_op jit(solution)/shard_map/ppermute | solution.py:41
  91.5 15.4 %collective-permute-done.14 = bf16[4,128,512]{2,1,0:T(8,128)(2,1)} collective-permute-done((bf16[4,128,512]{2,1,0:T(8,128)(2,1)S(1)}, bf16[4,128,512]{2,1,0:T(8,128)(2,1)}, u32[]{:S(2)}, u32[]{:S(2)}) %collective-permute-start.14) | collective-permute-done | bytes 524320 | tf_op jit(solution)/shard_map/ppermute | solution.py:41
  108.9 18.9 %collective-permute-done.16 = bf16[4,64,1024]{2,1,0:T(8,128)(2,1)} collective-permute-done((bf16[4,64,1024]{2,1,0:T(8,128)(2,1)S(1)}, bf16[4,64,1024]{2,1,0:T(8,128)(2,1)}, u32[]{:S(2)}, u32[]{:S(2)}) %collective-permute-start.16) | collective-permute-done | bytes 524320 | tf_op jit(solution)/shard_map/ppermute | solution.py:41
  131.6 2.7 collective-permute-start.18
  142.1 24.9 %collective-permute-done.18 = bf16[4,2,128,512]{3,2,1,0:T(8,128)(2,1)S(1)} collective-permute-done((bf16[4,2,128,512]{3,2,1,0:T(8,128)(2,1)S(1)}, bf16[4,2,128,512]{3,2,1,0:T(8,128)(2,1)S(1)}, u32[]{:S(2)}, u32[]{:S(2)}) %collective-permute-start.18) | collective-permute-done | bytes 1048608 | tf_op jit(solution)/shard_map/ppermute | solution.py:41
  167.0 21.3 %collective-permute-done.20 = bf16[4,2,64,1024]{3,2,1,0:T(8,128)(2,1)S(1)} collective-permute-done((bf16[4,2,64,1024]{3,2,1,0:T(8,128)(2,1)S(1)}, bf16[4,2,64,1024]{3,2,1,0:T(8,128)(2,1)S(1)}, u32[]{:S(2)}, u32[]{:S(2)}) %collective-permute-start.20) | collective-permute-done | bytes 1048608 | tf_op jit(solution)/shard_map/ppermute | solution.py:41
  195.8 8.0 %fusion.8.packed_ref = bf16[512,3072]{1,0:T(8,128)(2,1)} fusion(bf16[512,1024]{1,0:T(8,128)(2,1)S(1)} %multiply_convert_fusion.5, bf16[1024,8320]{1,0:T(8,128)(2,1)} %all-gather.2.cloned.1.call-done), kind=kOutput, calls=%fused_computation.16 | convolution fusion | flops 3222798336 | bytes 10485760 | tf_op jit(solution)/shard_map/dot_general | solution.py:299
  203.8 9.3 %shard_map.365 = bf16[512,1024]{1,0:T(8,128)(2,1)} custom-call(s32[1]{0:T(128)} %bitcast.13.scalar_ref, bf16[512,3072]{1,0:T(8,128)(2,1)} %fusion.8.packed_ref), custom_call_target="tpu_custom_call" | custom-call | flops 8999999488 | bytes 8388608 | tf_op jit(solution)/shard_map/pallas_call | solution.py:392
  213.1 3.2 fusion.60
  217.9 4.1 pad_maximum_fusion
  226.7 2.5 pad_maximum_fusion.1
  230.9 8.0 %fusion.11 = bf16[512,3072]{1,0:T(8,128)(2,1)} fusion(bf16[512,1024]{1,0:T(8,128)(2,1)S(1)} %fusion.34, bf16[1024,8320]{1,0:T(8,128)(2,1)} %all-gather.2.cloned.1.call-done), kind=kOutput, calls=%fused_computation.17 | convolution fusion | flops 3222798336 | bytes 10485760 | tf_op jit(solution)/shard_map/dot_general | solution.py:299
  238.9 8.9 %shard_map.366 = bf16[4,128,1024]{2,1,0:T(8,128)(2,1)} custom-call(s32[1]{0:T(128)} %bitcast.18.scalar_ref, bf16[4,128,3072]{2,1,0:T(8,128)(2,1)} %bitcast.621), custom_call_target="tpu_custom_call" | custom-call | flops 8999999488 | bytes 8388608 | tf_op jit(solution)/shard_map/pallas_call | solution.py:392
  247.8 3.3 multiply_reduce_fusion.8
  251.4 5.4 fusion.214
  256.8 6.0 fusion.215
  262.8 6.4 fusion.185
  269.3 5.2 multiply_reduce_fusion.7
  284.6 4.9 convolution_convert_fusion.3
  295.8 6.2 fusion.184
  302.0 8.1 %fusion.20 = bf16[512,2048]{1,0:T(8,128)(2,1)} fusion(f32[512,2048]{1,0:T(8,128)S(1)} %copy-done.139, bf16[512,1024]{1,0:T(8,128)(2,1)S(1)} %copy-done.55, bf16[2048,1024]{1,0:T(8,128)(2,1)} %bitcast.40), kind=kOutput, calls=%fused_computation.24 | convolution fusion | flops 2168455168 | bytes 11534336 | tf_op jit(solution)/shard_map/dot_general | solution.py:291
  310.1 7.2 %fusion.27 = bf16[512,2048]{1,0:T(8,128)(2,1)S(1)} fusion(f32[512,2048]{1,0:T(8,128)S(1)} %copy-done.142, bf16[512,1024]{1,0:T(8,128)(2,1)S(1)} %copy-done.55, bf16[2048,1024]{1,0:T(8,128)(2,1)} %collective-permute-done.23), kind=kOutput, calls=%fused_computation.31 | convolution fusion | flops 2168455168 | bytes 11534336 | tf_op jit(solution)/shard_map/dot_general | solution.py:291
  317.3 4.4 convolution_convert_fusion.2
  323.5 6.3 add_convert_fusion.1
  337.2 4.6 fusion.216
  341.8 5.1 multiply_reduce_fusion.2
  349.3 4.4 fusion.69
  355.4 22.0 %shard_map.367 = bf16[4,128,3072]{2,1,0:T(8,128)(2,1)} custom-call(s32[1]{0:T(128)} %bitcast.18.scalar_ref, bf16[4,128,3072]{2,1,0:T(8,128)(2,1)} %bitcast.622, bf16[4,128,1024]{2,1,0:T(8,128)(2,1)} %bitcast.629), custom_call_target="tpu_custom_call" | custom-call | flops 22000001024 | bytes 8388608 | tf_op jit(solution)/shard_map/pallas_call | solution.py:392
  380.3 5.2 add_convert_fusion
  392.1 6.3 fusion.40
  407.6 2.6 collective-permute-start.39
  414.0 2.6 collective-permute-done.40
  427.2 11.0 %collective-permute-done.46 = bf16[4,2,64,1024]{3,2,0,1:T(8,128)(2,1)S(1)} collective-permute-done((bf16[4,2,64,1024]{3,2,0,1:T(8,128)(2,1)S(1)}, bf16[4,2,64,1024]{3,2,0,1:T(8,128)(2,1)S(1)}, u32[]{:S(2)}, u32[]{:S(2)}) %collective-permute-start.46) | collective-permute-done | bytes 1048608 | tf_op jit(solution)/shard_map/ppermute | solution.py:41
  441.6 3.4 collective-permute-start.45
  445.0 3.9 fusion.66.up_ref
  448.9 2.8 collective-permute-done.48
  452.5 3.4 collective-permute-start.50
  456.0 4.3 collective-permute-start.52
  461.7 22.8 %shard_map.368 = bf16[512,3072]{1,0:T(8,128)(2,1)} custom-call(s32[1]{0:T(128)} %bitcast.13.scalar_ref, bf16[512,3072]{1,0:T(8,128)(2,1)} %fusion.8.packed_ref, bf16[512,1024]{1,0:T(8,128)(2,1)} %fusion.66.up_ref), custom_call_target="tpu_custom_call" | custom-call | flops 22000001024 | bytes 8388608 | tf_op jit(solution)/shard_map/pallas_call | solution.py:392
  497.3 14.8 %collective-permute-done.55 = bf16[4,64,512]{2,1,0:T(8,128)(2,1)S(1)} collective-permute-done((bf16[4,64,512]{2,1,0:T(8,128)(2,1)S(1)}, bf16[4,64,512]{2,1,0:T(8,128)(2,1)S(1)}, u32[]{:S(2)}, u32[]{:S(2)}) %collective-permute-start.55) | collective-permute-done | bytes 262176 | tf_op jit(solution)/shard_map/ppermute | solution.py:41
  517.5 3.0 collective-permute-start.61
  521.8 5.6 fusion.4
  532.0 2.9 collective-permute-start.62
  537.6 4.8 collective-permute-start.71
  557.4 15.0 %collective-permute-done.82 = bf16[4,2,64,768]{3,2,0,1:T(8,128)(2,1)} collective-permute-done((bf16[4,2,64,768]{3,2,0,1:T(8,128)(2,1)}, bf16[4,2,64,768]{3,2,0,1:T(8,128)(2,1)}, u32[]{:S(2)}, u32[]{:S(2)}) %collective-permute-start.82) | collective-permute-done | bytes 786464 | tf_op jit(solution)/shard_map/ppermute | solution.py:41
  581.7 4.2 collective-permute-start.77
  605.8 2.8 collective-permute-start.81
  609.5 4.0 collective-permute-done.75
  620.2 3.0 collective-permute-done.90
  631.5 5.3 collective-permute-done.87
  636.8 3.8 collective-permute-start.94
  640.6 3.4 collective-permute-start.95
  661.1 4.9 collective-permute-done.106
  669.6 3.2 collective-permute-start.109
  674.1 3.2 collective-permute-done.110
  682.5 2.6 multiply_subtract_fusion.4
  691.3 3.5 multiply_subtract_fusion
  (757 shorter events, 246.8 us)
Async XLA Ops:
  7.2 184.4 %all-gather.2.cloned.1.call-start = ((), (), s32[]{:S(2)}) async-start(), calls=%async_computation | async-start | bytes 17571840 | tf_op jit(solution)/shard_map/all_gather | solution.py:486
  14.5 26.1 %collective-permute-start.3 = (bf16[128,1024]{1,0:T(8,128)(2,1)S(1)}, bf16[128,1024]{1,0:T(8,128)(2,1)}, u32[]{:S(2)}, u32[]{:S(2)}) collective-permute-start(bf16[128,1024]{1,0:T(8,128)(2,1)S(1)} %convert_element_type.587), channel_id=1, source_target_pairs={{8,0},{16,8},{24,16},{0,24},{9,1},{17,9},{25,17},{1,25},{10,2},{18... | collective-permute-start | bytes 786440 | tf_op jit(solution)/shard_map/ppermute | solution.py:41
  19.7 21.0 %collective-permute-start.4 = (bf16[128,1024]{1,0:T(8,128)(2,1)S(1)}, bf16[128,1024]{1,0:T(8,128)(2,1)S(1)}, u32[]{:S(2)}, u32[]{:S(2)}) collective-permute-start(bf16[128,1024]{1,0:T(8,128)(2,1)S(1)} %convert_element_type.587), channel_id=1, source_target_pairs={{24,0},{0,8},{8,16},{16,24},{25,1},{1,9},{9,17},{17,25},{26,2},{2,... | collective-permute-start | bytes 786440 | tf_op jit(solution)/shard_map/ppermute | solution.py:41
  21.5 19.1 %collective-permute-start.2 = (bf16[32,2048]{1,0:T(8,128)(2,1)S(1)}, bf16[32,2048]{1,0:T(8,128)(2,1)S(1)}, u32[]{:S(2)}, u32[]{:S(2)}) collective-permute-start(bf16[32,2048]{1,0:T(8,128)(2,1)S(1)} %bitcast.608), channel_id=1, source_target_pairs={{1,0},{0,1},{3,2},{2,3},{5,4},{4,5},{7,6},{6,7},{9,8},{8,9},{11,10... | collective-permute-start | bytes 393224 | tf_op jit(solution)/shard_map/ppermute | solution.py:41
  22.6 48.9 %collective-permute-start.1 = (bf16[256,1024]{1,0:T(8,128)(2,1)S(1)}, bf16[256,1024]{1,0:T(8,128)(2,1)S(1)}, u32[]{:S(2)}, u32[]{:S(2)}) collective-permute-start(bf16[256,1024]{1,0:T(8,128)(2,1)S(1)} %get-tuple-element.344), channel_id=1, source_target_pairs={{2,0},{0,2},{3,1},{1,3},{6,4},{4,6},{7,5},{5,7},{10,8},{8,10},{11,... | collective-permute-start | bytes 1572872 | tf_op jit(solution)/shard_map/ppermute | solution.py:41
  40.7 30.8 %collective-permute-start.5 = (bf16[64,2048]{1,0:T(8,128)(2,1)S(1)}, bf16[64,2048]{1,0:T(8,128)(2,1)S(1)}, u32[]{:S(2)}, u32[]{:S(2)}) collective-permute-start(bf16[64,2048]{1,0:T(8,128)(2,1)S(1)} %bitcast.585), channel_id=1, source_target_pairs={{8,0},{16,8},{24,16},{0,24},{9,1},{17,9},{25,17},{1,25},{10,2},{18... | collective-permute-start | bytes 786440 | tf_op jit(solution)/shard_map/ppermute | solution.py:41
  44.9 26.6 %collective-permute-start.6 = (bf16[64,2048]{1,0:T(8,128)(2,1)S(1)}, bf16[64,2048]{1,0:T(8,128)(2,1)S(1)}, u32[]{:S(2)}, u32[]{:S(2)}) collective-permute-start(bf16[64,2048]{1,0:T(8,128)(2,1)S(1)} %bitcast.586), channel_id=1, source_target_pairs={{24,0},{0,8},{8,16},{16,24},{25,1},{1,9},{9,17},{17,25},{26,2},{2,... | collective-permute-start | bytes 786440 | tf_op jit(solution)/shard_map/ppermute | solution.py:41
  46.9 17.9 %collective-permute-start.7 = (bf16[128,512]{1,0:T(8,128)(2,1)S(1)}, bf16[128,512]{1,0:T(8,128)(2,1)S(1)}, u32[]{:S(2)}, u32[]{:S(2)}) collective-permute-start(bf16[128,512]{1,0:T(8,128)(2,1)S(1)} %slice.86), channel_id=1, source_target_pairs={{8,0},{16,8},{24,16},{0,24},{9,1},{17,9},{25,17},{1,25},{10,2},{18... | collective-permute-start | bytes 393224 | tf_op jit(solution)/shard_map/ppermute | solution.py:41
  50.8 18.9 %collective-permute-start.8 = (bf16[128,512]{1,0:T(8,128)(2,1)S(1)}, bf16[128,512]{1,0:T(8,128)(2,1)S(1)}, u32[]{:S(2)}, u32[]{:S(2)}) collective-permute-start(bf16[128,512]{1,0:T(8,128)(2,1)S(1)} %slice.87), channel_id=1, source_target_pairs={{24,0},{0,8},{8,16},{16,24},{25,1},{1,9},{9,17},{17,25},{26,2},{2,... | collective-permute-start | bytes 393224 | tf_op jit(solution)/shard_map/ppermute | solution.py:41
  64.8 126.7 %collective-permute-start = (bf16[256,1024]{1,0:T(8,128)(2,1)}, bf16[256,1024]{1,0:T(8,128)(2,1)}, u32[]{:S(2)}, u32[]{:S(2)}) collective-permute-start(bf16[256,1024]{1,0:T(8,128)(2,1)} %get-tuple-element.343), channel_id=1, source_target_pairs={{2,0},{0,2},{3,1},{1,3},{6,4},{4,6},{7,5},{5,7},{10,8},{8,10},{11,... | collective-permute-start | bytes 1572872 | tf_op jit(solution)/shard_map/ppermute | solution.py:41
  69.7 20.0 %collective-permute-start.27 = (f32[1,4]{1,0:T(1,128)S(1)}, f32[1,4]{1,0:T(1,128)S(1)}, u32[]{:S(2)}, u32[]{:S(2)}) collective-permute-start(f32[1,4]{1,0:T(1,128)S(1)} %bitcast_add_fusion.2), channel_id=1, source_target_pairs={{24,0},{0,8},{8,16},{16,24},{25,1},{1,9},{9,17},{17,25},{26,2},{2,... | collective-permute-start | bytes 56 | tf_op jit(solution)/shard_map/ppermute | solution.py:41
  71.7 17.8 %collective-permute-start.9 = (bf16[2,256,1024]{2,1,0:T(8,128)(2,1)S(1)}, bf16[2,256,1024]{2,1,0:T(8,128)(2,1)S(1)}, u32[]{:S(2)}, u32[]{:S(2)}) collective-permute-start(bf16[2,256,1024]{2,1,0:T(8,128)(2,1)S(1)} %bitcast_dynamic-update-slice_fusion.11), channel_id=1, source_target_pairs={{1,0},{0,1},{3,2},{2,3},{5,4},{4,5},{7,6},{6,7},{9,8},{8,9},{11,10... | collective-permute-start | bytes 3145736 | tf_op jit(solution)/shard_map/ppermute | solution.py:41
  71.8 15.2 %collective-permute-start.10 = (bf16[64,1024]{1,0:T(8,128)(2,1)S(1)}, bf16[64,1024]{1,0:T(8,128)(2,1)S(1)}, u32[]{:S(2)}, u32[]{:S(2)}) collective-permute-start(bf16[64,1024]{1,0:T(8,128)(2,1)S(1)} %slice.88), channel_id=1, source_target_pairs={{8,0},{16,8},{24,16},{0,24},{9,1},{17,9},{25,17},{1,25},{10,2},{18... | collective-permute-start | bytes 393224 | tf_op jit(solution)/shard_map/ppermute | solution.py:41
  87.1 19.9 %collective-permute-start.14 = (bf16[4,128,512]{2,1,0:T(8,128)(2,1)S(1)}, bf16[4,128,512]{2,1,0:T(8,128)(2,1)}, u32[]{:S(2)}, u32[]{:S(2)}) collective-permute-start(bf16[4,128,512]{2,1,0:T(8,128)(2,1)S(1)} %get-tuple-element.341), channel_id=1, source_target_pairs={{2,0},{0,2},{3,1},{1,3},{6,4},{4,6},{7,5},{5,7},{10,8},{8,10},{11,... | collective-permute-start | bytes 1572872 | tf_op jit(solution)/shard_map/ppermute | solution.py:41
  88.0 20.9 %collective-permute-start.15 = (bf16[4,128,512]{2,1,0:T(8,128)(2,1)S(1)}, bf16[4,128,512]{2,1,0:T(8,128)(2,1)}, u32[]{:S(2)}, u32[]{:S(2)}) collective-permute-start(bf16[4,128,512]{2,1,0:T(8,128)(2,1)S(1)} %get-tuple-element.342), channel_id=1, source_target_pairs={{4,0},{0,4},{5,1},{1,5},{6,2},{2,6},{7,3},{3,7},{12,8},{8,12},{13,... | collective-permute-start | bytes 1572872 | tf_op jit(solution)/shard_map/ppermute | solution.py:41
  89.7 38.2 %collective-permute-start.16 = (bf16[4,64,1024]{2,1,0:T(8,128)(2,1)S(1)}, bf16[4,64,1024]{2,1,0:T(8,128)(2,1)}, u32[]{:S(2)}, u32[]{:S(2)}) collective-permute-start(bf16[4,64,1024]{2,1,0:T(8,128)(2,1)S(1)} %get-tuple-element.340), channel_id=1, source_target_pairs={{2,0},{0,2},{3,1},{1,3},{6,4},{4,6},{7,5},{5,7},{10,8},{8,10},{11,... | collective-permute-start | bytes 1572872 | tf_op jit(solution)/shard_map/ppermute | solution.py:41
  90.5 39.9 %collective-permute-start.17 = (bf16[4,64,1024]{2,1,0:T(8,128)(2,1)S(1)}, bf16[4,64,1024]{2,1,0:T(8,128)(2,1)}, u32[]{:S(2)}, u32[]{:S(2)}) collective-permute-start(bf16[4,64,1024]{2,1,0:T(8,128)(2,1)S(1)} %get-tuple-element.339), channel_id=1, source_target_pairs={{4,0},{0,4},{5,1},{1,5},{6,2},{2,6},{7,3},{3,7},{12,8},{8,12},{13,... | collective-permute-start | bytes 1572872 | tf_op jit(solution)/shard_map/ppermute | solution.py:41
  131.6 35.4 %collective-permute-start.18 = (bf16[4,2,128,512]{3,2,1,0:T(8,128)(2,1)S(1)}, bf16[4,2,128,512]{3,2,1,0:T(8,128)(2,1)S(1)}, u32[]{:S(2)}, u32[]{:S(2)}) collective-permute-start(bf16[4,2,128,512]{3,2,1,0:T(8,128)(2,1)S(1)} %bitcast_dynamic-update-slice_fusion.6), channel_id=1, source_target_pairs={{4,0},{0,4},{5,1},{1,5},{6,2},{2,6},{7,3},{3,7},{12,8},{8,12},{13,... | collective-permute-start | bytes 3145736 | tf_op jit(solution)/shard_map/ppermute | solution.py:41
  135.6 31.5 %collective-permute-start.19 = (bf16[4,2,128,512]{3,2,1,0:T(8,128)(2,1)S(1)}, bf16[4,2,128,512]{3,2,1,0:T(8,128)(2,1)S(1)}, u32[]{:S(2)}, u32[]{:S(2)}) collective-permute-start(bf16[4,2,128,512]{3,2,1,0:T(8,128)(2,1)S(1)} %bitcast_dynamic-update-slice_fusion.9), channel_id=1, source_target_pairs={{2,0},{0,2},{3,1},{1,3},{6,4},{4,6},{7,5},{5,7},{10,8},{8,10},{11,... | collective-permute-start | bytes 3145736 | tf_op jit(solution)/shard_map/ppermute | solution.py:41
  137.0 51.3 %collective-permute-start.20 = (bf16[4,2,64,1024]{3,2,1,0:T(8,128)(2,1)S(1)}, bf16[4,2,64,1024]{3,2,1,0:T(8,128)(2,1)S(1)}, u32[]{:S(2)}, u32[]{:S(2)}) collective-permute-start(bf16[4,2,64,1024]{3,2,1,0:T(8,128)(2,1)S(1)} %bitcast_dynamic-update-slice_fusion.7), channel_id=1, source_target_pairs={{4,0},{0,4},{5,1},{1,5},{6,2},{2,6},{7,3},{3,7},{12,8},{8,12},{13,... | collective-permute-start | bytes 3145736 | tf_op jit(solution)/shard_map/ppermute | solution.py:41
  138.4 49.9 %collective-permute-start.21 = (bf16[4,2,64,1024]{3,2,1,0:T(8,128)(2,1)S(1)}, bf16[4,2,64,1024]{3,2,1,0:T(8,128)(2,1)S(1)}, u32[]{:S(2)}, u32[]{:S(2)}) collective-permute-start(bf16[4,2,64,1024]{3,2,1,0:T(8,128)(2,1)S(1)} %bitcast_dynamic-update-slice_fusion.8), channel_id=1, source_target_pairs={{2,0},{0,2},{3,1},{1,3},{6,4},{4,6},{7,5},{5,7},{10,8},{8,10},{11,... | collective-permute-start | bytes 3145736 | tf_op jit(solution)/shard_map/ppermute | solution.py:41
  222.0 34.8 %collective-permute-start.22 = (bf16[1024,2048]{1,0:T(8,128)(2,1)}, bf16[1024,2048]{1,0:T(8,128)(2,1)}, u32[]{:S(2)}, u32[]{:S(2)}) collective-permute-start(bf16[1024,2048]{1,0:T(8,128)(2,1)} %bitcast.37), channel_id=1, source_target_pairs={{1,0},{0,1},{3,2},{2,3},{5,4},{4,5},{7,6},{6,7},{9,8},{8,9},{11,10... | collective-permute-start | bytes 12582920 | tf_op jit(solution)/shard_map/ppermute | solution.py:41
  229.2 40.0 %collective-permute-start.23 = (bf16[2048,1024]{1,0:T(8,128)(2,1)}, bf16[2048,1024]{1,0:T(8,128)(2,1)}, u32[]{:S(2)}, u32[]{:S(2)}) collective-permute-start(bf16[2048,1024]{1,0:T(8,128)(2,1)} %bitcast.40), channel_id=1, source_target_pairs={{1,0},{0,1},{3,2},{2,3},{5,4},{4,5},{7,6},{6,7},{9,8},{8,9},{11,10... | collective-permute-start | bytes 12582920 | tf_op jit(solution)/shard_map/ppermute | solution.py:41
  289.6 27.7 %collective-permute-start.29 = (bf16[2048,1024]{1,0:T(8,128)(2,1)}, bf16[2048,1024]{1,0:T(8,128)(2,1)}, u32[]{:S(2)}, u32[]{:S(2)}) collective-permute-start(bf16[2048,1024]{1,0:T(8,128)(2,1)} %convolution_convert_fusion.3), channel_id=1, source_target_pairs={{1,0},{0,1},{3,2},{2,3},{5,4},{4,5},{7,6},{6,7},{9,8},{8,9},{11,10... | collective-permute-start | bytes 12582920 | tf_op jit(solution)/shard_map/ppermute | solution.py:41
  291.6 25.7 %collective-permute-start.28 = (bf16[1024,512]{1,0:T(8,128)(2,1)S(1)}, bf16[1024,512]{1,0:T(8,128)(2,1)S(1)}, u32[]{:S(2)}, u32[]{:S(2)}) collective-permute-start(bf16[1024,512]{1,0:T(8,128)(2,1)S(1)} %convolution_convert_fusion.6), channel_id=1, source_target_pairs={{1,0},{0,1},{3,2},{2,3},{5,4},{4,5},{7,6},{6,7},{9,8},{8,9},{11,10... | collective-permute-start | bytes 3145736 | tf_op jit(solution)/shard_map/ppermute | solution.py:41
  321.7 27.5 %collective-permute-start.31 = (bf16[1024,2048]{1,0:T(8,128)(2,1)}, bf16[1024,2048]{1,0:T(8,128)(2,1)}, u32[]{:S(2)}, u32[]{:S(2)}) collective-permute-start(bf16[1024,2048]{1,0:T(8,128)(2,1)} %convolution_convert_fusion.2), channel_id=1, source_target_pairs={{1,0},{0,1},{3,2},{2,3},{5,4},{4,5},{7,6},{6,7},{9,8},{8,9},{11,10... | collective-permute-start | bytes 12582920 | tf_op jit(solution)/shard_map/ppermute | solution.py:41
  323.2 26.0 %collective-permute-start.30 = (bf16[2,2,4,32,512]{4,3,0,2,1:T(8,128)(2,1)S(1)}, bf16[2,2,4,32,512]{4,3,0,2,1:T(8,128)(2,1)S(1)}, u32[]{:S(2)}, u32[]{:S(2)}) collective-permute-start(bf16[2,2,4,32,512]{4,3,0,2,1:T(8,128)(2,1)S(1)} %bitcast.601), channel_id=1, source_target_pairs={{2,0},{0,2},{3,1},{1,3},{6,4},{4,6},{7,5},{5,7},{10,8},{8,10},{11,... | collective-permute-start | bytes 1572872 | tf_op jit(solution)/shard_map/ppermute | solution.py:41
  331.7 56.2 %collective-permute-start.33 = (bf16[4,2,128,512]{3,2,0,1:T(8,128)(2,1)}, bf16[4,2,128,512]{3,2,0,1:T(8,128)(2,1)}, u32[]{:S(2)}, u32[]{:S(2)}) collective-permute-start(bf16[4,2,128,512]{3,2,0,1:T(8,128)(2,1)} %bitcast.555), channel_id=1, source_target_pairs={{2,0},{0,2},{3,1},{1,3},{6,4},{4,6},{7,5},{5,7},{10,8},{8,10},{11,... | collective-permute-start | bytes 3145736 | tf_op jit(solution)/shard_map/ppermute | solution.py:41
  335.7 52.2 %collective-permute-start.34 = (bf16[4,2,128,512]{3,2,0,1:T(8,128)(2,1)}, bf16[4,2,128,512]{3,2,0,1:T(8,128)(2,1)}, u32[]{:S(2)}, u32[]{:S(2)}) collective-permute-start(bf16[4,2,128,512]{3,2,0,1:T(8,128)(2,1)} %bitcast.554), channel_id=1, source_target_pairs={{4,0},{0,4},{5,1},{1,5},{6,2},{2,6},{7,3},{3,7},{12,8},{8,12},{13,... | collective-permute-start | bytes 3145736 | tf_op jit(solution)/shard_map/ppermute | solution.py:41
  391.6 27.6 %collective-permute-start.42 = (bf16[1024,1536]{1,0:T(8,128)(2,1)S(1)}, bf16[1024,1536]{1,0:T(8,128)(2,1)S(1)}, u32[]{:S(2)}, u32[]{:S(2)}) collective-permute-start(bf16[1024,1536]{1,0:T(8,128)(2,1)S(1)} %convolution_convert_fusion.1), channel_id=1, source_target_pairs={{1,0},{0,1},{3,2},{2,3},{5,4},{4,5},{7,6},{6,7},{9,8},{8,9},{11,10... | collective-permute-start | bytes 9437192 | tf_op jit(solution)/shard_map/ppermute | solution.py:41
  401.7 14.9 %collective-permute-start.40 = (bf16[4,128,512]{2,1,0:T(8,128)(2,1)S(1)}, bf16[4,128,512]{2,1,0:T(8,128)(2,1)S(1)}, u32[]{:S(2)}, u32[]{:S(2)}) collective-permute-start(bf16[4,128,512]{2,1,0:T(8,128)(2,1)S(1)} %dynamic-slice_bitcast_fusion.8), channel_id=1, source_target_pairs={{4,0},{0,4},{5,1},{1,5},{6,2},{2,6},{7,3},{3,7},{12,8},{8,12},{13,... | collective-permute-start | bytes 1572872 | tf_op jit(solution)/shard_map/ppermute | solution.py:41
  404.3 14.9 %collective-permute-start.41 = (bf16[4,128,512]{2,1,0:T(8,128)(2,1)S(1)}, bf16[4,128,512]{2,1,0:T(8,128)(2,1)S(1)}, u32[]{:S(2)}, u32[]{:S(2)}) collective-permute-start(bf16[4,128,512]{2,1,0:T(8,128)(2,1)S(1)} %dynamic-slice_bitcast_fusion.7), channel_id=1, source_target_pairs={{2,0},{0,2},{3,1},{1,3},{6,4},{4,6},{7,5},{5,7},{10,8},{8,10},{11,... | collective-permute-start | bytes 1572872 | tf_op jit(solution)/shard_map/ppermute | solution.py:41
  412.3 25.9 %collective-permute-start.46 = (bf16[4,2,64,1024]{3,2,0,1:T(8,128)(2,1)S(1)}, bf16[4,2,64,1024]{3,2,0,1:T(8,128)(2,1)S(1)}, u32[]{:S(2)}, u32[]{:S(2)}) collective-permute-start(bf16[4,2,64,1024]{3,2,0,1:T(8,128)(2,1)S(1)} %bitcast.588), channel_id=1, source_target_pairs={{4,0},{0,4},{5,1},{1,5},{6,2},{2,6},{7,3},{3,7},{12,8},{8,12},{13,... | collective-permute-start | bytes 3145736 | tf_op jit(solution)/shard_map/ppermute | solution.py:41
  413.6 28.0 %collective-permute-start.47 = (bf16[4,2,64,1024]{3,2,1,0:T(8,128)(2,1)S(1)}, bf16[4,2,64,1024]{3,2,1,0:T(8,128)(2,1)S(1)}, u32[]{:S(2)}, u32[]{:S(2)}) collective-permute-start(bf16[4,2,64,1024]{3,2,1,0:T(8,128)(2,1)S(1)} %dynamic-slice_bitcast_fusion), channel_id=1, source_target_pairs={{2,0},{0,2},{3,1},{1,3},{6,4},{4,6},{7,5},{5,7},{10,8},{8,10},{11,... | collective-permute-start | bytes 3145736 | tf_op jit(solution)/shard_map/ppermute | solution.py:41
  416.6 35.1 %collective-permute-start.48 = (bf16[4,2,64,512]{3,2,1,0:T(8,128)(2,1)S(1)}, bf16[4,2,64,512]{3,2,1,0:T(8,128)(2,1)S(1)}, u32[]{:S(2)}, u32[]{:S(2)}) collective-permute-start(bf16[4,2,64,512]{3,2,1,0:T(8,128)(2,1)S(1)} %dynamic-slice_bitcast_fusion.6), channel_id=1, source_target_pairs={{2,0},{0,2},{3,1},{1,3},{6,4},{4,6},{7,5},{5,7},{10,8},{8,10},{11,... | collective-permute-start | bytes 1572872 | tf_op jit(solution)/shard_map/ppermute | solution.py:41
  419.5 36.4 %collective-permute-start.43 = (bf16[128,1024]{1,0:T(8,128)(2,1)S(1)}, bf16[128,1024]{1,0:T(8,128)(2,1)S(1)}, u32[]{:S(2)}, u32[]{:S(2)}) collective-permute-start(bf16[128,1024]{1,0:T(8,128)(2,1)S(1)} %get-tuple-element.335), channel_id=1, source_target_pairs={{24,0},{0,8},{8,16},{16,24},{25,1},{1,9},{9,17},{17,25},{26,2},{2,... | collective-permute-start | bytes 786440 | tf_op jit(solution)/shard_map/ppermute | solution.py:41
  421.3 39.7 %collective-permute-start.49 = (bf16[1024,512]{1,0:T(8,128)(2,1)S(1)}, bf16[1024,512]{1,0:T(8,128)(2,1)}, u32[]{:S(2)}, u32[]{:S(2)}) collective-permute-start(bf16[1024,512]{1,0:T(8,128)(2,1)S(1)} %convolution_convert_fusion.4), channel_id=1, source_target_pairs={{1,0},{0,1},{3,2},{2,3},{5,4},{4,5},{7,6},{6,7},{9,8},{8,9},{11,10... | collective-permute-start | bytes 3145736 | tf_op jit(solution)/shard_map/ppermute | solution.py:41
  438.2 17.7 %collective-permute-start.44 = (bf16[128,1024]{1,0:T(8,128)(2,1)S(1)}, bf16[128,1024]{1,0:T(8,128)(2,1)}, u32[]{:S(2)}, u32[]{:S(2)}) collective-permute-start(bf16[128,1024]{1,0:T(8,128)(2,1)S(1)} %get-tuple-element.336), channel_id=1, source_target_pairs={{16,0},{24,8},{0,16},{8,24},{17,1},{25,9},{1,17},{9,25},{18,2},{26... | collective-permute-start | bytes 786440 | tf_op jit(solution)/shard_map/ppermute | solution.py:41
  441.6 18.6 %collective-permute-start.45 = (bf16[128,1024]{1,0:T(8,128)(2,1)S(1)}, bf16[128,1024]{1,0:T(8,128)(2,1)}, u32[]{:S(2)}, u32[]{:S(2)}) collective-permute-start(bf16[128,1024]{1,0:T(8,128)(2,1)S(1)} %get-tuple-element.334), channel_id=1, source_target_pairs={{8,0},{16,8},{24,16},{0,24},{9,1},{17,9},{25,17},{1,25},{10,2},{18... | collective-permute-start | bytes 786440 | tf_op jit(solution)/shard_map/ppermute | solution.py:41
  452.5 37.3 %collective-permute-start.50 = (bf16[2,32,512]{2,1,0:T(8,128)(2,1)S(1)}, bf16[2,32,512]{2,1,0:T(8,128)(2,1)S(1)}, u32[]{:S(2)}, u32[]{:S(2)}) collective-permute-start(bf16[2,32,512]{2,1,0:T(8,128)(2,1)S(1)} %get-tuple-element.366), channel_id=1, source_target_pairs={{8,0},{16,8},{24,16},{0,24},{9,1},{17,9},{25,17},{1,25},{10,2},{18... | collective-permute-start | bytes 196616 | tf_op jit(solution)/shard_map/ppermute | solution.py:41
  455.9 35.8 %collective-permute-start.51 = (bf16[2,32,512]{2,1,0:T(8,128)(2,1)S(1)}, bf16[2,32,512]{2,1,0:T(8,128)(2,1)}, u32[]{:S(2)}, u32[]{:S(2)}) collective-permute-start(bf16[2,32,512]{2,1,0:T(8,128)(2,1)S(1)} %get-tuple-element.366), channel_id=1, source_target_pairs={{16,0},{24,8},{0,16},{8,24},{17,1},{25,9},{1,17},{9,25},{18,2},{26... | collective-permute-start | bytes 196616 | tf_op jit(solution)/shard_map/ppermute | solution.py:41
  456.0 36.6 %collective-permute-start.52 = (bf16[2,32,512]{2,1,0:T(8,128)(2,1)S(1)}, bf16[2,32,512]{2,1,0:T(8,128)(2,1)}, u32[]{:S(2)}, u32[]{:S(2)}) collective-permute-start(bf16[2,32,512]{2,1,0:T(8,128)(2,1)S(1)} %get-tuple-element.366), channel_id=1, source_target_pairs={{24,0},{0,8},{8,16},{16,24},{25,1},{1,9},{9,17},{17,25},{26,2},{2,... | collective-permute-start | bytes 196616 | tf_op jit(solution)/shard_map/ppermute | solution.py:41
  460.2 36.2 %collective-permute-start.56 = (bf16[4,2,64,768]{3,2,0,1:T(8,128)(2,1)}, bf16[4,2,64,768]{3,2,0,1:T(8,128)(2,1)}, u32[]{:S(2)}, u32[]{:S(2)}) collective-permute-start(bf16[4,2,64,768]{3,2,0,1:T(8,128)(2,1)} %bitcast.557), channel_id=1, source_target_pairs={{2,0},{0,2},{3,1},{1,3},{6,4},{4,6},{7,5},{5,7},{10,8},{8,10},{11,... | collective-permute-start | bytes 2359304 | tf_op jit(solution)/shard_map/ppermute | solution.py:41
  460.9 36.3 %collective-permute-start.57 = (bf16[4,2,64,768]{3,2,1,0:T(8,128)(2,1)}, bf16[4,2,64,768]{3,2,1,0:T(8,128)(2,1)}, u32[]{:S(2)}, u32[]{:S(2)}) collective-permute-start(bf16[4,2,64,768]{3,2,1,0:T(8,128)(2,1)} %dynamic-slice_bitcast_fusion.2), channel_id=1, source_target_pairs={{4,0},{0,4},{5,1},{1,5},{6,2},{2,6},{7,3},{3,7},{12,8},{8,12},{13,... | collective-permute-start | bytes 2359304 | tf_op jit(solution)/shard_map/ppermute | solution.py:41
  489.8 22.3 %collective-permute-start.53 = (bf16[4,64,1024]{2,1,0:T(8,128)(2,1)S(1)}, bf16[4,64,1024]{2,1,0:T(8,128)(2,1)S(1)}, u32[]{:S(2)}, u32[]{:S(2)}) collective-permute-start(bf16[4,64,1024]{2,1,0:T(8,128)(2,1)S(1)} %dynamic-slice_bitcast_fusion.5), channel_id=1, source_target_pairs={{2,0},{0,2},{3,1},{1,3},{6,4},{4,6},{7,5},{5,7},{10,8},{8,10},{11,... | collective-permute-start | bytes 1572872 | tf_op jit(solution)/shard_map/ppermute | solution.py:41
  491.7 20.4 %collective-permute-start.54 = (bf16[4,64,1024]{2,1,0:T(8,128)(2,1)S(1)}, bf16[4,64,1024]{2,1,0:T(8,128)(2,1)S(1)}, u32[]{:S(2)}, u32[]{:S(2)}) collective-permute-start(bf16[4,64,1024]{2,1,0:T(8,128)(2,1)S(1)} %dynamic-slice_bitcast_fusion.4), channel_id=1, source_target_pairs={{4,0},{0,4},{5,1},{1,5},{6,2},{2,6},{7,3},{3,7},{12,8},{8,12},{13,... | collective-permute-start | bytes 1572872 | tf_op jit(solution)/shard_map/ppermute | solution.py:41
  492.5 19.6 %collective-permute-start.55 = (bf16[4,64,512]{2,1,0:T(8,128)(2,1)S(1)}, bf16[4,64,512]{2,1,0:T(8,128)(2,1)S(1)}, u32[]{:S(2)}, u32[]{:S(2)}) collective-permute-start(bf16[4,64,512]{2,1,0:T(8,128)(2,1)S(1)} %dynamic-slice_bitcast_fusion.18), channel_id=1, source_target_pairs={{4,0},{0,4},{5,1},{1,5},{6,2},{2,6},{7,3},{3,7},{12,8},{8,12},{13,... | collective-permute-start | bytes 786440 | tf_op jit(solution)/shard_map/ppermute | solution.py:41
  496.4 33.9 %collective-permute-start.65 = (bf16[4,2,64,512]{3,2,1,0:T(8,128)(2,1)S(1)}, bf16[4,2,64,512]{3,2,1,0:T(8,128)(2,1)S(1)}, u32[]{:S(2)}, u32[]{:S(2)}) collective-permute-start(bf16[4,2,64,512]{3,2,1,0:T(8,128)(2,1)S(1)} %dynamic-slice_bitcast_fusion.3), channel_id=1, source_target_pairs={{4,0},{0,4},{5,1},{1,5},{6,2},{2,6},{7,3},{3,7},{12,8},{8,12},{13,... | collective-permute-start | bytes 1572872 | tf_op jit(solution)/shard_map/ppermute | solution.py:41
  514.0 28.4 %collective-permute-start.58 = (bf16[1024,1536]{1,0:T(8,128)(2,1)S(1)}, bf16[1024,1536]{1,0:T(8,128)(2,1)S(1)}, u32[]{:S(2)}, u32[]{:S(2)}) collective-permute-start(bf16[1024,1536]{1,0:T(8,128)(2,1)S(1)} %convolution_convert_fusion), channel_id=1, source_target_pairs={{1,0},{0,1},{3,2},{2,3},{5,4},{4,5},{7,6},{6,7},{9,8},{8,9},{11,10... | collective-permute-start | bytes 9437192 | tf_op jit(solution)/shard_map/ppermute | solution.py:41
  515.9 21.7 %collective-permute-start.59 = (bf16[2,4,32,512]{3,2,1,0:T(8,128)(2,1)S(1)}, bf16[2,4,32,512]{3,2,1,0:T(8,128)(2,1)S(1)}, u32[]{:S(2)}, u32[]{:S(2)}) collective-permute-start(bf16[2,4,32,512]{3,2,1,0:T(8,128)(2,1)S(1)} %bitcast_dynamic-update-slice_fusion.28), channel_id=1, source_target_pairs={{4,0},{0,4},{5,1},{1,5},{6,2},{2,6},{7,3},{3,7},{12,8},{8,12},{13,... | collective-permute-start | bytes 786440 | tf_op jit(solution)/shard_map/ppermute | solution.py:41
  516.8 14.8 %collective-permute-start.60 = (bf16[64,512]{1,0:T(8,128)(2,1)S(1)}, bf16[64,512]{1,0:T(8,128)(2,1)S(1)}, u32[]{:S(2)}, u32[]{:S(2)}) collective-permute-start(bf16[64,512]{1,0:T(8,128)(2,1)S(1)} %get-tuple-element.375), channel_id=1, source_target_pairs={{24,0},{0,8},{8,16},{16,24},{25,1},{1,9},{9,17},{17,25},{26,2},{2,... | collective-permute-start | bytes 196616 | tf_op jit(solution)/shard_map/ppermute | solution.py:41
  517.5 14.5 %collective-permute-start.61 = (bf16[64,512]{1,0:T(8,128)(2,1)S(1)}, bf16[64,512]{1,0:T(8,128)(2,1)S(1)}, u32[]{:S(2)}, u32[]{:S(2)}) collective-permute-start(bf16[64,512]{1,0:T(8,128)(2,1)S(1)} %get-tuple-element.374), channel_id=1, source_target_pairs={{16,0},{24,8},{0,16},{8,24},{17,1},{25,9},{1,17},{9,25},{18,2},{26... | collective-permute-start | bytes 196616 | tf_op jit(solution)/shard_map/ppermute | solution.py:41
  537.4 38.8 %collective-permute-start.70 = (bf16[64,2048]{1,0:T(8,128)(2,1)}, bf16[64,2048]{1,0:T(8,128)(2,1)}, u32[]{:S(2)}, u32[]{:S(2)}) collective-permute-start(bf16[64,2048]{1,0:T(8,128)(2,1)} %get-tuple-element.332), channel_id=1, source_target_pairs={{24,0},{0,8},{8,16},{16,24},{25,1},{1,9},{9,17},{17,25},{26,2},{2,... | collective-permute-start | bytes 786440 | tf_op jit(solution)/shard_map/ppermute | solution.py:41
  537.6 41.9 %collective-permute-start.71 = (bf16[64,2048]{1,0:T(8,128)(2,1)}, bf16[64,2048]{1,0:T(8,128)(2,1)}, u32[]{:S(2)}, u32[]{:S(2)}) collective-permute-start(bf16[64,2048]{1,0:T(8,128)(2,1)} %get-tuple-element.333), channel_id=1, source_target_pairs={{16,0},{24,8},{0,16},{8,24},{17,1},{25,9},{1,17},{9,25},{18,2},{26... | collective-permute-start | bytes 786440 | tf_op jit(solution)/shard_map/ppermute | solution.py:41
  545.9 41.7 %collective-permute-start.66 = (bf16[1024,512]{1,0:T(8,128)(2,1)}, bf16[1024,512]{1,0:T(8,128)(2,1)}, u32[]{:S(2)}, u32[]{:S(2)}) collective-permute-start(bf16[1024,512]{1,0:T(8,128)(2,1)} %fusion.65), channel_id=1, source_target_pairs={{1,0},{0,1},{3,2},{2,3},{5,4},{4,5},{7,6},{6,7},{9,8},{8,9},{11,10... | collective-permute-start | bytes 3145736 | tf_op jit(solution)/shard_map/ppermute | solution.py:41
  552.0 20.3 %collective-permute-start.82 = (bf16[4,2,64,768]{3,2,0,1:T(8,128)(2,1)}, bf16[4,2,64,768]{3,2,0,1:T(8,128)(2,1)}, u32[]{:S(2)}, u32[]{:S(2)}) collective-permute-start(bf16[4,2,64,768]{3,2,0,1:T(8,128)(2,1)} %bitcast.556), channel_id=1, source_target_pairs={{4,0},{0,4},{5,1},{1,5},{6,2},{2,6},{7,3},{3,7},{12,8},{8,12},{13,... | collective-permute-start | bytes 2359304 | tf_op jit(solution)/shard_map/ppermute | solution.py:41
  554.2 20.4 %collective-permute-start.83 = (bf16[4,2,64,768]{3,2,1,0:T(8,128)(2,1)}, bf16[4,2,64,768]{3,2,1,0:T(8,128)(2,1)}, u32[]{:S(2)}, u32[]{:S(2)}) collective-permute-start(bf16[4,2,64,768]{3,2,1,0:T(8,128)(2,1)} %dynamic-slice_bitcast_fusion.1), channel_id=1, source_target_pairs={{2,0},{0,2},{3,1},{1,3},{6,4},{4,6},{7,5},{5,7},{10,8},{8,10},{11,... | collective-permute-start | bytes 2359304 | tf_op jit(solution)/shard_map/ppermute | solution.py:41
  581.2 22.5 %collective-permute-start.76 = (bf16[64,1536]{1,0:T(8,128)(2,1)}, bf16[64,1536]{1,0:T(8,128)(2,1)}, u32[]{:S(2)}, u32[]{:S(2)}) collective-permute-start(bf16[64,1536]{1,0:T(8,128)(2,1)} %get-tuple-element.353), channel_id=1, source_target_pairs={{24,0},{0,8},{8,16},{16,24},{25,1},{1,9},{9,17},{17,25},{26,2},{2,... | collective-permute-start | bytes 589832 | tf_op jit(solution)/shard_map/ppermute | solution.py:41
  581.7 23.7 %collective-permute-start.77 = (bf16[64,1536]{1,0:T(8,128)(2,1)}, bf16[64,1536]{1,0:T(8,128)(2,1)}, u32[]{:S(2)}, u32[]{:S(2)}) collective-permute-start(bf16[64,1536]{1,0:T(8,128)(2,1)} %get-tuple-element.354), channel_id=1, source_target_pairs={{16,0},{24,8},{0,16},{8,24},{17,1},{25,9},{1,17},{9,25},{18,2},{26... | collective-permute-start | bytes 589832 | tf_op jit(solution)/shard_map/ppermute | solution.py:41
  586.6 19.3 %collective-permute-start.78 = (bf16[64,1536]{1,0:T(8,128)(2,1)}, bf16[64,1536]{1,0:T(8,128)(2,1)}, u32[]{:S(2)}, u32[]{:S(2)}) collective-permute-start(bf16[64,1536]{1,0:T(8,128)(2,1)} %get-tuple-element.352), channel_id=1, source_target_pairs={{8,0},{16,8},{24,16},{0,24},{9,1},{17,9},{25,17},{1,25},{10,2},{18... | collective-permute-start | bytes 589832 | tf_op jit(solution)/shard_map/ppermute | solution.py:41
  625.0 15.5 %collective-permute-start.88 = (bf16[64,1536]{1,0:T(8,128)(2,1)}, bf16[64,1536]{1,0:T(8,128)(2,1)}, u32[]{:S(2)}, u32[]{:S(2)}) collective-permute-start(bf16[64,1536]{1,0:T(8,128)(2,1)} %get-tuple-element.349), channel_id=1, source_target_pairs={{8,0},{16,8},{24,16},{0,24},{9,1},{17,9},{25,17},{1,25},{10,2},{18... | collective-permute-start | bytes 589832 | tf_op jit(solution)/shard_map/ppermute | solution.py:41
  627.1 16.9 %collective-permute-start.97 = (f32[5,1024]{1,0:T(8,128)S(1)}, f32[5,1024]{1,0:T(8,128)S(1)}, u32[]{:S(2)}, u32[]{:S(2)}) collective-permute-start(f32[5,1024]{1,0:T(8,128)S(1)} %add.984), channel_id=1, source_target_pairs={{8,0},{16,8},{24,16},{0,24},{9,1},{17,9},{25,17},{1,25},{10,2},{18... | collective-permute-start | bytes 61448 | tf_op jit(solution)/shard_map/ppermute | solution.py:41
  627.7 17.4 %collective-permute-start.98 = (f32[5,1024]{1,0:T(8,128)S(1)}, f32[5,1024]{1,0:T(8,128)}, u32[]{:S(2)}, u32[]{:S(2)}) collective-permute-start(f32[5,1024]{1,0:T(8,128)S(1)} %add.984), channel_id=1, source_target_pairs={{16,0},{24,8},{0,16},{8,24},{17,1},{25,9},{1,17},{9,25},{18,2},{26... | collective-permute-start | bytes 61448 | tf_op jit(solution)/shard_map/ppermute | solution.py:41
  630.9 14.3 %collective-permute-start.99 = (f32[5,1024]{1,0:T(8,128)S(1)}, f32[5,1024]{1,0:T(8,128)S(1)}, u32[]{:S(2)}, u32[]{:S(2)}) collective-permute-start(f32[5,1024]{1,0:T(8,128)S(1)} %add.984), channel_id=1, source_target_pairs={{24,0},{0,8},{8,16},{16,24},{25,1},{1,9},{9,17},{17,25},{26,2},{2,... | collective-permute-start | bytes 61448 | tf_op jit(solution)/shard_map/ppermute | solution.py:41
  (194 other events, 1733.0 us)
Sparse Core Ops, SparseCore 0:
  14.6 161.0 all-gather.1

commit v7 on v6

--- a/solution.py
+++ b/solution.py
@@ -258,6 +258,23 @@
     return in_order(mine, other, 1).astype(WIDE)
 
 
+def sum_table(other, own):
+    (arrived,) = yield [shifted(other, "h", 1)]
+    total = (own() + arrived.astype(WIDE)).astype(LOW)
+    total = total.reshape(lax.axis_size("m"), -1, total.shape[-1])
+    pieces = yield pieces_of(total, 0, "m")
+    total = added(total, 0, "m", pieces).astype(LOW)
+    for axis in ("r", "z"):
+        shift = lax.axis_size(axis) // 2
+        while shift:
+            (other,) = yield [shifted(total, axis, shift)]
+            total = (total.astype(WIDE) + other.astype(WIDE)).astype(LOW)
+            shift //= 2
+    square = squares(total.astype(WIDE)) / (lax.axis_size("r") * lax.axis_size("z"))
+    mine, other = yield from swap_rows(total, square)
+    return in_order(mine, other, 1).astype(WIDE)
+
+
 def sum_over(part, axes):
     for axis in axes:
         n = lax.axis_size(axis)
@@ -299,9 +316,9 @@
     return jnp.dot(left, right, preferred_element_type=WIDE)
 
 
-def allowed_pairs(kind, scalar, count):
-    row = lax.broadcasted_iota(jnp.int32, (count, count), 0)
-    col = lax.broadcasted_iota(jnp.int32, (count, count), 1)
+def allowed_pairs(kind, scalar, count, query_dim=0):
+    row = lax.broadcasted_iota(jnp.int32, (count, count), query_dim)
+    col = lax.broadcasted_iota(jnp.int32, (count, count), 1 - query_dim)
     if kind == "space":
         return (scalar == 0) | (row // SMALL_TOKENS == col // SMALL_TOKENS)
     lanes = count // FRAMES
@@ -351,7 +368,7 @@
 
 
 def backward_body(kind, scalar_ref, packed_ref, up_ref, out_ref):
-    allowed = allowed_pairs(kind, scalar_ref[0], GROUP)
+    allowed = allowed_pairs(kind, scalar_ref[0], GROUP, 1)
     first = lax.broadcasted_iota(jnp.int32, (GROUP, LANES), 1) < HEAD
 
     def turn(pair, _):
@@ -365,11 +382,14 @@
         zero = jnp.zeros_like(query)
         grads = []
         for mine in (first, ~first):
-            probs = softmax_rows(jnp.where(mine, query, zero), key, allowed)
-            inner = dot_nt(jnp.where(mine, up, zero), value)
-            total = jnp.sum(probs * inner, axis=-1, keepdims=True)
+            scores = dot_nt(key, jnp.where(mine, query, zero)) * HEAD ** (-0.5)
+            scores = jnp.where(allowed, scores, NEG)
+            expd = jnp.exp(scores - jnp.max(scores, axis=0, keepdims=True))
+            probs = expd / jnp.sum(expd, axis=0, keepdims=True)
+            inner = dot_nt(value, jnp.where(mine, up, zero))
+            total = jnp.sum(probs * inner, axis=0, keepdims=True)
             scores = (probs * (inner - total) * HEAD ** (-0.5)).astype(LOW)
-            grads.append((dot_nn(scores, key), dot_tn(scores, query), dot_tn(probs.astype(LOW), up)))
+            grads.append((dot_tn(scores, key), dot_nn(scores, query), dot_nn(probs.astype(LOW), up)))
         for place, one, two in zip((start, key_at, value_at), *grads):
             store_to(out_ref, place, kind, jnp.where(first, one, two).astype(LOW))
         return 0
@@ -501,7 +521,6 @@
     picked = dot_nn((space_codes[:, None] == code_ids[None, :]).astype(LOW), table_in)
     token = advance(token, down_job, up_job)
     out_table_job = Job(gather_table(low_out))
-    token = advance(token, down_job, up_job)
     picked, token = lax.optimization_barrier((picked, token))
     gathered = advance(gathered, out_table_job)
     first_in, first_out, turned, next_in, next_out = (
@@ -531,6 +550,7 @@
     normed_space = norm_forward(start, gain_all[0]).astype(LOW)
     packed_space = dot_nn(normed_space, w_in[0]).astype(LOW)
     mixed_space = attention("space", small, packed_space)
+    mixed_space = advance(mixed_space, down_job, up_job)
     after_space = start + dot_nn(mixed_space, w_out[0])
     after_space = swap_slots(after_space.reshape(frames, SLOTS, D)).reshape(-1, D)
     normed_time = norm_forward(after_space, gain_all[1]).astype(LOW)
@@ -556,7 +576,7 @@
     def product(make, left, mine, other, *rest):
         return Job(make(dot_tn(left, other).astype(LOW), lambda: dot_tn(left, mine), *rest))
 
-    head_job = product(reduce_table, grad_logits, *halves(final, 1))
+    head_job = product(sum_table, grad_logits, *halves(final, 1))
     grad_final = dot_nn(grad_logits, table_out)
     grad_ffn, gain_three = norm_backward(after_ffn, gain_all[3], grad_final)
     up_low = grad_ffn.astype(LOW)
@@ -593,16 +613,18 @@
     up_low = advance(up_low, head_job, contract_job, in_job)
     first_out_job = product(reduce_layer, mixed_space, *halves(up_low, 1), ("r", "m", "z"))
     grad_mixed = dot_nt(up_low, w_out[0]).astype(LOW)
-    grad_mixed = advance(grad_mixed, contract_job, expand_job, out_job, first_out_job)
+    grad_mixed = advance(grad_mixed, out_job, first_out_job)
     grad_packed = attention("space", small, packed_space, grad_mixed)
     grad_packed = advance(
-        grad_packed, head_job, expand_job, out_job, in_job
+        grad_packed, head_job, contract_job, expand_job, in_job
     )
     first_in_job = product(
         reduce_layer, normed_space, *halves(grad_packed, 1), ("r", "m", "z"), None, 2
     )
     grad_normed = dot_nt(grad_packed, w_in[0])
-    grad_normed = advance(grad_normed, first_in_job, head_job, out_job, in_job, first_out_job)
+    grad_normed = advance(
+        grad_normed, first_in_job, head_job, expand_job, out_job, in_job, first_out_job
+    )
     inward, gain_zero = norm_backward(start, gain_all[0], grad_normed)
     grad_start = grad_space + inward
     mask_grad = jnp.sum(grad_start * space_mask[:, None], axis=0)

time: 712 us -> 720 us (1.011)
  waiting for transfers between devices: 210 us -> 222 us
  Pallas kernels: 63 us -> 54.8 us
    all_gather x1, waiting for transfers between devices: 0.01 us -> 25.8 us  [on_device(): gathered = lax.all_gather(gathered, ALL, axis=0, tiled=True)]
    ppermute x112 -> x107, waiting for transfers between devices: 210 us -> 196 us  [shifted(): return lax.ppermute(part, axis, [((i + shift) % n, i) for i in range(n)])]
    pallas_call x4, Pallas kernels: 63 us -> 54.8 us  [attention(): pl.pallas_call(functools.partial(body, kind), out_shape=jax.ShapeDtypeStr...]
    ppermute x112 -> x107, starting transfers between devices: 132 us -> 135 us  [shifted(): return lax.ppermute(part, axis, [((i + shift) % n, i) for i in range(n)])]
    convert_element_type x24 -> x22, other arithmetic: 17.4 us -> 15.3 us  [reduce_rows(): added(*each, arrived).astype(LOW)]
    unnamed x306 -> x322, local copies, waits for them, and re-layouts: 23.6 us -> 21.6 us
  transfers between devices with their start and end apart: 113 -> 108, of which waited for: 39 -> 37; matrix products, arithmetic and copies ran while one was open for 29% -> 29% of each run, Pallas kernels for 8% -> 8%
where the time goes in v7:
time: 720 us; the launch traced here: 711 us
  waiting for transfers between devices  222 us (31%)
  matrix products  139 us (19%)
  starting transfers between devices  135 us (19%)
  other arithmetic  72.6 us (10%)
  local copies, waits for them, and re-layouts  68.8 us (10%)
  Pallas kernels  54.8 us (8%)
  between operations  19.4 us (3%)
    ppermute x107, waiting for transfers between devices, shifted(): return lax.ppermute(part, axis, [((i + shift) % n, i) for i in range(n)])  196 us
    ppermute x107, starting transfers between devices, shifted(): return lax.ppermute(part, axis, [((i + shift) % n, i) for i in range(n)])  135 us
    pallas_call x4, Pallas kernels, attention(): pl.pallas_call(functools.partial(body, kind), out_shape=jax.ShapeDtypeStr...  54.8 us
    dot_general x10, matrix products, dot_nn(): return jnp.dot(left, right, preferred_element_type=WIDE)  48.3 us
    dot_general x9, matrix products, dot_nt(): lax.dot_general(left, right, (((1,), (1,)), ((), ())), preferred_element_...  47.1 us
    dot_general x16, matrix products, dot_tn(): lax.dot_general(left, right, (((0,), (0,)), ((), ())), preferred_element_...  43.1 us
    all_gather x1, waiting for transfers between devices, on_device(): gathered = lax.all_gather(gathered, ALL, axis=0, tiled=True)  25.8 us
    unnamed x322, local copies, waits for them, and re-layouts  21.6 us
  transfers between devices with their start and end apart: 108, of which 37 were waited for; matrix products, arithmetic and copies ran while one was open for 29% of the time, Pallas kernels for 8%

profile of v7, /device:TPU:0, one launch (start us, length us, event | category | flops | bytes accessed | tf_op | source)
XLA Modules:
  0.0 710.7 jit_solution(2265545790527944396)
XLA Ops:
  14.5 5.1 collective-permute-start.3
  29.8 3.9 collective-permute-start.25
  36.1 4.6 collective-permute-done.26
  42.4 4.0 collective-permute-done.27
  51.4 3.8 collective-permute-start.7
  55.4 23.9 %collective-permute-done.7 = bf16[128,512]{1,0:T(8,128)(2,1)S(1)} collective-permute-done((bf16[128,512]{1,0:T(8,128)(2,1)S(1)}, bf16[128,512]{1,0:T(8,128)(2,1)S(1)}, u32[]{:S(2)}, u32[]{:S(2)}) %collective-permute-start.7) | collective-permute-done | bytes 131104 | tf_op jit(solution)/shard_map/ppermute | solution.py:41
  84.2 4.6 collective-permute-done.10
  88.8 4.2 collective-permute-start.13
  95.4 21.1 %collective-permute-done.12 = bf16[4,128,512]{2,1,0:T(8,128)(2,1)S(1)} collective-permute-done((bf16[4,128,512]{2,1,0:T(8,128)(2,1)S(1)}, bf16[4,128,512]{2,1,0:T(8,128)(2,1)S(1)}, u32[]{:S(2)}, u32[]{:S(2)}) %collective-permute-start.12) | collective-permute-done | bytes 524320 | tf_op jit(solution)/shard_map/ppermute | solution.py:41
  116.8 16.8 %collective-permute-done.14 = bf16[4,64,1024]{2,1,0:T(8,128)(2,1)S(1)} collective-permute-done((bf16[4,64,1024]{2,1,0:T(8,128)(2,1)S(1)}, bf16[4,64,1024]{2,1,0:T(8,128)(2,1)S(1)}, u32[]{:S(2)}, u32[]{:S(2)}) %collective-permute-start.14) | collective-permute-done | bytes 524320 | tf_op jit(solution)/shard_map/ppermute | solution.py:41
  133.5 4.5 collective-permute-done.15
  138.1 2.5 collective-permute-start.16
  148.5 25.8 %all-gather.2.cloned.1.call-done = bf16[1024,8320]{1,0:T(8,128)(2,1)} async-done(((bf16[32,8320]{1,0:T(8,128)(2,1)}), bf16[1024,8320]{1,0:T(8,128)(2,1)}) %all-gather.2.cloned.1.call-update) | async-done | bytes 17039376 | tf_op jit(solution)/shard_map/all_gather | solution.py:506
  178.6 8.0 %fusion.8.packed_ref = bf16[512,3072]{1,0:T(8,128)(2,1)} fusion(bf16[512,1024]{1,0:T(8,128)(2,1)S(1)} %multiply_convert_fusion.5, bf16[1024,8320]{1,0:T(8,128)(2,1)} %all-gather.2.cloned.1.call-done), kind=kOutput, calls=%fused_computation.16 | convolution fusion | flops 3222798336 | bytes 10485760 | tf_op jit(solution)/shard_map/dot_general | solution.py:316
  186.6 9.3 %shard_map.365 = bf16[512,1024]{1,0:T(8,128)(2,1)} custom-call(s32[1]{0:T(128)} %bitcast.13.scalar_ref, bf16[512,3072]{1,0:T(8,128)(2,1)} %fusion.8.packed_ref), custom_call_target="tpu_custom_call" | custom-call | flops 8999999488 | bytes 8388608 | tf_op jit(solution)/shard_map/pallas_call | solution.py:412
  200.2 2.5 pad_maximum_fusion.1
  203.0 2.9 fusion.60
  218.0 8.3 %fusion.11 = bf16[512,3072]{1,0:T(8,128)(2,1)} fusion(bf16[512,1024]{1,0:T(8,128)(2,1)S(1)} %fusion.34, bf16[1024,8320]{1,0:T(8,128)(2,1)} %all-gather.2.cloned.1.call-done), kind=kOutput, calls=%fused_computation.17 | convolution fusion | flops 3222798336 | bytes 10485760 | tf_op jit(solution)/shard_map/dot_general | solution.py:316
  226.4 9.1 %shard_map.366 = bf16[4,128,1024]{2,1,0:T(8,128)(2,1)} custom-call(s32[1]{0:T(128)} %bitcast.32.scalar_ref, bf16[4,128,3072]{2,1,0:T(8,128)(2,1)} %bitcast.586), custom_call_target="tpu_custom_call" | custom-call | flops 8999999488 | bytes 8388608 | tf_op jit(solution)/shard_map/pallas_call | solution.py:412
  235.5 3.3 multiply_reduce_fusion.8
  241.1 4.9 fusion.210
  246.0 6.4 fusion.181
  252.4 4.6 fusion.211
  257.0 6.6 multiply_reduce_fusion.7
  271.5 4.9 convolution_convert_fusion.3
  282.6 6.2 fusion.180
  288.8 7.1 fusion.20
  295.9 8.0 %fusion.27 = bf16[512,2048]{1,0:T(8,128)(2,1)S(1)} fusion(f32[512,2048]{1,0:T(8,128)S(1)} %copy-done.150, bf16[512,1024]{1,0:T(8,128)(2,1)S(1)} %copy-done.49, bf16[2048,1024]{1,0:T(8,128)(2,1)} %collective-permute-done.23), kind=kOutput, calls=%fused_computation.31 | convolution fusion | flops 2168455168 | bytes 11534336 | tf_op jit(solution)/shard_map/dot_general | solution.py:308
  304.0 4.4 convolution_convert_fusion.2
  311.1 6.3 add_convert_fusion.1
  323.1 4.6 fusion.212
  327.7 5.1 multiply_reduce_fusion.2
  335.3 4.4 fusion.69
  341.5 17.8 %shard_map.367 = bf16[4,128,3072]{2,1,0:T(8,128)(2,1)} custom-call(s32[1]{0:T(128)} %bitcast.32.scalar_ref, bf16[4,128,3072]{2,1,0:T(8,128)(2,1)} %bitcast.587, bf16[4,128,1024]{2,1,0:T(8,128)(2,1)} %bitcast.594), custom_call_target="tpu_custom_call" | custom-call | flops 22000001024 | bytes 8388608 | tf_op jit(solution)/shard_map/pallas_call | solution.py:412
  361.9 5.5 add_convert_fusion
  369.6 4.6 collective-permute-done.32
  376.2 6.8 fusion.40
  393.6 16.2 %collective-permute-done.37 = bf16[512,512]{1,0:T(8,128)(2,1)S(1)} collective-permute-done((bf16[512,512]{1,0:T(8,128)(2,1)S(1)}, bf16[512,512]{1,0:T(8,128)(2,1)S(1)}, u32[]{:S(2)}, u32[]{:S(2)}) %collective-permute-start.37) | collective-permute-done | bytes 524320 | tf_op jit(solution)/shard_map/ppermute | solution.py:41
  419.1 3.9 fusion.66.up_ref
  423.9 22.3 %collective-permute-done.41 = bf16[4,2,64,512]{3,2,1,0:T(8,128)(2,1)S(1)} collective-permute-done((bf16[4,2,64,512]{3,2,1,0:T(8,128)(2,1)S(1)}, bf16[4,2,64,512]{3,2,1,0:T(8,128)(2,1)S(1)}, u32[]{:S(2)}, u32[]{:S(2)}) %collective-permute-start.41) | collective-permute-done | bytes 524320 | tf_op jit(solution)/shard_map/ppermute | solution.py:41
  447.9 2.7 collective-permute-start.46
  454.0 18.6 %shard_map.368 = bf16[512,3072]{1,0:T(8,128)(2,1)} custom-call(s32[1]{0:T(128)} %bitcast.13.scalar_ref, bf16[512,3072]{1,0:T(8,128)(2,1)} %fusion.8.packed_ref, bf16[512,1024]{1,0:T(8,128)(2,1)} %fusion.66.up_ref), custom_call_target="tpu_custom_call" | custom-call | flops 22000001024 | bytes 8388608 | tf_op jit(solution)/shard_map/pallas_call | solution.py:412
  472.7 3.6 convolution_convert_fusion
  489.2 6.0 fusion.4
  503.2 6.3 collective-permute-done.57
  511.6 10.3 %collective-permute-done.58 = bf16[4,2,64,512]{3,2,1,0:T(8,128)(2,1)S(1)} collective-permute-done((bf16[4,2,64,512]{3,2,1,0:T(8,128)(2,1)S(1)}, bf16[4,2,64,512]{3,2,1,0:T(8,128)(2,1)S(1)}, u32[]{:S(2)}, u32[]{:S(2)}) %collective-permute-start.58) | collective-permute-done | bytes 524320 | tf_op jit(solution)/shard_map/ppermute | solution.py:41
  529.2 3.9 collective-permute-start.61
  534.5 4.3 add_convert_fusion.2
  542.8 15.9 %collective-permute-done.76 = bf16[4,2,64,768]{3,2,0,1:T(8,128)(2,1)S(1)} collective-permute-done((bf16[4,2,64,768]{3,2,0,1:T(8,128)(2,1)S(1)}, bf16[4,2,64,768]{3,2,0,1:T(8,128)(2,1)S(1)}, u32[]{:S(2)}, u32[]{:S(2)}) %collective-permute-start.76) | collective-permute-done | bytes 786464 | tf_op jit(solution)/shard_map/ppermute | solution.py:41
  558.7 3.3 collective-permute-start.62
  565.4 3.6 collective-permute-start.66
  574.0 8.5 %collective-permute-start.70 = (bf16[64,1536]{1,0:T(8,128)(2,1)}, bf16[64,1536]{1,0:T(8,128)(2,1)}, u32[]{:S(2)}, u32[]{:S(2)}) collective-permute-start(bf16[64,1536]{1,0:T(8,128)(2,1)} %get-tuple-element.345), channel_id=1, source_target_pairs={{24,0},{0,8},{8,16},{16,24},{25,1},{1,9},{9,17},{17,25},{26,2},{2,... | collective-permute-start | bytes 589832 | tf_op jit(solution)/shard_map/ppermute | solution.py:41
  582.5 2.8 collective-permute-done.65
  585.2 11.0 %collective-permute-start.72 = (bf16[64,1536]{1,0:T(8,128)(2,1)}, bf16[64,1536]{1,0:T(8,128)(2,1)}, u32[]{:S(2)}, u32[]{:S(2)}) collective-permute-start(bf16[64,1536]{1,0:T(8,128)(2,1)} %get-tuple-element.344), channel_id=1, source_target_pairs={{8,0},{16,8},{24,16},{0,24},{9,1},{17,9},{25,17},{1,25},{10,2},{18... | collective-permute-start | bytes 589832 | tf_op jit(solution)/shard_map/ppermute | solution.py:41
  614.1 2.8 collective-permute-start.75
  625.9 4.2 collective-permute-done.84
  638.8 4.1 collective-permute-done.81
  642.9 4.4 collective-permute-start.88
  647.2 3.4 collective-permute-start.89
  667.5 4.4 collective-permute-done.101
  675.9 3.5 collective-permute-start.104
  680.6 3.2 collective-permute-done.105
  689.8 2.6 multiply_subtract_fusion.4
  698.7 3.5 multiply_subtract_fusion
  (755 shorter events, 236.0 us)
Async XLA Ops:
  7.2 167.1 %all-gather.2.cloned.1.call-start = ((), (), s32[]{:S(2)}) async-start(), calls=%async_computation | async-start | bytes 17571840 | tf_op jit(solution)/shard_map/all_gather | solution.py:506
  14.5 32.7 %collective-permute-start.3 = (bf16[128,1024]{1,0:T(8,128)(2,1)S(1)}, bf16[128,1024]{1,0:T(8,128)(2,1)}, u32[]{:S(2)}, u32[]{:S(2)}) collective-permute-start(bf16[128,1024]{1,0:T(8,128)(2,1)S(1)} %convert_element_type.587), channel_id=1, source_target_pairs={{8,0},{16,8},{24,16},{0,24},{9,1},{17,9},{25,17},{1,25},{10,2},{18... | collective-permute-start | bytes 786440 | tf_op jit(solution)/shard_map/ppermute | solution.py:41
  19.7 27.5 %collective-permute-start.4 = (bf16[128,1024]{1,0:T(8,128)(2,1)S(1)}, bf16[128,1024]{1,0:T(8,128)(2,1)S(1)}, u32[]{:S(2)}, u32[]{:S(2)}) collective-permute-start(bf16[128,1024]{1,0:T(8,128)(2,1)S(1)} %convert_element_type.587), channel_id=1, source_target_pairs={{24,0},{0,8},{8,16},{16,24},{25,1},{1,9},{9,17},{17,25},{26,2},{2,... | collective-permute-start | bytes 786440 | tf_op jit(solution)/shard_map/ppermute | solution.py:41
  22.1 25.1 %collective-permute-start.2 = (bf16[32,2048]{1,0:T(8,128)(2,1)}, bf16[32,2048]{1,0:T(8,128)(2,1)S(1)}, u32[]{:S(2)}, u32[]{:S(2)}) collective-permute-start(bf16[32,2048]{1,0:T(8,128)(2,1)} %bitcast.525), channel_id=1, source_target_pairs={{1,0},{0,1},{3,2},{2,3},{5,4},{4,5},{7,6},{6,7},{9,8},{8,9},{11,10... | collective-permute-start | bytes 393224 | tf_op jit(solution)/shard_map/ppermute | solution.py:41
  23.2 56.2 %collective-permute-start.1 = (bf16[256,1024]{1,0:T(8,128)(2,1)S(1)}, bf16[256,1024]{1,0:T(8,128)(2,1)S(1)}, u32[]{:S(2)}, u32[]{:S(2)}) collective-permute-start(bf16[256,1024]{1,0:T(8,128)(2,1)S(1)} %get-tuple-element.336), channel_id=1, source_target_pairs={{2,0},{0,2},{3,1},{1,3},{6,4},{4,6},{7,5},{5,7},{10,8},{8,10},{11,... | collective-permute-start | bytes 1572872 | tf_op jit(solution)/shard_map/ppermute | solution.py:41
  47.3 32.1 %collective-permute-start.5 = (bf16[64,2048]{1,0:T(8,128)(2,1)S(1)}, bf16[64,2048]{1,0:T(8,128)(2,1)S(1)}, u32[]{:S(2)}, u32[]{:S(2)}) collective-permute-start(bf16[64,2048]{1,0:T(8,128)(2,1)S(1)} %bitcast.551), channel_id=1, source_target_pairs={{8,0},{16,8},{24,16},{0,24},{9,1},{17,9},{25,17},{1,25},{10,2},{18... | collective-permute-start | bytes 786440 | tf_op jit(solution)/shard_map/ppermute | solution.py:41
  49.3 30.0 %collective-permute-start.6 = (bf16[64,2048]{1,0:T(8,128)(2,1)S(1)}, bf16[64,2048]{1,0:T(8,128)(2,1)S(1)}, u32[]{:S(2)}, u32[]{:S(2)}) collective-permute-start(bf16[64,2048]{1,0:T(8,128)(2,1)S(1)} %bitcast.552), channel_id=1, source_target_pairs={{24,0},{0,8},{8,16},{16,24},{25,1},{1,9},{9,17},{17,25},{26,2},{2,... | collective-permute-start | bytes 786440 | tf_op jit(solution)/shard_map/ppermute | solution.py:41
  51.4 27.9 %collective-permute-start.7 = (bf16[128,512]{1,0:T(8,128)(2,1)S(1)}, bf16[128,512]{1,0:T(8,128)(2,1)S(1)}, u32[]{:S(2)}, u32[]{:S(2)}) collective-permute-start(bf16[128,512]{1,0:T(8,128)(2,1)S(1)} %slice.86), channel_id=1, source_target_pairs={{8,0},{16,8},{24,16},{0,24},{9,1},{17,9},{25,17},{1,25},{10,2},{18... | collective-permute-start | bytes 393224 | tf_op jit(solution)/shard_map/ppermute | solution.py:41
  55.3 24.0 %collective-permute-start.8 = (bf16[128,512]{1,0:T(8,128)(2,1)S(1)}, bf16[128,512]{1,0:T(8,128)(2,1)S(1)}, u32[]{:S(2)}, u32[]{:S(2)}) collective-permute-start(bf16[128,512]{1,0:T(8,128)(2,1)S(1)} %slice.87), channel_id=1, source_target_pairs={{24,0},{0,8},{8,16},{16,24},{25,1},{1,9},{9,17},{17,25},{26,2},{2,... | collective-permute-start | bytes 393224 | tf_op jit(solution)/shard_map/ppermute | solution.py:41
  79.3 69.2 %collective-permute-start = (bf16[256,1024]{1,0:T(8,128)(2,1)}, bf16[256,1024]{1,0:T(8,128)(2,1)}, u32[]{:S(2)}, u32[]{:S(2)}) collective-permute-start(bf16[256,1024]{1,0:T(8,128)(2,1)} %get-tuple-element.335), channel_id=1, source_target_pairs={{2,0},{0,2},{3,1},{1,3},{6,4},{4,6},{7,5},{5,7},{10,8},{8,10},{11,... | collective-permute-start | bytes 1572872 | tf_op jit(solution)/shard_map/ppermute | solution.py:41
  79.5 13.5 %collective-permute-start.9 = (bf16[2,256,1024]{2,1,0:T(8,128)(2,1)S(1)}, bf16[2,256,1024]{2,1,0:T(8,128)(2,1)S(1)}, u32[]{:S(2)}, u32[]{:S(2)}) collective-permute-start(bf16[2,256,1024]{2,1,0:T(8,128)(2,1)S(1)} %bitcast_dynamic-update-slice_fusion.11), channel_id=1, source_target_pairs={{1,0},{0,1},{3,2},{2,3},{5,4},{4,5},{7,6},{6,7},{9,8},{8,9},{11,10... | collective-permute-start | bytes 3145736 | tf_op jit(solution)/shard_map/ppermute | solution.py:41
  79.8 36.8 %collective-permute-start.12 = (bf16[4,128,512]{2,1,0:T(8,128)(2,1)S(1)}, bf16[4,128,512]{2,1,0:T(8,128)(2,1)S(1)}, u32[]{:S(2)}, u32[]{:S(2)}) collective-permute-start(bf16[4,128,512]{2,1,0:T(8,128)(2,1)S(1)} %get-tuple-element.334), channel_id=1, source_target_pairs={{2,0},{0,2},{3,1},{1,3},{6,4},{4,6},{7,5},{5,7},{10,8},{8,10},{11,... | collective-permute-start | bytes 1572872 | tf_op jit(solution)/shard_map/ppermute | solution.py:41
  88.8 28.0 %collective-permute-start.13 = (bf16[4,128,512]{2,1,0:T(8,128)(2,1)S(1)}, bf16[4,128,512]{2,1,0:T(8,128)(2,1)S(1)}, u32[]{:S(2)}, u32[]{:S(2)}) collective-permute-start(bf16[4,128,512]{2,1,0:T(8,128)(2,1)S(1)} %get-tuple-element.333), channel_id=1, source_target_pairs={{4,0},{0,4},{5,1},{1,5},{6,2},{2,6},{7,3},{3,7},{12,8},{8,12},{13,... | collective-permute-start | bytes 1572872 | tf_op jit(solution)/shard_map/ppermute | solution.py:41
  93.1 40.4 %collective-permute-start.14 = (bf16[4,64,1024]{2,1,0:T(8,128)(2,1)S(1)}, bf16[4,64,1024]{2,1,0:T(8,128)(2,1)S(1)}, u32[]{:S(2)}, u32[]{:S(2)}) collective-permute-start(bf16[4,64,1024]{2,1,0:T(8,128)(2,1)S(1)} %get-tuple-element.332), channel_id=1, source_target_pairs={{2,0},{0,2},{3,1},{1,3},{6,4},{4,6},{7,5},{5,7},{10,8},{8,10},{11,... | collective-permute-start | bytes 1572872 | tf_op jit(solution)/shard_map/ppermute | solution.py:41
  93.2 44.8 %collective-permute-start.15 = (bf16[4,64,1024]{2,1,0:T(8,128)(2,1)S(1)}, bf16[4,64,1024]{2,1,0:T(8,128)(2,1)S(1)}, u32[]{:S(2)}, u32[]{:S(2)}) collective-permute-start(bf16[4,64,1024]{2,1,0:T(8,128)(2,1)S(1)} %get-tuple-element.331), channel_id=1, source_target_pairs={{4,0},{0,4},{5,1},{1,5},{6,2},{2,6},{7,3},{3,7},{12,8},{8,12},{13,... | collective-permute-start | bytes 1572872 | tf_op jit(solution)/shard_map/ppermute | solution.py:41
  138.1 57.7 %collective-permute-start.16 = (bf16[4,2,128,512]{3,2,1,0:T(8,128)(2,1)S(1)}, bf16[4,2,128,512]{3,2,1,0:T(8,128)(2,1)}, u32[]{:S(2)}, u32[]{:S(2)}) collective-permute-start(bf16[4,2,128,512]{3,2,1,0:T(8,128)(2,1)S(1)} %bitcast_dynamic-update-slice_fusion.7), channel_id=1, source_target_pairs={{4,0},{0,4},{5,1},{1,5},{6,2},{2,6},{7,3},{3,7},{12,8},{8,12},{13,... | collective-permute-start | bytes 3145736 | tf_op jit(solution)/shard_map/ppermute | solution.py:41
  142.6 53.3 %collective-permute-start.17 = (bf16[4,2,128,512]{3,2,1,0:T(8,128)(2,1)}, bf16[4,2,128,512]{3,2,1,0:T(8,128)(2,1)}, u32[]{:S(2)}, u32[]{:S(2)}) collective-permute-start(bf16[4,2,128,512]{3,2,1,0:T(8,128)(2,1)} %bitcast_dynamic-update-slice_fusion.10), channel_id=1, source_target_pairs={{2,0},{0,2},{3,1},{1,3},{6,4},{4,6},{7,5},{5,7},{10,8},{8,10},{11,... | collective-permute-start | bytes 3145736 | tf_op jit(solution)/shard_map/ppermute | solution.py:41
  144.5 51.3 %collective-permute-start.18 = (bf16[4,2,64,1024]{3,2,1,0:T(8,128)(2,1)}, bf16[4,2,64,1024]{3,2,1,0:T(8,128)(2,1)}, u32[]{:S(2)}, u32[]{:S(2)}) collective-permute-start(bf16[4,2,64,1024]{3,2,1,0:T(8,128)(2,1)} %bitcast_dynamic-update-slice_fusion.6), channel_id=1, source_target_pairs={{4,0},{0,4},{5,1},{1,5},{6,2},{2,6},{7,3},{3,7},{12,8},{8,12},{13,... | collective-permute-start | bytes 3145736 | tf_op jit(solution)/shard_map/ppermute | solution.py:41
  146.5 49.4 %collective-permute-start.19 = (bf16[4,2,64,1024]{3,2,1,0:T(8,128)(2,1)}, bf16[4,2,64,1024]{3,2,1,0:T(8,128)(2,1)}, u32[]{:S(2)}, u32[]{:S(2)}) collective-permute-start(bf16[4,2,64,1024]{3,2,1,0:T(8,128)(2,1)} %bitcast_dynamic-update-slice_fusion.9), channel_id=1, source_target_pairs={{2,0},{0,2},{3,1},{1,3},{6,4},{4,6},{7,5},{5,7},{10,8},{8,10},{11,... | collective-permute-start | bytes 3145736 | tf_op jit(solution)/shard_map/ppermute | solution.py:41
  202.8 54.2 %collective-permute-start.23 = (bf16[2048,1024]{1,0:T(8,128)(2,1)}, bf16[2048,1024]{1,0:T(8,128)(2,1)}, u32[]{:S(2)}, u32[]{:S(2)}) collective-permute-start(bf16[2048,1024]{1,0:T(8,128)(2,1)} %bitcast.40), channel_id=1, source_target_pairs={{1,0},{0,1},{3,2},{2,3},{5,4},{4,5},{7,6},{6,7},{9,8},{8,9},{11,10... | collective-permute-start | bytes 12582920 | tf_op jit(solution)/shard_map/ppermute | solution.py:41
  217.1 35.3 %collective-permute-start.22 = (bf16[1024,2048]{1,0:T(8,128)(2,1)}, bf16[1024,2048]{1,0:T(8,128)(2,1)}, u32[]{:S(2)}, u32[]{:S(2)}) collective-permute-start(bf16[1024,2048]{1,0:T(8,128)(2,1)} %bitcast.37), channel_id=1, source_target_pairs={{1,0},{0,1},{3,2},{2,3},{5,4},{4,5},{7,6},{6,7},{9,8},{8,9},{11,10... | collective-permute-start | bytes 12582920 | tf_op jit(solution)/shard_map/ppermute | solution.py:41
  276.4 27.6 %collective-permute-start.29 = (bf16[2048,1024]{1,0:T(8,128)(2,1)}, bf16[2048,1024]{1,0:T(8,128)(2,1)}, u32[]{:S(2)}, u32[]{:S(2)}) collective-permute-start(bf16[2048,1024]{1,0:T(8,128)(2,1)} %convolution_convert_fusion.3), channel_id=1, source_target_pairs={{1,0},{0,1},{3,2},{2,3},{5,4},{4,5},{7,6},{6,7},{9,8},{8,9},{11,10... | collective-permute-start | bytes 12582920 | tf_op jit(solution)/shard_map/ppermute | solution.py:41
  278.5 25.4 %collective-permute-start.28 = (bf16[1024,512]{1,0:T(8,128)(2,1)S(1)}, bf16[1024,512]{1,0:T(8,128)(2,1)S(1)}, u32[]{:S(2)}, u32[]{:S(2)}) collective-permute-start(bf16[1024,512]{1,0:T(8,128)(2,1)S(1)} %convolution_convert_fusion.6), channel_id=1, source_target_pairs={{1,0},{0,1},{3,2},{2,3},{5,4},{4,5},{7,6},{6,7},{9,8},{8,9},{11,10... | collective-permute-start | bytes 3145736 | tf_op jit(solution)/shard_map/ppermute | solution.py:41
  308.4 26.9 %collective-permute-start.31 = (bf16[1024,2048]{1,0:T(8,128)(2,1)}, bf16[1024,2048]{1,0:T(8,128)(2,1)}, u32[]{:S(2)}, u32[]{:S(2)}) collective-permute-start(bf16[1024,2048]{1,0:T(8,128)(2,1)} %convolution_convert_fusion.2), channel_id=1, source_target_pairs={{1,0},{0,1},{3,2},{2,3},{5,4},{4,5},{7,6},{6,7},{9,8},{8,9},{11,10... | collective-permute-start | bytes 12582920 | tf_op jit(solution)/shard_map/ppermute | solution.py:41
  310.1 25.2 %collective-permute-start.30 = (bf16[512,512]{1,0:T(8,128)(2,1)S(1)}, bf16[512,512]{1,0:T(8,128)(2,1)S(1)}, u32[]{:S(2)}, u32[]{:S(2)}) collective-permute-start(bf16[512,512]{1,0:T(8,128)(2,1)S(1)} %dynamic-slice_bitcast_fusion.9), channel_id=1, source_target_pairs={{2,0},{0,2},{3,1},{1,3},{6,4},{4,6},{7,5},{5,7},{10,8},{8,10},{11,... | collective-permute-start | bytes 1572872 | tf_op jit(solution)/shard_map/ppermute | solution.py:41
  319.0 50.6 %collective-permute-start.33 = (bf16[4,2,128,512]{3,2,0,1:T(8,128)(2,1)}, bf16[4,2,128,512]{3,2,0,1:T(8,128)(2,1)}, u32[]{:S(2)}, u32[]{:S(2)}) collective-permute-start(bf16[4,2,128,512]{3,2,0,1:T(8,128)(2,1)} %bitcast.521), channel_id=1, source_target_pairs={{2,0},{0,2},{3,1},{1,3},{6,4},{4,6},{7,5},{5,7},{10,8},{8,10},{11,... | collective-permute-start | bytes 3145736 | tf_op jit(solution)/shard_map/ppermute | solution.py:41
  322.2 47.4 %collective-permute-start.34 = (bf16[4,2,128,512]{3,2,0,1:T(8,128)(2,1)}, bf16[4,2,128,512]{3,2,0,1:T(8,128)(2,1)}, u32[]{:S(2)}, u32[]{:S(2)}) collective-permute-start(bf16[4,2,128,512]{3,2,0,1:T(8,128)(2,1)} %bitcast.520), channel_id=1, source_target_pairs={{4,0},{0,4},{5,1},{1,5},{6,2},{2,6},{7,3},{3,7},{12,8},{8,12},{13,... | collective-permute-start | bytes 3145736 | tf_op jit(solution)/shard_map/ppermute | solution.py:41
  360.6 13.5 %collective-permute-start.32 = (bf16[512,512]{1,0:T(8,128)(2,1)S(1)}, bf16[512,512]{1,0:T(8,128)(2,1)S(1)}, u32[]{:S(2)}, u32[]{:S(2)}) collective-permute-start(bf16[512,512]{1,0:T(8,128)(2,1)S(1)} %fusion.79), channel_id=1, source_target_pairs={{4,0},{0,4},{5,1},{1,5},{6,2},{2,6},{7,3},{3,7},{12,8},{8,12},{13,... | collective-permute-start | bytes 1572872 | tf_op jit(solution)/shard_map/ppermute | solution.py:41
  376.1 35.8 %collective-permute-start.40 = (bf16[1024,1536]{1,0:T(8,128)(2,1)S(1)}, bf16[1024,1536]{1,0:T(8,128)(2,1)S(1)}, u32[]{:S(2)}, u32[]{:S(2)}) collective-permute-start(bf16[1024,1536]{1,0:T(8,128)(2,1)S(1)} %convolution_convert_fusion.1), channel_id=1, source_target_pairs={{1,0},{0,1},{3,2},{2,3},{5,4},{4,5},{7,6},{6,7},{9,8},{8,9},{11,10... | collective-permute-start | bytes 9437192 | tf_op jit(solution)/shard_map/ppermute | solution.py:41
  384.3 25.5 %collective-permute-start.37 = (bf16[512,512]{1,0:T(8,128)(2,1)S(1)}, bf16[512,512]{1,0:T(8,128)(2,1)S(1)}, u32[]{:S(2)}, u32[]{:S(2)}) collective-permute-start(bf16[512,512]{1,0:T(8,128)(2,1)S(1)} %add_convert_fusion.10), channel_id=1, source_target_pairs={{16,0},{24,8},{0,16},{8,24},{17,1},{25,9},{1,17},{9,25},{18,2},{26... | collective-permute-start | bytes 1572872 | tf_op jit(solution)/shard_map/ppermute | solution.py:41
  387.1 24.1 %collective-permute-start.38 = (bf16[4,128,512]{2,1,0:T(8,128)(2,1)S(1)}, bf16[4,128,512]{2,1,0:T(8,128)(2,1)S(1)}, u32[]{:S(2)}, u32[]{:S(2)}) collective-permute-start(bf16[4,128,512]{2,1,0:T(8,128)(2,1)S(1)} %dynamic-slice_bitcast_fusion.8), channel_id=1, source_target_pairs={{4,0},{0,4},{5,1},{1,5},{6,2},{2,6},{7,3},{3,7},{12,8},{8,12},{13,... | collective-permute-start | bytes 1572872 | tf_op jit(solution)/shard_map/ppermute | solution.py:41
  390.0 21.9 %collective-permute-start.39 = (bf16[4,128,512]{2,1,0:T(8,128)(2,1)S(1)}, bf16[4,128,512]{2,1,0:T(8,128)(2,1)S(1)}, u32[]{:S(2)}, u32[]{:S(2)}) collective-permute-start(bf16[4,128,512]{2,1,0:T(8,128)(2,1)S(1)} %dynamic-slice_bitcast_fusion.7), channel_id=1, source_target_pairs={{2,0},{0,2},{3,1},{1,3},{6,4},{4,6},{7,5},{5,7},{10,8},{8,10},{11,... | collective-permute-start | bytes 1572872 | tf_op jit(solution)/shard_map/ppermute | solution.py:41
  392.2 55.7 %collective-permute-start.47 = (bf16[4,2,64,1024]{3,2,0,1:T(8,128)(2,1)S(1)}, bf16[4,2,64,1024]{3,2,0,1:T(8,128)(2,1)}, u32[]{:S(2)}, u32[]{:S(2)}) collective-permute-start(bf16[4,2,64,1024]{3,2,0,1:T(8,128)(2,1)S(1)} %bitcast.554), channel_id=1, source_target_pairs={{4,0},{0,4},{5,1},{1,5},{6,2},{2,6},{7,3},{3,7},{12,8},{8,12},{13,... | collective-permute-start | bytes 3145736 | tf_op jit(solution)/shard_map/ppermute | solution.py:41
  409.9 40.7 %collective-permute-start.48 = (bf16[4,2,64,1024]{3,2,1,0:T(8,128)(2,1)S(1)}, bf16[4,2,64,1024]{3,2,1,0:T(8,128)(2,1)S(1)}, u32[]{:S(2)}, u32[]{:S(2)}) collective-permute-start(bf16[4,2,64,1024]{3,2,1,0:T(8,128)(2,1)S(1)} %dynamic-slice_bitcast_fusion), channel_id=1, source_target_pairs={{2,0},{0,2},{3,1},{1,3},{6,4},{4,6},{7,5},{5,7},{10,8},{8,10},{11,... | collective-permute-start | bytes 3145736 | tf_op jit(solution)/shard_map/ppermute | solution.py:41
  411.2 35.0 %collective-permute-start.41 = (bf16[4,2,64,512]{3,2,1,0:T(8,128)(2,1)S(1)}, bf16[4,2,64,512]{3,2,1,0:T(8,128)(2,1)S(1)}, u32[]{:S(2)}, u32[]{:S(2)}) collective-permute-start(bf16[4,2,64,512]{3,2,1,0:T(8,128)(2,1)S(1)} %dynamic-slice_bitcast_fusion.6), channel_id=1, source_target_pairs={{2,0},{0,2},{3,1},{1,3},{6,4},{4,6},{7,5},{5,7},{10,8},{8,10},{11,... | collective-permute-start | bytes 1572872 | tf_op jit(solution)/shard_map/ppermute | solution.py:41
  412.7 35.2 %collective-permute-start.42 = (bf16[1024,512]{1,0:T(8,128)(2,1)S(1)}, bf16[1024,512]{1,0:T(8,128)(2,1)S(1)}, u32[]{:S(2)}, u32[]{:S(2)}) collective-permute-start(bf16[1024,512]{1,0:T(8,128)(2,1)S(1)} %convolution_convert_fusion.4), channel_id=1, source_target_pairs={{1,0},{0,1},{3,2},{2,3},{5,4},{4,5},{7,6},{6,7},{9,8},{8,9},{11,10... | collective-permute-start | bytes 3145736 | tf_op jit(solution)/shard_map/ppermute | solution.py:41
  413.9 39.0 %collective-permute-start.44 = (bf16[128,1024]{1,0:T(8,128)(2,1)S(1)}, bf16[128,1024]{1,0:T(8,128)(2,1)}, u32[]{:S(2)}, u32[]{:S(2)}) collective-permute-start(bf16[128,1024]{1,0:T(8,128)(2,1)S(1)} %get-tuple-element.329), channel_id=1, source_target_pairs={{24,0},{0,8},{8,16},{16,24},{25,1},{1,9},{9,17},{17,25},{26,2},{2,... | collective-permute-start | bytes 786440 | tf_op jit(solution)/shard_map/ppermute | solution.py:41
  446.2 26.5 %collective-permute-start.43 = (bf16[512,512]{1,0:T(8,128)(2,1)}, bf16[512,512]{1,0:T(8,128)(2,1)}, u32[]{:S(2)}, u32[]{:S(2)}) collective-permute-start(bf16[512,512]{1,0:T(8,128)(2,1)} %add_convert_fusion.9), channel_id=1, source_target_pairs={{8,0},{16,8},{24,16},{0,24},{9,1},{17,9},{25,17},{1,25},{10,2},{18... | collective-permute-start | bytes 1572872 | tf_op jit(solution)/shard_map/ppermute | solution.py:41
  447.9 24.8 %collective-permute-start.45 = (bf16[128,1024]{1,0:T(8,128)(2,1)}, bf16[128,1024]{1,0:T(8,128)(2,1)S(1)}, u32[]{:S(2)}, u32[]{:S(2)}) collective-permute-start(bf16[128,1024]{1,0:T(8,128)(2,1)} %get-tuple-element.330), channel_id=1, source_target_pairs={{16,0},{24,8},{0,16},{8,24},{17,1},{25,9},{1,17},{9,25},{18,2},{26... | collective-permute-start | bytes 786440 | tf_op jit(solution)/shard_map/ppermute | solution.py:41
  447.9 24.8 %collective-permute-start.46 = (bf16[128,1024]{1,0:T(8,128)(2,1)}, bf16[128,1024]{1,0:T(8,128)(2,1)}, u32[]{:S(2)}, u32[]{:S(2)}) collective-permute-start(bf16[128,1024]{1,0:T(8,128)(2,1)} %get-tuple-element.328), channel_id=1, source_target_pairs={{8,0},{16,8},{24,16},{0,24},{9,1},{17,9},{25,17},{1,25},{10,2},{18... | collective-permute-start | bytes 786440 | tf_op jit(solution)/shard_map/ppermute | solution.py:41
  451.6 21.1 %collective-permute-start.49 = (bf16[4,2,64,768]{3,2,0,1:T(8,128)(2,1)}, bf16[4,2,64,768]{3,2,0,1:T(8,128)(2,1)}, u32[]{:S(2)}, u32[]{:S(2)}) collective-permute-start(bf16[4,2,64,768]{3,2,0,1:T(8,128)(2,1)} %bitcast.523), channel_id=1, source_target_pairs={{2,0},{0,2},{3,1},{1,3},{6,4},{4,6},{7,5},{5,7},{10,8},{8,10},{11,... | collective-permute-start | bytes 2359304 | tf_op jit(solution)/shard_map/ppermute | solution.py:41
  452.9 19.8 %collective-permute-start.50 = (bf16[4,2,64,768]{3,2,1,0:T(8,128)(2,1)}, bf16[4,2,64,768]{3,2,1,0:T(8,128)(2,1)}, u32[]{:S(2)}, u32[]{:S(2)}) collective-permute-start(bf16[4,2,64,768]{3,2,1,0:T(8,128)(2,1)} %dynamic-slice_bitcast_fusion.2), channel_id=1, source_target_pairs={{4,0},{0,4},{5,1},{1,5},{6,2},{2,6},{7,3},{3,7},{12,8},{8,12},{13,... | collective-permute-start | bytes 2359304 | tf_op jit(solution)/shard_map/ppermute | solution.py:41
  476.4 45.6 %collective-permute-start.51 = (bf16[1024,1536]{1,0:T(8,128)(2,1)S(1)}, bf16[1024,1536]{1,0:T(8,128)(2,1)S(1)}, u32[]{:S(2)}, u32[]{:S(2)}) collective-permute-start(bf16[1024,1536]{1,0:T(8,128)(2,1)S(1)} %convolution_convert_fusion), channel_id=1, source_target_pairs={{1,0},{0,1},{3,2},{2,3},{5,4},{4,5},{7,6},{6,7},{9,8},{8,9},{11,10... | collective-permute-start | bytes 9437192 | tf_op jit(solution)/shard_map/ppermute | solution.py:41
  478.0 18.8 %collective-permute-start.52 = (bf16[256,512]{1,0:T(8,128)(2,1)S(1)}, bf16[256,512]{1,0:T(8,128)(2,1)S(1)}, u32[]{:S(2)}, u32[]{:S(2)}) collective-permute-start(bf16[256,512]{1,0:T(8,128)(2,1)S(1)} %dynamic-slice_bitcast_fusion.19), channel_id=1, source_target_pairs={{1,0},{0,1},{3,2},{2,3},{5,4},{4,5},{7,6},{6,7},{9,8},{8,9},{11,10... | collective-permute-start | bytes 786440 | tf_op jit(solution)/shard_map/ppermute | solution.py:41
  480.5 29.0 %collective-permute-start.53 = (bf16[4,64,1024]{2,1,0:T(8,128)(2,1)S(1)}, bf16[4,64,1024]{2,1,0:T(8,128)(2,1)S(1)}, u32[]{:S(2)}, u32[]{:S(2)}) collective-permute-start(bf16[4,64,1024]{2,1,0:T(8,128)(2,1)S(1)} %dynamic-slice_bitcast_fusion.5), channel_id=1, source_target_pairs={{2,0},{0,2},{3,1},{1,3},{6,4},{4,6},{7,5},{5,7},{10,8},{8,10},{11,... | collective-permute-start | bytes 1572872 | tf_op jit(solution)/shard_map/ppermute | solution.py:41
  481.6 16.2 %collective-permute-start.55 = (bf16[4,64,512]{2,1,0:T(8,128)(2,1)S(1)}, bf16[4,64,512]{2,1,0:T(8,128)(2,1)S(1)}, u32[]{:S(2)}, u32[]{:S(2)}) collective-permute-start(bf16[4,64,512]{2,1,0:T(8,128)(2,1)S(1)} %dynamic-slice_bitcast_fusion.18), channel_id=1, source_target_pairs={{4,0},{0,4},{5,1},{1,5},{6,2},{2,6},{7,3},{3,7},{12,8},{8,12},{13,... | collective-permute-start | bytes 786440 | tf_op jit(solution)/shard_map/ppermute | solution.py:41
  484.9 14.0 %collective-permute-start.56 = (bf16[4,64,768]{2,1,0:T(8,128)(2,1)S(1)}, bf16[4,64,768]{2,1,0:T(8,128)(2,1)S(1)}, u32[]{:S(2)}, u32[]{:S(2)}) collective-permute-start(bf16[4,64,768]{2,1,0:T(8,128)(2,1)S(1)} %dynamic-slice_bitcast_fusion.13), channel_id=1, source_target_pairs={{4,0},{0,4},{5,1},{1,5},{6,2},{2,6},{7,3},{3,7},{12,8},{8,12},{13,... | collective-permute-start | bytes 1179656 | tf_op jit(solution)/shard_map/ppermute | solution.py:41
  496.7 14.9 %collective-permute-start.54 = (bf16[4,64,1024]{2,1,0:T(8,128)(2,1)S(1)}, bf16[4,64,1024]{2,1,0:T(8,128)(2,1)S(1)}, u32[]{:S(2)}, u32[]{:S(2)}) collective-permute-start(bf16[4,64,1024]{2,1,0:T(8,128)(2,1)S(1)} %dynamic-slice_bitcast_fusion.4), channel_id=1, source_target_pairs={{4,0},{0,4},{5,1},{1,5},{6,2},{2,6},{7,3},{3,7},{12,8},{8,12},{13,... | collective-permute-start | bytes 1572872 | tf_op jit(solution)/shard_map/ppermute | solution.py:41
  497.8 24.1 %collective-permute-start.58 = (bf16[4,2,64,512]{3,2,1,0:T(8,128)(2,1)S(1)}, bf16[4,2,64,512]{3,2,1,0:T(8,128)(2,1)S(1)}, u32[]{:S(2)}, u32[]{:S(2)}) collective-permute-start(bf16[4,2,64,512]{3,2,1,0:T(8,128)(2,1)S(1)} %dynamic-slice_bitcast_fusion.3), channel_id=1, source_target_pairs={{4,0},{0,4},{5,1},{1,5},{6,2},{2,6},{7,3},{3,7},{12,8},{8,12},{13,... | collective-permute-start | bytes 1572872 | tf_op jit(solution)/shard_map/ppermute | solution.py:41
  526.3 71.1 %collective-permute-start.59 = (bf16[1024,512]{1,0:T(8,128)(2,1)}, bf16[1024,512]{1,0:T(8,128)(2,1)}, u32[]{:S(2)}, u32[]{:S(2)}) collective-permute-start(bf16[1024,512]{1,0:T(8,128)(2,1)} %fusion.65), channel_id=1, source_target_pairs={{1,0},{0,1},{3,2},{2,3},{5,4},{4,5},{7,6},{6,7},{9,8},{8,9},{11,10... | collective-permute-start | bytes 3145736 | tf_op jit(solution)/shard_map/ppermute | solution.py:41
  527.7 35.2 %collective-permute-start.60 = (f32[5,1024]{1,0:T(8,128)}, f32[5,1024]{1,0:T(8,128)S(1)}, u32[]{:S(2)}, u32[]{:S(2)}) collective-permute-start(f32[5,1024]{1,0:T(8,128)} %stack.56), channel_id=1, source_target_pairs={{1,0},{0,1},{3,2},{2,3},{5,4},{4,5},{7,6},{6,7},{9,8},{8,9},{11,10... | collective-permute-start | bytes 61448 | tf_op jit(solution)/shard_map/ppermute | solution.py:41
  529.2 35.1 %collective-permute-start.61 = (bf16[64,512]{1,0:T(8,128)(2,1)S(1)}, bf16[64,512]{1,0:T(8,128)(2,1)S(1)}, u32[]{:S(2)}, u32[]{:S(2)}) collective-permute-start(bf16[64,512]{1,0:T(8,128)(2,1)S(1)} %get-tuple-element.365), channel_id=1, source_target_pairs={{24,0},{0,8},{8,16},{16,24},{25,1},{1,9},{9,17},{17,25},{26,2},{2,... | collective-permute-start | bytes 196616 | tf_op jit(solution)/shard_map/ppermute | solution.py:41
  539.3 19.4 %collective-permute-start.76 = (bf16[4,2,64,768]{3,2,0,1:T(8,128)(2,1)S(1)}, bf16[4,2,64,768]{3,2,0,1:T(8,128)(2,1)S(1)}, u32[]{:S(2)}, u32[]{:S(2)}) collective-permute-start(bf16[4,2,64,768]{3,2,0,1:T(8,128)(2,1)S(1)} %bitcast.565), channel_id=1, source_target_pairs={{4,0},{0,4},{5,1},{1,5},{6,2},{2,6},{7,3},{3,7},{12,8},{8,12},{13,... | collective-permute-start | bytes 2359304 | tf_op jit(solution)/shard_map/ppermute | solution.py:41
  540.4 21.5 %collective-permute-start.77 = (bf16[4,2,64,768]{3,2,1,0:T(8,128)(2,1)S(1)}, bf16[4,2,64,768]{3,2,1,0:T(8,128)(2,1)S(1)}, u32[]{:S(2)}, u32[]{:S(2)}) collective-permute-start(bf16[4,2,64,768]{3,2,1,0:T(8,128)(2,1)S(1)} %dynamic-slice_bitcast_fusion.1), channel_id=1, source_target_pairs={{2,0},{0,2},{3,1},{1,3},{6,4},{4,6},{7,5},{5,7},{10,8},{8,10},{11,... | collective-permute-start | bytes 2359304 | tf_op jit(solution)/shard_map/ppermute | solution.py:41
  564.3 21.0 %collective-permute-start.65 = (bf16[64,2048]{1,0:T(8,128)(2,1)S(1)}, bf16[64,2048]{1,0:T(8,128)(2,1)S(1)}, u32[]{:S(2)}, u32[]{:S(2)}) collective-permute-start(bf16[64,2048]{1,0:T(8,128)(2,1)S(1)} %get-tuple-element.327), channel_id=1, source_target_pairs={{16,0},{24,8},{0,16},{8,24},{17,1},{25,9},{1,17},{9,25},{18,2},{26... | collective-permute-start | bytes 786440 | tf_op jit(solution)/shard_map/ppermute | solution.py:41
  565.4 19.8 %collective-permute-start.66 = (bf16[64,2048]{1,0:T(8,128)(2,1)S(1)}, bf16[64,2048]{1,0:T(8,128)(2,1)S(1)}, u32[]{:S(2)}, u32[]{:S(2)}) collective-permute-start(bf16[64,2048]{1,0:T(8,128)(2,1)S(1)} %get-tuple-element.325), channel_id=1, source_target_pairs={{8,0},{16,8},{24,16},{0,24},{9,1},{17,9},{25,17},{1,25},{10,2},{18... | collective-permute-start | bytes 786440 | tf_op jit(solution)/shard_map/ppermute | solution.py:41
  570.9 25.3 %collective-permute-start.67 = (bf16[4,64,512]{2,1,0:T(8,128)(2,1)S(1)}, bf16[4,64,512]{2,1,0:T(8,128)(2,1)S(1)}, u32[]{:S(2)}, u32[]{:S(2)}) collective-permute-start(bf16[4,64,512]{2,1,0:T(8,128)(2,1)S(1)} %dynamic-slice_bitcast_fusion.17), channel_id=1, source_target_pairs={{2,0},{0,2},{3,1},{1,3},{6,4},{4,6},{7,5},{5,7},{10,8},{8,10},{11,... | collective-permute-start | bytes 786440 | tf_op jit(solution)/shard_map/ppermute | solution.py:41
  574.0 38.0 %collective-permute-start.70 = (bf16[64,1536]{1,0:T(8,128)(2,1)}, bf16[64,1536]{1,0:T(8,128)(2,1)}, u32[]{:S(2)}, u32[]{:S(2)}) collective-permute-start(bf16[64,1536]{1,0:T(8,128)(2,1)} %get-tuple-element.345), channel_id=1, source_target_pairs={{24,0},{0,8},{8,16},{16,24},{25,1},{1,9},{9,17},{17,25},{26,2},{2,... | collective-permute-start | bytes 589832 | tf_op jit(solution)/shard_map/ppermute | solution.py:41
  585.2 27.4 %collective-permute-start.71 = (bf16[64,1536]{1,0:T(8,128)(2,1)}, bf16[64,1536]{1,0:T(8,128)(2,1)}, u32[]{:S(2)}, u32[]{:S(2)}) collective-permute-start(bf16[64,1536]{1,0:T(8,128)(2,1)} %get-tuple-element.346), channel_id=1, source_target_pairs={{16,0},{24,8},{0,16},{8,24},{17,1},{25,9},{1,17},{9,25},{18,2},{26... | collective-permute-start | bytes 589832 | tf_op jit(solution)/shard_map/ppermute | solution.py:41
  585.2 28.9 %collective-permute-start.72 = (bf16[64,1536]{1,0:T(8,128)(2,1)}, bf16[64,1536]{1,0:T(8,128)(2,1)}, u32[]{:S(2)}, u32[]{:S(2)}) collective-permute-start(bf16[64,1536]{1,0:T(8,128)(2,1)} %get-tuple-element.344), channel_id=1, source_target_pairs={{8,0},{16,8},{24,16},{0,24},{9,1},{17,9},{25,17},{1,25},{10,2},{18... | collective-permute-start | bytes 589832 | tf_op jit(solution)/shard_map/ppermute | solution.py:41
  625.2 13.5 %collective-permute-start.80 = (bf16[64,1536]{1,0:T(8,128)(2,1)}, bf16[64,1536]{1,0:T(8,128)(2,1)}, u32[]{:S(2)}, u32[]{:S(2)}) collective-permute-start(bf16[64,1536]{1,0:T(8,128)(2,1)} %get-tuple-element.342), channel_id=1, source_target_pairs={{24,0},{0,8},{8,16},{16,24},{25,1},{1,9},{9,17},{17,25},{26,2},{2,... | collective-permute-start | bytes 589832 | tf_op jit(solution)/shard_map/ppermute | solution.py:41
  631.8 15.4 %collective-permute-start.82 = (bf16[64,1536]{1,0:T(8,128)(2,1)}, bf16[64,1536]{1,0:T(8,128)(2,1)}, u32[]{:S(2)}, u32[]{:S(2)}) collective-permute-start(bf16[64,1536]{1,0:T(8,128)(2,1)} %get-tuple-element.341), channel_id=1, source_target_pairs={{8,0},{16,8},{24,16},{0,24},{9,1},{17,9},{25,17},{1,25},{10,2},{18... | collective-permute-start | bytes 589832 | tf_op jit(solution)/shard_map/ppermute | solution.py:41
  633.1 17.5 %collective-permute-start.91 = (f32[5,1024]{1,0:T(8,128)S(1)}, f32[5,1024]{1,0:T(8,128)S(1)}, u32[]{:S(2)}, u32[]{:S(2)}) collective-permute-start(f32[5,1024]{1,0:T(8,128)S(1)} %add.952), channel_id=1, source_target_pairs={{8,0},{16,8},{24,16},{0,24},{9,1},{17,9},{25,17},{1,25},{10,2},{18... | collective-permute-start | bytes 61448 | tf_op jit(solution)/shard_map/ppermute | solution.py:41
  634.5 16.8 %collective-permute-start.92 = (f32[5,1024]{1,0:T(8,128)S(1)}, f32[5,1024]{1,0:T(8,128)}, u32[]{:S(2)}, u32[]{:S(2)}) collective-permute-start(f32[5,1024]{1,0:T(8,128)S(1)} %add.952), channel_id=1, source_target_pairs={{16,0},{24,8},{0,16},{8,24},{17,1},{25,9},{1,17},{9,25},{18,2},{26... | collective-permute-start | bytes 61448 | tf_op jit(solution)/shard_map/ppermute | solution.py:41
  (197 other events, 1911.5 us)
Sparse Core Ops, SparseCore 0:
  14.6 159.6 all-gather.1

commit v8 on v7

--- a/solution.py
+++ b/solution.py
@@ -185,7 +185,7 @@
     return total
 
 
-def reduce_rows(other, own, names, order, parts=1):
+def reduce_flat(other, own, names, order, parts=1):
     (arrived,) = yield [shifted(other, "h", 1)]
     total = (own() + arrived.astype(WIDE)).astype(LOW)
     names = list(names)
@@ -202,8 +202,12 @@
         totals = [added(*each, arrived).astype(LOW) for each, arrived in zip(steps, pieces)]
         for names, dim in zip(left, dims):
             names.pop(dim)
-    total = totals[0] if parts == 1 else jnp.concatenate(totals, axis=-1)
-    dim = left[0].index(order[2])
+    return totals[0] if parts == 1 else jnp.concatenate(totals, axis=-1)
+
+
+def reduce_rows(other, own, names, order, parts=1):
+    total = yield from reduce_flat(other, own, names, order, parts)
+    dim = [name for name in names if name not in order[:2]].index(order[2])
     pieces = yield pieces_of(total, dim, order[2])
     return added(total, dim, order[2], pieces)
 
@@ -228,15 +232,28 @@
     )
 
 
-def reduce_layer(other, own, order, block=None, parts=1):
-    total = yield from reduce_rows(other, own, ("z", "r", "m"), order, parts)
-    total = total.reshape(-1, total.shape[-1])
-    mine, other = yield from swap_rows(total, squares(total))
-    if block is None:
-        return in_order(mine, other, 1)
-    rows = mine.shape[0]
-    mine, other = (half.reshape(rows, -1, 1, block) for half in (mine, other))
-    return in_order(mine, other, 2).reshape(rows, -1)
+def reduce_layer(other, own, order, parts=1):
+    return (yield from reduce_flat(other, own, ("z", "r", "m"), order, parts))
+
+
+def reduce_deep(totals, blocks):
+    ends = [0]
+    for total in totals:
+        ends.append(ends[-1] + total.shape[-1])
+    total = totals[0] if len(totals) == 1 else jnp.concatenate(totals, axis=-1)
+    pieces = yield pieces_of(total, 0, "z")
+    total = added(total, 0, "z", pieces)
+    pair = yield from swap_rows(total, squares(total))
+    grads = []
+    for start, end, block in zip(ends, ends[1:], blocks):
+        mine, other = (half[:, start:end] for half in pair)
+        if block is None:
+            grads.append(in_order(mine, other, 1))
+            continue
+        rows = mine.shape[0]
+        mine, other = (half.reshape(rows, -1, 1, block) for half in (mine, other))
+        grads.append(in_order(mine, other, 2).reshape(rows, -1))
+    return grads
 
 
 def reduce_owned(other, own, order, parts):
@@ -255,23 +272,6 @@
     others = yield sent_around(total, "r")
     total = placed(total, others, "r", 1)
     mine, other = yield from swap_rows(total.reshape(-1, total.shape[-1]))
-    return in_order(mine, other, 1).astype(WIDE)
-
-
-def sum_table(other, own):
-    (arrived,) = yield [shifted(other, "h", 1)]
-    total = (own() + arrived.astype(WIDE)).astype(LOW)
-    total = total.reshape(lax.axis_size("m"), -1, total.shape[-1])
-    pieces = yield pieces_of(total, 0, "m")
-    total = added(total, 0, "m", pieces).astype(LOW)
-    for axis in ("r", "z"):
-        shift = lax.axis_size(axis) // 2
-        while shift:
-            (other,) = yield [shifted(total, axis, shift)]
-            total = (total.astype(WIDE) + other.astype(WIDE)).astype(LOW)
-            shift //= 2
-    square = squares(total.astype(WIDE)) / (lax.axis_size("r") * lax.axis_size("z"))
-    mine, other = yield from swap_rows(total, square)
     return in_order(mine, other, 1).astype(WIDE)
 
 
@@ -576,7 +576,7 @@
     def product(make, left, mine, other, *rest):
         return Job(make(dot_tn(left, other).astype(LOW), lambda: dot_tn(left, mine), *rest))
 
-    head_job = product(sum_table, grad_logits, *halves(final, 1))
+    head_job = product(reduce_table, grad_logits, *halves(final, 1))
     grad_final = dot_nn(grad_logits, table_out)
     grad_ffn, gain_three = norm_backward(after_ffn, gain_all[3], grad_final)
     up_low = grad_ffn.astype(LOW)
@@ -592,7 +592,7 @@
     grad_pres = [gelu_backward(pre, grad).astype(LOW) for pre, grad in zip(pres, grad_activs)]
     grad_pres = advance(grad_pres, head_job, contract_job)
     expand_job = product(
-        reduce_layer, normed_ffn, grad_pres[0], grad_pres[1], ("r", "m", "z"), block, 2
+        reduce_layer, normed_ffn, grad_pres[0], grad_pres[1], ("r", "m", "z"), 2
     )
     grad_normed = dot_nt(grad_pres[0], ups[0]) + dot_nt(grad_pres[1], ups[1])
     inward, gain_two = norm_backward(after_time, gain_all[2], grad_normed)
@@ -604,7 +604,7 @@
     grad_packed = attention("time", half, packed_time, grad_mixed).reshape(-1, 3 * D)
     grad_packed = advance(grad_packed, head_job, contract_job, out_job)
     in_job = product(
-        reduce_layer, normed_time, *halves(grad_packed, 1), ("m", "r", "z"), None, 2
+        reduce_layer, normed_time, *halves(grad_packed, 1), ("m", "r", "z"), 2
     )
     grad_normed = dot_nt(grad_packed, w_in[1])
     inward, gain_one = norm_backward(after_space, gain_all[1], grad_normed)
@@ -613,18 +613,17 @@
     up_low = advance(up_low, head_job, contract_job, in_job)
     first_out_job = product(reduce_layer, mixed_space, *halves(up_low, 1), ("r", "m", "z"))
     grad_mixed = dot_nt(up_low, w_out[0]).astype(LOW)
-    grad_mixed = advance(grad_mixed, out_job, first_out_job)
+    grad_mixed = advance(grad_mixed, first_out_job)
     grad_packed = attention("space", small, packed_space, grad_mixed)
     grad_packed = advance(
-        grad_packed, head_job, contract_job, expand_job, in_job
+        grad_packed, head_job, contract_job, expand_job, out_job, in_job
     )
     first_in_job = product(
-        reduce_layer, normed_space, *halves(grad_packed, 1), ("r", "m", "z"), None, 2
+        reduce_layer, normed_space, *halves(grad_packed, 1), ("r", "m", "z"), 2
     )
     grad_normed = dot_nt(grad_packed, w_in[0])
-    grad_normed = advance(
-        grad_normed, first_in_job, head_job, expand_job, out_job, in_job, first_out_job
-    )
+    grad_normed = advance(grad_normed, first_in_job, head_job, expand_job, out_job)
+    early_job = Job(reduce_deep([expand_job.result, out_job.result], [block, None]))
     inward, gain_zero = norm_backward(start, gain_all[0], grad_normed)
     grad_start = grad_space + inward
     mask_grad = jnp.sum(grad_start * space_mask[:, None], axis=0)
@@ -635,20 +634,21 @@
     gain_grads = jnp.stack([gain_zero, gain_one, gain_two, gain_three, mask_grad])
     gain_job = Job(sum_over(gain_grads, ("h", "m", "r", "z")))
     token = jnp.zeros((), WIDE)
-    token = advance(token, embed_job, gain_job, head_job, out_job, expand_job, first_out_job)
+    token = advance(token, embed_job, gain_job, head_job, in_job, first_out_job)
     token = advance(token, first_in_job)
-    token = advance(token, embed_job, gain_job, in_job, first_out_job)
+    token = advance(token, embed_job, gain_job, head_job, early_job, first_out_job)
+    late_job = Job(reduce_deep([in_job.result, first_out_job.result], [None, None]))
     token = advance(token, first_in_job)
-    token = advance(token, embed_job, gain_job, expand_job, in_job, first_out_job)
-    token = advance(token, first_in_job, embed_job, gain_job, first_out_job)
+    last_job = Job(reduce_deep([first_in_job.result], [None]))
+    token = advance(token, embed_job, gain_job, early_job, late_job)
+    token = advance(token, last_job, embed_job, gain_job)
 
     owner = jnp.int32(0)
     for axis in ALL:
         owner = owner * lax.axis_size(axis) + lax.axis_index(axis)
     width = gains.shape[1]
     gain_grads = lax.dynamic_slice_in_dim(gain_job.finish(), owner * width, width, 1)
-    jobs = (in_job, first_in_job, out_job, first_out_job, expand_job, contract_job)
-    jobs = jobs + (embed_job, head_job)
+    jobs = (early_job, late_job, last_job, contract_job, embed_job, head_job)
     lane = jnp.arange(LANES)
     small_square = jnp.pad(jnp.sum(gain_grads * gain_grads, axis=0), (0, LANES - width))
     owned = sum(job.square for job in jobs) + small_square
@@ -656,19 +656,18 @@
     norm_job = Job(sum_over(sums, ("h", "m", "r", "z")))
     while norm_job.flight is not None:
         token = advance(token, norm_job, *jobs)
-    results = [(job.finish(), None) for job in jobs]
+    (up_grad, next_out), (next_in, first_out), (first_in,) = (job.finish() for job in jobs[:3])
     square_sum, loss = jnp.sum(norm_job.result, axis=1)
     norm = jnp.sqrt(square_sum)
     factor = jnp.minimum(1.0, CLIP / (norm + 1e-06))
 
-    made = [grad for grad, _ in results]
     grads = (
-        jnp.stack([made[1], made[0]]),
-        jnp.stack([made[3], made[2]]),
-        made[4],
-        made[5],
+        jnp.stack([first_in, next_in]),
+        jnp.stack([first_out, next_out]),
+        up_grad,
+        contract_job.finish(),
         gain_grads,
-        jnp.stack([made[6], made[7]]),
+        jnp.stack([embed_job.finish(), head_job.finish()]),
     )
     params = (attend_in, attend_out, expand, contract, gains, tables)
     firsts = (mean_in, mean_out, mean_expand, mean_contract, mean_gains, mean_tables)

time: 720 us -> 684 us (0.950)
  waiting for transfers between devices: 222 us -> 192 us
    ppermute x107 -> x104, waiting for transfers between devices: 196 us -> 166 us  [shifted(): return lax.ppermute(part, axis, [((i + shift) % n, i) for i in range(n)])]
    unnamed x322 -> x266, local copies, waits for them, and re-layouts: 21.6 us -> 23.3 us
    convert_element_type x27 -> x26, other arithmetic: 24.3 us -> 25 us  [the longest x24 18.2 us: reduce_flat(): added(*each, arrived).astype(LOW)]
    ppermute x107 -> x104, starting transfers between devices: 135 us -> 135 us  [shifted(): return lax.ppermute(part, axis, [((i + shift) % n, i) for i in range(n)])]
  transfers between devices with their start and end apart: 108 -> 105, of which waited for: 37 -> 38; matrix products, arithmetic and copies ran while one was open for 29% -> 30% of each run, Pallas kernels for 8% -> 8%
where the time goes in v8:
time: 684 us; the launch traced here: 675 us
  waiting for transfers between devices  192 us (28%)
  starting transfers between devices  135 us (20%)
  matrix products  135 us (20%)
  other arithmetic  71.5 us (10%)
  local copies, waits for them, and re-layouts  68.1 us (10%)
  Pallas kernels  54.6 us (8%)
  between operations  19.1 us (3%)
    ppermute x104, waiting for transfers between devices, shifted(): return lax.ppermute(part, axis, [((i + shift) % n, i) for i in range(n)])  166 us
    ppermute x104, starting transfers between devices, shifted(): return lax.ppermute(part, axis, [((i + shift) % n, i) for i in range(n)])  135 us
    pallas_call x4, Pallas kernels, attention(): pl.pallas_call(functools.partial(body, kind), out_shape=jax.ShapeDtypeStr...  54.6 us
    dot_general x10, matrix products, dot_nn(): return jnp.dot(left, right, preferred_element_type=WIDE)  48.2 us
    dot_general x9, matrix products, dot_nt(): lax.dot_general(left, right, (((1,), (1,)), ((), ())), preferred_element_...  46.1 us
    dot_general x16, matrix products, dot_tn(): lax.dot_general(left, right, (((0,), (0,)), ((), ())), preferred_element_...  40.6 us
    all_gather x1, waiting for transfers between devices, on_device(): gathered = lax.all_gather(gathered, ALL, axis=0, tiled=True)  25.8 us
    unnamed x266, local copies, waits for them, and re-layouts  23.3 us
  transfers between devices with their start and end apart: 105, of which 38 were waited for; matrix products, arithmetic and copies ran while one was open for 30% of the time, Pallas kernels for 8%

profile of v8, /device:TPU:0, one launch (start us, length us, event | category | flops | bytes accessed | tf_op | source)
XLA Modules:
  0.0 674.8 jit_solution(12511372000856045443)
XLA Ops:
  14.5 5.1 collective-permute-start.3
  29.8 3.9 collective-permute-start.25
  33.7 2.4 collective-permute-done.25
  36.1 4.6 collective-permute-done.26
  42.4 4.0 collective-permute-done.27
  51.4 3.8 collective-permute-start.7
  55.4 23.9 %collective-permute-done.7 = bf16[128,512]{1,0:T(8,128)(2,1)S(1)} collective-permute-done((bf16[128,512]{1,0:T(8,128)(2,1)S(1)}, bf16[128,512]{1,0:T(8,128)(2,1)S(1)}, u32[]{:S(2)}, u32[]{:S(2)}) %collective-permute-start.7) | collective-permute-done | bytes 131104 | tf_op jit(solution)/shard_map/ppermute | solution.py:41
  84.2 4.6 collective-permute-done.10
  88.8 4.2 collective-permute-start.13
  95.4 21.1 %collective-permute-done.12 = bf16[4,128,512]{2,1,0:T(8,128)(2,1)S(1)} collective-permute-done((bf16[4,128,512]{2,1,0:T(8,128)(2,1)S(1)}, bf16[4,128,512]{2,1,0:T(8,128)(2,1)S(1)}, u32[]{:S(2)}, u32[]{:S(2)}) %collective-permute-start.12) | collective-permute-done | bytes 524320 | tf_op jit(solution)/shard_map/ppermute | solution.py:41
  116.8 16.8 %collective-permute-done.14 = bf16[4,64,1024]{2,1,0:T(8,128)(2,1)S(1)} collective-permute-done((bf16[4,64,1024]{2,1,0:T(8,128)(2,1)S(1)}, bf16[4,64,1024]{2,1,0:T(8,128)(2,1)S(1)}, u32[]{:S(2)}, u32[]{:S(2)}) %collective-permute-start.14) | collective-permute-done | bytes 524320 | tf_op jit(solution)/shard_map/ppermute | solution.py:41
  133.5 4.5 collective-permute-done.15
  138.1 2.5 collective-permute-start.16
  148.5 25.8 %all-gather.2.cloned.1.call-done = bf16[1024,8320]{1,0:T(8,128)(2,1)} async-done(((bf16[32,8320]{1,0:T(8,128)(2,1)}), bf16[1024,8320]{1,0:T(8,128)(2,1)}) %all-gather.2.cloned.1.call-update) | async-done | bytes 17039376 | tf_op jit(solution)/shard_map/all_gather | solution.py:506
  178.6 7.9 %fusion.8.packed_ref = bf16[512,3072]{1,0:T(8,128)(2,1)} fusion(bf16[512,1024]{1,0:T(8,128)(2,1)S(1)} %multiply_convert_fusion.5, bf16[1024,8320]{1,0:T(8,128)(2,1)} %all-gather.2.cloned.1.call-done), kind=kOutput, calls=%fused_computation.16 | convolution fusion | flops 3222798336 | bytes 10485760 | tf_op jit(solution)/shard_map/dot_general | solution.py:316
  186.5 9.3 %shard_map.365 = bf16[512,1024]{1,0:T(8,128)(2,1)} custom-call(s32[1]{0:T(128)} %bitcast.13.scalar_ref, bf16[512,3072]{1,0:T(8,128)(2,1)} %fusion.8.packed_ref), custom_call_target="tpu_custom_call" | custom-call | flops 8999999488 | bytes 8388608 | tf_op jit(solution)/shard_map/pallas_call | solution.py:412
  200.2 2.5 pad_maximum_fusion.1
  203.0 2.9 fusion.60
  214.6 2.5 pad_maximum_fusion
  218.0 8.3 %fusion.11 = bf16[512,3072]{1,0:T(8,128)(2,1)} fusion(bf16[512,1024]{1,0:T(8,128)(2,1)S(1)} %fusion.34, bf16[1024,8320]{1,0:T(8,128)(2,1)} %all-gather.2.cloned.1.call-done), kind=kOutput, calls=%fused_computation.17 | convolution fusion | flops 3222798336 | bytes 10485760 | tf_op jit(solution)/shard_map/dot_general | solution.py:316
  226.3 9.1 %shard_map.366 = bf16[4,128,1024]{2,1,0:T(8,128)(2,1)} custom-call(s32[1]{0:T(128)} %bitcast.30.scalar_ref, bf16[4,128,3072]{2,1,0:T(8,128)(2,1)} %bitcast.591), custom_call_target="tpu_custom_call" | custom-call | flops 8999999488 | bytes 8388608 | tf_op jit(solution)/shard_map/pallas_call | solution.py:412
  235.4 3.3 multiply_reduce_fusion.8
  241.0 4.9 fusion.192
  245.9 6.4 fusion.165
  252.4 4.5 fusion.193
  257.0 6.6 multiply_reduce_fusion.7
  271.4 5.0 convolution_convert_fusion.3
  282.6 6.3 fusion.164
  288.9 7.1 %fusion.20 = bf16[512,2048]{1,0:T(8,128)(2,1)S(1)} fusion(f32[512,2048]{1,0:T(8,128)S(1)} %copy-done.118, bf16[512,1024]{1,0:T(8,128)(2,1)S(1)} %copy-done.43, bf16[2048,1024]{1,0:T(8,128)(2,1)} %bitcast.40), kind=kOutput, calls=%fused_computation.24 | convolution fusion | flops 2168455168 | bytes 11534336 | tf_op jit(solution)/shard_map/dot_general | solution.py:308
  296.0 8.0 %fusion.27 = bf16[512,2048]{1,0:T(8,128)(2,1)S(1)} fusion(f32[512,2048]{1,0:T(8,128)S(1)} %copy-done.121, bf16[512,1024]{1,0:T(8,128)(2,1)S(1)} %copy-done.43, bf16[2048,1024]{1,0:T(8,128)(2,1)} %collective-permute-done.23), kind=kOutput, calls=%fused_computation.31 | convolution fusion | flops 2168455168 | bytes 11534336 | tf_op jit(solution)/shard_map/dot_general | solution.py:308
  304.1 4.4 convolution_convert_fusion.2
  311.2 6.4 add_convert_fusion
  323.3 4.5 fusion.194
  327.9 5.1 multiply_reduce_fusion.2
  333.0 2.6 fusion.178
  335.6 4.4 fusion.69
  341.7 17.8 %shard_map.367 = bf16[4,128,3072]{2,1,0:T(8,128)(2,1)} custom-call(s32[1]{0:T(128)} %bitcast.30.scalar_ref, bf16[4,128,3072]{2,1,0:T(8,128)(2,1)} %bitcast.592, bf16[4,128,1024]{2,1,0:T(8,128)(2,1)} %bitcast.599), custom_call_target="tpu_custom_call" | custom-call | flops 22000001024 | bytes 8388608 | tf_op jit(solution)/shard_map/pallas_call | solution.py:412
  362.3 5.2 add_convert_fusion.1
  374.0 5.9 fusion.40
  401.5 3.7 collective-permute-start.44
  411.7 3.9 fusion.66.up_ref
  415.5 4.4 collective-permute-done.50
  421.6 2.4 collective-permute-start.46
  425.7 7.7 %collective-permute-done.52 = bf16[4,2,64,512]{3,2,0,1:T(8,128)(2,1)} collective-permute-done((bf16[4,2,64,512]{3,2,0,1:T(8,128)(2,1)S(1)}, bf16[4,2,64,512]{3,2,0,1:T(8,128)(2,1)}, u32[]{:S(2)}, u32[]{:S(2)}) %collective-permute-start.52) | collective-permute-done | bytes 524320 | tf_op jit(solution)/shard_map/ppermute | solution.py:41
  440.2 18.4 %shard_map.368 = bf16[512,3072]{1,0:T(8,128)(2,1)} custom-call(s32[1]{0:T(128)} %bitcast.13.scalar_ref, bf16[512,3072]{1,0:T(8,128)(2,1)} %fusion.8.packed_ref, bf16[512,1024]{1,0:T(8,128)(2,1)} %fusion.66.up_ref), custom_call_target="tpu_custom_call" | custom-call | flops 22000001024 | bytes 8388608 | tf_op jit(solution)/shard_map/pallas_call | solution.py:412
  458.7 3.7 convolution_convert_fusion
  475.3 5.8 fusion.4
  503.7 13.9 %collective-permute-done.78 = bf16[4,2,64,768]{3,2,0,1:T(8,128)(2,1)} collective-permute-done((bf16[4,2,64,768]{3,2,0,1:T(8,128)(2,1)}, bf16[4,2,64,768]{3,2,0,1:T(8,128)(2,1)}, u32[]{:S(2)}, u32[]{:S(2)}) %collective-permute-start.78) | collective-permute-done | bytes 786464 | tf_op jit(solution)/shard_map/ppermute | solution.py:41
  523.2 7.8 %collective-permute-done.65 = bf16[4,2,64,512]{3,2,0,1:T(8,128)(2,1)S(1)} collective-permute-done((bf16[4,2,64,512]{3,2,0,1:T(8,128)(2,1)S(1)}, bf16[4,2,64,512]{3,2,0,1:T(8,128)(2,1)S(1)}, u32[]{:S(2)}, u32[]{:S(2)}) %collective-permute-start.65) | collective-permute-done | bytes 524320 | tf_op jit(solution)/shard_map/ppermute | solution.py:41
  540.8 4.2 collective-permute-done.80
  548.5 6.9 %collective-permute-done.70 = bf16[64,2560]{1,0:T(8,128)(2,1)S(1)} collective-permute-done((bf16[64,2560]{1,0:T(8,128)(2,1)S(1)}, bf16[64,2560]{1,0:T(8,128)(2,1)S(1)}, u32[]{:S(2)}, u32[]{:S(2)}) %collective-permute-start.70) | collective-permute-done | bytes 327712 | tf_op jit(solution)/shard_map/ppermute | solution.py:41
  555.4 4.5 collective-permute-done.67
  564.5 2.4 collective-permute-done.73
  569.1 5.0 collective-permute-done.75
  574.1 10.2 %collective-permute-start.83 = (bf16[64,1536]{1,0:T(8,128)(2,1)S(1)}, bf16[64,1536]{1,0:T(8,128)(2,1)S(1)}, u32[]{:S(2)}, u32[]{:S(2)}) collective-permute-start(bf16[64,1536]{1,0:T(8,128)(2,1)S(1)} %get-tuple-element.340), channel_id=1, source_target_pairs={{16,0},{24,8},{0,16},{8,24},{17,1},{25,9},{1,17},{9,25},{18,2},{26... | collective-permute-start | bytes 589832 | tf_op jit(solution)/shard_map/ppermute | solution.py:41
  584.5 10.6 %collective-permute-start.84 = (bf16[64,1536]{1,0:T(8,128)(2,1)S(1)}, bf16[64,1536]{1,0:T(8,128)(2,1)S(1)}, u32[]{:S(2)}, u32[]{:S(2)}) collective-permute-start(bf16[64,1536]{1,0:T(8,128)(2,1)S(1)} %get-tuple-element.338), channel_id=1, source_target_pairs={{8,0},{16,8},{24,16},{0,24},{9,1},{17,9},{25,17},{1,25},{10,2},{18... | collective-permute-start | bytes 589832 | tf_op jit(solution)/shard_map/ppermute | solution.py:41
  595.2 5.4 collective-permute-start.89
  603.1 3.3 collective-permute-start.85
  606.4 3.4 collective-permute-start.86
  619.5 3.0 collective-permute-start.94
  625.0 4.0 collective-permute-done.95
  633.4 4.7 collective-permute-done.98
  654.0 2.6 multiply_subtract_fusion.4
  662.9 3.5 multiply_subtract_fusion
  (695 shorter events, 232.2 us)
Async XLA Ops:
  7.2 167.1 %all-gather.2.cloned.1.call-start = ((), (), s32[]{:S(2)}) async-start(), calls=%async_computation | async-start | bytes 17571840 | tf_op jit(solution)/shard_map/all_gather | solution.py:506
  14.5 32.7 %collective-permute-start.3 = (bf16[128,1024]{1,0:T(8,128)(2,1)S(1)}, bf16[128,1024]{1,0:T(8,128)(2,1)}, u32[]{:S(2)}, u32[]{:S(2)}) collective-permute-start(bf16[128,1024]{1,0:T(8,128)(2,1)S(1)} %convert_element_type.557), channel_id=1, source_target_pairs={{8,0},{16,8},{24,16},{0,24},{9,1},{17,9},{25,17},{1,25},{10,2},{18... | collective-permute-start | bytes 786440 | tf_op jit(solution)/shard_map/ppermute | solution.py:41
  19.7 27.5 %collective-permute-start.4 = (bf16[128,1024]{1,0:T(8,128)(2,1)S(1)}, bf16[128,1024]{1,0:T(8,128)(2,1)S(1)}, u32[]{:S(2)}, u32[]{:S(2)}) collective-permute-start(bf16[128,1024]{1,0:T(8,128)(2,1)S(1)} %convert_element_type.557), channel_id=1, source_target_pairs={{24,0},{0,8},{8,16},{16,24},{25,1},{1,9},{9,17},{17,25},{26,2},{2,... | collective-permute-start | bytes 786440 | tf_op jit(solution)/shard_map/ppermute | solution.py:41
  22.1 25.1 %collective-permute-start.2 = (bf16[32,2048]{1,0:T(8,128)(2,1)}, bf16[32,2048]{1,0:T(8,128)(2,1)S(1)}, u32[]{:S(2)}, u32[]{:S(2)}) collective-permute-start(bf16[32,2048]{1,0:T(8,128)(2,1)} %bitcast.541), channel_id=1, source_target_pairs={{1,0},{0,1},{3,2},{2,3},{5,4},{4,5},{7,6},{6,7},{9,8},{8,9},{11,10... | collective-permute-start | bytes 393224 | tf_op jit(solution)/shard_map/ppermute | solution.py:41
  23.2 56.2 %collective-permute-start.1 = (bf16[256,1024]{1,0:T(8,128)(2,1)S(1)}, bf16[256,1024]{1,0:T(8,128)(2,1)S(1)}, u32[]{:S(2)}, u32[]{:S(2)}) collective-permute-start(bf16[256,1024]{1,0:T(8,128)(2,1)S(1)} %get-tuple-element.333), channel_id=1, source_target_pairs={{2,0},{0,2},{3,1},{1,3},{6,4},{4,6},{7,5},{5,7},{10,8},{8,10},{11,... | collective-permute-start | bytes 1572872 | tf_op jit(solution)/shard_map/ppermute | solution.py:41
  47.3 32.1 %collective-permute-start.5 = (bf16[64,2048]{1,0:T(8,128)(2,1)S(1)}, bf16[64,2048]{1,0:T(8,128)(2,1)S(1)}, u32[]{:S(2)}, u32[]{:S(2)}) collective-permute-start(bf16[64,2048]{1,0:T(8,128)(2,1)S(1)} %bitcast.561), channel_id=1, source_target_pairs={{8,0},{16,8},{24,16},{0,24},{9,1},{17,9},{25,17},{1,25},{10,2},{18... | collective-permute-start | bytes 786440 | tf_op jit(solution)/shard_map/ppermute | solution.py:41
  49.3 30.0 %collective-permute-start.6 = (bf16[64,2048]{1,0:T(8,128)(2,1)S(1)}, bf16[64,2048]{1,0:T(8,128)(2,1)S(1)}, u32[]{:S(2)}, u32[]{:S(2)}) collective-permute-start(bf16[64,2048]{1,0:T(8,128)(2,1)S(1)} %bitcast.562), channel_id=1, source_target_pairs={{24,0},{0,8},{8,16},{16,24},{25,1},{1,9},{9,17},{17,25},{26,2},{2,... | collective-permute-start | bytes 786440 | tf_op jit(solution)/shard_map/ppermute | solution.py:41
  51.4 27.9 %collective-permute-start.7 = (bf16[128,512]{1,0:T(8,128)(2,1)S(1)}, bf16[128,512]{1,0:T(8,128)(2,1)S(1)}, u32[]{:S(2)}, u32[]{:S(2)}) collective-permute-start(bf16[128,512]{1,0:T(8,128)(2,1)S(1)} %slice.110), channel_id=1, source_target_pairs={{8,0},{16,8},{24,16},{0,24},{9,1},{17,9},{25,17},{1,25},{10,2},{18... | collective-permute-start | bytes 393224 | tf_op jit(solution)/shard_map/ppermute | solution.py:41
  55.3 24.0 %collective-permute-start.8 = (bf16[128,512]{1,0:T(8,128)(2,1)S(1)}, bf16[128,512]{1,0:T(8,128)(2,1)S(1)}, u32[]{:S(2)}, u32[]{:S(2)}) collective-permute-start(bf16[128,512]{1,0:T(8,128)(2,1)S(1)} %slice.111), channel_id=1, source_target_pairs={{24,0},{0,8},{8,16},{16,24},{25,1},{1,9},{9,17},{17,25},{26,2},{2,... | collective-permute-start | bytes 393224 | tf_op jit(solution)/shard_map/ppermute | solution.py:41
  79.3 69.2 %collective-permute-start = (bf16[256,1024]{1,0:T(8,128)(2,1)}, bf16[256,1024]{1,0:T(8,128)(2,1)}, u32[]{:S(2)}, u32[]{:S(2)}) collective-permute-start(bf16[256,1024]{1,0:T(8,128)(2,1)} %get-tuple-element.332), channel_id=1, source_target_pairs={{2,0},{0,2},{3,1},{1,3},{6,4},{4,6},{7,5},{5,7},{10,8},{8,10},{11,... | collective-permute-start | bytes 1572872 | tf_op jit(solution)/shard_map/ppermute | solution.py:41
  79.8 36.8 %collective-permute-start.12 = (bf16[4,128,512]{2,1,0:T(8,128)(2,1)S(1)}, bf16[4,128,512]{2,1,0:T(8,128)(2,1)S(1)}, u32[]{:S(2)}, u32[]{:S(2)}) collective-permute-start(bf16[4,128,512]{2,1,0:T(8,128)(2,1)S(1)} %get-tuple-element.331), channel_id=1, source_target_pairs={{2,0},{0,2},{3,1},{1,3},{6,4},{4,6},{7,5},{5,7},{10,8},{8,10},{11,... | collective-permute-start | bytes 1572872 | tf_op jit(solution)/shard_map/ppermute | solution.py:41
  88.8 28.0 %collective-permute-start.13 = (bf16[4,128,512]{2,1,0:T(8,128)(2,1)S(1)}, bf16[4,128,512]{2,1,0:T(8,128)(2,1)S(1)}, u32[]{:S(2)}, u32[]{:S(2)}) collective-permute-start(bf16[4,128,512]{2,1,0:T(8,128)(2,1)S(1)} %get-tuple-element.330), channel_id=1, source_target_pairs={{4,0},{0,4},{5,1},{1,5},{6,2},{2,6},{7,3},{3,7},{12,8},{8,12},{13,... | collective-permute-start | bytes 1572872 | tf_op jit(solution)/shard_map/ppermute | solution.py:41
  93.1 40.4 %collective-permute-start.14 = (bf16[4,64,1024]{2,1,0:T(8,128)(2,1)S(1)}, bf16[4,64,1024]{2,1,0:T(8,128)(2,1)S(1)}, u32[]{:S(2)}, u32[]{:S(2)}) collective-permute-start(bf16[4,64,1024]{2,1,0:T(8,128)(2,1)S(1)} %get-tuple-element.329), channel_id=1, source_target_pairs={{2,0},{0,2},{3,1},{1,3},{6,4},{4,6},{7,5},{5,7},{10,8},{8,10},{11,... | collective-permute-start | bytes 1572872 | tf_op jit(solution)/shard_map/ppermute | solution.py:41
  93.2 44.8 %collective-permute-start.15 = (bf16[4,64,1024]{2,1,0:T(8,128)(2,1)S(1)}, bf16[4,64,1024]{2,1,0:T(8,128)(2,1)S(1)}, u32[]{:S(2)}, u32[]{:S(2)}) collective-permute-start(bf16[4,64,1024]{2,1,0:T(8,128)(2,1)S(1)} %get-tuple-element.328), channel_id=1, source_target_pairs={{4,0},{0,4},{5,1},{1,5},{6,2},{2,6},{7,3},{3,7},{12,8},{8,12},{13,... | collective-permute-start | bytes 1572872 | tf_op jit(solution)/shard_map/ppermute | solution.py:41
  138.1 57.6 %collective-permute-start.16 = (bf16[4,2,128,512]{3,2,1,0:T(8,128)(2,1)S(1)}, bf16[4,2,128,512]{3,2,1,0:T(8,128)(2,1)}, u32[]{:S(2)}, u32[]{:S(2)}) collective-permute-start(bf16[4,2,128,512]{3,2,1,0:T(8,128)(2,1)S(1)} %bitcast_dynamic-update-slice_fusion.7), channel_id=1, source_target_pairs={{4,0},{0,4},{5,1},{1,5},{6,2},{2,6},{7,3},{3,7},{12,8},{8,12},{13,... | collective-permute-start | bytes 3145736 | tf_op jit(solution)/shard_map/ppermute | solution.py:41
  142.6 53.2 %collective-permute-start.17 = (bf16[4,2,128,512]{3,2,1,0:T(8,128)(2,1)}, bf16[4,2,128,512]{3,2,1,0:T(8,128)(2,1)}, u32[]{:S(2)}, u32[]{:S(2)}) collective-permute-start(bf16[4,2,128,512]{3,2,1,0:T(8,128)(2,1)} %bitcast_dynamic-update-slice_fusion.10), channel_id=1, source_target_pairs={{2,0},{0,2},{3,1},{1,3},{6,4},{4,6},{7,5},{5,7},{10,8},{8,10},{11,... | collective-permute-start | bytes 3145736 | tf_op jit(solution)/shard_map/ppermute | solution.py:41
  144.5 51.3 %collective-permute-start.18 = (bf16[4,2,64,1024]{3,2,1,0:T(8,128)(2,1)}, bf16[4,2,64,1024]{3,2,1,0:T(8,128)(2,1)}, u32[]{:S(2)}, u32[]{:S(2)}) collective-permute-start(bf16[4,2,64,1024]{3,2,1,0:T(8,128)(2,1)} %bitcast_dynamic-update-slice_fusion.6), channel_id=1, source_target_pairs={{4,0},{0,4},{5,1},{1,5},{6,2},{2,6},{7,3},{3,7},{12,8},{8,12},{13,... | collective-permute-start | bytes 3145736 | tf_op jit(solution)/shard_map/ppermute | solution.py:41
  146.5 49.3 %collective-permute-start.19 = (bf16[4,2,64,1024]{3,2,1,0:T(8,128)(2,1)}, bf16[4,2,64,1024]{3,2,1,0:T(8,128)(2,1)}, u32[]{:S(2)}, u32[]{:S(2)}) collective-permute-start(bf16[4,2,64,1024]{3,2,1,0:T(8,128)(2,1)} %bitcast_dynamic-update-slice_fusion.9), channel_id=1, source_target_pairs={{2,0},{0,2},{3,1},{1,3},{6,4},{4,6},{7,5},{5,7},{10,8},{8,10},{11,... | collective-permute-start | bytes 3145736 | tf_op jit(solution)/shard_map/ppermute | solution.py:41
  202.7 54.2 %collective-permute-start.23 = (bf16[2048,1024]{1,0:T(8,128)(2,1)}, bf16[2048,1024]{1,0:T(8,128)(2,1)}, u32[]{:S(2)}, u32[]{:S(2)}) collective-permute-start(bf16[2048,1024]{1,0:T(8,128)(2,1)} %bitcast.40), channel_id=1, source_target_pairs={{1,0},{0,1},{3,2},{2,3},{5,4},{4,5},{7,6},{6,7},{9,8},{8,9},{11,10... | collective-permute-start | bytes 12582920 | tf_op jit(solution)/shard_map/ppermute | solution.py:41
  217.1 35.3 %collective-permute-start.22 = (bf16[1024,2048]{1,0:T(8,128)(2,1)}, bf16[1024,2048]{1,0:T(8,128)(2,1)}, u32[]{:S(2)}, u32[]{:S(2)}) collective-permute-start(bf16[1024,2048]{1,0:T(8,128)(2,1)} %bitcast.37), channel_id=1, source_target_pairs={{1,0},{0,1},{3,2},{2,3},{5,4},{4,5},{7,6},{6,7},{9,8},{8,9},{11,10... | collective-permute-start | bytes 12582920 | tf_op jit(solution)/shard_map/ppermute | solution.py:41
  276.4 27.7 %collective-permute-start.29 = (bf16[2048,1024]{1,0:T(8,128)(2,1)}, bf16[2048,1024]{1,0:T(8,128)(2,1)}, u32[]{:S(2)}, u32[]{:S(2)}) collective-permute-start(bf16[2048,1024]{1,0:T(8,128)(2,1)} %convolution_convert_fusion.3), channel_id=1, source_target_pairs={{1,0},{0,1},{3,2},{2,3},{5,4},{4,5},{7,6},{6,7},{9,8},{8,9},{11,10... | collective-permute-start | bytes 12582920 | tf_op jit(solution)/shard_map/ppermute | solution.py:41
  278.5 25.5 %collective-permute-start.28 = (bf16[1024,512]{1,0:T(8,128)(2,1)S(1)}, bf16[1024,512]{1,0:T(8,128)(2,1)S(1)}, u32[]{:S(2)}, u32[]{:S(2)}) collective-permute-start(bf16[1024,512]{1,0:T(8,128)(2,1)S(1)} %convolution_convert_fusion.6), channel_id=1, source_target_pairs={{1,0},{0,1},{3,2},{2,3},{5,4},{4,5},{7,6},{6,7},{9,8},{8,9},{11,10... | collective-permute-start | bytes 3145736 | tf_op jit(solution)/shard_map/ppermute | solution.py:41
  308.5 27.0 %collective-permute-start.31 = (bf16[1024,2048]{1,0:T(8,128)(2,1)}, bf16[1024,2048]{1,0:T(8,128)(2,1)}, u32[]{:S(2)}, u32[]{:S(2)}) collective-permute-start(bf16[1024,2048]{1,0:T(8,128)(2,1)} %convolution_convert_fusion.2), channel_id=1, source_target_pairs={{1,0},{0,1},{3,2},{2,3},{5,4},{4,5},{7,6},{6,7},{9,8},{8,9},{11,10... | collective-permute-start | bytes 12582920 | tf_op jit(solution)/shard_map/ppermute | solution.py:41
  310.1 25.5 %collective-permute-start.30 = (bf16[2,2,4,32,512]{4,3,0,2,1:T(8,128)(2,1)S(1)}, bf16[2,2,4,32,512]{4,3,0,2,1:T(8,128)(2,1)S(1)}, u32[]{:S(2)}, u32[]{:S(2)}) collective-permute-start(bf16[2,2,4,32,512]{4,3,0,2,1:T(8,128)(2,1)S(1)} %bitcast.575), channel_id=1, source_target_pairs={{2,0},{0,2},{3,1},{1,3},{6,4},{4,6},{7,5},{5,7},{10,8},{8,10},{11,... | collective-permute-start | bytes 1572872 | tf_op jit(solution)/shard_map/ppermute | solution.py:41
  319.2 50.5 %collective-permute-start.33 = (bf16[4,2,128,512]{3,2,0,1:T(8,128)(2,1)}, bf16[4,2,128,512]{3,2,0,1:T(8,128)(2,1)}, u32[]{:S(2)}, u32[]{:S(2)}) collective-permute-start(bf16[4,2,128,512]{3,2,0,1:T(8,128)(2,1)} %bitcast.534), channel_id=1, source_target_pairs={{2,0},{0,2},{3,1},{1,3},{6,4},{4,6},{7,5},{5,7},{10,8},{8,10},{11,... | collective-permute-start | bytes 3145736 | tf_op jit(solution)/shard_map/ppermute | solution.py:41
  322.4 47.3 %collective-permute-start.34 = (bf16[4,2,128,512]{3,2,0,1:T(8,128)(2,1)}, bf16[4,2,128,512]{3,2,0,1:T(8,128)(2,1)}, u32[]{:S(2)}, u32[]{:S(2)}) collective-permute-start(bf16[4,2,128,512]{3,2,0,1:T(8,128)(2,1)} %bitcast.533), channel_id=1, source_target_pairs={{4,0},{0,4},{5,1},{1,5},{6,2},{2,6},{7,3},{3,7},{12,8},{8,12},{13,... | collective-permute-start | bytes 3145736 | tf_op jit(solution)/shard_map/ppermute | solution.py:41
  373.4 27.2 %collective-permute-start.42 = (bf16[1024,1536]{1,0:T(8,128)(2,1)S(1)}, bf16[1024,1536]{1,0:T(8,128)(2,1)S(1)}, u32[]{:S(2)}, u32[]{:S(2)}) collective-permute-start(bf16[1024,1536]{1,0:T(8,128)(2,1)S(1)} %convolution_convert_fusion.1), channel_id=1, source_target_pairs={{1,0},{0,1},{3,2},{2,3},{5,4},{4,5},{7,6},{6,7},{9,8},{8,9},{11,10... | collective-permute-start | bytes 9437192 | tf_op jit(solution)/shard_map/ppermute | solution.py:41
  383.0 14.9 %collective-permute-start.40 = (bf16[4,128,512]{2,1,0:T(8,128)(2,1)S(1)}, bf16[4,128,512]{2,1,0:T(8,128)(2,1)S(1)}, u32[]{:S(2)}, u32[]{:S(2)}) collective-permute-start(bf16[4,128,512]{2,1,0:T(8,128)(2,1)S(1)} %dynamic-slice_bitcast_fusion.6), channel_id=1, source_target_pairs={{4,0},{0,4},{5,1},{1,5},{6,2},{2,6},{7,3},{3,7},{12,8},{8,12},{13,... | collective-permute-start | bytes 1572872 | tf_op jit(solution)/shard_map/ppermute | solution.py:41
  385.8 14.9 %collective-permute-start.41 = (bf16[4,128,512]{2,1,0:T(8,128)(2,1)S(1)}, bf16[4,128,512]{2,1,0:T(8,128)(2,1)S(1)}, u32[]{:S(2)}, u32[]{:S(2)}) collective-permute-start(bf16[4,128,512]{2,1,0:T(8,128)(2,1)S(1)} %dynamic-slice_bitcast_fusion.5), channel_id=1, source_target_pairs={{2,0},{0,2},{3,1},{1,3},{6,4},{4,6},{7,5},{5,7},{10,8},{8,10},{11,... | collective-permute-start | bytes 1572872 | tf_op jit(solution)/shard_map/ppermute | solution.py:41
  394.5 25.4 %collective-permute-start.50 = (bf16[4,2,64,1024]{3,2,0,1:T(8,128)(2,1)S(1)}, bf16[4,2,64,1024]{3,2,0,1:T(8,128)(2,1)}, u32[]{:S(2)}, u32[]{:S(2)}) collective-permute-start(bf16[4,2,64,1024]{3,2,0,1:T(8,128)(2,1)S(1)} %bitcast.564), channel_id=1, source_target_pairs={{4,0},{0,4},{5,1},{1,5},{6,2},{2,6},{7,3},{3,7},{12,8},{8,12},{13,... | collective-permute-start | bytes 3145736 | tf_op jit(solution)/shard_map/ppermute | solution.py:41
  395.7 28.4 %collective-permute-start.51 = (bf16[4,2,64,1024]{3,2,1,0:T(8,128)(2,1)S(1)}, bf16[4,2,64,1024]{3,2,1,0:T(8,128)(2,1)S(1)}, u32[]{:S(2)}, u32[]{:S(2)}) collective-permute-start(bf16[4,2,64,1024]{3,2,1,0:T(8,128)(2,1)S(1)} %dynamic-slice_bitcast_fusion), channel_id=1, source_target_pairs={{2,0},{0,2},{3,1},{1,3},{6,4},{4,6},{7,5},{5,7},{10,8},{8,10},{11,... | collective-permute-start | bytes 3145736 | tf_op jit(solution)/shard_map/ppermute | solution.py:41
  397.9 35.6 %collective-permute-start.52 = (bf16[4,2,64,512]{3,2,0,1:T(8,128)(2,1)S(1)}, bf16[4,2,64,512]{3,2,0,1:T(8,128)(2,1)}, u32[]{:S(2)}, u32[]{:S(2)}) collective-permute-start(bf16[4,2,64,512]{3,2,0,1:T(8,128)(2,1)S(1)} %bitcast.573), channel_id=1, source_target_pairs={{2,0},{0,2},{3,1},{1,3},{6,4},{4,6},{7,5},{5,7},{10,8},{8,10},{11,... | collective-permute-start | bytes 1572872 | tf_op jit(solution)/shard_map/ppermute | solution.py:41
  401.4 20.2 %collective-permute-start.43 = (bf16[1024,512]{1,0:T(8,128)(2,1)S(1)}, bf16[1024,512]{1,0:T(8,128)(2,1)S(1)}, u32[]{:S(2)}, u32[]{:S(2)}) collective-permute-start(bf16[1024,512]{1,0:T(8,128)(2,1)S(1)} %convolution_convert_fusion.4), channel_id=1, source_target_pairs={{1,0},{0,1},{3,2},{2,3},{5,4},{4,5},{7,6},{6,7},{9,8},{8,9},{11,10... | collective-permute-start | bytes 3145736 | tf_op jit(solution)/shard_map/ppermute | solution.py:41
  401.5 33.7 %collective-permute-start.44 = (bf16[2,32,512]{2,1,0:T(8,128)(2,1)S(1)}, bf16[2,32,512]{2,1,0:T(8,128)(2,1)S(1)}, u32[]{:S(2)}, u32[]{:S(2)}) collective-permute-start(bf16[2,32,512]{2,1,0:T(8,128)(2,1)S(1)} %get-tuple-element.358), channel_id=1, source_target_pairs={{8,0},{16,8},{24,16},{0,24},{9,1},{17,9},{25,17},{1,25},{10,2},{18... | collective-permute-start | bytes 196616 | tf_op jit(solution)/shard_map/ppermute | solution.py:41
  419.9 17.4 %collective-permute-start.45 = (bf16[2,32,512]{2,1,0:T(8,128)(2,1)S(1)}, bf16[2,32,512]{2,1,0:T(8,128)(2,1)S(1)}, u32[]{:S(2)}, u32[]{:S(2)}) collective-permute-start(bf16[2,32,512]{2,1,0:T(8,128)(2,1)S(1)} %get-tuple-element.358), channel_id=1, source_target_pairs={{16,0},{24,8},{0,16},{8,24},{17,1},{25,9},{1,17},{9,25},{18,2},{26... | collective-permute-start | bytes 196616 | tf_op jit(solution)/shard_map/ppermute | solution.py:41
  421.6 17.0 %collective-permute-start.46 = (bf16[2,32,512]{2,1,0:T(8,128)(2,1)S(1)}, bf16[2,32,512]{2,1,0:T(8,128)(2,1)S(1)}, u32[]{:S(2)}, u32[]{:S(2)}) collective-permute-start(bf16[2,32,512]{2,1,0:T(8,128)(2,1)S(1)} %get-tuple-element.358), channel_id=1, source_target_pairs={{24,0},{0,8},{8,16},{16,24},{25,1},{1,9},{9,17},{17,25},{26,2},{2,... | collective-permute-start | bytes 196616 | tf_op jit(solution)/shard_map/ppermute | solution.py:41
  425.0 33.6 %collective-permute-start.47 = (bf16[128,1024]{1,0:T(8,128)(2,1)}, bf16[128,1024]{1,0:T(8,128)(2,1)S(1)}, u32[]{:S(2)}, u32[]{:S(2)}) collective-permute-start(bf16[128,1024]{1,0:T(8,128)(2,1)} %get-tuple-element.324), channel_id=1, source_target_pairs={{24,0},{0,8},{8,16},{16,24},{25,1},{1,9},{9,17},{17,25},{26,2},{2,... | collective-permute-start | bytes 786440 | tf_op jit(solution)/shard_map/ppermute | solution.py:41
  433.5 25.2 %collective-permute-start.48 = (bf16[128,1024]{1,0:T(8,128)(2,1)}, bf16[128,1024]{1,0:T(8,128)(2,1)}, u32[]{:S(2)}, u32[]{:S(2)}) collective-permute-start(bf16[128,1024]{1,0:T(8,128)(2,1)} %get-tuple-element.325), channel_id=1, source_target_pairs={{16,0},{24,8},{0,16},{8,24},{17,1},{25,9},{1,17},{9,25},{18,2},{26... | collective-permute-start | bytes 786440 | tf_op jit(solution)/shard_map/ppermute | solution.py:41
  435.2 23.4 %collective-permute-start.49 = (bf16[128,1024]{1,0:T(8,128)(2,1)}, bf16[128,1024]{1,0:T(8,128)(2,1)}, u32[]{:S(2)}, u32[]{:S(2)}) collective-permute-start(bf16[128,1024]{1,0:T(8,128)(2,1)} %get-tuple-element.323), channel_id=1, source_target_pairs={{8,0},{16,8},{24,16},{0,24},{9,1},{17,9},{25,17},{1,25},{10,2},{18... | collective-permute-start | bytes 786440 | tf_op jit(solution)/shard_map/ppermute | solution.py:41
  437.3 21.3 %collective-permute-start.53 = (bf16[4,2,64,768]{3,2,0,1:T(8,128)(2,1)}, bf16[4,2,64,768]{3,2,0,1:T(8,128)(2,1)}, u32[]{:S(2)}, u32[]{:S(2)}) collective-permute-start(bf16[4,2,64,768]{3,2,0,1:T(8,128)(2,1)} %bitcast.536), channel_id=1, source_target_pairs={{2,0},{0,2},{3,1},{1,3},{6,4},{4,6},{7,5},{5,7},{10,8},{8,10},{11,... | collective-permute-start | bytes 2359304 | tf_op jit(solution)/shard_map/ppermute | solution.py:41
  439.3 19.4 %collective-permute-start.54 = (bf16[4,2,64,768]{3,2,1,0:T(8,128)(2,1)}, bf16[4,2,64,768]{3,2,1,0:T(8,128)(2,1)}, u32[]{:S(2)}, u32[]{:S(2)}) collective-permute-start(bf16[4,2,64,768]{3,2,1,0:T(8,128)(2,1)} %dynamic-slice_bitcast_fusion.2), channel_id=1, source_target_pairs={{4,0},{0,4},{5,1},{1,5},{6,2},{2,6},{7,3},{3,7},{12,8},{8,12},{13,... | collective-permute-start | bytes 2359304 | tf_op jit(solution)/shard_map/ppermute | solution.py:41
  462.3 26.5 %collective-permute-start.55 = (bf16[1024,1536]{1,0:T(8,128)(2,1)S(1)}, bf16[1024,1536]{1,0:T(8,128)(2,1)S(1)}, u32[]{:S(2)}, u32[]{:S(2)}) collective-permute-start(bf16[1024,1536]{1,0:T(8,128)(2,1)S(1)} %convolution_convert_fusion), channel_id=1, source_target_pairs={{1,0},{0,1},{3,2},{2,3},{5,4},{4,5},{7,6},{6,7},{9,8},{8,9},{11,10... | collective-permute-start | bytes 9437192 | tf_op jit(solution)/shard_map/ppermute | solution.py:41
  462.5 24.0 %collective-permute-start.56 = (bf16[2,4,32,512]{3,2,1,0:T(8,128)(2,1)S(1)}, bf16[2,4,32,512]{3,2,1,0:T(8,128)(2,1)S(1)}, u32[]{:S(2)}, u32[]{:S(2)}) collective-permute-start(bf16[2,4,32,512]{3,2,1,0:T(8,128)(2,1)S(1)} %bitcast_dynamic-update-slice_fusion.28), channel_id=1, source_target_pairs={{4,0},{0,4},{5,1},{1,5},{6,2},{2,6},{7,3},{3,7},{12,8},{8,12},{13,... | collective-permute-start | bytes 786440 | tf_op jit(solution)/shard_map/ppermute | solution.py:41
  465.4 23.4 %collective-permute-start.57 = (bf16[4,64,1024]{2,1,0:T(8,128)(2,1)S(1)}, bf16[4,64,1024]{2,1,0:T(8,128)(2,1)S(1)}, u32[]{:S(2)}, u32[]{:S(2)}) collective-permute-start(bf16[4,64,1024]{2,1,0:T(8,128)(2,1)S(1)} %dynamic-slice_bitcast_fusion.4), channel_id=1, source_target_pairs={{2,0},{0,2},{3,1},{1,3},{6,4},{4,6},{7,5},{5,7},{10,8},{8,10},{11,... | collective-permute-start | bytes 1572872 | tf_op jit(solution)/shard_map/ppermute | solution.py:41
  466.7 22.1 %collective-permute-start.58 = (bf16[4,64,1024]{2,1,0:T(8,128)(2,1)S(1)}, bf16[4,64,1024]{2,1,0:T(8,128)(2,1)S(1)}, u32[]{:S(2)}, u32[]{:S(2)}) collective-permute-start(bf16[4,64,1024]{2,1,0:T(8,128)(2,1)S(1)} %dynamic-slice_bitcast_fusion.3), channel_id=1, source_target_pairs={{4,0},{0,4},{5,1},{1,5},{6,2},{2,6},{7,3},{3,7},{12,8},{8,12},{13,... | collective-permute-start | bytes 1572872 | tf_op jit(solution)/shard_map/ppermute | solution.py:41
  469.0 19.2 %collective-permute-start.59 = (bf16[4,64,512]{2,1,0:T(8,128)(2,1)S(1)}, bf16[4,64,512]{2,1,0:T(8,128)(2,1)S(1)}, u32[]{:S(2)}, u32[]{:S(2)}) collective-permute-start(bf16[4,64,512]{2,1,0:T(8,128)(2,1)S(1)} %dynamic-slice_bitcast_fusion.25), channel_id=1, source_target_pairs={{4,0},{0,4},{5,1},{1,5},{6,2},{2,6},{7,3},{3,7},{12,8},{8,12},{13,... | collective-permute-start | bytes 786440 | tf_op jit(solution)/shard_map/ppermute | solution.py:41
  486.5 35.8 %collective-permute-start.63 = (bf16[4,64,768]{2,1,0:T(8,128)(2,1)}, bf16[4,64,768]{2,1,0:T(8,128)(2,1)}, u32[]{:S(2)}, u32[]{:S(2)}) collective-permute-start(bf16[4,64,768]{2,1,0:T(8,128)(2,1)} %dynamic-slice_bitcast_fusion.10), channel_id=1, source_target_pairs={{4,0},{0,4},{5,1},{1,5},{6,2},{2,6},{7,3},{3,7},{12,8},{8,12},{13,... | collective-permute-start | bytes 1179656 | tf_op jit(solution)/shard_map/ppermute | solution.py:41
  488.1 34.7 %collective-permute-start.64 = (bf16[4,64,768]{2,1,0:T(8,128)(2,1)}, bf16[4,64,768]{2,1,0:T(8,128)(2,1)}, u32[]{:S(2)}, u32[]{:S(2)}) collective-permute-start(bf16[4,64,768]{2,1,0:T(8,128)(2,1)} %dynamic-slice_bitcast_fusion.9), channel_id=1, source_target_pairs={{2,0},{0,2},{3,1},{1,3},{6,4},{4,6},{7,5},{5,7},{10,8},{8,10},{11,... | collective-permute-start | bytes 1179656 | tf_op jit(solution)/shard_map/ppermute | solution.py:41
  492.9 42.1 %collective-permute-start.60 = (bf16[1024,512]{1,0:T(8,128)(2,1)}, bf16[1024,512]{1,0:T(8,128)(2,1)}, u32[]{:S(2)}, u32[]{:S(2)}) collective-permute-start(bf16[1024,512]{1,0:T(8,128)(2,1)} %fusion.65), channel_id=1, source_target_pairs={{1,0},{0,1},{3,2},{2,3},{5,4},{4,5},{7,6},{6,7},{9,8},{8,9},{11,10... | collective-permute-start | bytes 3145736 | tf_op jit(solution)/shard_map/ppermute | solution.py:41
  497.5 20.2 %collective-permute-start.78 = (bf16[4,2,64,768]{3,2,0,1:T(8,128)(2,1)}, bf16[4,2,64,768]{3,2,0,1:T(8,128)(2,1)}, u32[]{:S(2)}, u32[]{:S(2)}) collective-permute-start(bf16[4,2,64,768]{3,2,0,1:T(8,128)(2,1)} %bitcast.535), channel_id=1, source_target_pairs={{4,0},{0,4},{5,1},{1,5},{6,2},{2,6},{7,3},{3,7},{12,8},{8,12},{13,... | collective-permute-start | bytes 2359304 | tf_op jit(solution)/shard_map/ppermute | solution.py:41
  499.6 19.9 %collective-permute-start.79 = (bf16[4,2,64,768]{3,2,1,0:T(8,128)(2,1)}, bf16[4,2,64,768]{3,2,1,0:T(8,128)(2,1)}, u32[]{:S(2)}, u32[]{:S(2)}) collective-permute-start(bf16[4,2,64,768]{3,2,1,0:T(8,128)(2,1)} %dynamic-slice_bitcast_fusion.1), channel_id=1, source_target_pairs={{2,0},{0,2},{3,1},{1,3},{6,4},{4,6},{7,5},{5,7},{10,8},{8,10},{11,... | collective-permute-start | bytes 2359304 | tf_op jit(solution)/shard_map/ppermute | solution.py:41
  519.4 14.6 %collective-permute-start.62 = (bf16[256,512]{1,0:T(8,128)(2,1)S(1)}, bf16[256,512]{1,0:T(8,128)(2,1)S(1)}, u32[]{:S(2)}, u32[]{:S(2)}) collective-permute-start(bf16[256,512]{1,0:T(8,128)(2,1)S(1)} %copy-done.66), channel_id=1, source_target_pairs={{1,0},{0,1},{3,2},{2,3},{5,4},{4,5},{7,6},{6,7},{9,8},{8,9},{11,10... | collective-permute-start | bytes 786440 | tf_op jit(solution)/shard_map/ppermute | solution.py:41
  522.9 24.2 %collective-permute-start.68 = (bf16[64,2560]{1,0:T(8,128)(2,1)S(1)}, bf16[64,2560]{1,0:T(8,128)(2,1)S(1)}, u32[]{:S(2)}, u32[]{:S(2)}) collective-permute-start(bf16[64,2560]{1,0:T(8,128)(2,1)S(1)} %get-tuple-element.313), channel_id=1, source_target_pairs={{24,0},{0,8},{8,16},{16,24},{25,1},{1,9},{9,17},{17,25},{26,2},{2,... | collective-permute-start | bytes 983048 | tf_op jit(solution)/shard_map/ppermute | solution.py:41
  531.0 17.5 %collective-permute-start.69 = (bf16[64,2560]{1,0:T(8,128)(2,1)S(1)}, bf16[64,2560]{1,0:T(8,128)(2,1)S(1)}, u32[]{:S(2)}, u32[]{:S(2)}) collective-permute-start(bf16[64,2560]{1,0:T(8,128)(2,1)S(1)} %get-tuple-element.312), channel_id=1, source_target_pairs={{16,0},{24,8},{0,16},{8,24},{17,1},{25,9},{1,17},{9,25},{18,2},{26... | collective-permute-start | bytes 983048 | tf_op jit(solution)/shard_map/ppermute | solution.py:41
  537.3 22.7 %collective-permute-start.66 = (bf16[2,2,4,32,512]{4,3,0,2,1:T(8,128)(2,1)S(1)}, bf16[2,2,4,32,512]{4,3,0,2,1:T(8,128)(2,1)S(1)}, u32[]{:S(2)}, u32[]{:S(2)}) collective-permute-start(bf16[2,2,4,32,512]{4,3,0,2,1:T(8,128)(2,1)S(1)} %bitcast.574), channel_id=1, source_target_pairs={{2,0},{0,2},{3,1},{1,3},{6,4},{4,6},{7,5},{5,7},{10,8},{8,10},{11,... | collective-permute-start | bytes 1572872 | tf_op jit(solution)/shard_map/ppermute | solution.py:41
  562.6 32.5 %collective-permute-start.74 = (f32[32,2560]{1,0:T(8,128)S(1)}, f32[32,2560]{1,0:T(8,128)S(1)}, u32[]{:S(2)}, u32[]{:S(2)}) collective-permute-start(f32[32,2560]{1,0:T(8,128)S(1)} %get-tuple-element.346), channel_id=1, source_target_pairs={{1,0},{0,1},{3,2},{2,3},{5,4},{4,5},{7,6},{6,7},{9,8},{8,9},{11,10... | collective-permute-start | bytes 983048 | tf_op jit(solution)/shard_map/ppermute | solution.py:41
  563.0 21.5 %collective-permute-start.76 = (bf16[64,2048]{1,0:T(8,128)(2,1)S(1)}, bf16[64,2048]{1,0:T(8,128)(2,1)S(1)}, u32[]{:S(2)}, u32[]{:S(2)}) collective-permute-start(bf16[64,2048]{1,0:T(8,128)(2,1)S(1)} %get-tuple-element.315), channel_id=1, source_target_pairs={{16,0},{24,8},{0,16},{8,24},{17,1},{25,9},{1,17},{9,25},{18,2},{26... | collective-permute-start | bytes 786440 | tf_op jit(solution)/shard_map/ppermute | solution.py:41
  567.0 28.1 %collective-permute-start.77 = (bf16[64,2048]{1,0:T(8,128)(2,1)S(1)}, bf16[64,2048]{1,0:T(8,128)(2,1)S(1)}, u32[]{:S(2)}, u32[]{:S(2)}) collective-permute-start(bf16[64,2048]{1,0:T(8,128)(2,1)S(1)} %get-tuple-element.314), channel_id=1, source_target_pairs={{8,0},{16,8},{24,16},{0,24},{9,1},{17,9},{25,17},{1,25},{10,2},{18... | collective-permute-start | bytes 786440 | tf_op jit(solution)/shard_map/ppermute | solution.py:41
  568.0 33.7 %collective-permute-start.82 = (bf16[64,1536]{1,0:T(8,128)(2,1)S(1)}, bf16[64,1536]{1,0:T(8,128)(2,1)S(1)}, u32[]{:S(2)}, u32[]{:S(2)}) collective-permute-start(bf16[64,1536]{1,0:T(8,128)(2,1)S(1)} %get-tuple-element.339), channel_id=1, source_target_pairs={{24,0},{0,8},{8,16},{16,24},{25,1},{1,9},{9,17},{17,25},{26,2},{2,... | collective-permute-start | bytes 589832 | tf_op jit(solution)/shard_map/ppermute | solution.py:41
  574.1 29.0 %collective-permute-start.83 = (bf16[64,1536]{1,0:T(8,128)(2,1)S(1)}, bf16[64,1536]{1,0:T(8,128)(2,1)S(1)}, u32[]{:S(2)}, u32[]{:S(2)}) collective-permute-start(bf16[64,1536]{1,0:T(8,128)(2,1)S(1)} %get-tuple-element.340), channel_id=1, source_target_pairs={{16,0},{24,8},{0,16},{8,24},{17,1},{25,9},{1,17},{9,25},{18,2},{26... | collective-permute-start | bytes 589832 | tf_op jit(solution)/shard_map/ppermute | solution.py:41
  584.5 21.8 %collective-permute-start.84 = (bf16[64,1536]{1,0:T(8,128)(2,1)S(1)}, bf16[64,1536]{1,0:T(8,128)(2,1)S(1)}, u32[]{:S(2)}, u32[]{:S(2)}) collective-permute-start(bf16[64,1536]{1,0:T(8,128)(2,1)S(1)} %get-tuple-element.338), channel_id=1, source_target_pairs={{8,0},{16,8},{24,16},{0,24},{9,1},{17,9},{25,17},{1,25},{10,2},{18... | collective-permute-start | bytes 589832 | tf_op jit(solution)/shard_map/ppermute | solution.py:41
  595.1 14.7 %collective-permute-start.88 = (f32[5,1024]{1,0:T(8,128)S(1)}, f32[5,1024]{1,0:T(8,128)S(1)}, u32[]{:S(2)}, u32[]{:S(2)}) collective-permute-start(f32[5,1024]{1,0:T(8,128)S(1)} %add.931), channel_id=1, source_target_pairs={{8,0},{16,8},{24,16},{0,24},{9,1},{17,9},{25,17},{1,25},{10,2},{18... | collective-permute-start | bytes 61448 | tf_op jit(solution)/shard_map/ppermute | solution.py:41
  595.2 16.9 %collective-permute-start.89 = (f32[5,1024]{1,0:T(8,128)S(1)}, f32[5,1024]{1,0:T(8,128)S(1)}, u32[]{:S(2)}, u32[]{:S(2)}) collective-permute-start(f32[5,1024]{1,0:T(8,128)S(1)} %add.931), channel_id=1, source_target_pairs={{16,0},{24,8},{0,16},{8,24},{17,1},{25,9},{1,17},{9,25},{18,2},{26... | collective-permute-start | bytes 61448 | tf_op jit(solution)/shard_map/ppermute | solution.py:41
  612.0 17.0 %collective-permute-start.92 = (f32[32,2048]{1,0:T(8,128)}, f32[32,2048]{1,0:T(8,128)}, u32[]{:S(2)}, u32[]{:S(2)}) collective-permute-start(f32[32,2048]{1,0:T(8,128)} %get-tuple-element.354), channel_id=1, source_target_pairs={{1,0},{0,1},{3,2},{2,3},{5,4},{4,5},{7,6},{6,7},{9,8},{8,9},{11,10... | collective-permute-start | bytes 786440 | tf_op jit(solution)/shard_map/ppermute | solution.py:41
  (165 other events, 1392.5 us)
Sparse Core Ops, SparseCore 0:
  14.6 159.6 all-gather.1

commit v9 on v8

--- a/solution.py
+++ b/solution.py
@@ -616,14 +616,14 @@
     grad_mixed = advance(grad_mixed, first_out_job)
     grad_packed = attention("space", small, packed_space, grad_mixed)
     grad_packed = advance(
-        grad_packed, head_job, contract_job, expand_job, out_job, in_job
+        grad_packed, head_job, contract_job, expand_job, in_job
     )
     first_in_job = product(
         reduce_layer, normed_space, *halves(grad_packed, 1), ("r", "m", "z"), 2
     )
     grad_normed = dot_nt(grad_packed, w_in[0])
     grad_normed = advance(grad_normed, first_in_job, head_job, expand_job, out_job)
-    early_job = Job(reduce_deep([expand_job.result, out_job.result], [block, None]))
+    early_job = Job(reduce_deep([expand_job.result], [block]))
     inward, gain_zero = norm_backward(start, gain_all[0], grad_normed)
     grad_start = grad_space + inward
     mask_grad = jnp.sum(grad_start * space_mask[:, None], axis=0)
@@ -634,14 +634,16 @@
     gain_grads = jnp.stack([gain_zero, gain_one, gain_two, gain_three, mask_grad])
     gain_job = Job(sum_over(gain_grads, ("h", "m", "r", "z")))
     token = jnp.zeros((), WIDE)
-    token = advance(token, embed_job, gain_job, head_job, in_job, first_out_job)
+    token = advance(token, embed_job, gain_job, head_job, in_job, out_job, first_out_job)
     token = advance(token, first_in_job)
     token = advance(token, embed_job, gain_job, head_job, early_job, first_out_job)
-    late_job = Job(reduce_deep([in_job.result, first_out_job.result], [None, None]))
     token = advance(token, first_in_job)
     last_job = Job(reduce_deep([first_in_job.result], [None]))
-    token = advance(token, embed_job, gain_job, early_job, late_job)
-    token = advance(token, last_job, embed_job, gain_job)
+    held = [in_job.result, first_out_job.result, out_job.result]
+    token, held = lax.optimization_barrier((token, held))
+    late_job = Job(reduce_deep(held, [None, None, None]))
+    token = advance(token, embed_job, gain_job, early_job)
+    token = advance(token, last_job, embed_job, gain_job, late_job)
 
     owner = jnp.int32(0)
     for axis in ALL:
@@ -656,7 +658,7 @@
     norm_job = Job(sum_over(sums, ("h", "m", "r", "z")))
     while norm_job.flight is not None:
         token = advance(token, norm_job, *jobs)
-    (up_grad, next_out), (next_in, first_out), (first_in,) = (job.finish() for job in jobs[:3])
+    (up_grad,), (next_in, first_out, next_out), (first_in,) = (job.finish() for job in jobs[:3])
     square_sum, loss = jnp.sum(norm_job.result, axis=1)
     norm = jnp.sqrt(square_sum)
     factor = jnp.minimum(1.0, CLIP / (norm + 1e-06))

time: 684 us -> 672 us (0.982)
  waiting for transfers between devices: 192 us -> 179 us
    ppermute x104, waiting for transfers between devices: 166 us -> 154 us  [shifted(): return lax.ppermute(part, axis, [((i + shift) % n, i) for i in range(n)])]
    unnamed x266 -> x274, local copies, waits for them, and re-layouts: 23.3 us -> 20.6 us
  transfers between devices with their start and end apart: 105 -> 105, of which waited for: 38 -> 36; matrix products, arithmetic and copies ran while one was open for 30% -> 32% of each run, Pallas kernels for 8% -> 8%
where the time goes in v9:
time: 672 us; the launch traced here: 663 us
  waiting for transfers between devices  179 us (27%)
  matrix products  135 us (20%)
  starting transfers between devices  130 us (19%)
  local copies, waits for them, and re-layouts  72.8 us (11%)
  other arithmetic  72.3 us (11%)
  Pallas kernels  54.6 us (8%)
  between operations  19.1 us (3%)
    ppermute x104, waiting for transfers between devices, shifted(): return lax.ppermute(part, axis, [((i + shift) % n, i) for i in range(n)])  154 us
    ppermute x104, starting transfers between devices, shifted(): return lax.ppermute(part, axis, [((i + shift) % n, i) for i in range(n)])  130 us
    pallas_call x4, Pallas kernels, attention(): pl.pallas_call(functools.partial(body, kind), out_shape=jax.ShapeDtypeStr...  54.6 us
    dot_general x10, matrix products, dot_nn(): return jnp.dot(left, right, preferred_element_type=WIDE)  48.3 us
    dot_general x9, matrix products, dot_nt(): lax.dot_general(left, right, (((1,), (1,)), ((), ())), preferred_element_...  46.1 us
    dot_general x16, matrix products, dot_tn(): lax.dot_general(left, right, (((0,), (0,)), ((), ())), preferred_element_...  40.5 us
    all_gather x1, waiting for transfers between devices, on_device(): gathered = lax.all_gather(gathered, ALL, axis=0, tiled=True)  24.7 us
    unnamed x274, local copies, waits for them, and re-layouts  20.6 us
  transfers between devices with their start and end apart: 105, of which 36 were waited for; matrix products, arithmetic and copies ran while one was open for 32% of the time, Pallas kernels for 8%

profile of v9, /device:TPU:0, one launch (start us, length us, event | category | flops | bytes accessed | tf_op | source)
XLA Modules:
  0.0 662.5 jit_solution(3037084614431966706)
XLA Ops:
  14.5 5.1 collective-permute-start.3
  29.9 3.9 collective-permute-start.25
  33.8 2.2 collective-permute-done.25
  36.1 4.5 collective-permute-done.26
  42.4 4.0 collective-permute-done.27
  51.4 3.8 collective-permute-start.7
  55.4 23.9 %collective-permute-done.7 = bf16[128,512]{1,0:T(8,128)(2,1)S(1)} collective-permute-done((bf16[128,512]{1,0:T(8,128)(2,1)S(1)}, bf16[128,512]{1,0:T(8,128)(2,1)S(1)}, u32[]{:S(2)}, u32[]{:S(2)}) %collective-permute-start.7) | collective-permute-done | bytes 131104 | tf_op jit(solution)/shard_map/ppermute | solution.py:41
  84.2 4.6 collective-permute-done.10
  88.8 5.0 collective-permute-start.13
  95.9 20.0 %collective-permute-done.12 = bf16[4,128,512]{2,1,0:T(8,128)(2,1)S(1)} collective-permute-done((bf16[4,128,512]{2,1,0:T(8,128)(2,1)S(1)}, bf16[4,128,512]{2,1,0:T(8,128)(2,1)S(1)}, u32[]{:S(2)}, u32[]{:S(2)}) %collective-permute-start.12) | collective-permute-done | bytes 524320 | tf_op jit(solution)/shard_map/ppermute | solution.py:41
  117.5 15.4 %collective-permute-done.14 = bf16[4,64,1024]{2,1,0:T(8,128)(2,1)S(1)} collective-permute-done((bf16[4,64,1024]{2,1,0:T(8,128)(2,1)S(1)}, bf16[4,64,1024]{2,1,0:T(8,128)(2,1)S(1)}, u32[]{:S(2)}, u32[]{:S(2)}) %collective-permute-start.14) | collective-permute-done | bytes 524320 | tf_op jit(solution)/shard_map/ppermute | solution.py:41
  132.9 5.8 collective-permute-done.15
  138.9 2.5 collective-permute-start.16
  149.2 24.7 %all-gather.2.cloned.1.call-done = bf16[1024,8320]{1,0:T(8,128)(2,1)} async-done(((bf16[32,8320]{1,0:T(8,128)(2,1)}), bf16[1024,8320]{1,0:T(8,128)(2,1)}) %all-gather.2.cloned.1.call-update) | async-done | bytes 17039376 | tf_op jit(solution)/shard_map/all_gather | solution.py:506
  178.2 7.9 %fusion.8.packed_ref = bf16[512,3072]{1,0:T(8,128)(2,1)} fusion(bf16[512,1024]{1,0:T(8,128)(2,1)S(1)} %multiply_convert_fusion.5, bf16[1024,8320]{1,0:T(8,128)(2,1)} %all-gather.2.cloned.1.call-done), kind=kOutput, calls=%fused_computation.16 | convolution fusion | flops 3222798336 | bytes 10485760 | tf_op jit(solution)/shard_map/dot_general | solution.py:316
  186.2 9.3 %shard_map.365 = bf16[512,1024]{1,0:T(8,128)(2,1)} custom-call(s32[1]{0:T(128)} %bitcast.13.scalar_ref, bf16[512,3072]{1,0:T(8,128)(2,1)} %fusion.8.packed_ref), custom_call_target="tpu_custom_call" | custom-call | flops 8999999488 | bytes 8388608 | tf_op jit(solution)/shard_map/pallas_call | solution.py:412
  199.8 2.6 pad_maximum_fusion.1
  202.6 2.9 fusion.60
  214.2 2.5 pad_maximum_fusion
  217.6 8.3 %fusion.11 = bf16[512,3072]{1,0:T(8,128)(2,1)} fusion(bf16[512,1024]{1,0:T(8,128)(2,1)S(1)} %fusion.34, bf16[1024,8320]{1,0:T(8,128)(2,1)} %all-gather.2.cloned.1.call-done), kind=kOutput, calls=%fused_computation.17 | convolution fusion | flops 3222798336 | bytes 10485760 | tf_op jit(solution)/shard_map/dot_general | solution.py:316
  226.0 9.1 %shard_map.366 = bf16[4,128,1024]{2,1,0:T(8,128)(2,1)} custom-call(s32[1]{0:T(128)} %bitcast.30.scalar_ref, bf16[4,128,3072]{2,1,0:T(8,128)(2,1)} %bitcast.579), custom_call_target="tpu_custom_call" | custom-call | flops 8999999488 | bytes 8388608 | tf_op jit(solution)/shard_map/pallas_call | solution.py:412
  235.1 3.3 multiply_reduce_fusion.8
  240.7 4.9 fusion.200
  245.6 6.4 fusion.173
  252.1 4.5 fusion.201
  256.6 6.6 multiply_reduce_fusion.7
  271.1 4.9 convolution_convert_fusion.3
  282.2 6.3 fusion.172
  288.5 7.1 %fusion.20 = bf16[512,2048]{1,0:T(8,128)(2,1)S(1)} fusion(f32[512,2048]{1,0:T(8,128)S(1)} %copy-done.122, bf16[512,1024]{1,0:T(8,128)(2,1)S(1)} %copy-done.41, bf16[2048,1024]{1,0:T(8,128)(2,1)} %bitcast.40), kind=kOutput, calls=%fused_computation.24 | convolution fusion | flops 2168455168 | bytes 11534336 | tf_op jit(solution)/shard_map/dot_general | solution.py:308
  295.6 8.0 %fusion.27 = bf16[512,2048]{1,0:T(8,128)(2,1)S(1)} fusion(f32[512,2048]{1,0:T(8,128)S(1)} %copy-done.125, bf16[512,1024]{1,0:T(8,128)(2,1)S(1)} %copy-done.41, bf16[2048,1024]{1,0:T(8,128)(2,1)} %collective-permute-done.23), kind=kOutput, calls=%fused_computation.31 | convolution fusion | flops 2168455168 | bytes 11534336 | tf_op jit(solution)/shard_map/dot_general | solution.py:308
  303.7 4.4 convolution_convert_fusion.2
  311.7 6.4 add_convert_fusion
  323.6 4.6 fusion.202
  328.2 5.1 multiply_reduce_fusion.2
  333.3 2.6 fusion.186
  335.9 4.4 fusion.69
  342.0 17.8 %shard_map.367 = bf16[4,128,3072]{2,1,0:T(8,128)(2,1)} custom-call(s32[1]{0:T(128)} %bitcast.30.scalar_ref, bf16[4,128,3072]{2,1,0:T(8,128)(2,1)} %bitcast.580, bf16[4,128,1024]{2,1,0:T(8,128)(2,1)} %bitcast.587), custom_call_target="tpu_custom_call" | custom-call | flops 22000001024 | bytes 8388608 | tf_op jit(solution)/shard_map/pallas_call | solution.py:412
  362.3 5.2 add_convert_fusion.1
  374.0 5.9 fusion.40
  391.6 2.2 collective-permute-start.39
  398.3 2.9 collective-permute-done.41
  401.3 3.5 collective-permute-start.44
  412.1 3.8 fusion.66.up_ref
  416.6 3.5 collective-permute-done.50
  425.3 2.3 collective-permute-start.49
  430.4 18.4 %shard_map.368 = bf16[512,3072]{1,0:T(8,128)(2,1)} custom-call(s32[1]{0:T(128)} %bitcast.13.scalar_ref, bf16[512,3072]{1,0:T(8,128)(2,1)} %fusion.8.packed_ref, bf16[512,1024]{1,0:T(8,128)(2,1)} %fusion.66.up_ref), custom_call_target="tpu_custom_call" | custom-call | flops 22000001024 | bytes 8388608 | tf_op jit(solution)/shard_map/pallas_call | solution.py:412
  449.7 3.6 convolution_convert_fusion
  464.5 5.8 fusion.4
  494.8 10.6 %collective-permute-done.72 = bf16[4,2,64,768]{3,2,0,1:T(8,128)(2,1)} collective-permute-done((bf16[4,2,64,768]{3,2,0,1:T(8,128)(2,1)}, bf16[4,2,64,768]{3,2,0,1:T(8,128)(2,1)}, u32[]{:S(2)}, u32[]{:S(2)}) %collective-permute-start.72) | collective-permute-done | bytes 786464 | tf_op jit(solution)/shard_map/ppermute | solution.py:41
  511.2 9.1 %collective-permute-done.65 = bf16[4,2,64,512]{3,2,0,1:T(8,128)(2,1)S(1)} collective-permute-done((bf16[4,2,64,512]{3,2,0,1:T(8,128)(2,1)}, bf16[4,2,64,512]{3,2,0,1:T(8,128)(2,1)S(1)}, u32[]{:S(2)}, u32[]{:S(2)}) %collective-permute-start.65) | collective-permute-done | bytes 524320 | tf_op jit(solution)/shard_map/ppermute | solution.py:41
  521.9 2.9 collective-permute-start.70
  537.9 7.3 %collective-permute-start.76 = (bf16[64,1536]{1,0:T(8,128)(2,1)S(1)}, bf16[64,1536]{1,0:T(8,128)(2,1)S(1)}, u32[]{:S(2)}, u32[]{:S(2)}) collective-permute-start(bf16[64,1536]{1,0:T(8,128)(2,1)S(1)} %get-tuple-element.343), channel_id=1, source_target_pairs={{24,0},{0,8},{8,16},{16,24},{25,1},{1,9},{9,17},{17,25},{26,2},{2,... | collective-permute-start | bytes 589832 | tf_op jit(solution)/shard_map/ppermute | solution.py:41
  545.2 3.5 collective-permute-start.77
  554.3 3.2 collective-permute-done.80
  557.9 2.6 collective-permute-start.85
  561.9 2.4 collective-permute-start.89
  564.3 6.3 collective-permute-done.78
  572.0 6.5 collective-permute-start.87
  581.6 5.9 collective-permute-done.87
  587.5 8.9 %collective-permute-start.83 = (bf16[2,32,512]{2,1,0:T(8,128)(2,1)}, bf16[2,32,512]{2,1,0:T(8,128)(2,1)}, u32[]{:S(2)}, u32[]{:S(2)}) collective-permute-start(bf16[2,32,512]{2,1,0:T(8,128)(2,1)} %get-tuple-element.364), channel_id=1, source_target_pairs={{16,0},{24,8},{0,16},{8,24},{17,1},{25,9},{1,17},{9,25},{18,2},{26... | collective-permute-start | bytes 196616 | tf_op jit(solution)/shard_map/ppermute | solution.py:41
  618.5 6.9 %collective-permute-done.98 = bf16[2,4,32,512]{3,2,1,0:T(8,128)(2,1)S(1)} collective-permute-done((bf16[2,4,32,512]{3,2,1,0:T(8,128)(2,1)S(1)}, bf16[2,4,32,512]{3,2,1,0:T(8,128)(2,1)S(1)}, u32[]{:S(2)}, u32[]{:S(2)}) %collective-permute-start.98) | collective-permute-done | bytes 262176 | tf_op jit(solution)/shard_map/ppermute | solution.py:41
  632.8 2.9 collective-permute-done.102
  641.7 2.6 multiply_subtract_fusion.4
  650.6 3.5 multiply_subtract_fusion
  (703 shorter events, 235.9 us)
Async XLA Ops:
  7.2 166.7 %all-gather.2.cloned.1.call-start = ((), (), s32[]{:S(2)}) async-start(), calls=%async_computation | async-start | bytes 17571840 | tf_op jit(solution)/shard_map/all_gather | solution.py:506
  14.5 32.7 %collective-permute-start.3 = (bf16[128,1024]{1,0:T(8,128)(2,1)S(1)}, bf16[128,1024]{1,0:T(8,128)(2,1)}, u32[]{:S(2)}, u32[]{:S(2)}) collective-permute-start(bf16[128,1024]{1,0:T(8,128)(2,1)S(1)} %convert_element_type.557), channel_id=1, source_target_pairs={{8,0},{16,8},{24,16},{0,24},{9,1},{17,9},{25,17},{1,25},{10,2},{18... | collective-permute-start | bytes 786440 | tf_op jit(solution)/shard_map/ppermute | solution.py:41
  19.7 27.5 %collective-permute-start.4 = (bf16[128,1024]{1,0:T(8,128)(2,1)S(1)}, bf16[128,1024]{1,0:T(8,128)(2,1)S(1)}, u32[]{:S(2)}, u32[]{:S(2)}) collective-permute-start(bf16[128,1024]{1,0:T(8,128)(2,1)S(1)} %convert_element_type.557), channel_id=1, source_target_pairs={{24,0},{0,8},{8,16},{16,24},{25,1},{1,9},{9,17},{17,25},{26,2},{2,... | collective-permute-start | bytes 786440 | tf_op jit(solution)/shard_map/ppermute | solution.py:41
  21.5 25.7 %collective-permute-start.2 = (bf16[32,2048]{1,0:T(8,128)(2,1)S(1)}, bf16[32,2048]{1,0:T(8,128)(2,1)S(1)}, u32[]{:S(2)}, u32[]{:S(2)}) collective-permute-start(bf16[32,2048]{1,0:T(8,128)(2,1)S(1)} %bitcast.565), channel_id=1, source_target_pairs={{1,0},{0,1},{3,2},{2,3},{5,4},{4,5},{7,6},{6,7},{9,8},{8,9},{11,10... | collective-permute-start | bytes 393224 | tf_op jit(solution)/shard_map/ppermute | solution.py:41
  22.6 56.7 %collective-permute-start.1 = (bf16[256,1024]{1,0:T(8,128)(2,1)S(1)}, bf16[256,1024]{1,0:T(8,128)(2,1)S(1)}, u32[]{:S(2)}, u32[]{:S(2)}) collective-permute-start(bf16[256,1024]{1,0:T(8,128)(2,1)S(1)} %get-tuple-element.337), channel_id=1, source_target_pairs={{2,0},{0,2},{3,1},{1,3},{6,4},{4,6},{7,5},{5,7},{10,8},{8,10},{11,... | collective-permute-start | bytes 1572872 | tf_op jit(solution)/shard_map/ppermute | solution.py:41
  47.3 32.1 %collective-permute-start.5 = (bf16[64,2048]{1,0:T(8,128)(2,1)S(1)}, bf16[64,2048]{1,0:T(8,128)(2,1)S(1)}, u32[]{:S(2)}, u32[]{:S(2)}) collective-permute-start(bf16[64,2048]{1,0:T(8,128)(2,1)S(1)} %bitcast.546), channel_id=1, source_target_pairs={{8,0},{16,8},{24,16},{0,24},{9,1},{17,9},{25,17},{1,25},{10,2},{18... | collective-permute-start | bytes 786440 | tf_op jit(solution)/shard_map/ppermute | solution.py:41
  49.3 30.0 %collective-permute-start.6 = (bf16[64,2048]{1,0:T(8,128)(2,1)S(1)}, bf16[64,2048]{1,0:T(8,128)(2,1)S(1)}, u32[]{:S(2)}, u32[]{:S(2)}) collective-permute-start(bf16[64,2048]{1,0:T(8,128)(2,1)S(1)} %bitcast.547), channel_id=1, source_target_pairs={{24,0},{0,8},{8,16},{16,24},{25,1},{1,9},{9,17},{17,25},{26,2},{2,... | collective-permute-start | bytes 786440 | tf_op jit(solution)/shard_map/ppermute | solution.py:41
  51.4 27.9 %collective-permute-start.7 = (bf16[128,512]{1,0:T(8,128)(2,1)S(1)}, bf16[128,512]{1,0:T(8,128)(2,1)S(1)}, u32[]{:S(2)}, u32[]{:S(2)}) collective-permute-start(bf16[128,512]{1,0:T(8,128)(2,1)S(1)} %slice.104), channel_id=1, source_target_pairs={{8,0},{16,8},{24,16},{0,24},{9,1},{17,9},{25,17},{1,25},{10,2},{18... | collective-permute-start | bytes 393224 | tf_op jit(solution)/shard_map/ppermute | solution.py:41
  55.3 24.0 %collective-permute-start.8 = (bf16[128,512]{1,0:T(8,128)(2,1)S(1)}, bf16[128,512]{1,0:T(8,128)(2,1)S(1)}, u32[]{:S(2)}, u32[]{:S(2)}) collective-permute-start(bf16[128,512]{1,0:T(8,128)(2,1)S(1)} %slice.105), channel_id=1, source_target_pairs={{24,0},{0,8},{8,16},{16,24},{25,1},{1,9},{9,17},{17,25},{26,2},{2,... | collective-permute-start | bytes 393224 | tf_op jit(solution)/shard_map/ppermute | solution.py:41
  79.3 69.9 %collective-permute-start = (bf16[256,1024]{1,0:T(8,128)(2,1)}, bf16[256,1024]{1,0:T(8,128)(2,1)}, u32[]{:S(2)}, u32[]{:S(2)}) collective-permute-start(bf16[256,1024]{1,0:T(8,128)(2,1)} %get-tuple-element.336), channel_id=1, source_target_pairs={{2,0},{0,2},{3,1},{1,3},{6,4},{4,6},{7,5},{5,7},{10,8},{8,10},{11,... | collective-permute-start | bytes 1572872 | tf_op jit(solution)/shard_map/ppermute | solution.py:41
  79.8 36.2 %collective-permute-start.12 = (bf16[4,128,512]{2,1,0:T(8,128)(2,1)S(1)}, bf16[4,128,512]{2,1,0:T(8,128)(2,1)S(1)}, u32[]{:S(2)}, u32[]{:S(2)}) collective-permute-start(bf16[4,128,512]{2,1,0:T(8,128)(2,1)S(1)} %get-tuple-element.335), channel_id=1, source_target_pairs={{2,0},{0,2},{3,1},{1,3},{6,4},{4,6},{7,5},{5,7},{10,8},{8,10},{11,... | collective-permute-start | bytes 1572872 | tf_op jit(solution)/shard_map/ppermute | solution.py:41
  88.8 28.8 %collective-permute-start.13 = (bf16[4,128,512]{2,1,0:T(8,128)(2,1)S(1)}, bf16[4,128,512]{2,1,0:T(8,128)(2,1)S(1)}, u32[]{:S(2)}, u32[]{:S(2)}) collective-permute-start(bf16[4,128,512]{2,1,0:T(8,128)(2,1)S(1)} %get-tuple-element.334), channel_id=1, source_target_pairs={{4,0},{0,4},{5,1},{1,5},{6,2},{2,6},{7,3},{3,7},{12,8},{8,12},{13,... | collective-permute-start | bytes 1572872 | tf_op jit(solution)/shard_map/ppermute | solution.py:41
  93.9 39.1 %collective-permute-start.14 = (bf16[4,64,1024]{2,1,0:T(8,128)(2,1)S(1)}, bf16[4,64,1024]{2,1,0:T(8,128)(2,1)S(1)}, u32[]{:S(2)}, u32[]{:S(2)}) collective-permute-start(bf16[4,64,1024]{2,1,0:T(8,128)(2,1)S(1)} %get-tuple-element.333), channel_id=1, source_target_pairs={{2,0},{0,2},{3,1},{1,3},{6,4},{4,6},{7,5},{5,7},{10,8},{8,10},{11,... | collective-permute-start | bytes 1572872 | tf_op jit(solution)/shard_map/ppermute | solution.py:41
  94.2 44.5 %collective-permute-start.15 = (bf16[4,64,1024]{2,1,0:T(8,128)(2,1)S(1)}, bf16[4,64,1024]{2,1,0:T(8,128)(2,1)S(1)}, u32[]{:S(2)}, u32[]{:S(2)}) collective-permute-start(bf16[4,64,1024]{2,1,0:T(8,128)(2,1)S(1)} %get-tuple-element.332), channel_id=1, source_target_pairs={{4,0},{0,4},{5,1},{1,5},{6,2},{2,6},{7,3},{3,7},{12,8},{8,12},{13,... | collective-permute-start | bytes 1572872 | tf_op jit(solution)/shard_map/ppermute | solution.py:41
  138.9 56.5 %collective-permute-start.16 = (bf16[4,2,128,512]{3,2,1,0:T(8,128)(2,1)S(1)}, bf16[4,2,128,512]{3,2,1,0:T(8,128)(2,1)}, u32[]{:S(2)}, u32[]{:S(2)}) collective-permute-start(bf16[4,2,128,512]{3,2,1,0:T(8,128)(2,1)S(1)} %bitcast_dynamic-update-slice_fusion.7), channel_id=1, source_target_pairs={{4,0},{0,4},{5,1},{1,5},{6,2},{2,6},{7,3},{3,7},{12,8},{8,12},{13,... | collective-permute-start | bytes 3145736 | tf_op jit(solution)/shard_map/ppermute | solution.py:41
  143.3 52.1 %collective-permute-start.17 = (bf16[4,2,128,512]{3,2,1,0:T(8,128)(2,1)}, bf16[4,2,128,512]{3,2,1,0:T(8,128)(2,1)}, u32[]{:S(2)}, u32[]{:S(2)}) collective-permute-start(bf16[4,2,128,512]{3,2,1,0:T(8,128)(2,1)} %bitcast_dynamic-update-slice_fusion.10), channel_id=1, source_target_pairs={{2,0},{0,2},{3,1},{1,3},{6,4},{4,6},{7,5},{5,7},{10,8},{8,10},{11,... | collective-permute-start | bytes 3145736 | tf_op jit(solution)/shard_map/ppermute | solution.py:41
  145.3 50.2 %collective-permute-start.18 = (bf16[4,2,64,1024]{3,2,1,0:T(8,128)(2,1)}, bf16[4,2,64,1024]{3,2,1,0:T(8,128)(2,1)}, u32[]{:S(2)}, u32[]{:S(2)}) collective-permute-start(bf16[4,2,64,1024]{3,2,1,0:T(8,128)(2,1)} %bitcast_dynamic-update-slice_fusion.6), channel_id=1, source_target_pairs={{4,0},{0,4},{5,1},{1,5},{6,2},{2,6},{7,3},{3,7},{12,8},{8,12},{13,... | collective-permute-start | bytes 3145736 | tf_op jit(solution)/shard_map/ppermute | solution.py:41
  147.2 48.2 %collective-permute-start.19 = (bf16[4,2,64,1024]{3,2,1,0:T(8,128)(2,1)}, bf16[4,2,64,1024]{3,2,1,0:T(8,128)(2,1)}, u32[]{:S(2)}, u32[]{:S(2)}) collective-permute-start(bf16[4,2,64,1024]{3,2,1,0:T(8,128)(2,1)} %bitcast_dynamic-update-slice_fusion.9), channel_id=1, source_target_pairs={{2,0},{0,2},{3,1},{1,3},{6,4},{4,6},{7,5},{5,7},{10,8},{8,10},{11,... | collective-permute-start | bytes 3145736 | tf_op jit(solution)/shard_map/ppermute | solution.py:41
  202.4 54.3 %collective-permute-start.23 = (bf16[2048,1024]{1,0:T(8,128)(2,1)}, bf16[2048,1024]{1,0:T(8,128)(2,1)}, u32[]{:S(2)}, u32[]{:S(2)}) collective-permute-start(bf16[2048,1024]{1,0:T(8,128)(2,1)} %bitcast.40), channel_id=1, source_target_pairs={{1,0},{0,1},{3,2},{2,3},{5,4},{4,5},{7,6},{6,7},{9,8},{8,9},{11,10... | collective-permute-start | bytes 12582920 | tf_op jit(solution)/shard_map/ppermute | solution.py:41
  216.7 35.3 %collective-permute-start.22 = (bf16[1024,2048]{1,0:T(8,128)(2,1)}, bf16[1024,2048]{1,0:T(8,128)(2,1)}, u32[]{:S(2)}, u32[]{:S(2)}) collective-permute-start(bf16[1024,2048]{1,0:T(8,128)(2,1)} %bitcast.37), channel_id=1, source_target_pairs={{1,0},{0,1},{3,2},{2,3},{5,4},{4,5},{7,6},{6,7},{9,8},{8,9},{11,10... | collective-permute-start | bytes 12582920 | tf_op jit(solution)/shard_map/ppermute | solution.py:41
  276.1 27.6 %collective-permute-start.29 = (bf16[2048,1024]{1,0:T(8,128)(2,1)}, bf16[2048,1024]{1,0:T(8,128)(2,1)}, u32[]{:S(2)}, u32[]{:S(2)}) collective-permute-start(bf16[2048,1024]{1,0:T(8,128)(2,1)} %convolution_convert_fusion.3), channel_id=1, source_target_pairs={{1,0},{0,1},{3,2},{2,3},{5,4},{4,5},{7,6},{6,7},{9,8},{8,9},{11,10... | collective-permute-start | bytes 12582920 | tf_op jit(solution)/shard_map/ppermute | solution.py:41
  278.2 25.4 %collective-permute-start.28 = (bf16[1024,512]{1,0:T(8,128)(2,1)S(1)}, bf16[1024,512]{1,0:T(8,128)(2,1)S(1)}, u32[]{:S(2)}, u32[]{:S(2)}) collective-permute-start(bf16[1024,512]{1,0:T(8,128)(2,1)S(1)} %convolution_convert_fusion.6), channel_id=1, source_target_pairs={{1,0},{0,1},{3,2},{2,3},{5,4},{4,5},{7,6},{6,7},{9,8},{8,9},{11,10... | collective-permute-start | bytes 3145736 | tf_op jit(solution)/shard_map/ppermute | solution.py:41
  308.1 27.8 %collective-permute-start.31 = (bf16[1024,2048]{1,0:T(8,128)(2,1)}, bf16[1024,2048]{1,0:T(8,128)(2,1)}, u32[]{:S(2)}, u32[]{:S(2)}) collective-permute-start(bf16[1024,2048]{1,0:T(8,128)(2,1)} %convolution_convert_fusion.2), channel_id=1, source_target_pairs={{1,0},{0,1},{3,2},{2,3},{5,4},{4,5},{7,6},{6,7},{9,8},{8,9},{11,10... | collective-permute-start | bytes 12582920 | tf_op jit(solution)/shard_map/ppermute | solution.py:41
  309.7 26.2 %collective-permute-start.30 = (bf16[2,2,4,32,512]{4,3,0,2,1:T(8,128)(2,1)S(1)}, bf16[2,2,4,32,512]{4,3,0,2,1:T(8,128)(2,1)S(1)}, u32[]{:S(2)}, u32[]{:S(2)}) collective-permute-start(bf16[2,2,4,32,512]{4,3,0,2,1:T(8,128)(2,1)S(1)} %bitcast.562), channel_id=1, source_target_pairs={{2,0},{0,2},{3,1},{1,3},{6,4},{4,6},{7,5},{5,7},{10,8},{8,10},{11,... | collective-permute-start | bytes 1572872 | tf_op jit(solution)/shard_map/ppermute | solution.py:41
  319.7 50.0 %collective-permute-start.33 = (bf16[4,2,128,512]{3,2,0,1:T(8,128)(2,1)}, bf16[4,2,128,512]{3,2,0,1:T(8,128)(2,1)}, u32[]{:S(2)}, u32[]{:S(2)}) collective-permute-start(bf16[4,2,128,512]{3,2,0,1:T(8,128)(2,1)} %bitcast.518), channel_id=1, source_target_pairs={{2,0},{0,2},{3,1},{1,3},{6,4},{4,6},{7,5},{5,7},{10,8},{8,10},{11,... | collective-permute-start | bytes 3145736 | tf_op jit(solution)/shard_map/ppermute | solution.py:41
  322.0 47.7 %collective-permute-start.34 = (bf16[4,2,128,512]{3,2,0,1:T(8,128)(2,1)}, bf16[4,2,128,512]{3,2,0,1:T(8,128)(2,1)}, u32[]{:S(2)}, u32[]{:S(2)}) collective-permute-start(bf16[4,2,128,512]{3,2,0,1:T(8,128)(2,1)} %bitcast.517), channel_id=1, source_target_pairs={{4,0},{0,4},{5,1},{1,5},{6,2},{2,6},{7,3},{3,7},{12,8},{8,12},{13,... | collective-permute-start | bytes 3145736 | tf_op jit(solution)/shard_map/ppermute | solution.py:41
  373.5 27.8 %collective-permute-start.42 = (bf16[1024,1536]{1,0:T(8,128)(2,1)S(1)}, bf16[1024,1536]{1,0:T(8,128)(2,1)S(1)}, u32[]{:S(2)}, u32[]{:S(2)}) collective-permute-start(bf16[1024,1536]{1,0:T(8,128)(2,1)S(1)} %convolution_convert_fusion.1), channel_id=1, source_target_pairs={{1,0},{0,1},{3,2},{2,3},{5,4},{4,5},{7,6},{6,7},{9,8},{8,9},{11,10... | collective-permute-start | bytes 9437192 | tf_op jit(solution)/shard_map/ppermute | solution.py:41
  383.5 14.9 %collective-permute-start.40 = (bf16[4,128,512]{2,1,0:T(8,128)(2,1)S(1)}, bf16[4,128,512]{2,1,0:T(8,128)(2,1)S(1)}, u32[]{:S(2)}, u32[]{:S(2)}) collective-permute-start(bf16[4,128,512]{2,1,0:T(8,128)(2,1)S(1)} %dynamic-slice_bitcast_fusion.7), channel_id=1, source_target_pairs={{4,0},{0,4},{5,1},{1,5},{6,2},{2,6},{7,3},{3,7},{12,8},{8,12},{13,... | collective-permute-start | bytes 1572872 | tf_op jit(solution)/shard_map/ppermute | solution.py:41
  386.4 14.9 %collective-permute-start.41 = (bf16[4,128,512]{2,1,0:T(8,128)(2,1)S(1)}, bf16[4,128,512]{2,1,0:T(8,128)(2,1)S(1)}, u32[]{:S(2)}, u32[]{:S(2)}) collective-permute-start(bf16[4,128,512]{2,1,0:T(8,128)(2,1)S(1)} %dynamic-slice_bitcast_fusion.6), channel_id=1, source_target_pairs={{2,0},{0,2},{3,1},{1,3},{6,4},{4,6},{7,5},{5,7},{10,8},{8,10},{11,... | collective-permute-start | bytes 1572872 | tf_op jit(solution)/shard_map/ppermute | solution.py:41
  395.1 25.0 %collective-permute-start.50 = (bf16[4,2,64,1024]{3,2,0,1:T(8,128)(2,1)S(1)}, bf16[4,2,64,1024]{3,2,0,1:T(8,128)(2,1)}, u32[]{:S(2)}, u32[]{:S(2)}) collective-permute-start(bf16[4,2,64,1024]{3,2,0,1:T(8,128)(2,1)S(1)} %bitcast.549), channel_id=1, source_target_pairs={{4,0},{0,4},{5,1},{1,5},{6,2},{2,6},{7,3},{3,7},{12,8},{8,12},{13,... | collective-permute-start | bytes 3145736 | tf_op jit(solution)/shard_map/ppermute | solution.py:41
  396.2 26.4 %collective-permute-start.51 = (bf16[4,2,64,1024]{3,2,1,0:T(8,128)(2,1)S(1)}, bf16[4,2,64,1024]{3,2,1,0:T(8,128)(2,1)S(1)}, u32[]{:S(2)}, u32[]{:S(2)}) collective-permute-start(bf16[4,2,64,1024]{3,2,1,0:T(8,128)(2,1)S(1)} %dynamic-slice_bitcast_fusion), channel_id=1, source_target_pairs={{2,0},{0,2},{3,1},{1,3},{6,4},{4,6},{7,5},{5,7},{10,8},{8,10},{11,... | collective-permute-start | bytes 3145736 | tf_op jit(solution)/shard_map/ppermute | solution.py:41
  401.3 24.0 %collective-permute-start.44 = (bf16[2,32,512]{2,1,0:T(8,128)(2,1)S(1)}, bf16[2,32,512]{2,1,0:T(8,128)(2,1)S(1)}, u32[]{:S(2)}, u32[]{:S(2)}) collective-permute-start(bf16[2,32,512]{2,1,0:T(8,128)(2,1)S(1)} %get-tuple-element.362), channel_id=1, source_target_pairs={{8,0},{16,8},{24,16},{0,24},{9,1},{17,9},{25,17},{1,25},{10,2},{18... | collective-permute-start | bytes 196616 | tf_op jit(solution)/shard_map/ppermute | solution.py:41
  404.8 22.8 %collective-permute-start.45 = (bf16[2,32,512]{2,1,0:T(8,128)(2,1)S(1)}, bf16[2,32,512]{2,1,0:T(8,128)(2,1)S(1)}, u32[]{:S(2)}, u32[]{:S(2)}) collective-permute-start(bf16[2,32,512]{2,1,0:T(8,128)(2,1)S(1)} %get-tuple-element.362), channel_id=1, source_target_pairs={{16,0},{24,8},{0,16},{8,24},{17,1},{25,9},{1,17},{9,25},{18,2},{26... | collective-permute-start | bytes 196616 | tf_op jit(solution)/shard_map/ppermute | solution.py:41
  420.1 28.8 %collective-permute-start.47 = (bf16[128,1024]{1,0:T(8,128)(2,1)}, bf16[128,1024]{1,0:T(8,128)(2,1)S(1)}, u32[]{:S(2)}, u32[]{:S(2)}) collective-permute-start(bf16[128,1024]{1,0:T(8,128)(2,1)} %get-tuple-element.328), channel_id=1, source_target_pairs={{24,0},{0,8},{8,16},{16,24},{25,1},{1,9},{9,17},{17,25},{26,2},{2,... | collective-permute-start | bytes 786440 | tf_op jit(solution)/shard_map/ppermute | solution.py:41
  423.6 26.1 %collective-permute-start.48 = (bf16[128,1024]{1,0:T(8,128)(2,1)}, bf16[128,1024]{1,0:T(8,128)(2,1)}, u32[]{:S(2)}, u32[]{:S(2)}) collective-permute-start(bf16[128,1024]{1,0:T(8,128)(2,1)} %get-tuple-element.329), channel_id=1, source_target_pairs={{16,0},{24,8},{0,16},{8,24},{17,1},{25,9},{1,17},{9,25},{18,2},{26... | collective-permute-start | bytes 786440 | tf_op jit(solution)/shard_map/ppermute | solution.py:41
  425.3 24.4 %collective-permute-start.49 = (bf16[128,1024]{1,0:T(8,128)(2,1)}, bf16[128,1024]{1,0:T(8,128)(2,1)}, u32[]{:S(2)}, u32[]{:S(2)}) collective-permute-start(bf16[128,1024]{1,0:T(8,128)(2,1)} %get-tuple-element.327), channel_id=1, source_target_pairs={{8,0},{16,8},{24,16},{0,24},{9,1},{17,9},{25,17},{1,25},{10,2},{18... | collective-permute-start | bytes 786440 | tf_op jit(solution)/shard_map/ppermute | solution.py:41
  427.6 22.1 %collective-permute-start.52 = (bf16[4,2,64,768]{3,2,0,1:T(8,128)(2,1)}, bf16[4,2,64,768]{3,2,0,1:T(8,128)(2,1)}, u32[]{:S(2)}, u32[]{:S(2)}) collective-permute-start(bf16[4,2,64,768]{3,2,0,1:T(8,128)(2,1)} %bitcast.520), channel_id=1, source_target_pairs={{2,0},{0,2},{3,1},{1,3},{6,4},{4,6},{7,5},{5,7},{10,8},{8,10},{11,... | collective-permute-start | bytes 2359304 | tf_op jit(solution)/shard_map/ppermute | solution.py:41
  429.5 20.1 %collective-permute-start.53 = (bf16[4,2,64,768]{3,2,1,0:T(8,128)(2,1)}, bf16[4,2,64,768]{3,2,1,0:T(8,128)(2,1)}, u32[]{:S(2)}, u32[]{:S(2)}) collective-permute-start(bf16[4,2,64,768]{3,2,1,0:T(8,128)(2,1)} %dynamic-slice_bitcast_fusion.2), channel_id=1, source_target_pairs={{4,0},{0,4},{5,1},{1,5},{6,2},{2,6},{7,3},{3,7},{12,8},{8,12},{13,... | collective-permute-start | bytes 2359304 | tf_op jit(solution)/shard_map/ppermute | solution.py:41
  448.8 27.4 %collective-permute-start.58 = (bf16[4,2,64,512]{3,2,1,0:T(8,128)(2,1)}, bf16[4,2,64,512]{3,2,1,0:T(8,128)(2,1)S(1)}, u32[]{:S(2)}, u32[]{:S(2)}) collective-permute-start(bf16[4,2,64,512]{3,2,1,0:T(8,128)(2,1)} %dynamic-slice_bitcast_fusion.3), channel_id=1, source_target_pairs={{2,0},{0,2},{3,1},{1,3},{6,4},{4,6},{7,5},{5,7},{10,8},{8,10},{11,... | collective-permute-start | bytes 1572872 | tf_op jit(solution)/shard_map/ppermute | solution.py:41
  453.2 24.7 %collective-permute-start.54 = (bf16[1024,1536]{1,0:T(8,128)(2,1)S(1)}, bf16[1024,1536]{1,0:T(8,128)(2,1)S(1)}, u32[]{:S(2)}, u32[]{:S(2)}) collective-permute-start(bf16[1024,1536]{1,0:T(8,128)(2,1)S(1)} %convolution_convert_fusion), channel_id=1, source_target_pairs={{1,0},{0,1},{3,2},{2,3},{5,4},{4,5},{7,6},{6,7},{9,8},{8,9},{11,10... | collective-permute-start | bytes 9437192 | tf_op jit(solution)/shard_map/ppermute | solution.py:41
  453.4 23.8 %collective-permute-start.55 = (bf16[2,4,32,512]{3,2,1,0:T(8,128)(2,1)S(1)}, bf16[2,4,32,512]{3,2,1,0:T(8,128)(2,1)S(1)}, u32[]{:S(2)}, u32[]{:S(2)}) collective-permute-start(bf16[2,4,32,512]{3,2,1,0:T(8,128)(2,1)S(1)} %bitcast_dynamic-update-slice_fusion.28), channel_id=1, source_target_pairs={{4,0},{0,4},{5,1},{1,5},{6,2},{2,6},{7,3},{3,7},{12,8},{8,12},{13,... | collective-permute-start | bytes 786440 | tf_op jit(solution)/shard_map/ppermute | solution.py:41
  456.4 21.5 %collective-permute-start.56 = (bf16[4,64,1024]{2,1,0:T(8,128)(2,1)S(1)}, bf16[4,64,1024]{2,1,0:T(8,128)(2,1)S(1)}, u32[]{:S(2)}, u32[]{:S(2)}) collective-permute-start(bf16[4,64,1024]{2,1,0:T(8,128)(2,1)S(1)} %dynamic-slice_bitcast_fusion.5), channel_id=1, source_target_pairs={{2,0},{0,2},{3,1},{1,3},{6,4},{4,6},{7,5},{5,7},{10,8},{8,10},{11,... | collective-permute-start | bytes 1572872 | tf_op jit(solution)/shard_map/ppermute | solution.py:41
  458.3 19.7 %collective-permute-start.57 = (bf16[4,64,1024]{2,1,0:T(8,128)(2,1)S(1)}, bf16[4,64,1024]{2,1,0:T(8,128)(2,1)S(1)}, u32[]{:S(2)}, u32[]{:S(2)}) collective-permute-start(bf16[4,64,1024]{2,1,0:T(8,128)(2,1)S(1)} %dynamic-slice_bitcast_fusion.4), channel_id=1, source_target_pairs={{4,0},{0,4},{5,1},{1,5},{6,2},{2,6},{7,3},{3,7},{12,8},{8,12},{13,... | collective-permute-start | bytes 1572872 | tf_op jit(solution)/shard_map/ppermute | solution.py:41
  476.2 32.2 %collective-permute-start.62 = (bf16[4,64,768]{2,1,0:T(8,128)(2,1)}, bf16[4,64,768]{2,1,0:T(8,128)(2,1)}, u32[]{:S(2)}, u32[]{:S(2)}) collective-permute-start(bf16[4,64,768]{2,1,0:T(8,128)(2,1)} %dynamic-slice_bitcast_fusion.11), channel_id=1, source_target_pairs={{4,0},{0,4},{5,1},{1,5},{6,2},{2,6},{7,3},{3,7},{12,8},{8,12},{13,... | collective-permute-start | bytes 1179656 | tf_op jit(solution)/shard_map/ppermute | solution.py:41
  477.2 33.7 %collective-permute-start.63 = (bf16[4,64,768]{2,1,0:T(8,128)(2,1)}, bf16[4,64,768]{2,1,0:T(8,128)(2,1)}, u32[]{:S(2)}, u32[]{:S(2)}) collective-permute-start(bf16[4,64,768]{2,1,0:T(8,128)(2,1)} %dynamic-slice_bitcast_fusion.10), channel_id=1, source_target_pairs={{2,0},{0,2},{3,1},{1,3},{6,4},{4,6},{7,5},{5,7},{10,8},{8,10},{11,... | collective-permute-start | bytes 1179656 | tf_op jit(solution)/shard_map/ppermute | solution.py:41
  481.4 44.9 %collective-permute-start.59 = (bf16[1024,512]{1,0:T(8,128)(2,1)}, bf16[1024,512]{1,0:T(8,128)(2,1)}, u32[]{:S(2)}, u32[]{:S(2)}) collective-permute-start(bf16[1024,512]{1,0:T(8,128)(2,1)} %fusion.65), channel_id=1, source_target_pairs={{1,0},{0,1},{3,2},{2,3},{5,4},{4,5},{7,6},{6,7},{9,8},{8,9},{11,10... | collective-permute-start | bytes 3145736 | tf_op jit(solution)/shard_map/ppermute | solution.py:41
  485.9 19.5 %collective-permute-start.72 = (bf16[4,2,64,768]{3,2,0,1:T(8,128)(2,1)}, bf16[4,2,64,768]{3,2,0,1:T(8,128)(2,1)}, u32[]{:S(2)}, u32[]{:S(2)}) collective-permute-start(bf16[4,2,64,768]{3,2,0,1:T(8,128)(2,1)} %bitcast.519), channel_id=1, source_target_pairs={{4,0},{0,4},{5,1},{1,5},{6,2},{2,6},{7,3},{3,7},{12,8},{8,12},{13,... | collective-permute-start | bytes 2359304 | tf_op jit(solution)/shard_map/ppermute | solution.py:41
  487.8 19.2 %collective-permute-start.73 = (bf16[4,2,64,768]{3,2,1,0:T(8,128)(2,1)}, bf16[4,2,64,768]{3,2,1,0:T(8,128)(2,1)}, u32[]{:S(2)}, u32[]{:S(2)}) collective-permute-start(bf16[4,2,64,768]{3,2,1,0:T(8,128)(2,1)} %dynamic-slice_bitcast_fusion.1), channel_id=1, source_target_pairs={{2,0},{0,2},{3,1},{1,3},{6,4},{4,6},{7,5},{5,7},{10,8},{8,10},{11,... | collective-permute-start | bytes 2359304 | tf_op jit(solution)/shard_map/ppermute | solution.py:41
  505.4 15.0 %collective-permute-start.65 = (bf16[4,2,64,512]{3,2,0,1:T(8,128)(2,1)}, bf16[4,2,64,512]{3,2,0,1:T(8,128)(2,1)S(1)}, u32[]{:S(2)}, u32[]{:S(2)}) collective-permute-start(bf16[4,2,64,512]{3,2,0,1:T(8,128)(2,1)} %bitcast.560), channel_id=1, source_target_pairs={{4,0},{0,4},{5,1},{1,5},{6,2},{2,6},{7,3},{3,7},{12,8},{8,12},{13,... | collective-permute-start | bytes 1572872 | tf_op jit(solution)/shard_map/ppermute | solution.py:41
  507.0 14.9 %collective-permute-start.61 = (bf16[256,512]{1,0:T(8,128)(2,1)S(1)}, bf16[256,512]{1,0:T(8,128)(2,1)S(1)}, u32[]{:S(2)}, u32[]{:S(2)}) collective-permute-start(bf16[256,512]{1,0:T(8,128)(2,1)S(1)} %dynamic-slice_bitcast_fusion.22), channel_id=1, source_target_pairs={{1,0},{0,1},{3,2},{2,3},{5,4},{4,5},{7,6},{6,7},{9,8},{8,9},{11,10... | collective-permute-start | bytes 786440 | tf_op jit(solution)/shard_map/ppermute | solution.py:41
  508.4 16.4 %collective-permute-start.64 = (bf16[4,64,512]{2,1,0:T(8,128)(2,1)S(1)}, bf16[4,64,512]{2,1,0:T(8,128)(2,1)S(1)}, u32[]{:S(2)}, u32[]{:S(2)}) collective-permute-start(bf16[4,64,512]{2,1,0:T(8,128)(2,1)S(1)} %dynamic-slice_bitcast_fusion.21), channel_id=1, source_target_pairs={{4,0},{0,4},{5,1},{1,5},{6,2},{2,6},{7,3},{3,7},{12,8},{8,12},{13,... | collective-permute-start | bytes 786440 | tf_op jit(solution)/shard_map/ppermute | solution.py:41
  520.4 16.0 %collective-permute-start.68 = (bf16[64,2048]{1,0:T(8,128)(2,1)S(1)}, bf16[64,2048]{1,0:T(8,128)(2,1)S(1)}, u32[]{:S(2)}, u32[]{:S(2)}) collective-permute-start(bf16[64,2048]{1,0:T(8,128)(2,1)S(1)} %copy-done.71), channel_id=1, source_target_pairs={{24,0},{0,8},{8,16},{16,24},{25,1},{1,9},{9,17},{17,25},{26,2},{2,... | collective-permute-start | bytes 786440 | tf_op jit(solution)/shard_map/ppermute | solution.py:41
  520.4 17.5 %collective-permute-start.69 = (bf16[64,2048]{1,0:T(8,128)(2,1)S(1)}, bf16[64,2048]{1,0:T(8,128)(2,1)S(1)}, u32[]{:S(2)}, u32[]{:S(2)}) collective-permute-start(bf16[64,2048]{1,0:T(8,128)(2,1)S(1)} %copy-done.70), channel_id=1, source_target_pairs={{16,0},{24,8},{0,16},{8,24},{17,1},{25,9},{1,17},{9,25},{18,2},{26... | collective-permute-start | bytes 786440 | tf_op jit(solution)/shard_map/ppermute | solution.py:41
  521.9 23.3 %collective-permute-start.70 = (bf16[64,2048]{1,0:T(8,128)(2,1)S(1)}, bf16[64,2048]{1,0:T(8,128)(2,1)S(1)}, u32[]{:S(2)}, u32[]{:S(2)}) collective-permute-start(bf16[64,2048]{1,0:T(8,128)(2,1)S(1)} %copy-done.69), channel_id=1, source_target_pairs={{8,0},{16,8},{24,16},{0,24},{9,1},{17,9},{25,17},{1,25},{10,2},{18... | collective-permute-start | bytes 786440 | tf_op jit(solution)/shard_map/ppermute | solution.py:41
  534.1 16.3 %collective-permute-start.66 = (bf16[2,2,4,32,512]{4,3,0,2,1:T(8,128)(2,1)S(1)}, bf16[2,2,4,32,512]{4,3,0,2,1:T(8,128)(2,1)S(1)}, u32[]{:S(2)}, u32[]{:S(2)}) collective-permute-start(bf16[2,2,4,32,512]{4,3,0,2,1:T(8,128)(2,1)S(1)} %bitcast.561), channel_id=1, source_target_pairs={{2,0},{0,2},{3,1},{1,3},{6,4},{4,6},{7,5},{5,7},{10,8},{8,10},{11,... | collective-permute-start | bytes 1572872 | tf_op jit(solution)/shard_map/ppermute | solution.py:41
  535.6 14.9 %collective-permute-start.71 = (bf16[4,64,512]{2,1,0:T(8,128)(2,1)S(1)}, bf16[4,64,512]{2,1,0:T(8,128)(2,1)S(1)}, u32[]{:S(2)}, u32[]{:S(2)}) collective-permute-start(bf16[4,64,512]{2,1,0:T(8,128)(2,1)S(1)} %dynamic-slice_bitcast_fusion.20), channel_id=1, source_target_pairs={{2,0},{0,2},{3,1},{1,3},{6,4},{4,6},{7,5},{5,7},{10,8},{8,10},{11,... | collective-permute-start | bytes 786440 | tf_op jit(solution)/shard_map/ppermute | solution.py:41
  537.9 23.9 %collective-permute-start.76 = (bf16[64,1536]{1,0:T(8,128)(2,1)S(1)}, bf16[64,1536]{1,0:T(8,128)(2,1)S(1)}, u32[]{:S(2)}, u32[]{:S(2)}) collective-permute-start(bf16[64,1536]{1,0:T(8,128)(2,1)S(1)} %get-tuple-element.343), channel_id=1, source_target_pairs={{24,0},{0,8},{8,16},{16,24},{25,1},{1,9},{9,17},{17,25},{26,2},{2,... | collective-permute-start | bytes 589832 | tf_op jit(solution)/shard_map/ppermute | solution.py:41
  545.2 16.7 %collective-permute-start.77 = (bf16[64,1536]{1,0:T(8,128)(2,1)S(1)}, bf16[64,1536]{1,0:T(8,128)(2,1)S(1)}, u32[]{:S(2)}, u32[]{:S(2)}) collective-permute-start(bf16[64,1536]{1,0:T(8,128)(2,1)S(1)} %get-tuple-element.344), channel_id=1, source_target_pairs={{16,0},{24,8},{0,16},{8,24},{17,1},{25,9},{1,17},{9,25},{18,2},{26... | collective-permute-start | bytes 589832 | tf_op jit(solution)/shard_map/ppermute | solution.py:41
  560.5 18.8 %collective-permute-start.86 = (f32[5,1024]{1,0:T(8,128)S(1)}, f32[5,1024]{1,0:T(8,128)S(1)}, u32[]{:S(2)}, u32[]{:S(2)}) collective-permute-start(f32[5,1024]{1,0:T(8,128)S(1)} %add.927), channel_id=1, source_target_pairs={{16,0},{24,8},{0,16},{8,24},{17,1},{25,9},{1,17},{9,25},{18,2},{26... | collective-permute-start | bytes 61448 | tf_op jit(solution)/shard_map/ppermute | solution.py:41
  561.8 39.7 %collective-permute-start.88 = (bf16[64,2560]{1,0:T(8,128)(2,1)}, bf16[64,2560]{1,0:T(8,128)(2,1)}, u32[]{:S(2)}, u32[]{:S(2)}) collective-permute-start(bf16[64,2560]{1,0:T(8,128)(2,1)} %get-tuple-element.319), channel_id=1, source_target_pairs={{24,0},{0,8},{8,16},{16,24},{25,1},{1,9},{9,17},{17,25},{26,2},{2,... | collective-permute-start | bytes 983048 | tf_op jit(solution)/shard_map/ppermute | solution.py:41
  561.9 39.5 %collective-permute-start.89 = (bf16[64,2560]{1,0:T(8,128)(2,1)}, bf16[64,2560]{1,0:T(8,128)(2,1)}, u32[]{:S(2)}, u32[]{:S(2)}) collective-permute-start(bf16[64,2560]{1,0:T(8,128)(2,1)} %get-tuple-element.318), channel_id=1, source_target_pairs={{16,0},{24,8},{0,16},{8,24},{17,1},{25,9},{1,17},{9,25},{18,2},{26... | collective-permute-start | bytes 983048 | tf_op jit(solution)/shard_map/ppermute | solution.py:41
  570.6 30.9 %collective-permute-start.90 = (bf16[64,2560]{1,0:T(8,128)(2,1)}, bf16[64,2560]{1,0:T(8,128)(2,1)}, u32[]{:S(2)}, u32[]{:S(2)}) collective-permute-start(bf16[64,2560]{1,0:T(8,128)(2,1)} %get-tuple-element.317), channel_id=1, source_target_pairs={{8,0},{16,8},{24,16},{0,24},{9,1},{17,9},{25,17},{1,25},{10,2},{18... | collective-permute-start | bytes 983048 | tf_op jit(solution)/shard_map/ppermute | solution.py:41
  572.0 15.5 %collective-permute-start.87 = (f32[5,1024]{1,0:T(8,128)S(1)}, f32[5,1024]{1,0:T(8,128)}, u32[]{:S(2)}, u32[]{:S(2)}) collective-permute-start(f32[5,1024]{1,0:T(8,128)S(1)} %add.927), channel_id=1, source_target_pairs={{24,0},{0,8},{8,16},{16,24},{25,1},{1,9},{9,17},{17,25},{26,2},{2,... | collective-permute-start | bytes 61448 | tf_op jit(solution)/shard_map/ppermute | solution.py:41
  579.3 17.0 %collective-permute-start.82 = (bf16[2,32,512]{2,1,0:T(8,128)(2,1)}, bf16[2,32,512]{2,1,0:T(8,128)(2,1)S(1)}, u32[]{:S(2)}, u32[]{:S(2)}) collective-permute-start(bf16[2,32,512]{2,1,0:T(8,128)(2,1)} %get-tuple-element.365), channel_id=1, source_target_pairs={{24,0},{0,8},{8,16},{16,24},{25,1},{1,9},{9,17},{17,25},{26,2},{2,... | collective-permute-start | bytes 196616 | tf_op jit(solution)/shard_map/ppermute | solution.py:41
  (169 other events, 1463.9 us)
Sparse Core Ops, SparseCore 0:
  14.6 159.2 all-gather.1

commit v10 on v9

--- a/solution.py
+++ b/solution.py
@@ -635,14 +635,12 @@
     gain_job = Job(sum_over(gain_grads, ("h", "m", "r", "z")))
     token = jnp.zeros((), WIDE)
     token = advance(token, embed_job, gain_job, head_job, in_job, out_job, first_out_job)
+    late_job = Job(reduce_deep([in_job.result, out_job.result], [None, None]))
     token = advance(token, first_in_job)
     token = advance(token, embed_job, gain_job, head_job, early_job, first_out_job)
     token = advance(token, first_in_job)
-    last_job = Job(reduce_deep([first_in_job.result], [None]))
-    held = [in_job.result, first_out_job.result, out_job.result]
-    token, held = lax.optimization_barrier((token, held))
-    late_job = Job(reduce_deep(held, [None, None, None]))
-    token = advance(token, embed_job, gain_job, early_job)
+    last_job = Job(reduce_deep([first_in_job.result, first_out_job.result], [None, None]))
+    token = advance(token, embed_job, gain_job, early_job, late_job)
     token = advance(token, last_job, embed_job, gain_job, late_job)
 
     owner = jnp.int32(0)
@@ -658,7 +656,7 @@
     norm_job = Job(sum_over(sums, ("h", "m", "r", "z")))
     while norm_job.flight is not None:
         token = advance(token, norm_job, *jobs)
-    (up_grad,), (next_in, first_out, next_out), (first_in,) = (job.finish() for job in jobs[:3])
+    (up_grad,), (next_in, next_out), (first_in, first_out) = (job.finish() for job in jobs[:3])
     square_sum, loss = jnp.sum(norm_job.result, axis=1)
     norm = jnp.sqrt(square_sum)
     factor = jnp.minimum(1.0, CLIP / (norm + 1e-06))

time: 672 us -> 662 us (0.985)
  waiting for transfers between devices: 179 us -> 162 us
  starting transfers between devices: 130 us -> 138 us
    ppermute x104, waiting for transfers between devices: 154 us -> 138 us  [shifted(): return lax.ppermute(part, axis, [((i + shift) % n, i) for i in range(n)])]
    ppermute x104, starting transfers between devices: 130 us -> 138 us  [shifted(): return lax.ppermute(part, axis, [((i + shift) % n, i) for i in range(n)])]
    unnamed x274 -> x264, local copies, waits for them, and re-layouts: 20.6 us -> 20.5 us
  transfers between devices with their start and end apart: 105 -> 105, of which waited for: 36 -> 33; matrix products, arithmetic and copies ran while one was open for 32% -> 33% of each run, Pallas kernels for 8% -> 8%
where the time goes in v10:
time: 662 us; the launch traced here: 653 us
  waiting for transfers between devices  162 us (24%)
  starting transfers between devices  138 us (21%)
  matrix products  135 us (20%)
  other arithmetic  73.2 us (11%)
  local copies, waits for them, and re-layouts  70.3 us (11%)
  Pallas kernels  54.6 us (8%)
  between operations  19.1 us (3%)
    ppermute x104, starting transfers between devices, shifted(): return lax.ppermute(part, axis, [((i + shift) % n, i) for i in range(n)])  138 us
    ppermute x104, waiting for transfers between devices, shifted(): return lax.ppermute(part, axis, [((i + shift) % n, i) for i in range(n)])  138 us
    pallas_call x4, Pallas kernels, attention(): pl.pallas_call(functools.partial(body, kind), out_shape=jax.ShapeDtypeStr...  54.6 us
    dot_general x10, matrix products, dot_nn(): return jnp.dot(left, right, preferred_element_type=WIDE)  48.3 us
    dot_general x9, matrix products, dot_nt(): lax.dot_general(left, right, (((1,), (1,)), ((), ())), preferred_element_...  46.5 us
    dot_general x16, matrix products, dot_tn(): lax.dot_general(left, right, (((0,), (0,)), ((), ())), preferred_element_...  40.5 us
    all_gather x1, waiting for transfers between devices, on_device(): gathered = lax.all_gather(gathered, ALL, axis=0, tiled=True)  24.7 us
    unnamed x264, local copies, waits for them, and re-layouts  20.5 us
  transfers between devices with their start and end apart: 105, of which 33 were waited for; matrix products, arithmetic and copies ran while one was open for 33% of the time, Pallas kernels for 8%

profile of v10, /device:TPU:0, one launch (start us, length us, event | category | flops | bytes accessed | tf_op | source)
XLA Modules:
  0.0 652.8 jit_solution(10340721772556003447)
XLA Ops:
  14.5 5.1 collective-permute-start.3
  29.9 3.9 collective-permute-start.25
  36.1 4.5 collective-permute-done.26
  42.4 4.0 collective-permute-done.27
  51.4 3.8 collective-permute-start.7
  55.4 23.9 %collective-permute-done.7 = bf16[128,512]{1,0:T(8,128)(2,1)S(1)} collective-permute-done((bf16[128,512]{1,0:T(8,128)(2,1)S(1)}, bf16[128,512]{1,0:T(8,128)(2,1)S(1)}, u32[]{:S(2)}, u32[]{:S(2)}) %collective-permute-start.7) | collective-permute-done | bytes 131104 | tf_op jit(solution)/shard_map/ppermute | solution.py:41
  84.2 4.6 collective-permute-done.10
  88.8 5.0 collective-permute-start.13
  95.9 20.0 %collective-permute-done.12 = bf16[4,128,512]{2,1,0:T(8,128)(2,1)S(1)} collective-permute-done((bf16[4,128,512]{2,1,0:T(8,128)(2,1)S(1)}, bf16[4,128,512]{2,1,0:T(8,128)(2,1)S(1)}, u32[]{:S(2)}, u32[]{:S(2)}) %collective-permute-start.12) | collective-permute-done | bytes 524320 | tf_op jit(solution)/shard_map/ppermute | solution.py:41
  117.5 15.4 %collective-permute-done.14 = bf16[4,64,1024]{2,1,0:T(8,128)(2,1)S(1)} collective-permute-done((bf16[4,64,1024]{2,1,0:T(8,128)(2,1)S(1)}, bf16[4,64,1024]{2,1,0:T(8,128)(2,1)S(1)}, u32[]{:S(2)}, u32[]{:S(2)}) %collective-permute-start.14) | collective-permute-done | bytes 524320 | tf_op jit(solution)/shard_map/ppermute | solution.py:41
  132.9 5.8 collective-permute-done.15
  138.9 2.5 collective-permute-start.16
  149.2 24.7 %all-gather.2.cloned.1.call-done = bf16[1024,8320]{1,0:T(8,128)(2,1)} async-done(((bf16[32,8320]{1,0:T(8,128)(2,1)}), bf16[1024,8320]{1,0:T(8,128)(2,1)}) %all-gather.2.cloned.1.call-update) | async-done | bytes 17039376 | tf_op jit(solution)/shard_map/all_gather | solution.py:506
  178.2 7.9 %fusion.8.packed_ref = bf16[512,3072]{1,0:T(8,128)(2,1)} fusion(bf16[512,1024]{1,0:T(8,128)(2,1)S(1)} %multiply_convert_fusion.5, bf16[1024,8320]{1,0:T(8,128)(2,1)} %all-gather.2.cloned.1.call-done), kind=kOutput, calls=%fused_computation.16 | convolution fusion | flops 3222798336 | bytes 10485760 | tf_op jit(solution)/shard_map/dot_general | solution.py:316
  186.1 9.3 %shard_map.365 = bf16[512,1024]{1,0:T(8,128)(2,1)} custom-call(s32[1]{0:T(128)} %bitcast.13.scalar_ref, bf16[512,3072]{1,0:T(8,128)(2,1)} %fusion.8.packed_ref), custom_call_target="tpu_custom_call" | custom-call | flops 8999999488 | bytes 8388608 | tf_op jit(solution)/shard_map/pallas_call | solution.py:412
  199.8 2.5 pad_maximum_fusion.1
  202.6 2.9 fusion.60
  214.2 2.5 pad_maximum_fusion
  217.6 8.3 %fusion.11 = bf16[512,3072]{1,0:T(8,128)(2,1)} fusion(bf16[512,1024]{1,0:T(8,128)(2,1)S(1)} %fusion.34, bf16[1024,8320]{1,0:T(8,128)(2,1)} %all-gather.2.cloned.1.call-done), kind=kOutput, calls=%fused_computation.17 | convolution fusion | flops 3222798336 | bytes 10485760 | tf_op jit(solution)/shard_map/dot_general | solution.py:316
  225.9 9.1 %shard_map.366 = bf16[4,128,1024]{2,1,0:T(8,128)(2,1)} custom-call(s32[1]{0:T(128)} %bitcast.30.scalar_ref, bf16[4,128,3072]{2,1,0:T(8,128)(2,1)} %bitcast.572), custom_call_target="tpu_custom_call" | custom-call | flops 8999999488 | bytes 8388608 | tf_op jit(solution)/shard_map/pallas_call | solution.py:412
  235.0 3.3 multiply_reduce_fusion.8
  240.6 4.9 fusion.192
  245.6 6.4 fusion.165
  252.0 4.6 fusion.193
  256.6 6.6 %multiply_reduce_fusion.7 = (f32[512]{0:T(512)S(1)}, f32[512,1024]{1,0:T(8,128)S(1)}) fusion(bf16[2048,1024]{1,0:T(8,128)(2,1)} %collective-permute-done.23, f32[512,2048]{1,0:T(8,128)S(1)} %fusion.193, f32[512,1024]{1,0:T(8,128)S(1)} %get-tuple-element.376, f32[512,1024]{1,0:T(8,128)S(1)} %fusion.165), kind=kOutput, calls=%fused_computation.91 | convolution fusion | flops 2159017472 | bytes 14682112 | tf_op jit(solution)/shard_map/dot_general | solution.py:316
  271.1 4.9 convolution_convert_fusion.3
  282.2 6.3 fusion.164
  288.5 7.1 %fusion.20 = bf16[512,2048]{1,0:T(8,128)(2,1)S(1)} fusion(f32[512,2048]{1,0:T(8,128)S(1)} %copy-done.118, bf16[512,1024]{1,0:T(8,128)(2,1)S(1)} %copy-done.41, bf16[2048,1024]{1,0:T(8,128)(2,1)} %bitcast.40), kind=kOutput, calls=%fused_computation.24 | convolution fusion | flops 2168455168 | bytes 11534336 | tf_op jit(solution)/shard_map/dot_general | solution.py:308
  295.6 8.0 %fusion.27 = bf16[512,2048]{1,0:T(8,128)(2,1)S(1)} fusion(f32[512,2048]{1,0:T(8,128)S(1)} %copy-done.121, bf16[512,1024]{1,0:T(8,128)(2,1)S(1)} %copy-done.41, bf16[2048,1024]{1,0:T(8,128)(2,1)} %collective-permute-done.23), kind=kOutput, calls=%fused_computation.31 | convolution fusion | flops 2168455168 | bytes 11534336 | tf_op jit(solution)/shard_map/dot_general | solution.py:308
  303.7 4.4 convolution_convert_fusion.2
  311.7 6.3 add_convert_fusion
  323.6 4.6 fusion.194
  328.2 5.1 multiply_reduce_fusion.2
  333.2 2.6 fusion.178
  335.8 4.4 fusion.69
  342.0 17.8 %shard_map.367 = bf16[4,128,3072]{2,1,0:T(8,128)(2,1)} custom-call(s32[1]{0:T(128)} %bitcast.30.scalar_ref, bf16[4,128,3072]{2,1,0:T(8,128)(2,1)} %bitcast.573, bf16[4,128,1024]{2,1,0:T(8,128)(2,1)} %bitcast.580), custom_call_target="tpu_custom_call" | custom-call | flops 22000001024 | bytes 8388608 | tf_op jit(solution)/shard_map/pallas_call | solution.py:412
  362.3 5.2 add_convert_fusion.1
  374.0 5.9 fusion.40
  398.3 2.9 collective-permute-done.41
  401.3 3.5 collective-permute-start.44
  412.0 3.9 fusion.66.up_ref
  416.5 3.5 collective-permute-done.50
  425.2 2.3 collective-permute-start.49
  430.4 18.4 %shard_map.368 = bf16[512,3072]{1,0:T(8,128)(2,1)} custom-call(s32[1]{0:T(128)} %bitcast.13.scalar_ref, bf16[512,3072]{1,0:T(8,128)(2,1)} %fusion.8.packed_ref, bf16[512,1024]{1,0:T(8,128)(2,1)} %fusion.66.up_ref), custom_call_target="tpu_custom_call" | custom-call | flops 22000001024 | bytes 8388608 | tf_op jit(solution)/shard_map/pallas_call | solution.py:412
  449.6 3.6 convolution_convert_fusion
  464.5 6.2 fusion.4
  493.9 10.6 %collective-permute-done.78 = bf16[4,2,64,768]{3,2,0,1:T(8,128)(2,1)} collective-permute-done((bf16[4,2,64,768]{3,2,0,1:T(8,128)(2,1)}, bf16[4,2,64,768]{3,2,0,1:T(8,128)(2,1)}, u32[]{:S(2)}, u32[]{:S(2)}) %collective-permute-start.78) | collective-permute-done | bytes 786464 | tf_op jit(solution)/shard_map/ppermute | solution.py:41
  510.3 9.2 %collective-permute-done.65 = bf16[4,2,64,512]{3,2,1,0:T(8,128)(2,1)S(1)} collective-permute-done((bf16[4,2,64,512]{3,2,1,0:T(8,128)(2,1)}, bf16[4,2,64,512]{3,2,1,0:T(8,128)(2,1)S(1)}, u32[]{:S(2)}, u32[]{:S(2)}) %collective-permute-start.65) | collective-permute-done | bytes 524320 | tf_op jit(solution)/shard_map/ppermute | solution.py:41
  531.9 4.0 collective-permute-start.70
  539.4 4.9 collective-permute-done.70
  544.3 6.7 %collective-permute-start.76 = (bf16[64,2048]{1,0:T(8,128)(2,1)S(1)}, bf16[64,2048]{1,0:T(8,128)(2,1)}, u32[]{:S(2)}, u32[]{:S(2)}) collective-permute-start(bf16[64,2048]{1,0:T(8,128)(2,1)S(1)} %get-tuple-element.315), channel_id=1, source_target_pairs={{16,0},{24,8},{0,16},{8,24},{17,1},{25,9},{1,17},{9,25},{18,2},{26... | collective-permute-start | bytes 786440 | tf_op jit(solution)/shard_map/ppermute | solution.py:41
  551.0 3.4 collective-permute-start.77
  561.0 4.0 collective-permute-start.82
  565.0 3.5 collective-permute-start.83
  575.5 9.5 %collective-permute-start.89 = (f32[5,1024]{1,0:T(8,128)S(1)}, f32[5,1024]{1,0:T(8,128)S(1)}, u32[]{:S(2)}, u32[]{:S(2)}) collective-permute-start(f32[5,1024]{1,0:T(8,128)S(1)} %add.927), channel_id=1, source_target_pairs={{16,0},{24,8},{0,16},{8,24},{17,1},{25,9},{1,17},{9,25},{18,2},{26... | collective-permute-start | bytes 61448 | tf_op jit(solution)/shard_map/ppermute | solution.py:41
  586.8 2.9 collective-permute-start.85
  590.4 2.9 collective-permute-start.87
  593.3 2.3 collective-permute-done.86
  595.6 3.8 collective-permute-start.94
  609.1 5.3 collective-permute-done.98
  618.3 3.2 collective-permute-start.101
  622.8 3.2 collective-permute-done.102
  632.0 2.6 multiply_subtract_fusion.4
  640.8 3.5 multiply_subtract_fusion
  (693 shorter events, 230.0 us)
Async XLA Ops:
  7.2 166.7 %all-gather.2.cloned.1.call-start = ((), (), s32[]{:S(2)}) async-start(), calls=%async_computation | async-start | bytes 17571840 | tf_op jit(solution)/shard_map/all_gather | solution.py:506
  14.5 32.7 %collective-permute-start.3 = (bf16[128,1024]{1,0:T(8,128)(2,1)S(1)}, bf16[128,1024]{1,0:T(8,128)(2,1)}, u32[]{:S(2)}, u32[]{:S(2)}) collective-permute-start(bf16[128,1024]{1,0:T(8,128)(2,1)S(1)} %convert_element_type.557), channel_id=1, source_target_pairs={{8,0},{16,8},{24,16},{0,24},{9,1},{17,9},{25,17},{1,25},{10,2},{18... | collective-permute-start | bytes 786440 | tf_op jit(solution)/shard_map/ppermute | solution.py:41
  19.7 27.5 %collective-permute-start.4 = (bf16[128,1024]{1,0:T(8,128)(2,1)S(1)}, bf16[128,1024]{1,0:T(8,128)(2,1)S(1)}, u32[]{:S(2)}, u32[]{:S(2)}) collective-permute-start(bf16[128,1024]{1,0:T(8,128)(2,1)S(1)} %convert_element_type.557), channel_id=1, source_target_pairs={{24,0},{0,8},{8,16},{16,24},{25,1},{1,9},{9,17},{17,25},{26,2},{2,... | collective-permute-start | bytes 786440 | tf_op jit(solution)/shard_map/ppermute | solution.py:41
  21.5 25.7 %collective-permute-start.2 = (bf16[32,2048]{1,0:T(8,128)(2,1)S(1)}, bf16[32,2048]{1,0:T(8,128)(2,1)S(1)}, u32[]{:S(2)}, u32[]{:S(2)}) collective-permute-start(bf16[32,2048]{1,0:T(8,128)(2,1)S(1)} %bitcast.558), channel_id=1, source_target_pairs={{1,0},{0,1},{3,2},{2,3},{5,4},{4,5},{7,6},{6,7},{9,8},{8,9},{11,10... | collective-permute-start | bytes 393224 | tf_op jit(solution)/shard_map/ppermute | solution.py:41
  22.6 56.7 %collective-permute-start.1 = (bf16[256,1024]{1,0:T(8,128)(2,1)S(1)}, bf16[256,1024]{1,0:T(8,128)(2,1)S(1)}, u32[]{:S(2)}, u32[]{:S(2)}) collective-permute-start(bf16[256,1024]{1,0:T(8,128)(2,1)S(1)} %get-tuple-element.332), channel_id=1, source_target_pairs={{2,0},{0,2},{3,1},{1,3},{6,4},{4,6},{7,5},{5,7},{10,8},{8,10},{11,... | collective-permute-start | bytes 1572872 | tf_op jit(solution)/shard_map/ppermute | solution.py:41
  47.3 32.1 %collective-permute-start.5 = (bf16[64,2048]{1,0:T(8,128)(2,1)S(1)}, bf16[64,2048]{1,0:T(8,128)(2,1)S(1)}, u32[]{:S(2)}, u32[]{:S(2)}) collective-permute-start(bf16[64,2048]{1,0:T(8,128)(2,1)S(1)} %bitcast.539), channel_id=1, source_target_pairs={{8,0},{16,8},{24,16},{0,24},{9,1},{17,9},{25,17},{1,25},{10,2},{18... | collective-permute-start | bytes 786440 | tf_op jit(solution)/shard_map/ppermute | solution.py:41
  49.3 30.0 %collective-permute-start.6 = (bf16[64,2048]{1,0:T(8,128)(2,1)S(1)}, bf16[64,2048]{1,0:T(8,128)(2,1)S(1)}, u32[]{:S(2)}, u32[]{:S(2)}) collective-permute-start(bf16[64,2048]{1,0:T(8,128)(2,1)S(1)} %bitcast.540), channel_id=1, source_target_pairs={{24,0},{0,8},{8,16},{16,24},{25,1},{1,9},{9,17},{17,25},{26,2},{2,... | collective-permute-start | bytes 786440 | tf_op jit(solution)/shard_map/ppermute | solution.py:41
  51.4 27.9 %collective-permute-start.7 = (bf16[128,512]{1,0:T(8,128)(2,1)S(1)}, bf16[128,512]{1,0:T(8,128)(2,1)S(1)}, u32[]{:S(2)}, u32[]{:S(2)}) collective-permute-start(bf16[128,512]{1,0:T(8,128)(2,1)S(1)} %slice.110), channel_id=1, source_target_pairs={{8,0},{16,8},{24,16},{0,24},{9,1},{17,9},{25,17},{1,25},{10,2},{18... | collective-permute-start | bytes 393224 | tf_op jit(solution)/shard_map/ppermute | solution.py:41
  55.3 24.0 %collective-permute-start.8 = (bf16[128,512]{1,0:T(8,128)(2,1)S(1)}, bf16[128,512]{1,0:T(8,128)(2,1)S(1)}, u32[]{:S(2)}, u32[]{:S(2)}) collective-permute-start(bf16[128,512]{1,0:T(8,128)(2,1)S(1)} %slice.111), channel_id=1, source_target_pairs={{24,0},{0,8},{8,16},{16,24},{25,1},{1,9},{9,17},{17,25},{26,2},{2,... | collective-permute-start | bytes 393224 | tf_op jit(solution)/shard_map/ppermute | solution.py:41
  79.3 69.9 %collective-permute-start = (bf16[256,1024]{1,0:T(8,128)(2,1)}, bf16[256,1024]{1,0:T(8,128)(2,1)}, u32[]{:S(2)}, u32[]{:S(2)}) collective-permute-start(bf16[256,1024]{1,0:T(8,128)(2,1)} %get-tuple-element.331), channel_id=1, source_target_pairs={{2,0},{0,2},{3,1},{1,3},{6,4},{4,6},{7,5},{5,7},{10,8},{8,10},{11,... | collective-permute-start | bytes 1572872 | tf_op jit(solution)/shard_map/ppermute | solution.py:41
  79.5 14.2 %collective-permute-start.9 = (bf16[2,256,1024]{2,1,0:T(8,128)(2,1)S(1)}, bf16[2,256,1024]{2,1,0:T(8,128)(2,1)S(1)}, u32[]{:S(2)}, u32[]{:S(2)}) collective-permute-start(bf16[2,256,1024]{2,1,0:T(8,128)(2,1)S(1)} %bitcast_dynamic-update-slice_fusion.11), channel_id=1, source_target_pairs={{1,0},{0,1},{3,2},{2,3},{5,4},{4,5},{7,6},{6,7},{9,8},{8,9},{11,10... | collective-permute-start | bytes 3145736 | tf_op jit(solution)/shard_map/ppermute | solution.py:41
  79.8 36.2 %collective-permute-start.12 = (bf16[4,128,512]{2,1,0:T(8,128)(2,1)S(1)}, bf16[4,128,512]{2,1,0:T(8,128)(2,1)S(1)}, u32[]{:S(2)}, u32[]{:S(2)}) collective-permute-start(bf16[4,128,512]{2,1,0:T(8,128)(2,1)S(1)} %get-tuple-element.330), channel_id=1, source_target_pairs={{2,0},{0,2},{3,1},{1,3},{6,4},{4,6},{7,5},{5,7},{10,8},{8,10},{11,... | collective-permute-start | bytes 1572872 | tf_op jit(solution)/shard_map/ppermute | solution.py:41
  88.8 28.8 %collective-permute-start.13 = (bf16[4,128,512]{2,1,0:T(8,128)(2,1)S(1)}, bf16[4,128,512]{2,1,0:T(8,128)(2,1)S(1)}, u32[]{:S(2)}, u32[]{:S(2)}) collective-permute-start(bf16[4,128,512]{2,1,0:T(8,128)(2,1)S(1)} %get-tuple-element.329), channel_id=1, source_target_pairs={{4,0},{0,4},{5,1},{1,5},{6,2},{2,6},{7,3},{3,7},{12,8},{8,12},{13,... | collective-permute-start | bytes 1572872 | tf_op jit(solution)/shard_map/ppermute | solution.py:41
  93.9 39.1 %collective-permute-start.14 = (bf16[4,64,1024]{2,1,0:T(8,128)(2,1)S(1)}, bf16[4,64,1024]{2,1,0:T(8,128)(2,1)S(1)}, u32[]{:S(2)}, u32[]{:S(2)}) collective-permute-start(bf16[4,64,1024]{2,1,0:T(8,128)(2,1)S(1)} %get-tuple-element.328), channel_id=1, source_target_pairs={{2,0},{0,2},{3,1},{1,3},{6,4},{4,6},{7,5},{5,7},{10,8},{8,10},{11,... | collective-permute-start | bytes 1572872 | tf_op jit(solution)/shard_map/ppermute | solution.py:41
  94.2 44.5 %collective-permute-start.15 = (bf16[4,64,1024]{2,1,0:T(8,128)(2,1)S(1)}, bf16[4,64,1024]{2,1,0:T(8,128)(2,1)S(1)}, u32[]{:S(2)}, u32[]{:S(2)}) collective-permute-start(bf16[4,64,1024]{2,1,0:T(8,128)(2,1)S(1)} %get-tuple-element.327), channel_id=1, source_target_pairs={{4,0},{0,4},{5,1},{1,5},{6,2},{2,6},{7,3},{3,7},{12,8},{8,12},{13,... | collective-permute-start | bytes 1572872 | tf_op jit(solution)/shard_map/ppermute | solution.py:41
  138.9 56.5 %collective-permute-start.16 = (bf16[4,2,128,512]{3,2,1,0:T(8,128)(2,1)S(1)}, bf16[4,2,128,512]{3,2,1,0:T(8,128)(2,1)}, u32[]{:S(2)}, u32[]{:S(2)}) collective-permute-start(bf16[4,2,128,512]{3,2,1,0:T(8,128)(2,1)S(1)} %bitcast_dynamic-update-slice_fusion.7), channel_id=1, source_target_pairs={{4,0},{0,4},{5,1},{1,5},{6,2},{2,6},{7,3},{3,7},{12,8},{8,12},{13,... | collective-permute-start | bytes 3145736 | tf_op jit(solution)/shard_map/ppermute | solution.py:41
  143.3 52.1 %collective-permute-start.17 = (bf16[4,2,128,512]{3,2,1,0:T(8,128)(2,1)}, bf16[4,2,128,512]{3,2,1,0:T(8,128)(2,1)}, u32[]{:S(2)}, u32[]{:S(2)}) collective-permute-start(bf16[4,2,128,512]{3,2,1,0:T(8,128)(2,1)} %bitcast_dynamic-update-slice_fusion.10), channel_id=1, source_target_pairs={{2,0},{0,2},{3,1},{1,3},{6,4},{4,6},{7,5},{5,7},{10,8},{8,10},{11,... | collective-permute-start | bytes 3145736 | tf_op jit(solution)/shard_map/ppermute | solution.py:41
  145.3 50.1 %collective-permute-start.18 = (bf16[4,2,64,1024]{3,2,1,0:T(8,128)(2,1)}, bf16[4,2,64,1024]{3,2,1,0:T(8,128)(2,1)}, u32[]{:S(2)}, u32[]{:S(2)}) collective-permute-start(bf16[4,2,64,1024]{3,2,1,0:T(8,128)(2,1)} %bitcast_dynamic-update-slice_fusion.6), channel_id=1, source_target_pairs={{4,0},{0,4},{5,1},{1,5},{6,2},{2,6},{7,3},{3,7},{12,8},{8,12},{13,... | collective-permute-start | bytes 3145736 | tf_op jit(solution)/shard_map/ppermute | solution.py:41
  147.2 48.2 %collective-permute-start.19 = (bf16[4,2,64,1024]{3,2,1,0:T(8,128)(2,1)}, bf16[4,2,64,1024]{3,2,1,0:T(8,128)(2,1)}, u32[]{:S(2)}, u32[]{:S(2)}) collective-permute-start(bf16[4,2,64,1024]{3,2,1,0:T(8,128)(2,1)} %bitcast_dynamic-update-slice_fusion.9), channel_id=1, source_target_pairs={{2,0},{0,2},{3,1},{1,3},{6,4},{4,6},{7,5},{5,7},{10,8},{8,10},{11,... | collective-permute-start | bytes 3145736 | tf_op jit(solution)/shard_map/ppermute | solution.py:41
  202.3 54.3 %collective-permute-start.23 = (bf16[2048,1024]{1,0:T(8,128)(2,1)}, bf16[2048,1024]{1,0:T(8,128)(2,1)}, u32[]{:S(2)}, u32[]{:S(2)}) collective-permute-start(bf16[2048,1024]{1,0:T(8,128)(2,1)} %bitcast.40), channel_id=1, source_target_pairs={{1,0},{0,1},{3,2},{2,3},{5,4},{4,5},{7,6},{6,7},{9,8},{8,9},{11,10... | collective-permute-start | bytes 12582920 | tf_op jit(solution)/shard_map/ppermute | solution.py:41
  216.7 35.3 %collective-permute-start.22 = (bf16[1024,2048]{1,0:T(8,128)(2,1)}, bf16[1024,2048]{1,0:T(8,128)(2,1)}, u32[]{:S(2)}, u32[]{:S(2)}) collective-permute-start(bf16[1024,2048]{1,0:T(8,128)(2,1)} %bitcast.37), channel_id=1, source_target_pairs={{1,0},{0,1},{3,2},{2,3},{5,4},{4,5},{7,6},{6,7},{9,8},{8,9},{11,10... | collective-permute-start | bytes 12582920 | tf_op jit(solution)/shard_map/ppermute | solution.py:41
  276.0 27.6 %collective-permute-start.29 = (bf16[2048,1024]{1,0:T(8,128)(2,1)}, bf16[2048,1024]{1,0:T(8,128)(2,1)}, u32[]{:S(2)}, u32[]{:S(2)}) collective-permute-start(bf16[2048,1024]{1,0:T(8,128)(2,1)} %convolution_convert_fusion.3), channel_id=1, source_target_pairs={{1,0},{0,1},{3,2},{2,3},{5,4},{4,5},{7,6},{6,7},{9,8},{8,9},{11,10... | collective-permute-start | bytes 12582920 | tf_op jit(solution)/shard_map/ppermute | solution.py:41
  278.2 25.5 %collective-permute-start.28 = (bf16[1024,512]{1,0:T(8,128)(2,1)S(1)}, bf16[1024,512]{1,0:T(8,128)(2,1)S(1)}, u32[]{:S(2)}, u32[]{:S(2)}) collective-permute-start(bf16[1024,512]{1,0:T(8,128)(2,1)S(1)} %convolution_convert_fusion.6), channel_id=1, source_target_pairs={{1,0},{0,1},{3,2},{2,3},{5,4},{4,5},{7,6},{6,7},{9,8},{8,9},{11,10... | collective-permute-start | bytes 3145736 | tf_op jit(solution)/shard_map/ppermute | solution.py:41
  308.1 27.7 %collective-permute-start.31 = (bf16[1024,2048]{1,0:T(8,128)(2,1)}, bf16[1024,2048]{1,0:T(8,128)(2,1)}, u32[]{:S(2)}, u32[]{:S(2)}) collective-permute-start(bf16[1024,2048]{1,0:T(8,128)(2,1)} %convolution_convert_fusion.2), channel_id=1, source_target_pairs={{1,0},{0,1},{3,2},{2,3},{5,4},{4,5},{7,6},{6,7},{9,8},{8,9},{11,10... | collective-permute-start | bytes 12582920 | tf_op jit(solution)/shard_map/ppermute | solution.py:41
  309.7 26.1 %collective-permute-start.30 = (bf16[2,2,4,32,512]{4,3,0,2,1:T(8,128)(2,1)S(1)}, bf16[2,2,4,32,512]{4,3,0,2,1:T(8,128)(2,1)S(1)}, u32[]{:S(2)}, u32[]{:S(2)}) collective-permute-start(bf16[2,2,4,32,512]{4,3,0,2,1:T(8,128)(2,1)S(1)} %bitcast.555), channel_id=1, source_target_pairs={{2,0},{0,2},{3,1},{1,3},{6,4},{4,6},{7,5},{5,7},{10,8},{8,10},{11,... | collective-permute-start | bytes 1572872 | tf_op jit(solution)/shard_map/ppermute | solution.py:41
  319.7 50.0 %collective-permute-start.33 = (bf16[4,2,128,512]{3,2,0,1:T(8,128)(2,1)}, bf16[4,2,128,512]{3,2,0,1:T(8,128)(2,1)}, u32[]{:S(2)}, u32[]{:S(2)}) collective-permute-start(bf16[4,2,128,512]{3,2,0,1:T(8,128)(2,1)} %bitcast.513), channel_id=1, source_target_pairs={{2,0},{0,2},{3,1},{1,3},{6,4},{4,6},{7,5},{5,7},{10,8},{8,10},{11,... | collective-permute-start | bytes 3145736 | tf_op jit(solution)/shard_map/ppermute | solution.py:41
  322.0 47.7 %collective-permute-start.34 = (bf16[4,2,128,512]{3,2,0,1:T(8,128)(2,1)}, bf16[4,2,128,512]{3,2,0,1:T(8,128)(2,1)}, u32[]{:S(2)}, u32[]{:S(2)}) collective-permute-start(bf16[4,2,128,512]{3,2,0,1:T(8,128)(2,1)} %bitcast.512), channel_id=1, source_target_pairs={{4,0},{0,4},{5,1},{1,5},{6,2},{2,6},{7,3},{3,7},{12,8},{8,12},{13,... | collective-permute-start | bytes 3145736 | tf_op jit(solution)/shard_map/ppermute | solution.py:41
  373.4 27.8 %collective-permute-start.42 = (bf16[1024,1536]{1,0:T(8,128)(2,1)S(1)}, bf16[1024,1536]{1,0:T(8,128)(2,1)S(1)}, u32[]{:S(2)}, u32[]{:S(2)}) collective-permute-start(bf16[1024,1536]{1,0:T(8,128)(2,1)S(1)} %convolution_convert_fusion.1), channel_id=1, source_target_pairs={{1,0},{0,1},{3,2},{2,3},{5,4},{4,5},{7,6},{6,7},{9,8},{8,9},{11,10... | collective-permute-start | bytes 9437192 | tf_op jit(solution)/shard_map/ppermute | solution.py:41
  383.4 14.9 %collective-permute-start.40 = (bf16[4,128,512]{2,1,0:T(8,128)(2,1)S(1)}, bf16[4,128,512]{2,1,0:T(8,128)(2,1)S(1)}, u32[]{:S(2)}, u32[]{:S(2)}) collective-permute-start(bf16[4,128,512]{2,1,0:T(8,128)(2,1)S(1)} %dynamic-slice_bitcast_fusion.8), channel_id=1, source_target_pairs={{4,0},{0,4},{5,1},{1,5},{6,2},{2,6},{7,3},{3,7},{12,8},{8,12},{13,... | collective-permute-start | bytes 1572872 | tf_op jit(solution)/shard_map/ppermute | solution.py:41
  386.3 14.9 %collective-permute-start.41 = (bf16[4,128,512]{2,1,0:T(8,128)(2,1)S(1)}, bf16[4,128,512]{2,1,0:T(8,128)(2,1)S(1)}, u32[]{:S(2)}, u32[]{:S(2)}) collective-permute-start(bf16[4,128,512]{2,1,0:T(8,128)(2,1)S(1)} %dynamic-slice_bitcast_fusion.7), channel_id=1, source_target_pairs={{2,0},{0,2},{3,1},{1,3},{6,4},{4,6},{7,5},{5,7},{10,8},{8,10},{11,... | collective-permute-start | bytes 1572872 | tf_op jit(solution)/shard_map/ppermute | solution.py:41
  395.0 25.1 %collective-permute-start.50 = (bf16[4,2,64,1024]{3,2,0,1:T(8,128)(2,1)S(1)}, bf16[4,2,64,1024]{3,2,0,1:T(8,128)(2,1)}, u32[]{:S(2)}, u32[]{:S(2)}) collective-permute-start(bf16[4,2,64,1024]{3,2,0,1:T(8,128)(2,1)S(1)} %bitcast.542), channel_id=1, source_target_pairs={{4,0},{0,4},{5,1},{1,5},{6,2},{2,6},{7,3},{3,7},{12,8},{8,12},{13,... | collective-permute-start | bytes 3145736 | tf_op jit(solution)/shard_map/ppermute | solution.py:41
  396.1 26.4 %collective-permute-start.51 = (bf16[4,2,64,1024]{3,2,1,0:T(8,128)(2,1)S(1)}, bf16[4,2,64,1024]{3,2,1,0:T(8,128)(2,1)S(1)}, u32[]{:S(2)}, u32[]{:S(2)}) collective-permute-start(bf16[4,2,64,1024]{3,2,1,0:T(8,128)(2,1)S(1)} %dynamic-slice_bitcast_fusion), channel_id=1, source_target_pairs={{2,0},{0,2},{3,1},{1,3},{6,4},{4,6},{7,5},{5,7},{10,8},{8,10},{11,... | collective-permute-start | bytes 3145736 | tf_op jit(solution)/shard_map/ppermute | solution.py:41
  401.3 24.0 %collective-permute-start.44 = (bf16[2,32,512]{2,1,0:T(8,128)(2,1)S(1)}, bf16[2,32,512]{2,1,0:T(8,128)(2,1)S(1)}, u32[]{:S(2)}, u32[]{:S(2)}) collective-permute-start(bf16[2,32,512]{2,1,0:T(8,128)(2,1)S(1)} %get-tuple-element.356), channel_id=1, source_target_pairs={{8,0},{16,8},{24,16},{0,24},{9,1},{17,9},{25,17},{1,25},{10,2},{18... | collective-permute-start | bytes 196616 | tf_op jit(solution)/shard_map/ppermute | solution.py:41
  404.7 22.8 %collective-permute-start.45 = (bf16[2,32,512]{2,1,0:T(8,128)(2,1)S(1)}, bf16[2,32,512]{2,1,0:T(8,128)(2,1)S(1)}, u32[]{:S(2)}, u32[]{:S(2)}) collective-permute-start(bf16[2,32,512]{2,1,0:T(8,128)(2,1)S(1)} %get-tuple-element.356), channel_id=1, source_target_pairs={{16,0},{24,8},{0,16},{8,24},{17,1},{25,9},{1,17},{9,25},{18,2},{26... | collective-permute-start | bytes 196616 | tf_op jit(solution)/shard_map/ppermute | solution.py:41
  420.0 28.8 %collective-permute-start.47 = (bf16[128,1024]{1,0:T(8,128)(2,1)}, bf16[128,1024]{1,0:T(8,128)(2,1)S(1)}, u32[]{:S(2)}, u32[]{:S(2)}) collective-permute-start(bf16[128,1024]{1,0:T(8,128)(2,1)} %get-tuple-element.323), channel_id=1, source_target_pairs={{24,0},{0,8},{8,16},{16,24},{25,1},{1,9},{9,17},{17,25},{26,2},{2,... | collective-permute-start | bytes 786440 | tf_op jit(solution)/shard_map/ppermute | solution.py:41
  423.5 26.1 %collective-permute-start.48 = (bf16[128,1024]{1,0:T(8,128)(2,1)}, bf16[128,1024]{1,0:T(8,128)(2,1)}, u32[]{:S(2)}, u32[]{:S(2)}) collective-permute-start(bf16[128,1024]{1,0:T(8,128)(2,1)} %get-tuple-element.324), channel_id=1, source_target_pairs={{16,0},{24,8},{0,16},{8,24},{17,1},{25,9},{1,17},{9,25},{18,2},{26... | collective-permute-start | bytes 786440 | tf_op jit(solution)/shard_map/ppermute | solution.py:41
  425.2 24.4 %collective-permute-start.49 = (bf16[128,1024]{1,0:T(8,128)(2,1)}, bf16[128,1024]{1,0:T(8,128)(2,1)}, u32[]{:S(2)}, u32[]{:S(2)}) collective-permute-start(bf16[128,1024]{1,0:T(8,128)(2,1)} %get-tuple-element.322), channel_id=1, source_target_pairs={{8,0},{16,8},{24,16},{0,24},{9,1},{17,9},{25,17},{1,25},{10,2},{18... | collective-permute-start | bytes 786440 | tf_op jit(solution)/shard_map/ppermute | solution.py:41
  427.5 22.1 %collective-permute-start.52 = (bf16[4,2,64,768]{3,2,0,1:T(8,128)(2,1)}, bf16[4,2,64,768]{3,2,0,1:T(8,128)(2,1)}, u32[]{:S(2)}, u32[]{:S(2)}) collective-permute-start(bf16[4,2,64,768]{3,2,0,1:T(8,128)(2,1)} %bitcast.515), channel_id=1, source_target_pairs={{2,0},{0,2},{3,1},{1,3},{6,4},{4,6},{7,5},{5,7},{10,8},{8,10},{11,... | collective-permute-start | bytes 2359304 | tf_op jit(solution)/shard_map/ppermute | solution.py:41
  429.5 20.2 %collective-permute-start.53 = (bf16[4,2,64,768]{3,2,1,0:T(8,128)(2,1)}, bf16[4,2,64,768]{3,2,1,0:T(8,128)(2,1)}, u32[]{:S(2)}, u32[]{:S(2)}) collective-permute-start(bf16[4,2,64,768]{3,2,1,0:T(8,128)(2,1)} %dynamic-slice_bitcast_fusion.2), channel_id=1, source_target_pairs={{4,0},{0,4},{5,1},{1,5},{6,2},{2,6},{7,3},{3,7},{12,8},{8,12},{13,... | collective-permute-start | bytes 2359304 | tf_op jit(solution)/shard_map/ppermute | solution.py:41
  448.8 26.5 %collective-permute-start.58 = (bf16[4,2,64,512]{3,2,1,0:T(8,128)(2,1)}, bf16[4,2,64,512]{3,2,1,0:T(8,128)(2,1)S(1)}, u32[]{:S(2)}, u32[]{:S(2)}) collective-permute-start(bf16[4,2,64,512]{3,2,1,0:T(8,128)(2,1)} %dynamic-slice_bitcast_fusion.4), channel_id=1, source_target_pairs={{2,0},{0,2},{3,1},{1,3},{6,4},{4,6},{7,5},{5,7},{10,8},{8,10},{11,... | collective-permute-start | bytes 1572872 | tf_op jit(solution)/shard_map/ppermute | solution.py:41
  453.2 23.9 %collective-permute-start.54 = (bf16[1024,1536]{1,0:T(8,128)(2,1)S(1)}, bf16[1024,1536]{1,0:T(8,128)(2,1)S(1)}, u32[]{:S(2)}, u32[]{:S(2)}) collective-permute-start(bf16[1024,1536]{1,0:T(8,128)(2,1)S(1)} %convolution_convert_fusion), channel_id=1, source_target_pairs={{1,0},{0,1},{3,2},{2,3},{5,4},{4,5},{7,6},{6,7},{9,8},{8,9},{11,10... | collective-permute-start | bytes 9437192 | tf_op jit(solution)/shard_map/ppermute | solution.py:41
  453.4 22.9 %collective-permute-start.55 = (bf16[2,4,32,512]{3,2,1,0:T(8,128)(2,1)S(1)}, bf16[2,4,32,512]{3,2,1,0:T(8,128)(2,1)S(1)}, u32[]{:S(2)}, u32[]{:S(2)}) collective-permute-start(bf16[2,4,32,512]{3,2,1,0:T(8,128)(2,1)S(1)} %bitcast_dynamic-update-slice_fusion.28), channel_id=1, source_target_pairs={{4,0},{0,4},{5,1},{1,5},{6,2},{2,6},{7,3},{3,7},{12,8},{8,12},{13,... | collective-permute-start | bytes 786440 | tf_op jit(solution)/shard_map/ppermute | solution.py:41
  456.4 20.7 %collective-permute-start.56 = (bf16[4,64,1024]{2,1,0:T(8,128)(2,1)S(1)}, bf16[4,64,1024]{2,1,0:T(8,128)(2,1)S(1)}, u32[]{:S(2)}, u32[]{:S(2)}) collective-permute-start(bf16[4,64,1024]{2,1,0:T(8,128)(2,1)S(1)} %dynamic-slice_bitcast_fusion.6), channel_id=1, source_target_pairs={{2,0},{0,2},{3,1},{1,3},{6,4},{4,6},{7,5},{5,7},{10,8},{8,10},{11,... | collective-permute-start | bytes 1572872 | tf_op jit(solution)/shard_map/ppermute | solution.py:41
  458.2 18.8 %collective-permute-start.57 = (bf16[4,64,1024]{2,1,0:T(8,128)(2,1)S(1)}, bf16[4,64,1024]{2,1,0:T(8,128)(2,1)S(1)}, u32[]{:S(2)}, u32[]{:S(2)}) collective-permute-start(bf16[4,64,1024]{2,1,0:T(8,128)(2,1)S(1)} %dynamic-slice_bitcast_fusion.5), channel_id=1, source_target_pairs={{4,0},{0,4},{5,1},{1,5},{6,2},{2,6},{7,3},{3,7},{12,8},{8,12},{13,... | collective-permute-start | bytes 1572872 | tf_op jit(solution)/shard_map/ppermute | solution.py:41
  475.3 32.2 %collective-permute-start.62 = (bf16[4,64,768]{2,1,0:T(8,128)(2,1)}, bf16[4,64,768]{2,1,0:T(8,128)(2,1)}, u32[]{:S(2)}, u32[]{:S(2)}) collective-permute-start(bf16[4,64,768]{2,1,0:T(8,128)(2,1)} %dynamic-slice_bitcast_fusion.12), channel_id=1, source_target_pairs={{4,0},{0,4},{5,1},{1,5},{6,2},{2,6},{7,3},{3,7},{12,8},{8,12},{13,... | collective-permute-start | bytes 1179656 | tf_op jit(solution)/shard_map/ppermute | solution.py:41
  476.3 33.7 %collective-permute-start.63 = (bf16[4,64,768]{2,1,0:T(8,128)(2,1)}, bf16[4,64,768]{2,1,0:T(8,128)(2,1)}, u32[]{:S(2)}, u32[]{:S(2)}) collective-permute-start(bf16[4,64,768]{2,1,0:T(8,128)(2,1)} %dynamic-slice_bitcast_fusion.11), channel_id=1, source_target_pairs={{2,0},{0,2},{3,1},{1,3},{6,4},{4,6},{7,5},{5,7},{10,8},{8,10},{11,... | collective-permute-start | bytes 1179656 | tf_op jit(solution)/shard_map/ppermute | solution.py:41
  480.5 43.5 %collective-permute-start.59 = (bf16[1024,512]{1,0:T(8,128)(2,1)}, bf16[1024,512]{1,0:T(8,128)(2,1)}, u32[]{:S(2)}, u32[]{:S(2)}) collective-permute-start(bf16[1024,512]{1,0:T(8,128)(2,1)} %fusion.65), channel_id=1, source_target_pairs={{1,0},{0,1},{3,2},{2,3},{5,4},{4,5},{7,6},{6,7},{9,8},{8,9},{11,10... | collective-permute-start | bytes 3145736 | tf_op jit(solution)/shard_map/ppermute | solution.py:41
  485.0 19.5 %collective-permute-start.78 = (bf16[4,2,64,768]{3,2,0,1:T(8,128)(2,1)}, bf16[4,2,64,768]{3,2,0,1:T(8,128)(2,1)}, u32[]{:S(2)}, u32[]{:S(2)}) collective-permute-start(bf16[4,2,64,768]{3,2,0,1:T(8,128)(2,1)} %bitcast.514), channel_id=1, source_target_pairs={{4,0},{0,4},{5,1},{1,5},{6,2},{2,6},{7,3},{3,7},{12,8},{8,12},{13,... | collective-permute-start | bytes 2359304 | tf_op jit(solution)/shard_map/ppermute | solution.py:41
  487.0 19.2 %collective-permute-start.79 = (bf16[4,2,64,768]{3,2,1,0:T(8,128)(2,1)}, bf16[4,2,64,768]{3,2,1,0:T(8,128)(2,1)}, u32[]{:S(2)}, u32[]{:S(2)}) collective-permute-start(bf16[4,2,64,768]{3,2,1,0:T(8,128)(2,1)} %dynamic-slice_bitcast_fusion.1), channel_id=1, source_target_pairs={{2,0},{0,2},{3,1},{1,3},{6,4},{4,6},{7,5},{5,7},{10,8},{8,10},{11,... | collective-permute-start | bytes 2359304 | tf_op jit(solution)/shard_map/ppermute | solution.py:41
  504.5 15.0 %collective-permute-start.65 = (bf16[4,2,64,512]{3,2,1,0:T(8,128)(2,1)}, bf16[4,2,64,512]{3,2,1,0:T(8,128)(2,1)S(1)}, u32[]{:S(2)}, u32[]{:S(2)}) collective-permute-start(bf16[4,2,64,512]{3,2,1,0:T(8,128)(2,1)} %dynamic-slice_bitcast_fusion.3), channel_id=1, source_target_pairs={{4,0},{0,4},{5,1},{1,5},{6,2},{2,6},{7,3},{3,7},{12,8},{8,12},{13,... | collective-permute-start | bytes 1572872 | tf_op jit(solution)/shard_map/ppermute | solution.py:41
  506.2 14.9 %collective-permute-start.61 = (bf16[256,512]{1,0:T(8,128)(2,1)S(1)}, bf16[256,512]{1,0:T(8,128)(2,1)S(1)}, u32[]{:S(2)}, u32[]{:S(2)}) collective-permute-start(bf16[256,512]{1,0:T(8,128)(2,1)S(1)} %dynamic-slice_bitcast_fusion.28), channel_id=1, source_target_pairs={{1,0},{0,1},{3,2},{2,3},{5,4},{4,5},{7,6},{6,7},{9,8},{8,9},{11,10... | collective-permute-start | bytes 786440 | tf_op jit(solution)/shard_map/ppermute | solution.py:41
  507.5 15.5 %collective-permute-start.64 = (bf16[4,64,512]{2,1,0:T(8,128)(2,1)S(1)}, bf16[4,64,512]{2,1,0:T(8,128)(2,1)S(1)}, u32[]{:S(2)}, u32[]{:S(2)}) collective-permute-start(bf16[4,64,512]{2,1,0:T(8,128)(2,1)S(1)} %dynamic-slice_bitcast_fusion.27), channel_id=1, source_target_pairs={{4,0},{0,4},{5,1},{1,5},{6,2},{2,6},{7,3},{3,7},{12,8},{8,12},{13,... | collective-permute-start | bytes 786440 | tf_op jit(solution)/shard_map/ppermute | solution.py:41
  519.5 17.9 %collective-permute-start.68 = (bf16[64,2048]{1,0:T(8,128)(2,1)S(1)}, bf16[64,2048]{1,0:T(8,128)(2,1)S(1)}, u32[]{:S(2)}, u32[]{:S(2)}) collective-permute-start(bf16[64,2048]{1,0:T(8,128)(2,1)S(1)} %copy-done.74), channel_id=1, source_target_pairs={{24,0},{0,8},{8,16},{16,24},{25,1},{1,9},{9,17},{17,25},{26,2},{2,... | collective-permute-start | bytes 786440 | tf_op jit(solution)/shard_map/ppermute | solution.py:41
  519.5 18.7 %collective-permute-start.69 = (bf16[64,2048]{1,0:T(8,128)(2,1)S(1)}, bf16[64,2048]{1,0:T(8,128)(2,1)S(1)}, u32[]{:S(2)}, u32[]{:S(2)}) collective-permute-start(bf16[64,2048]{1,0:T(8,128)(2,1)S(1)} %copy-done.73), channel_id=1, source_target_pairs={{16,0},{24,8},{0,16},{8,24},{17,1},{25,9},{1,17},{9,25},{18,2},{26... | collective-permute-start | bytes 786440 | tf_op jit(solution)/shard_map/ppermute | solution.py:41
  526.3 28.1 %collective-permute-start.66 = (bf16[2,2,4,32,512]{4,3,0,2,1:T(8,128)(2,1)S(1)}, bf16[2,2,4,32,512]{4,3,0,2,1:T(8,128)(2,1)S(1)}, u32[]{:S(2)}, u32[]{:S(2)}) collective-permute-start(bf16[2,2,4,32,512]{4,3,0,2,1:T(8,128)(2,1)S(1)} %bitcast.554), channel_id=1, source_target_pairs={{2,0},{0,2},{3,1},{1,3},{6,4},{4,6},{7,5},{5,7},{10,8},{8,10},{11,... | collective-permute-start | bytes 1572872 | tf_op jit(solution)/shard_map/ppermute | solution.py:41
  535.9 18.5 %collective-permute-start.71 = (bf16[4,64,512]{2,1,0:T(8,128)(2,1)S(1)}, bf16[4,64,512]{2,1,0:T(8,128)(2,1)S(1)}, u32[]{:S(2)}, u32[]{:S(2)}) collective-permute-start(bf16[4,64,512]{2,1,0:T(8,128)(2,1)S(1)} %dynamic-slice_bitcast_fusion.26), channel_id=1, source_target_pairs={{2,0},{0,2},{3,1},{1,3},{6,4},{4,6},{7,5},{5,7},{10,8},{8,10},{11,... | collective-permute-start | bytes 786440 | tf_op jit(solution)/shard_map/ppermute | solution.py:41
  538.2 20.1 %collective-permute-start.75 = (bf16[64,2048]{1,0:T(8,128)(2,1)S(1)}, bf16[64,2048]{1,0:T(8,128)(2,1)S(1)}, u32[]{:S(2)}, u32[]{:S(2)}) collective-permute-start(bf16[64,2048]{1,0:T(8,128)(2,1)S(1)} %get-tuple-element.316), channel_id=1, source_target_pairs={{24,0},{0,8},{8,16},{16,24},{25,1},{1,9},{9,17},{17,25},{26,2},{2,... | collective-permute-start | bytes 786440 | tf_op jit(solution)/shard_map/ppermute | solution.py:41
  544.3 16.8 %collective-permute-start.76 = (bf16[64,2048]{1,0:T(8,128)(2,1)S(1)}, bf16[64,2048]{1,0:T(8,128)(2,1)}, u32[]{:S(2)}, u32[]{:S(2)}) collective-permute-start(bf16[64,2048]{1,0:T(8,128)(2,1)S(1)} %get-tuple-element.315), channel_id=1, source_target_pairs={{16,0},{24,8},{0,16},{8,24},{17,1},{25,9},{1,17},{9,25},{18,2},{26... | collective-permute-start | bytes 786440 | tf_op jit(solution)/shard_map/ppermute | solution.py:41
  561.0 14.4 %collective-permute-start.82 = (bf16[64,2048]{1,0:T(8,128)(2,1)}, bf16[64,2048]{1,0:T(8,128)(2,1)}, u32[]{:S(2)}, u32[]{:S(2)}) collective-permute-start(bf16[64,2048]{1,0:T(8,128)(2,1)} %get-tuple-element.313), channel_id=1, source_target_pairs={{24,0},{0,8},{8,16},{16,24},{25,1},{1,9},{9,17},{17,25},{26,2},{2,... | collective-permute-start | bytes 786440 | tf_op jit(solution)/shard_map/ppermute | solution.py:41
  565.0 20.0 %collective-permute-start.83 = (bf16[64,2048]{1,0:T(8,128)(2,1)}, bf16[64,2048]{1,0:T(8,128)(2,1)}, u32[]{:S(2)}, u32[]{:S(2)}) collective-permute-start(bf16[64,2048]{1,0:T(8,128)(2,1)} %get-tuple-element.312), channel_id=1, source_target_pairs={{16,0},{24,8},{0,16},{8,24},{17,1},{25,9},{1,17},{9,25},{18,2},{26... | collective-permute-start | bytes 786440 | tf_op jit(solution)/shard_map/ppermute | solution.py:41
  568.5 18.3 %collective-permute-start.84 = (bf16[64,2048]{1,0:T(8,128)(2,1)}, bf16[64,2048]{1,0:T(8,128)(2,1)}, u32[]{:S(2)}, u32[]{:S(2)}) collective-permute-start(bf16[64,2048]{1,0:T(8,128)(2,1)} %get-tuple-element.311), channel_id=1, source_target_pairs={{8,0},{16,8},{24,16},{0,24},{9,1},{17,9},{25,17},{1,25},{10,2},{18... | collective-permute-start | bytes 786440 | tf_op jit(solution)/shard_map/ppermute | solution.py:41
  568.6 21.1 %collective-permute-start.88 = (f32[5,1024]{1,0:T(8,128)S(1)}, f32[5,1024]{1,0:T(8,128)S(1)}, u32[]{:S(2)}, u32[]{:S(2)}) collective-permute-start(f32[5,1024]{1,0:T(8,128)S(1)} %add.927), channel_id=1, source_target_pairs={{8,0},{16,8},{24,16},{0,24},{9,1},{17,9},{25,17},{1,25},{10,2},{18... | collective-permute-start | bytes 61448 | tf_op jit(solution)/shard_map/ppermute | solution.py:41
  571.8 23.8 %collective-permute-start.91 = (f32[32,2048]{1,0:T(8,128)S(1)}, f32[32,2048]{1,0:T(8,128)}, u32[]{:S(2)}, u32[]{:S(2)}) collective-permute-start(f32[32,2048]{1,0:T(8,128)S(1)} %get-tuple-element.352), channel_id=1, source_target_pairs={{1,0},{0,1},{3,2},{2,3},{5,4},{4,5},{7,6},{6,7},{9,8},{8,9},{11,10... | collective-permute-start | bytes 786440 | tf_op jit(solution)/shard_map/ppermute | solution.py:41
  575.5 14.9 %collective-permute-start.89 = (f32[5,1024]{1,0:T(8,128)S(1)}, f32[5,1024]{1,0:T(8,128)S(1)}, u32[]{:S(2)}, u32[]{:S(2)}) collective-permute-start(f32[5,1024]{1,0:T(8,128)S(1)} %add.927), channel_id=1, source_target_pairs={{16,0},{24,8},{0,16},{8,24},{17,1},{25,9},{1,17},{9,25},{18,2},{26... | collective-permute-start | bytes 61448 | tf_op jit(solution)/shard_map/ppermute | solution.py:41
  (165 other events, 1426.7 us)
Sparse Core Ops, SparseCore 0:
  14.6 159.2 all-gather.1

commit v11 on v10

--- a/solution.py
+++ b/solution.py
@@ -275,10 +275,10 @@
     return in_order(mine, other, 1).astype(WIDE)
 
 
-def sum_over(part, axes):
+def sum_over(part, axes, direct=4):
     for axis in axes:
         n = lax.axis_size(axis)
-        if n == 4:
+        if n == direct:
             others = yield sent_around(part, axis)
             part = jnp.sum(placed(part, others, axis, 0), axis=0)
             continue
@@ -407,7 +407,7 @@
     narrow = pl.BlockSpec(block + (D,), where)
     body, last, ins, flops = forward_body, D, (packed,), 9e9
     if up is not None:
-        body, last, flops = backward_body, 3 * D, 22e9
+        body, last, flops = backward_body, 3 * D, 40e9
         ins = (packed, up.reshape(shape + (D,)))
     return pl.pallas_call(
         functools.partial(body, kind),
@@ -653,7 +653,7 @@
     small_square = jnp.pad(jnp.sum(gain_grads * gain_grads, axis=0), (0, LANES - width))
     owned = sum(job.square for job in jobs) + small_square
     sums = jnp.stack([owned, jnp.where(lane == 0, loss_part, 0.0)])
-    norm_job = Job(sum_over(sums, ("h", "m", "r", "z")))
+    norm_job = Job(sum_over(sums, ("h", "m", "r", "z"), 0))
     while norm_job.flight is not None:
         token = advance(token, norm_job, *jobs)
     (up_grad,), (next_in, next_out), (first_in, first_out) = (job.finish() for job in jobs[:3])

time: 662 us -> 662 us (level)
    ppermute x104 -> x103, waiting for transfers between devices: 138 us -> 135 us  [shifted(): return lax.ppermute(part, axis, [((i + shift) % n, i) for i in range(n)])]
    unnamed x264 -> x272, local copies, waits for them, and re-layouts: 20.5 us -> 21.5 us
    ppermute x104 -> x103, starting transfers between devices: 138 us -> 138 us  [shifted(): return lax.ppermute(part, axis, [((i + shift) % n, i) for i in range(n)])]
  transfers between devices with their start and end apart: 105 -> 104, of which waited for: 33 -> 31; matrix products, arithmetic and copies ran while one was open for 33% -> 33% of each run, Pallas kernels for 8% -> 8%
where the time goes in v11:
time: 662 us; the launch traced here: 653 us
  waiting for transfers between devices  160 us (24%)
  starting transfers between devices  138 us (21%)
  matrix products  136 us (21%)
  other arithmetic  72.2 us (11%)
  local copies, waits for them, and re-layouts  72 us (11%)
  Pallas kernels  54.7 us (8%)
  between operations  19.1 us (3%)
    ppermute x103, starting transfers between devices, shifted(): return lax.ppermute(part, axis, [((i + shift) % n, i) for i in range(n)])  138 us
    ppermute x103, waiting for transfers between devices, shifted(): return lax.ppermute(part, axis, [((i + shift) % n, i) for i in range(n)])  135 us
    pallas_call x4, Pallas kernels, attention(): pl.pallas_call(functools.partial(body, kind), out_shape=jax.ShapeDtypeStr...  54.7 us
    dot_general x10, matrix products, dot_nn(): return jnp.dot(left, right, preferred_element_type=WIDE)  48.7 us
    dot_general x9, matrix products, dot_nt(): lax.dot_general(left, right, (((1,), (1,)), ((), ())), preferred_element_...  47.1 us
    dot_general x16, matrix products, dot_tn(): lax.dot_general(left, right, (((0,), (0,)), ((), ())), preferred_element_...  40.5 us
    all_gather x1, waiting for transfers between devices, on_device(): gathered = lax.all_gather(gathered, ALL, axis=0, tiled=True)  25.8 us
    unnamed x272, local copies, waits for them, and re-layouts  21.5 us
  transfers between devices with their start and end apart: 104, of which 31 were waited for; matrix products, arithmetic and copies ran while one was open for 33% of the time, Pallas kernels for 8%

profile of v11, /device:TPU:0, one launch (start us, length us, event | category | flops | bytes accessed | tf_op | source)
XLA Modules:
  0.0 653.3 jit_solution(274485505416295302)
XLA Ops:
  14.5 5.1 collective-permute-start.3
  29.8 3.9 collective-permute-start.25
  33.7 2.4 collective-permute-done.25
  36.1 4.6 collective-permute-done.26
  42.4 4.0 collective-permute-done.27
  51.4 3.8 collective-permute-start.7
  55.4 23.9 %collective-permute-done.7 = bf16[128,512]{1,0:T(8,128)(2,1)S(1)} collective-permute-done((bf16[128,512]{1,0:T(8,128)(2,1)S(1)}, bf16[128,512]{1,0:T(8,128)(2,1)S(1)}, u32[]{:S(2)}, u32[]{:S(2)}) %collective-permute-start.7) | collective-permute-done | bytes 131104 | tf_op jit(solution)/shard_map/ppermute | solution.py:41
  84.2 4.6 collective-permute-done.10
  88.8 4.2 collective-permute-start.13
  95.4 21.1 %collective-permute-done.12 = bf16[4,128,512]{2,1,0:T(8,128)(2,1)S(1)} collective-permute-done((bf16[4,128,512]{2,1,0:T(8,128)(2,1)S(1)}, bf16[4,128,512]{2,1,0:T(8,128)(2,1)S(1)}, u32[]{:S(2)}, u32[]{:S(2)}) %collective-permute-start.12) | collective-permute-done | bytes 524320 | tf_op jit(solution)/shard_map/ppermute | solution.py:41
  116.8 16.8 %collective-permute-done.14 = bf16[4,64,1024]{2,1,0:T(8,128)(2,1)S(1)} collective-permute-done((bf16[4,64,1024]{2,1,0:T(8,128)(2,1)S(1)}, bf16[4,64,1024]{2,1,0:T(8,128)(2,1)S(1)}, u32[]{:S(2)}, u32[]{:S(2)}) %collective-permute-start.14) | collective-permute-done | bytes 524320 | tf_op jit(solution)/shard_map/ppermute | solution.py:41
  133.5 4.5 collective-permute-done.15
  138.1 2.5 collective-permute-start.16
  148.5 25.8 %all-gather.2.cloned.1.call-done = bf16[1024,8320]{1,0:T(8,128)(2,1)} async-done(((bf16[32,8320]{1,0:T(8,128)(2,1)}), bf16[1024,8320]{1,0:T(8,128)(2,1)}) %all-gather.2.cloned.1.call-update) | async-done | bytes 17039376 | tf_op jit(solution)/shard_map/all_gather | solution.py:506
  178.6 7.9 %fusion.8.packed_ref = bf16[512,3072]{1,0:T(8,128)(2,1)} fusion(bf16[512,1024]{1,0:T(8,128)(2,1)S(1)} %multiply_convert_fusion.5, bf16[1024,8320]{1,0:T(8,128)(2,1)} %all-gather.2.cloned.1.call-done), kind=kOutput, calls=%fused_computation.16 | convolution fusion | flops 3222798336 | bytes 10485760 | tf_op jit(solution)/shard_map/dot_general | solution.py:316
  186.5 9.3 %shard_map.365 = bf16[512,1024]{1,0:T(8,128)(2,1)} custom-call(s32[1]{0:T(128)} %bitcast.13.scalar_ref, bf16[512,3072]{1,0:T(8,128)(2,1)} %fusion.8.packed_ref), custom_call_target="tpu_custom_call" | custom-call | flops 8999999488 | bytes 8388608 | tf_op jit(solution)/shard_map/pallas_call | solution.py:412
  200.2 2.6 pad_maximum_fusion.1
  203.0 2.9 fusion.60
  214.6 2.5 pad_maximum_fusion
  218.0 8.8 %fusion.11 = bf16[512,3072]{1,0:T(8,128)(2,1)} fusion(bf16[512,1024]{1,0:T(8,128)(2,1)S(1)} %fusion.34, bf16[1024,8320]{1,0:T(8,128)(2,1)} %all-gather.2.cloned.1.call-done), kind=kOutput, calls=%fused_computation.17 | convolution fusion | flops 3222798336 | bytes 10485760 | tf_op jit(solution)/shard_map/dot_general | solution.py:316
  226.8 9.1 %shard_map.366 = bf16[4,128,1024]{2,1,0:T(8,128)(2,1)} custom-call(s32[1]{0:T(128)} %bitcast.30.scalar_ref, bf16[4,128,3072]{2,1,0:T(8,128)(2,1)} %bitcast.565), custom_call_target="tpu_custom_call" | custom-call | flops 8999999488 | bytes 8388608 | tf_op jit(solution)/shard_map/pallas_call | solution.py:412
  235.9 3.3 multiply_reduce_fusion.8
  241.5 4.9 fusion.192
  246.4 6.4 fusion.165
  252.9 4.5 fusion.193
  257.5 6.6 %multiply_reduce_fusion.7 = (f32[512]{0:T(512)S(1)}, f32[512,1024]{1,0:T(8,128)S(1)}) fusion(bf16[2048,1024]{1,0:T(8,128)(2,1)} %collective-permute-done.23, f32[512,2048]{1,0:T(8,128)S(1)} %fusion.193, f32[512,1024]{1,0:T(8,128)S(1)} %get-tuple-element.370, f32[512,1024]{1,0:T(8,128)S(1)} %fusion.165), kind=kOutput, calls=%fused_computation.91 | convolution fusion | flops 2159017472 | bytes 14682112 | tf_op jit(solution)/shard_map/dot_general | solution.py:316
  271.9 4.9 convolution_convert_fusion.3
  283.1 6.3 fusion.164
  289.4 7.1 %fusion.20 = bf16[512,2048]{1,0:T(8,128)(2,1)S(1)} fusion(f32[512,2048]{1,0:T(8,128)S(1)} %copy-done.122, bf16[512,1024]{1,0:T(8,128)(2,1)S(1)} %copy-done.42, bf16[2048,1024]{1,0:T(8,128)(2,1)} %bitcast.40), kind=kOutput, calls=%fused_computation.24 | convolution fusion | flops 2168455168 | bytes 11534336 | tf_op jit(solution)/shard_map/dot_general | solution.py:308
  296.5 8.0 %fusion.27 = bf16[512,2048]{1,0:T(8,128)(2,1)S(1)} fusion(f32[512,2048]{1,0:T(8,128)S(1)} %copy-done.125, bf16[512,1024]{1,0:T(8,128)(2,1)S(1)} %copy-done.42, bf16[2048,1024]{1,0:T(8,128)(2,1)} %collective-permute-done.23), kind=kOutput, calls=%fused_computation.31 | convolution fusion | flops 2168455168 | bytes 11534336 | tf_op jit(solution)/shard_map/dot_general | solution.py:308
  304.6 4.4 convolution_convert_fusion.2
  311.6 6.4 add_convert_fusion
  323.7 4.5 fusion.194
  328.3 5.7 multiply_reduce_fusion.2
  334.0 2.6 fusion.178
  336.6 4.4 fusion.69
  342.8 17.9 %shard_map.367 = bf16[4,128,3072]{2,1,0:T(8,128)(2,1)} custom-call(s32[1]{0:T(128)} %bitcast.30.scalar_ref, bf16[4,128,3072]{2,1,0:T(8,128)(2,1)} %bitcast.566, bf16[4,128,1024]{2,1,0:T(8,128)(2,1)} %bitcast.573), custom_call_target="tpu_custom_call" | custom-call | flops 40000000000 | bytes 8388608 | tf_op jit(solution)/shard_map/pallas_call | solution.py:412
  362.2 5.2 add_convert_fusion.1
  373.9 6.0 fusion.40
  398.0 2.8 collective-permute-done.41
  400.9 3.9 collective-permute-start.44
  412.0 3.9 fusion.66.up_ref
  416.5 3.3 collective-permute-done.50
  429.8 18.4 %shard_map.368 = bf16[512,3072]{1,0:T(8,128)(2,1)} custom-call(s32[1]{0:T(128)} %bitcast.13.scalar_ref, bf16[512,3072]{1,0:T(8,128)(2,1)} %fusion.8.packed_ref, bf16[512,1024]{1,0:T(8,128)(2,1)} %fusion.66.up_ref), custom_call_target="tpu_custom_call" | custom-call | flops 40000000000 | bytes 8388608 | tf_op jit(solution)/shard_map/pallas_call | solution.py:412
  449.1 3.6 convolution_convert_fusion
  463.9 6.2 fusion.4
  493.3 10.5 %collective-permute-done.78 = bf16[4,2,64,768]{3,2,0,1:T(8,128)(2,1)} collective-permute-done((bf16[4,2,64,768]{3,2,0,1:T(8,128)(2,1)}, bf16[4,2,64,768]{3,2,0,1:T(8,128)(2,1)}, u32[]{:S(2)}, u32[]{:S(2)}) %collective-permute-start.78) | collective-permute-done | bytes 786464 | tf_op jit(solution)/shard_map/ppermute | solution.py:41
  509.7 9.2 %collective-permute-done.65 = bf16[4,2,64,512]{3,2,1,0:T(8,128)(2,1)S(1)} collective-permute-done((bf16[4,2,64,512]{3,2,1,0:T(8,128)(2,1)}, bf16[4,2,64,512]{3,2,1,0:T(8,128)(2,1)S(1)}, u32[]{:S(2)}, u32[]{:S(2)}) %collective-permute-start.65) | collective-permute-done | bytes 524320 | tf_op jit(solution)/shard_map/ppermute | solution.py:41
  531.3 4.2 collective-permute-start.70
  539.4 4.2 collective-permute-done.70
  543.7 6.4 collective-permute-start.76
  550.0 3.4 collective-permute-start.77
  560.1 3.8 collective-permute-start.82
  563.9 3.5 collective-permute-start.83
  574.3 10.6 %collective-permute-start.89 = (f32[5,1024]{1,0:T(8,128)S(1)}, f32[5,1024]{1,0:T(8,128)S(1)}, u32[]{:S(2)}, u32[]{:S(2)}) collective-permute-start(f32[5,1024]{1,0:T(8,128)S(1)} %add.923), channel_id=1, source_target_pairs={{16,0},{24,8},{0,16},{8,24},{17,1},{25,9},{1,17},{9,25},{18,2},{26... | collective-permute-start | bytes 61448 | tf_op jit(solution)/shard_map/ppermute | solution.py:41
  587.5 2.5 collective-permute-start.86
  590.0 2.9 collective-permute-start.87
  592.9 2.3 collective-permute-done.86
  595.3 3.8 collective-permute-start.94
  608.9 5.7 collective-permute-done.98
  615.9 2.5 collective-permute-done.99
  623.0 3.2 collective-permute-start.102
  632.5 2.6 multiply_subtract_fusion.4
  641.3 3.5 multiply_subtract_fusion
  (696 shorter events, 228.3 us)
Async XLA Ops:
  7.2 167.1 %all-gather.2.cloned.1.call-start = ((), (), s32[]{:S(2)}) async-start(), calls=%async_computation | async-start | bytes 17571840 | tf_op jit(solution)/shard_map/all_gather | solution.py:506
  14.5 32.7 %collective-permute-start.3 = (bf16[128,1024]{1,0:T(8,128)(2,1)S(1)}, bf16[128,1024]{1,0:T(8,128)(2,1)}, u32[]{:S(2)}, u32[]{:S(2)}) collective-permute-start(bf16[128,1024]{1,0:T(8,128)(2,1)S(1)} %convert_element_type.557), channel_id=1, source_target_pairs={{8,0},{16,8},{24,16},{0,24},{9,1},{17,9},{25,17},{1,25},{10,2},{18... | collective-permute-start | bytes 786440 | tf_op jit(solution)/shard_map/ppermute | solution.py:41
  19.7 27.5 %collective-permute-start.4 = (bf16[128,1024]{1,0:T(8,128)(2,1)S(1)}, bf16[128,1024]{1,0:T(8,128)(2,1)S(1)}, u32[]{:S(2)}, u32[]{:S(2)}) collective-permute-start(bf16[128,1024]{1,0:T(8,128)(2,1)S(1)} %convert_element_type.557), channel_id=1, source_target_pairs={{24,0},{0,8},{8,16},{16,24},{25,1},{1,9},{9,17},{17,25},{26,2},{2,... | collective-permute-start | bytes 786440 | tf_op jit(solution)/shard_map/ppermute | solution.py:41
  22.1 25.1 %collective-permute-start.2 = (bf16[32,2048]{1,0:T(8,128)(2,1)}, bf16[32,2048]{1,0:T(8,128)(2,1)S(1)}, u32[]{:S(2)}, u32[]{:S(2)}) collective-permute-start(bf16[32,2048]{1,0:T(8,128)(2,1)} %bitcast.512), channel_id=1, source_target_pairs={{1,0},{0,1},{3,2},{2,3},{5,4},{4,5},{7,6},{6,7},{9,8},{8,9},{11,10... | collective-permute-start | bytes 393224 | tf_op jit(solution)/shard_map/ppermute | solution.py:41
  23.2 56.2 %collective-permute-start.1 = (bf16[256,1024]{1,0:T(8,128)(2,1)S(1)}, bf16[256,1024]{1,0:T(8,128)(2,1)S(1)}, u32[]{:S(2)}, u32[]{:S(2)}) collective-permute-start(bf16[256,1024]{1,0:T(8,128)(2,1)S(1)} %get-tuple-element.326), channel_id=1, source_target_pairs={{2,0},{0,2},{3,1},{1,3},{6,4},{4,6},{7,5},{5,7},{10,8},{8,10},{11,... | collective-permute-start | bytes 1572872 | tf_op jit(solution)/shard_map/ppermute | solution.py:41
  47.3 32.1 %collective-permute-start.5 = (bf16[64,2048]{1,0:T(8,128)(2,1)S(1)}, bf16[64,2048]{1,0:T(8,128)(2,1)S(1)}, u32[]{:S(2)}, u32[]{:S(2)}) collective-permute-start(bf16[64,2048]{1,0:T(8,128)(2,1)S(1)} %bitcast.533), channel_id=1, source_target_pairs={{8,0},{16,8},{24,16},{0,24},{9,1},{17,9},{25,17},{1,25},{10,2},{18... | collective-permute-start | bytes 786440 | tf_op jit(solution)/shard_map/ppermute | solution.py:41
  49.3 30.0 %collective-permute-start.6 = (bf16[64,2048]{1,0:T(8,128)(2,1)S(1)}, bf16[64,2048]{1,0:T(8,128)(2,1)S(1)}, u32[]{:S(2)}, u32[]{:S(2)}) collective-permute-start(bf16[64,2048]{1,0:T(8,128)(2,1)S(1)} %bitcast.534), channel_id=1, source_target_pairs={{24,0},{0,8},{8,16},{16,24},{25,1},{1,9},{9,17},{17,25},{26,2},{2,... | collective-permute-start | bytes 786440 | tf_op jit(solution)/shard_map/ppermute | solution.py:41
  51.4 27.9 %collective-permute-start.7 = (bf16[128,512]{1,0:T(8,128)(2,1)S(1)}, bf16[128,512]{1,0:T(8,128)(2,1)S(1)}, u32[]{:S(2)}, u32[]{:S(2)}) collective-permute-start(bf16[128,512]{1,0:T(8,128)(2,1)S(1)} %slice.110), channel_id=1, source_target_pairs={{8,0},{16,8},{24,16},{0,24},{9,1},{17,9},{25,17},{1,25},{10,2},{18... | collective-permute-start | bytes 393224 | tf_op jit(solution)/shard_map/ppermute | solution.py:41
  55.3 24.0 %collective-permute-start.8 = (bf16[128,512]{1,0:T(8,128)(2,1)S(1)}, bf16[128,512]{1,0:T(8,128)(2,1)S(1)}, u32[]{:S(2)}, u32[]{:S(2)}) collective-permute-start(bf16[128,512]{1,0:T(8,128)(2,1)S(1)} %slice.111), channel_id=1, source_target_pairs={{24,0},{0,8},{8,16},{16,24},{25,1},{1,9},{9,17},{17,25},{26,2},{2,... | collective-permute-start | bytes 393224 | tf_op jit(solution)/shard_map/ppermute | solution.py:41
  79.3 69.2 %collective-permute-start = (bf16[256,1024]{1,0:T(8,128)(2,1)}, bf16[256,1024]{1,0:T(8,128)(2,1)}, u32[]{:S(2)}, u32[]{:S(2)}) collective-permute-start(bf16[256,1024]{1,0:T(8,128)(2,1)} %get-tuple-element.325), channel_id=1, source_target_pairs={{2,0},{0,2},{3,1},{1,3},{6,4},{4,6},{7,5},{5,7},{10,8},{8,10},{11,... | collective-permute-start | bytes 1572872 | tf_op jit(solution)/shard_map/ppermute | solution.py:41
  79.8 36.8 %collective-permute-start.12 = (bf16[4,128,512]{2,1,0:T(8,128)(2,1)S(1)}, bf16[4,128,512]{2,1,0:T(8,128)(2,1)S(1)}, u32[]{:S(2)}, u32[]{:S(2)}) collective-permute-start(bf16[4,128,512]{2,1,0:T(8,128)(2,1)S(1)} %get-tuple-element.324), channel_id=1, source_target_pairs={{2,0},{0,2},{3,1},{1,3},{6,4},{4,6},{7,5},{5,7},{10,8},{8,10},{11,... | collective-permute-start | bytes 1572872 | tf_op jit(solution)/shard_map/ppermute | solution.py:41
  88.8 28.0 %collective-permute-start.13 = (bf16[4,128,512]{2,1,0:T(8,128)(2,1)S(1)}, bf16[4,128,512]{2,1,0:T(8,128)(2,1)S(1)}, u32[]{:S(2)}, u32[]{:S(2)}) collective-permute-start(bf16[4,128,512]{2,1,0:T(8,128)(2,1)S(1)} %get-tuple-element.323), channel_id=1, source_target_pairs={{4,0},{0,4},{5,1},{1,5},{6,2},{2,6},{7,3},{3,7},{12,8},{8,12},{13,... | collective-permute-start | bytes 1572872 | tf_op jit(solution)/shard_map/ppermute | solution.py:41
  93.1 40.4 %collective-permute-start.14 = (bf16[4,64,1024]{2,1,0:T(8,128)(2,1)S(1)}, bf16[4,64,1024]{2,1,0:T(8,128)(2,1)S(1)}, u32[]{:S(2)}, u32[]{:S(2)}) collective-permute-start(bf16[4,64,1024]{2,1,0:T(8,128)(2,1)S(1)} %get-tuple-element.322), channel_id=1, source_target_pairs={{2,0},{0,2},{3,1},{1,3},{6,4},{4,6},{7,5},{5,7},{10,8},{8,10},{11,... | collective-permute-start | bytes 1572872 | tf_op jit(solution)/shard_map/ppermute | solution.py:41
  93.2 44.8 %collective-permute-start.15 = (bf16[4,64,1024]{2,1,0:T(8,128)(2,1)S(1)}, bf16[4,64,1024]{2,1,0:T(8,128)(2,1)S(1)}, u32[]{:S(2)}, u32[]{:S(2)}) collective-permute-start(bf16[4,64,1024]{2,1,0:T(8,128)(2,1)S(1)} %get-tuple-element.321), channel_id=1, source_target_pairs={{4,0},{0,4},{5,1},{1,5},{6,2},{2,6},{7,3},{3,7},{12,8},{8,12},{13,... | collective-permute-start | bytes 1572872 | tf_op jit(solution)/shard_map/ppermute | solution.py:41
  138.1 57.7 %collective-permute-start.16 = (bf16[4,2,128,512]{3,2,1,0:T(8,128)(2,1)S(1)}, bf16[4,2,128,512]{3,2,1,0:T(8,128)(2,1)}, u32[]{:S(2)}, u32[]{:S(2)}) collective-permute-start(bf16[4,2,128,512]{3,2,1,0:T(8,128)(2,1)S(1)} %bitcast_dynamic-update-slice_fusion.7), channel_id=1, source_target_pairs={{4,0},{0,4},{5,1},{1,5},{6,2},{2,6},{7,3},{3,7},{12,8},{8,12},{13,... | collective-permute-start | bytes 3145736 | tf_op jit(solution)/shard_map/ppermute | solution.py:41
  142.6 53.2 %collective-permute-start.17 = (bf16[4,2,128,512]{3,2,1,0:T(8,128)(2,1)}, bf16[4,2,128,512]{3,2,1,0:T(8,128)(2,1)}, u32[]{:S(2)}, u32[]{:S(2)}) collective-permute-start(bf16[4,2,128,512]{3,2,1,0:T(8,128)(2,1)} %bitcast_dynamic-update-slice_fusion.10), channel_id=1, source_target_pairs={{2,0},{0,2},{3,1},{1,3},{6,4},{4,6},{7,5},{5,7},{10,8},{8,10},{11,... | collective-permute-start | bytes 3145736 | tf_op jit(solution)/shard_map/ppermute | solution.py:41
  144.5 51.3 %collective-permute-start.18 = (bf16[4,2,64,1024]{3,2,1,0:T(8,128)(2,1)}, bf16[4,2,64,1024]{3,2,1,0:T(8,128)(2,1)}, u32[]{:S(2)}, u32[]{:S(2)}) collective-permute-start(bf16[4,2,64,1024]{3,2,1,0:T(8,128)(2,1)} %bitcast_dynamic-update-slice_fusion.6), channel_id=1, source_target_pairs={{4,0},{0,4},{5,1},{1,5},{6,2},{2,6},{7,3},{3,7},{12,8},{8,12},{13,... | collective-permute-start | bytes 3145736 | tf_op jit(solution)/shard_map/ppermute | solution.py:41
  146.5 49.4 %collective-permute-start.19 = (bf16[4,2,64,1024]{3,2,1,0:T(8,128)(2,1)}, bf16[4,2,64,1024]{3,2,1,0:T(8,128)(2,1)}, u32[]{:S(2)}, u32[]{:S(2)}) collective-permute-start(bf16[4,2,64,1024]{3,2,1,0:T(8,128)(2,1)} %bitcast_dynamic-update-slice_fusion.9), channel_id=1, source_target_pairs={{2,0},{0,2},{3,1},{1,3},{6,4},{4,6},{7,5},{5,7},{10,8},{8,10},{11,... | collective-permute-start | bytes 3145736 | tf_op jit(solution)/shard_map/ppermute | solution.py:41
  202.8 54.7 %collective-permute-start.23 = (bf16[2048,1024]{1,0:T(8,128)(2,1)}, bf16[2048,1024]{1,0:T(8,128)(2,1)}, u32[]{:S(2)}, u32[]{:S(2)}) collective-permute-start(bf16[2048,1024]{1,0:T(8,128)(2,1)} %bitcast.40), channel_id=1, source_target_pairs={{1,0},{0,1},{3,2},{2,3},{5,4},{4,5},{7,6},{6,7},{9,8},{8,9},{11,10... | collective-permute-start | bytes 12582920 | tf_op jit(solution)/shard_map/ppermute | solution.py:41
  217.1 35.8 %collective-permute-start.22 = (bf16[1024,2048]{1,0:T(8,128)(2,1)}, bf16[1024,2048]{1,0:T(8,128)(2,1)}, u32[]{:S(2)}, u32[]{:S(2)}) collective-permute-start(bf16[1024,2048]{1,0:T(8,128)(2,1)} %bitcast.37), channel_id=1, source_target_pairs={{1,0},{0,1},{3,2},{2,3},{5,4},{4,5},{7,6},{6,7},{9,8},{8,9},{11,10... | collective-permute-start | bytes 12582920 | tf_op jit(solution)/shard_map/ppermute | solution.py:41
  276.8 27.7 %collective-permute-start.29 = (bf16[2048,1024]{1,0:T(8,128)(2,1)}, bf16[2048,1024]{1,0:T(8,128)(2,1)}, u32[]{:S(2)}, u32[]{:S(2)}) collective-permute-start(bf16[2048,1024]{1,0:T(8,128)(2,1)} %convolution_convert_fusion.3), channel_id=1, source_target_pairs={{1,0},{0,1},{3,2},{2,3},{5,4},{4,5},{7,6},{6,7},{9,8},{8,9},{11,10... | collective-permute-start | bytes 12582920 | tf_op jit(solution)/shard_map/ppermute | solution.py:41
  279.0 25.6 %collective-permute-start.28 = (bf16[1024,512]{1,0:T(8,128)(2,1)S(1)}, bf16[1024,512]{1,0:T(8,128)(2,1)S(1)}, u32[]{:S(2)}, u32[]{:S(2)}) collective-permute-start(bf16[1024,512]{1,0:T(8,128)(2,1)S(1)} %convolution_convert_fusion.6), channel_id=1, source_target_pairs={{1,0},{0,1},{3,2},{2,3},{5,4},{4,5},{7,6},{6,7},{9,8},{8,9},{11,10... | collective-permute-start | bytes 3145736 | tf_op jit(solution)/shard_map/ppermute | solution.py:41
  309.0 27.6 %collective-permute-start.31 = (bf16[1024,2048]{1,0:T(8,128)(2,1)}, bf16[1024,2048]{1,0:T(8,128)(2,1)}, u32[]{:S(2)}, u32[]{:S(2)}) collective-permute-start(bf16[1024,2048]{1,0:T(8,128)(2,1)} %convolution_convert_fusion.2), channel_id=1, source_target_pairs={{1,0},{0,1},{3,2},{2,3},{5,4},{4,5},{7,6},{6,7},{9,8},{8,9},{11,10... | collective-permute-start | bytes 12582920 | tf_op jit(solution)/shard_map/ppermute | solution.py:41
  310.5 26.1 %collective-permute-start.30 = (bf16[2,2,4,32,512]{4,3,0,2,1:T(8,128)(2,1)S(1)}, bf16[2,2,4,32,512]{4,3,0,2,1:T(8,128)(2,1)S(1)}, u32[]{:S(2)}, u32[]{:S(2)}) collective-permute-start(bf16[2,2,4,32,512]{4,3,0,2,1:T(8,128)(2,1)S(1)} %bitcast.549), channel_id=1, source_target_pairs={{2,0},{0,2},{3,1},{1,3},{6,4},{4,6},{7,5},{5,7},{10,8},{8,10},{11,... | collective-permute-start | bytes 1572872 | tf_op jit(solution)/shard_map/ppermute | solution.py:41
  319.6 50.0 %collective-permute-start.33 = (bf16[4,2,128,512]{3,2,0,1:T(8,128)(2,1)}, bf16[4,2,128,512]{3,2,0,1:T(8,128)(2,1)}, u32[]{:S(2)}, u32[]{:S(2)}) collective-permute-start(bf16[4,2,128,512]{3,2,0,1:T(8,128)(2,1)} %bitcast.507), channel_id=1, source_target_pairs={{2,0},{0,2},{3,1},{1,3},{6,4},{4,6},{7,5},{5,7},{10,8},{8,10},{11,... | collective-permute-start | bytes 3145736 | tf_op jit(solution)/shard_map/ppermute | solution.py:41
  322.9 46.7 %collective-permute-start.34 = (bf16[4,2,128,512]{3,2,0,1:T(8,128)(2,1)}, bf16[4,2,128,512]{3,2,0,1:T(8,128)(2,1)}, u32[]{:S(2)}, u32[]{:S(2)}) collective-permute-start(bf16[4,2,128,512]{3,2,0,1:T(8,128)(2,1)} %bitcast.506), channel_id=1, source_target_pairs={{4,0},{0,4},{5,1},{1,5},{6,2},{2,6},{7,3},{3,7},{12,8},{8,12},{13,... | collective-permute-start | bytes 3145736 | tf_op jit(solution)/shard_map/ppermute | solution.py:41
  373.3 27.5 %collective-permute-start.42 = (bf16[1024,1536]{1,0:T(8,128)(2,1)S(1)}, bf16[1024,1536]{1,0:T(8,128)(2,1)S(1)}, u32[]{:S(2)}, u32[]{:S(2)}) collective-permute-start(bf16[1024,1536]{1,0:T(8,128)(2,1)S(1)} %convolution_convert_fusion.1), channel_id=1, source_target_pairs={{1,0},{0,1},{3,2},{2,3},{5,4},{4,5},{7,6},{6,7},{9,8},{8,9},{11,10... | collective-permute-start | bytes 9437192 | tf_op jit(solution)/shard_map/ppermute | solution.py:41
  383.2 14.9 %collective-permute-start.40 = (bf16[4,128,512]{2,1,0:T(8,128)(2,1)S(1)}, bf16[4,128,512]{2,1,0:T(8,128)(2,1)S(1)}, u32[]{:S(2)}, u32[]{:S(2)}) collective-permute-start(bf16[4,128,512]{2,1,0:T(8,128)(2,1)S(1)} %dynamic-slice_bitcast_fusion.8), channel_id=1, source_target_pairs={{4,0},{0,4},{5,1},{1,5},{6,2},{2,6},{7,3},{3,7},{12,8},{8,12},{13,... | collective-permute-start | bytes 1572872 | tf_op jit(solution)/shard_map/ppermute | solution.py:41
  385.9 14.9 %collective-permute-start.41 = (bf16[4,128,512]{2,1,0:T(8,128)(2,1)S(1)}, bf16[4,128,512]{2,1,0:T(8,128)(2,1)S(1)}, u32[]{:S(2)}, u32[]{:S(2)}) collective-permute-start(bf16[4,128,512]{2,1,0:T(8,128)(2,1)S(1)} %dynamic-slice_bitcast_fusion.7), channel_id=1, source_target_pairs={{2,0},{0,2},{3,1},{1,3},{6,4},{4,6},{7,5},{5,7},{10,8},{8,10},{11,... | collective-permute-start | bytes 1572872 | tf_op jit(solution)/shard_map/ppermute | solution.py:41
  394.4 25.3 %collective-permute-start.50 = (bf16[4,2,64,1024]{3,2,0,1:T(8,128)(2,1)S(1)}, bf16[4,2,64,1024]{3,2,0,1:T(8,128)(2,1)}, u32[]{:S(2)}, u32[]{:S(2)}) collective-permute-start(bf16[4,2,64,1024]{3,2,0,1:T(8,128)(2,1)S(1)} %bitcast.536), channel_id=1, source_target_pairs={{4,0},{0,4},{5,1},{1,5},{6,2},{2,6},{7,3},{3,7},{12,8},{8,12},{13,... | collective-permute-start | bytes 3145736 | tf_op jit(solution)/shard_map/ppermute | solution.py:41
  395.6 26.5 %collective-permute-start.51 = (bf16[4,2,64,1024]{3,2,1,0:T(8,128)(2,1)S(1)}, bf16[4,2,64,1024]{3,2,1,0:T(8,128)(2,1)S(1)}, u32[]{:S(2)}, u32[]{:S(2)}) collective-permute-start(bf16[4,2,64,1024]{3,2,1,0:T(8,128)(2,1)S(1)} %dynamic-slice_bitcast_fusion), channel_id=1, source_target_pairs={{2,0},{0,2},{3,1},{1,3},{6,4},{4,6},{7,5},{5,7},{10,8},{8,10},{11,... | collective-permute-start | bytes 3145736 | tf_op jit(solution)/shard_map/ppermute | solution.py:41
  400.9 24.0 %collective-permute-start.44 = (bf16[2,32,512]{2,1,0:T(8,128)(2,1)S(1)}, bf16[2,32,512]{2,1,0:T(8,128)(2,1)S(1)}, u32[]{:S(2)}, u32[]{:S(2)}) collective-permute-start(bf16[2,32,512]{2,1,0:T(8,128)(2,1)S(1)} %get-tuple-element.350), channel_id=1, source_target_pairs={{8,0},{16,8},{24,16},{0,24},{9,1},{17,9},{25,17},{1,25},{10,2},{18... | collective-permute-start | bytes 196616 | tf_op jit(solution)/shard_map/ppermute | solution.py:41
  404.7 22.2 %collective-permute-start.45 = (bf16[2,32,512]{2,1,0:T(8,128)(2,1)S(1)}, bf16[2,32,512]{2,1,0:T(8,128)(2,1)S(1)}, u32[]{:S(2)}, u32[]{:S(2)}) collective-permute-start(bf16[2,32,512]{2,1,0:T(8,128)(2,1)S(1)} %get-tuple-element.350), channel_id=1, source_target_pairs={{16,0},{24,8},{0,16},{8,24},{17,1},{25,9},{1,17},{9,25},{18,2},{26... | collective-permute-start | bytes 196616 | tf_op jit(solution)/shard_map/ppermute | solution.py:41
  419.8 28.5 %collective-permute-start.47 = (bf16[128,1024]{1,0:T(8,128)(2,1)}, bf16[128,1024]{1,0:T(8,128)(2,1)S(1)}, u32[]{:S(2)}, u32[]{:S(2)}) collective-permute-start(bf16[128,1024]{1,0:T(8,128)(2,1)} %get-tuple-element.317), channel_id=1, source_target_pairs={{24,0},{0,8},{8,16},{16,24},{25,1},{1,9},{9,17},{17,25},{26,2},{2,... | collective-permute-start | bytes 786440 | tf_op jit(solution)/shard_map/ppermute | solution.py:41
  423.1 25.9 %collective-permute-start.48 = (bf16[128,1024]{1,0:T(8,128)(2,1)}, bf16[128,1024]{1,0:T(8,128)(2,1)}, u32[]{:S(2)}, u32[]{:S(2)}) collective-permute-start(bf16[128,1024]{1,0:T(8,128)(2,1)} %get-tuple-element.318), channel_id=1, source_target_pairs={{16,0},{24,8},{0,16},{8,24},{17,1},{25,9},{1,17},{9,25},{18,2},{26... | collective-permute-start | bytes 786440 | tf_op jit(solution)/shard_map/ppermute | solution.py:41
  424.9 24.2 %collective-permute-start.49 = (bf16[128,1024]{1,0:T(8,128)(2,1)}, bf16[128,1024]{1,0:T(8,128)(2,1)}, u32[]{:S(2)}, u32[]{:S(2)}) collective-permute-start(bf16[128,1024]{1,0:T(8,128)(2,1)} %get-tuple-element.316), channel_id=1, source_target_pairs={{8,0},{16,8},{24,16},{0,24},{9,1},{17,9},{25,17},{1,25},{10,2},{18... | collective-permute-start | bytes 786440 | tf_op jit(solution)/shard_map/ppermute | solution.py:41
  426.9 22.2 %collective-permute-start.52 = (bf16[4,2,64,768]{3,2,0,1:T(8,128)(2,1)}, bf16[4,2,64,768]{3,2,0,1:T(8,128)(2,1)}, u32[]{:S(2)}, u32[]{:S(2)}) collective-permute-start(bf16[4,2,64,768]{3,2,0,1:T(8,128)(2,1)} %bitcast.509), channel_id=1, source_target_pairs={{2,0},{0,2},{3,1},{1,3},{6,4},{4,6},{7,5},{5,7},{10,8},{8,10},{11,... | collective-permute-start | bytes 2359304 | tf_op jit(solution)/shard_map/ppermute | solution.py:41
  428.9 20.2 %collective-permute-start.53 = (bf16[4,2,64,768]{3,2,1,0:T(8,128)(2,1)}, bf16[4,2,64,768]{3,2,1,0:T(8,128)(2,1)}, u32[]{:S(2)}, u32[]{:S(2)}) collective-permute-start(bf16[4,2,64,768]{3,2,1,0:T(8,128)(2,1)} %dynamic-slice_bitcast_fusion.2), channel_id=1, source_target_pairs={{4,0},{0,4},{5,1},{1,5},{6,2},{2,6},{7,3},{3,7},{12,8},{8,12},{13,... | collective-permute-start | bytes 2359304 | tf_op jit(solution)/shard_map/ppermute | solution.py:41
  448.3 26.5 %collective-permute-start.58 = (bf16[4,2,64,512]{3,2,1,0:T(8,128)(2,1)}, bf16[4,2,64,512]{3,2,1,0:T(8,128)(2,1)S(1)}, u32[]{:S(2)}, u32[]{:S(2)}) collective-permute-start(bf16[4,2,64,512]{3,2,1,0:T(8,128)(2,1)} %dynamic-slice_bitcast_fusion.4), channel_id=1, source_target_pairs={{2,0},{0,2},{3,1},{1,3},{6,4},{4,6},{7,5},{5,7},{10,8},{8,10},{11,... | collective-permute-start | bytes 1572872 | tf_op jit(solution)/shard_map/ppermute | solution.py:41
  452.6 23.8 %collective-permute-start.54 = (bf16[1024,1536]{1,0:T(8,128)(2,1)S(1)}, bf16[1024,1536]{1,0:T(8,128)(2,1)S(1)}, u32[]{:S(2)}, u32[]{:S(2)}) collective-permute-start(bf16[1024,1536]{1,0:T(8,128)(2,1)S(1)} %convolution_convert_fusion), channel_id=1, source_target_pairs={{1,0},{0,1},{3,2},{2,3},{5,4},{4,5},{7,6},{6,7},{9,8},{8,9},{11,10... | collective-permute-start | bytes 9437192 | tf_op jit(solution)/shard_map/ppermute | solution.py:41
  452.8 22.9 %collective-permute-start.55 = (bf16[2,4,32,512]{3,2,1,0:T(8,128)(2,1)S(1)}, bf16[2,4,32,512]{3,2,1,0:T(8,128)(2,1)S(1)}, u32[]{:S(2)}, u32[]{:S(2)}) collective-permute-start(bf16[2,4,32,512]{3,2,1,0:T(8,128)(2,1)S(1)} %bitcast_dynamic-update-slice_fusion.28), channel_id=1, source_target_pairs={{4,0},{0,4},{5,1},{1,5},{6,2},{2,6},{7,3},{3,7},{12,8},{8,12},{13,... | collective-permute-start | bytes 786440 | tf_op jit(solution)/shard_map/ppermute | solution.py:41
  455.7 20.7 %collective-permute-start.56 = (bf16[4,64,1024]{2,1,0:T(8,128)(2,1)S(1)}, bf16[4,64,1024]{2,1,0:T(8,128)(2,1)S(1)}, u32[]{:S(2)}, u32[]{:S(2)}) collective-permute-start(bf16[4,64,1024]{2,1,0:T(8,128)(2,1)S(1)} %dynamic-slice_bitcast_fusion.6), channel_id=1, source_target_pairs={{2,0},{0,2},{3,1},{1,3},{6,4},{4,6},{7,5},{5,7},{10,8},{8,10},{11,... | collective-permute-start | bytes 1572872 | tf_op jit(solution)/shard_map/ppermute | solution.py:41
  457.6 18.8 %collective-permute-start.57 = (bf16[4,64,1024]{2,1,0:T(8,128)(2,1)S(1)}, bf16[4,64,1024]{2,1,0:T(8,128)(2,1)S(1)}, u32[]{:S(2)}, u32[]{:S(2)}) collective-permute-start(bf16[4,64,1024]{2,1,0:T(8,128)(2,1)S(1)} %dynamic-slice_bitcast_fusion.5), channel_id=1, source_target_pairs={{4,0},{0,4},{5,1},{1,5},{6,2},{2,6},{7,3},{3,7},{12,8},{8,12},{13,... | collective-permute-start | bytes 1572872 | tf_op jit(solution)/shard_map/ppermute | solution.py:41
  474.7 32.2 %collective-permute-start.62 = (bf16[4,64,768]{2,1,0:T(8,128)(2,1)}, bf16[4,64,768]{2,1,0:T(8,128)(2,1)}, u32[]{:S(2)}, u32[]{:S(2)}) collective-permute-start(bf16[4,64,768]{2,1,0:T(8,128)(2,1)} %dynamic-slice_bitcast_fusion.12), channel_id=1, source_target_pairs={{4,0},{0,4},{5,1},{1,5},{6,2},{2,6},{7,3},{3,7},{12,8},{8,12},{13,... | collective-permute-start | bytes 1179656 | tf_op jit(solution)/shard_map/ppermute | solution.py:41
  475.7 33.6 %collective-permute-start.63 = (bf16[4,64,768]{2,1,0:T(8,128)(2,1)}, bf16[4,64,768]{2,1,0:T(8,128)(2,1)}, u32[]{:S(2)}, u32[]{:S(2)}) collective-permute-start(bf16[4,64,768]{2,1,0:T(8,128)(2,1)} %dynamic-slice_bitcast_fusion.11), channel_id=1, source_target_pairs={{2,0},{0,2},{3,1},{1,3},{6,4},{4,6},{7,5},{5,7},{10,8},{8,10},{11,... | collective-permute-start | bytes 1179656 | tf_op jit(solution)/shard_map/ppermute | solution.py:41
  479.8 43.5 %collective-permute-start.59 = (bf16[1024,512]{1,0:T(8,128)(2,1)}, bf16[1024,512]{1,0:T(8,128)(2,1)}, u32[]{:S(2)}, u32[]{:S(2)}) collective-permute-start(bf16[1024,512]{1,0:T(8,128)(2,1)} %fusion.65), channel_id=1, source_target_pairs={{1,0},{0,1},{3,2},{2,3},{5,4},{4,5},{7,6},{6,7},{9,8},{8,9},{11,10... | collective-permute-start | bytes 3145736 | tf_op jit(solution)/shard_map/ppermute | solution.py:41
  484.3 19.5 %collective-permute-start.78 = (bf16[4,2,64,768]{3,2,0,1:T(8,128)(2,1)}, bf16[4,2,64,768]{3,2,0,1:T(8,128)(2,1)}, u32[]{:S(2)}, u32[]{:S(2)}) collective-permute-start(bf16[4,2,64,768]{3,2,0,1:T(8,128)(2,1)} %bitcast.508), channel_id=1, source_target_pairs={{4,0},{0,4},{5,1},{1,5},{6,2},{2,6},{7,3},{3,7},{12,8},{8,12},{13,... | collective-permute-start | bytes 2359304 | tf_op jit(solution)/shard_map/ppermute | solution.py:41
  486.3 19.2 %collective-permute-start.79 = (bf16[4,2,64,768]{3,2,1,0:T(8,128)(2,1)}, bf16[4,2,64,768]{3,2,1,0:T(8,128)(2,1)}, u32[]{:S(2)}, u32[]{:S(2)}) collective-permute-start(bf16[4,2,64,768]{3,2,1,0:T(8,128)(2,1)} %dynamic-slice_bitcast_fusion.1), channel_id=1, source_target_pairs={{2,0},{0,2},{3,1},{1,3},{6,4},{4,6},{7,5},{5,7},{10,8},{8,10},{11,... | collective-permute-start | bytes 2359304 | tf_op jit(solution)/shard_map/ppermute | solution.py:41
  503.8 15.0 %collective-permute-start.65 = (bf16[4,2,64,512]{3,2,1,0:T(8,128)(2,1)}, bf16[4,2,64,512]{3,2,1,0:T(8,128)(2,1)S(1)}, u32[]{:S(2)}, u32[]{:S(2)}) collective-permute-start(bf16[4,2,64,512]{3,2,1,0:T(8,128)(2,1)} %dynamic-slice_bitcast_fusion.3), channel_id=1, source_target_pairs={{4,0},{0,4},{5,1},{1,5},{6,2},{2,6},{7,3},{3,7},{12,8},{8,12},{13,... | collective-permute-start | bytes 1572872 | tf_op jit(solution)/shard_map/ppermute | solution.py:41
  505.5 15.2 %collective-permute-start.61 = (bf16[256,512]{1,0:T(8,128)(2,1)S(1)}, bf16[256,512]{1,0:T(8,128)(2,1)S(1)}, u32[]{:S(2)}, u32[]{:S(2)}) collective-permute-start(bf16[256,512]{1,0:T(8,128)(2,1)S(1)} %dynamic-slice_bitcast_fusion.28), channel_id=1, source_target_pairs={{1,0},{0,1},{3,2},{2,3},{5,4},{4,5},{7,6},{6,7},{9,8},{8,9},{11,10... | collective-permute-start | bytes 786440 | tf_op jit(solution)/shard_map/ppermute | solution.py:41
  506.9 15.5 %collective-permute-start.64 = (bf16[4,64,512]{2,1,0:T(8,128)(2,1)S(1)}, bf16[4,64,512]{2,1,0:T(8,128)(2,1)S(1)}, u32[]{:S(2)}, u32[]{:S(2)}) collective-permute-start(bf16[4,64,512]{2,1,0:T(8,128)(2,1)S(1)} %dynamic-slice_bitcast_fusion.27), channel_id=1, source_target_pairs={{4,0},{0,4},{5,1},{1,5},{6,2},{2,6},{7,3},{3,7},{12,8},{8,12},{13,... | collective-permute-start | bytes 786440 | tf_op jit(solution)/shard_map/ppermute | solution.py:41
  518.8 18.0 %collective-permute-start.68 = (bf16[64,2048]{1,0:T(8,128)(2,1)S(1)}, bf16[64,2048]{1,0:T(8,128)(2,1)S(1)}, u32[]{:S(2)}, u32[]{:S(2)}) collective-permute-start(bf16[64,2048]{1,0:T(8,128)(2,1)S(1)} %copy-done.75), channel_id=1, source_target_pairs={{24,0},{0,8},{8,16},{16,24},{25,1},{1,9},{9,17},{17,25},{26,2},{2,... | collective-permute-start | bytes 786440 | tf_op jit(solution)/shard_map/ppermute | solution.py:41
  519.3 18.6 %collective-permute-start.69 = (bf16[64,2048]{1,0:T(8,128)(2,1)S(1)}, bf16[64,2048]{1,0:T(8,128)(2,1)S(1)}, u32[]{:S(2)}, u32[]{:S(2)}) collective-permute-start(bf16[64,2048]{1,0:T(8,128)(2,1)S(1)} %copy-done.74), channel_id=1, source_target_pairs={{16,0},{24,8},{0,16},{8,24},{17,1},{25,9},{1,17},{9,25},{18,2},{26... | collective-permute-start | bytes 786440 | tf_op jit(solution)/shard_map/ppermute | solution.py:41
  525.6 27.8 %collective-permute-start.66 = (bf16[2,2,4,32,512]{4,3,0,2,1:T(8,128)(2,1)S(1)}, bf16[2,2,4,32,512]{4,3,0,2,1:T(8,128)(2,1)S(1)}, u32[]{:S(2)}, u32[]{:S(2)}) collective-permute-start(bf16[2,2,4,32,512]{4,3,0,2,1:T(8,128)(2,1)S(1)} %bitcast.548), channel_id=1, source_target_pairs={{2,0},{0,2},{3,1},{1,3},{6,4},{4,6},{7,5},{5,7},{10,8},{8,10},{11,... | collective-permute-start | bytes 1572872 | tf_op jit(solution)/shard_map/ppermute | solution.py:41
  535.6 17.9 %collective-permute-start.71 = (bf16[4,64,512]{2,1,0:T(8,128)(2,1)S(1)}, bf16[4,64,512]{2,1,0:T(8,128)(2,1)S(1)}, u32[]{:S(2)}, u32[]{:S(2)}) collective-permute-start(bf16[4,64,512]{2,1,0:T(8,128)(2,1)S(1)} %dynamic-slice_bitcast_fusion.26), channel_id=1, source_target_pairs={{2,0},{0,2},{3,1},{1,3},{6,4},{4,6},{7,5},{5,7},{10,8},{8,10},{11,... | collective-permute-start | bytes 786440 | tf_op jit(solution)/shard_map/ppermute | solution.py:41
  537.9 19.5 %collective-permute-start.75 = (bf16[64,2048]{1,0:T(8,128)(2,1)S(1)}, bf16[64,2048]{1,0:T(8,128)(2,1)S(1)}, u32[]{:S(2)}, u32[]{:S(2)}) collective-permute-start(bf16[64,2048]{1,0:T(8,128)(2,1)S(1)} %get-tuple-element.310), channel_id=1, source_target_pairs={{24,0},{0,8},{8,16},{16,24},{25,1},{1,9},{9,17},{17,25},{26,2},{2,... | collective-permute-start | bytes 786440 | tf_op jit(solution)/shard_map/ppermute | solution.py:41
  543.7 16.4 %collective-permute-start.76 = (bf16[64,2048]{1,0:T(8,128)(2,1)S(1)}, bf16[64,2048]{1,0:T(8,128)(2,1)}, u32[]{:S(2)}, u32[]{:S(2)}) collective-permute-start(bf16[64,2048]{1,0:T(8,128)(2,1)S(1)} %get-tuple-element.309), channel_id=1, source_target_pairs={{16,0},{24,8},{0,16},{8,24},{17,1},{25,9},{1,17},{9,25},{18,2},{26... | collective-permute-start | bytes 786440 | tf_op jit(solution)/shard_map/ppermute | solution.py:41
  550.0 13.8 %collective-permute-start.77 = (bf16[64,2048]{1,0:T(8,128)(2,1)S(1)}, bf16[64,2048]{1,0:T(8,128)(2,1)}, u32[]{:S(2)}, u32[]{:S(2)}) collective-permute-start(bf16[64,2048]{1,0:T(8,128)(2,1)S(1)} %get-tuple-element.308), channel_id=1, source_target_pairs={{8,0},{16,8},{24,16},{0,24},{9,1},{17,9},{25,17},{1,25},{10,2},{18... | collective-permute-start | bytes 786440 | tf_op jit(solution)/shard_map/ppermute | solution.py:41
  560.1 14.2 %collective-permute-start.82 = (bf16[64,2048]{1,0:T(8,128)(2,1)}, bf16[64,2048]{1,0:T(8,128)(2,1)}, u32[]{:S(2)}, u32[]{:S(2)}) collective-permute-start(bf16[64,2048]{1,0:T(8,128)(2,1)} %get-tuple-element.307), channel_id=1, source_target_pairs={{24,0},{0,8},{8,16},{16,24},{25,1},{1,9},{9,17},{17,25},{26,2},{2,... | collective-permute-start | bytes 786440 | tf_op jit(solution)/shard_map/ppermute | solution.py:41
  563.9 21.1 %collective-permute-start.83 = (bf16[64,2048]{1,0:T(8,128)(2,1)}, bf16[64,2048]{1,0:T(8,128)(2,1)}, u32[]{:S(2)}, u32[]{:S(2)}) collective-permute-start(bf16[64,2048]{1,0:T(8,128)(2,1)} %get-tuple-element.306), channel_id=1, source_target_pairs={{16,0},{24,8},{0,16},{8,24},{17,1},{25,9},{1,17},{9,25},{18,2},{26... | collective-permute-start | bytes 786440 | tf_op jit(solution)/shard_map/ppermute | solution.py:41
  567.3 19.2 %collective-permute-start.84 = (bf16[64,2048]{1,0:T(8,128)(2,1)S(1)}, bf16[64,2048]{1,0:T(8,128)(2,1)}, u32[]{:S(2)}, u32[]{:S(2)}) collective-permute-start(bf16[64,2048]{1,0:T(8,128)(2,1)S(1)} %get-tuple-element.305), channel_id=1, source_target_pairs={{8,0},{16,8},{24,16},{0,24},{9,1},{17,9},{25,17},{1,25},{10,2},{18... | collective-permute-start | bytes 786440 | tf_op jit(solution)/shard_map/ppermute | solution.py:41
  567.4 20.2 %collective-permute-start.88 = (f32[5,1024]{1,0:T(8,128)S(1)}, f32[5,1024]{1,0:T(8,128)S(1)}, u32[]{:S(2)}, u32[]{:S(2)}) collective-permute-start(f32[5,1024]{1,0:T(8,128)S(1)} %add.923), channel_id=1, source_target_pairs={{8,0},{16,8},{24,16},{0,24},{9,1},{17,9},{25,17},{1,25},{10,2},{18... | collective-permute-start | bytes 61448 | tf_op jit(solution)/shard_map/ppermute | solution.py:41
  570.6 24.6 %collective-permute-start.91 = (f32[32,2048]{1,0:T(8,128)S(1)}, f32[32,2048]{1,0:T(8,128)}, u32[]{:S(2)}, u32[]{:S(2)}) collective-permute-start(f32[32,2048]{1,0:T(8,128)S(1)} %get-tuple-element.346), channel_id=1, source_target_pairs={{1,0},{0,1},{3,2},{2,3},{5,4},{4,5},{7,6},{6,7},{9,8},{8,9},{11,10... | collective-permute-start | bytes 786440 | tf_op jit(solution)/shard_map/ppermute | solution.py:41
  574.3 15.7 %collective-permute-start.89 = (f32[5,1024]{1,0:T(8,128)S(1)}, f32[5,1024]{1,0:T(8,128)S(1)}, u32[]{:S(2)}, u32[]{:S(2)}) collective-permute-start(f32[5,1024]{1,0:T(8,128)S(1)} %add.923), channel_id=1, source_target_pairs={{16,0},{24,8},{0,16},{8,24},{17,1},{25,9},{1,17},{9,25},{18,2},{26... | collective-permute-start | bytes 61448 | tf_op jit(solution)/shard_map/ppermute | solution.py:41
  (168 other events, 1467.7 us)
Sparse Core Ops, SparseCore 0:
  14.6 159.6 all-gather.1
